TPU v7x, 32 devices: a whole 2x2x4 slice. The times are simulated.
32 devices in a mesh: seq: 8 (over y, x, core), tp: 4 (over z).
Axes of the slice: x: 2, y: 2, z: 4, core: 2. Of those that a mesh axis runs over, the one named last changes fastest.
Arguments:
- layer_input: bfloat16 [4, 2048, 1536], P('tp', 'seq'), may hold values from -6 to 6
- doc_ids: int32 [4, 2048], P('tp', 'seq'), may hold values from 0 to 3, as said below
- positions: int32 [4, 2048], P('tp', 'seq'), may hold values from 0 to 4088, as said below
- first_gain: bfloat16 [1536], P(('seq', 'tp')), may hold values from 0.099609375 to 1.8984375
- query_weight: bfloat16 [1536, 1536], P(('seq', 'tp')), may hold values from -0.15625 to 0.15625
- key_weight: bfloat16 [1536, 768], P(('seq', 'tp')), may hold values from -0.15625 to 0.15625
- value_weight: bfloat16 [1536, 768], P(('seq', 'tp')), may hold values from -0.15625 to 0.15625
- output_weight: bfloat16 [1536, 1536], P(('seq', 'tp')), may hold values from -0.625 to 0.625
- second_gain: bfloat16 [1536], P(('seq', 'tp')), may hold values from 0.099609375 to 1.8984375
- gate_weight: bfloat16 [1536, 4096], P('seq', 'tp'), may hold values from -0.15625 to 0.15625
- up_weight: bfloat16 [1536, 4096], P('seq', 'tp'), may hold values from -0.15625 to 0.15625
- down_weight: bfloat16 [1536, 4096], P('seq', 'tp'), may hold values from -0.09375 to 0.09375
- out_grad: bfloat16 [4, 2048, 1536], P('tp', 'seq'), may hold values from -6 to 6
Outputs:
- layer_output: bfloat16 [4, 2048, 1536], P('tp', 'seq')
- input_grad: float32 [4, 2048, 1536], P('tp', 'seq')
- first_gain_grad: float32 [1536], P(('seq', 'tp'))
- query_grad: float32 [1536, 1536], P(('seq', 'tp'))
- key_grad: float32 [1536, 768], P(('seq', 'tp'))
- value_grad: float32 [1536, 768], P(('seq', 'tp'))
- output_grad: float32 [1536, 1536], P(('seq', 'tp'))
- second_gain_grad: float32 [1536], P(('seq', 'tp'))
- gate_grad: float32 [1536, 4096], P('seq', 'tp')
- up_grad: float32 [1536, 4096], P('seq', 'tp')
- down_grad: float32 [1536, 4096], P('seq', 'tp')
Inputs may be any that keep to these rules, and one draw needn't show every extreme that they name: `doc_ids`: within each sequence the ids never fall, start at 0, and each of 0 to 3 holds one contiguous run of tokens. `positions`: 0 at each document's first token; within a document it rises by 1 or 2 from one token to the next.
All inputs are finite; a program needn't handle non-finite values.
Results may differ from a plain program's by a relative error of at most 0.018.
Values may be sent and summed in bfloat16 or wider, within the bound.
A program may use at most 256 MiB of HBM per device.

v0:
```python
import math

import jax
import jax.numpy as jnp
from jax import lax
from jax.sharding import PartitionSpec as P

QUERY_HEADS = 16
KEY_VALUE_HEADS = 8
HEAD_SIZE = 96


norm_epsilon = 1e-05
rope_base = 100000.0
mask_fill_value = -1e30


def rope_tables(places):
    half = HEAD_SIZE // 2
    inverse = rope_base ** (-(jnp.arange(half, dtype=jnp.float32) * 2.0 / HEAD_SIZE))
    angles = places.astype(jnp.float32)[:, None] * inverse[None, :]
    return (jnp.cos(angles), jnp.sin(angles))


def apply_rotary(value_rows, cosine_table, sine_table, heads, direction):
    sequence_length = value_rows.shape[0]
    split = value_rows.reshape(sequence_length, heads, 2, HEAD_SIZE // 2)
    first = split[:, :, 0]
    second = split[:, :, 1]
    cosine = cosine_table[:, None, :]
    sine = direction * sine_table[:, None, :]
    turned = jnp.stack([first * cosine - second * sine, second * cosine + first * sine], axis=2)
    return turned.reshape(sequence_length, heads * HEAD_SIZE)


def outer_product(left, right):
    return lax.dot_general(
        left, right, (((0,), (0,)), ((), ())), preferred_element_type=jnp.float32
    )


def times_transpose(left, right):
    return lax.dot_general(
        left, right, (((1,), (1,)), ((), ())), preferred_element_type=jnp.float32
    )


def norm_backward(inputs, scale, gain, upstream):
    inner = gain * upstream
    moment = jnp.mean(inputs * inner, axis=1, keepdims=True)
    return (
        scale * inner - inputs * scale * scale * scale * moment,
        jnp.sum(upstream * inputs * scale, axis=0),
    )


def on_device(
    layer_input,
    doc_ids,
    positions,
    first_gain,
    query_weight,
    key_weight,
    value_weight,
    output_weight,
    second_gain,
    gate_weight,
    up_weight,
    down_weight,
    out_grad,
):
    token_rows = layer_input.shape[1]
    query_groups = QUERY_HEADS // KEY_VALUE_HEADS
    scale_of_scores = 1.0 / math.sqrt(HEAD_SIZE)
    inputs_f = layer_input[0].astype(jnp.float32)
    my_docs = doc_ids[0]
    gain_one, query_full, complete_keys, value_full, output_full, gain_two = (
        lax.all_gather(first_gain, ("seq", "tp"), axis=0, tiled=True),
        lax.all_gather(query_weight, ("seq", "tp"), axis=0, tiled=True),
        lax.all_gather(key_weight, ("seq", "tp"), axis=0, tiled=True),
        lax.all_gather(value_weight, ("seq", "tp"), axis=0, tiled=True),
        lax.all_gather(output_weight, ("seq", "tp"), axis=0, tiled=True),
        lax.all_gather(second_gain, ("seq", "tp"), axis=0, tiled=True),
    )
    gain_one_f = gain_one.astype(jnp.float32)
    gain_two_f = gain_two.astype(jnp.float32)
    scale_one = lax.rsqrt(jnp.mean(inputs_f * inputs_f, axis=1, keepdims=True) + norm_epsilon)
    first_normalized = (inputs_f * scale_one * gain_one_f).astype(jnp.bfloat16)
    cosine_table, sine_table = rope_tables(positions[0])
    rotated_query = apply_rotary(
        jnp.dot(first_normalized, query_full, preferred_element_type=jnp.float32),
        cosine_table,
        sine_table,
        QUERY_HEADS,
        1.0,
    ).astype(jnp.bfloat16)
    key_rot = apply_rotary(
        jnp.dot(first_normalized, complete_keys, preferred_element_type=jnp.float32),
        cosine_table,
        sine_table,
        KEY_VALUE_HEADS,
        1.0,
    ).astype(jnp.bfloat16)
    value_low = jnp.dot(first_normalized, value_full, preferred_element_type=jnp.float32).astype(
        jnp.bfloat16
    )
    gathered_keys, gathered_values, doc_all = (
        lax.all_gather(key_rot, "seq", axis=0, tiled=True),
        lax.all_gather(value_low, "seq", axis=0, tiled=True),
        lax.all_gather(my_docs.astype(jnp.bfloat16), "seq", axis=0, tiled=True),
    )
    sequence_length = gathered_keys.shape[0]
    block_number = math.gcd(512, sequence_length)
    block_count = sequence_length // block_number
    query_index = lax.axis_index("seq") * token_rows + jnp.arange(token_rows, dtype=jnp.int32)
    my_doc_f = my_docs.astype(jnp.float32)
    heads_of_query = rotated_query.reshape(token_rows, KEY_VALUE_HEADS, query_groups, HEAD_SIZE)
    layer_entries = (
        gathered_keys.reshape(block_count, block_number, KEY_VALUE_HEADS, HEAD_SIZE),
        gathered_values.reshape(block_count, block_number, KEY_VALUE_HEADS, HEAD_SIZE),
        doc_all.astype(jnp.float32).reshape(block_count, block_number),
        jnp.arange(block_count, dtype=jnp.int32) * block_number,
    )

    def allowed_of(doc_piece, start):
        key_index = start + jnp.arange(block_number, dtype=jnp.int32)
        return (key_index[None, :] <= query_index[:, None]) & (
            doc_piece[None, :] == my_doc_f[:, None]
        )

    def scores_of(key_piece, allowed):
        raw = (
            jnp.einsum(
                "tgrd,kgd->tgrk", heads_of_query, key_piece, preferred_element_type=jnp.float32
            )
            * scale_of_scores
        )
        return jnp.where(allowed[:, None, None, :], raw, mask_fill_value)

    def total_step(carry, item):
        key_piece, value_piece, doc_piece, start = item
        allowed = allowed_of(doc_piece, start)

        def total_work(state):
            top, total = state
            scores = scores_of(key_piece, allowed)
            new_top = jnp.maximum(top, jnp.max(scores, axis=3))
            weights = jnp.where(
                allowed[:, None, None, :], jnp.exp(scores - new_top[..., None]), 0.0
            )
            return (new_top, total * jnp.exp(top - new_top) + jnp.sum(weights, axis=3))

        return (lax.cond(jnp.any(allowed), total_work, lambda state: state, carry), None)

    start_state = (
        jnp.full((token_rows, KEY_VALUE_HEADS, query_groups), mask_fill_value, jnp.float32),
        jnp.zeros((token_rows, KEY_VALUE_HEADS, query_groups), jnp.float32),
    )
    (top, total), unused_result = lax.scan(total_step, start_state, layer_entries)
    log_total = top + jnp.log(total)

    def probs_of(key_piece, allowed):
        scores = scores_of(key_piece, allowed)
        return jnp.where(allowed[:, None, None, :], jnp.exp(scores - log_total[..., None]), 0.0)

    def output_update(accum, item):
        key_piece, value_piece, doc_piece, start = item
        allowed = allowed_of(doc_piece, start)

        def output_work(state):
            probs = probs_of(key_piece, allowed).astype(jnp.bfloat16)
            return state + jnp.einsum(
                "tgrk,kgd->tgrd", probs, value_piece, preferred_element_type=jnp.float32
            )

        return (lax.cond(jnp.any(allowed), output_work, lambda state: state, accum), None)

    heads_output, unused_result = lax.scan(
        output_update,
        jnp.zeros((token_rows, KEY_VALUE_HEADS, query_groups, HEAD_SIZE), jnp.float32),
        layer_entries,
    )
    attn_low = heads_output.reshape(token_rows, QUERY_HEADS * HEAD_SIZE).astype(jnp.bfloat16)
    resid = inputs_f + jnp.dot(attn_low, output_full, preferred_element_type=jnp.float32)
    scale_two = lax.rsqrt(jnp.mean(resid * resid, axis=1, keepdims=True) + norm_epsilon)
    normed_two = (resid * scale_two * gain_two_f).astype(jnp.bfloat16)
    rows_all = lax.all_gather(normed_two, "tp", axis=0, tiled=True)
    gate_cols, up_cols, down_cols = (
        lax.all_gather(gate_weight, "seq", axis=0, tiled=True),
        lax.all_gather(up_weight, "seq", axis=0, tiled=True),
        lax.all_gather(down_weight, "seq", axis=0, tiled=True),
    )
    gate_pre = jnp.dot(rows_all, gate_cols, preferred_element_type=jnp.float32)
    up_pre = jnp.dot(rows_all, up_cols, preferred_element_type=jnp.float32)
    gate_sig = jax.nn.sigmoid(gate_pre)
    gate_act = gate_pre * gate_sig
    hidden = (gate_act * up_pre).astype(jnp.bfloat16)
    mixed = lax.psum_scatter(
        times_transpose(hidden, down_cols).astype(jnp.bfloat16),
        "tp",
        scatter_dimension=0,
        tiled=True,
    ).astype(jnp.float32)
    layer_output = (resid + mixed).astype(jnp.bfloat16)[None]
    grad_low = out_grad[0]
    grad_f = grad_low.astype(jnp.float32)
    grad_all = lax.all_gather(grad_low, "tp", axis=0, tiled=True)
    dhidden = jnp.dot(grad_all, down_cols, preferred_element_type=jnp.float32)
    dgate = (dhidden * up_pre * gate_sig * (1.0 + gate_pre * (1.0 - gate_sig))).astype(jnp.bfloat16)
    dup = (dhidden * gate_act).astype(jnp.bfloat16)
    gate_term = outer_product(rows_all, dgate)
    up_term = outer_product(rows_all, dup)
    down_term_grad = outer_product(grad_all, hidden)
    dnorm_two = lax.psum_scatter(
        (times_transpose(dgate, gate_cols) + times_transpose(dup, up_cols)).astype(jnp.bfloat16),
        "tp",
        scatter_dimension=0,
        tiled=True,
    ).astype(jnp.float32)
    gate_grad, up_grad, down_grad = (
        lax.psum_scatter(
            gate_term.astype(jnp.bfloat16), "seq", scatter_dimension=0, tiled=True
        ).astype(jnp.float32),
        lax.psum_scatter(
            up_term.astype(jnp.bfloat16), "seq", scatter_dimension=0, tiled=True
        ).astype(jnp.float32),
        lax.psum_scatter(
            down_term_grad.astype(jnp.bfloat16), "seq", scatter_dimension=0, tiled=True
        ).astype(jnp.float32),
    )
    resid_part, gain_two_term = norm_backward(resid, scale_two, gain_two_f, dnorm_two)
    dresid = grad_f + resid_part
    dbranch = dresid.astype(jnp.bfloat16)
    output_term = outer_product(attn_low, dbranch)
    heads_gradient = times_transpose(dbranch, output_full).astype(jnp.bfloat16)
    grouped_heads_gradient = heads_gradient.reshape(
        token_rows, KEY_VALUE_HEADS, query_groups, HEAD_SIZE
    )
    delta = jnp.sum(grouped_heads_gradient.astype(jnp.float32) * heads_output, axis=3)

    def gradient_update(dquery, item):
        key_piece, value_piece, doc_piece, start = item
        allowed = allowed_of(doc_piece, start)

        def gradient_work(state):
            probs = probs_of(key_piece, allowed)
            value_piece_grad = jnp.einsum(
                "tgrk,tgrd->kgd",
                probs.astype(jnp.bfloat16),
                grouped_heads_gradient,
                preferred_element_type=jnp.float32,
            )
            prob_grad = jnp.einsum(
                "tgrd,kgd->tgrk",
                grouped_heads_gradient,
                value_piece,
                preferred_element_type=jnp.float32,
            )
            score_grad = (probs * (prob_grad - delta[..., None])).astype(jnp.bfloat16)
            key_piece_grad = jnp.einsum(
                "tgrk,tgrd->kgd", score_grad, heads_of_query, preferred_element_type=jnp.float32
            )
            updated = state + jnp.einsum(
                "tgrk,kgd->tgrd", score_grad, key_piece, preferred_element_type=jnp.float32
            )
            return (updated, (key_piece_grad, value_piece_grad))

        def skip(state):
            blank_tensor = jnp.zeros((block_number, KEY_VALUE_HEADS, HEAD_SIZE), jnp.float32)
            return (state, (blank_tensor, blank_tensor))

        return lax.cond(jnp.any(allowed), gradient_work, skip, dquery)

    dquery, (key_contributions, value_contributions) = lax.scan(
        gradient_update,
        jnp.zeros((token_rows, KEY_VALUE_HEADS, query_groups, HEAD_SIZE), jnp.float32),
        layer_entries,
    )
    gathered_key_contributions = (
        key_contributions.reshape(sequence_length, KEY_VALUE_HEADS * HEAD_SIZE) * scale_of_scores
    )
    gathered_value_contributions = value_contributions.reshape(
        sequence_length, KEY_VALUE_HEADS * HEAD_SIZE
    )
    local_keys, value_mine = (
        lax.psum_scatter(
            gathered_key_contributions.astype(jnp.bfloat16), "seq", scatter_dimension=0, tiled=True
        ).astype(jnp.float32),
        lax.psum_scatter(
            gathered_value_contributions.astype(jnp.bfloat16),
            "seq",
            scatter_dimension=0,
            tiled=True,
        ).astype(jnp.float32),
    )
    dq_pre = apply_rotary(
        dquery.reshape(token_rows, QUERY_HEADS * HEAD_SIZE) * scale_of_scores,
        cosine_table,
        sine_table,
        QUERY_HEADS,
        -1.0,
    ).astype(jnp.bfloat16)
    key_gradient_unrotated = apply_rotary(
        local_keys, cosine_table, sine_table, KEY_VALUE_HEADS, -1.0
    ).astype(jnp.bfloat16)
    dv_pre = value_mine.astype(jnp.bfloat16)
    dnorm_one = (
        times_transpose(dq_pre, query_full)
        + times_transpose(key_gradient_unrotated, complete_keys)
        + times_transpose(dv_pre, value_full)
    )
    input_part, gain_one_term = norm_backward(inputs_f, scale_one, gain_one_f, dnorm_one)
    input_grad = (dresid + input_part)[None]
    query_term = outer_product(first_normalized, dq_pre)
    key_term = outer_product(first_normalized, key_gradient_unrotated)
    value_term = outer_product(first_normalized, dv_pre)
    first_gain_grad, query_grad, key_grad, value_grad, output_grad, second_gain_grad = (
        lax.psum_scatter(gain_one_term, ("seq", "tp"), scatter_dimension=0, tiled=True),
        lax.psum_scatter(query_term, ("seq", "tp"), scatter_dimension=0, tiled=True),
        lax.psum_scatter(key_term, ("seq", "tp"), scatter_dimension=0, tiled=True),
        lax.psum_scatter(value_term, ("seq", "tp"), scatter_dimension=0, tiled=True),
        lax.psum_scatter(output_term, ("seq", "tp"), scatter_dimension=0, tiled=True),
        lax.psum_scatter(gain_two_term, ("seq", "tp"), scatter_dimension=0, tiled=True),
    )
    return (
        layer_output,
        input_grad,
        first_gain_grad,
        query_grad,
        key_grad,
        value_grad,
        output_grad,
        second_gain_grad,
        gate_grad,
        up_grad,
        down_grad,
    )


def solution(mesh):
    return jax.shard_map(
        on_device,
        mesh=mesh,
        in_specs=(
            P("tp", "seq", None),
            P("tp", "seq"),
            P("tp", "seq"),
            P(("seq", "tp")),
            P(("seq", "tp"), None),
            P(("seq", "tp"), None),
            P(("seq", "tp"), None),
            P(("seq", "tp"), None),
            P(("seq", "tp")),
            P("seq", "tp"),
            P("seq", "tp"),
            P("seq", "tp"),
            P("tp", "seq", None),
        ),
        out_specs=(
            P("tp", "seq", None),
            P("tp", "seq", None),
            P(("seq", "tp")),
            P(("seq", "tp"), None),
            P(("seq", "tp"), None),
            P(("seq", "tp"), None),
            P(("seq", "tp"), None),
            P(("seq", "tp")),
            P("seq", "tp"),
            P("seq", "tp"),
            P("seq", "tp"),
        ),
        check_vma=False,
    )
```

profile of v0, /device:TPU:0, one launch (start us, length us, event | category | flops | bytes accessed | tf_op | source)
XLA Modules:
  0.0 1556.3 jit_solution(13443135380987295002)
XLA Ops:
  11.2 42.1 %all-reduce.5 = (bf16[1536]{0:T(1024)(128)(2,1)S(1)}, bf16[1536]{0:T(1024)(128)(2,1)S(1)}) all-reduce(bf16[1536]{0:T(1024)(128)(2,1)S(1)} %dynamic-update-slice, bf16[1536]{0:T(1024)(128)(2,1)S(1)} %dynamic-update-slice.1), channel_id=1, replica_groups=mesh['seq'=8,'tp'=4] {'seq','tp'}, use_global_device_ids=true, to_apply=%add | all-reduce | flops 3072 | bytes 12288
  78.7 51.2 %all-gather.20.cloned.1.call-done = bf16[1536,768]{1,0:T(8,128)(2,1)} async-done(((bf16[48,768]{1,0:T(8,128)(2,1)}), bf16[1536,768]{1,0:T(8,128)(2,1)}) %all-gather.20.cloned.1.call-update) | async-done | bytes 2359312 | tf_op jit(solution)/shard_map/all_gather | solution.py:81
  143.5 51.7 %all-gather.18.cloned.1.call-done = bf16[1536,1536]{1,0:T(8,128)(2,1)} async-done(((bf16[48,1536]{1,0:T(8,128)(2,1)}), bf16[1536,1536]{1,0:T(8,128)(2,1)}) %all-gather.18.cloned.1.call-update) | async-done | bytes 4718608 | tf_op jit(solution)/shard_map/all_gather | solution.py:79
  206.5 22.7 %all-gather.16.cloned.1.call-done = bf16[2048,768]{0,1:T(8,128)(2,1)} async-done(((bf16[256,768]{0,1:T(8,128)(2,1)}), bf16[2048,768]{0,1:T(8,128)(2,1)}) %all-gather.16.cloned.1.call-update) | async-done | bytes 3145744 | tf_op jit(solution)/shard_map/all_gather | solution.py:108
  239.7 24.2 %all-gather.22.cloned.1.call-done = bf16[2048,768]{1,0:T(8,128)(2,1)} async-done(((bf16[256,768]{1,0:T(8,128)(2,1)}), bf16[2048,768]{1,0:T(8,128)(2,1)}) %all-gather.22.cloned.1.call-update) | async-done | bytes 3145744 | tf_op jit(solution)/shard_map/all_gather | solution.py:109
  312.2 17.9 %all-gather.24.cloned.1.call-done = bf16[1536,1536]{1,0:T(8,128)(2,1)} async-done(((bf16[48,1536]{1,0:T(8,128)(2,1)}), bf16[1536,1536]{1,0:T(8,128)(2,1)}) %all-gather.24.cloned.1.call-update) | async-done | bytes 4718608 | tf_op jit(solution)/shard_map/all_gather | solution.py:82
  337.7 25.5 %all-gather.28.cloned.1.call-done = bf16[1536,1024]{1,0:T(8,128)(2,1)} async-done(((bf16[192,1024]{1,0:T(8,128)(2,1)}), bf16[1536,1024]{1,0:T(8,128)(2,1)}) %all-gather.28.cloned.1.call-update) | async-done | bytes 3145744 | tf_op jit(solution)/shard_map/all_gather | solution.py:189
  363.2 65.7 %all-gather.26.cloned.1.call-done = bf16[1024,1536]{1,0:T(8,128)(2,1)} async-done(((bf16[256,1536]{1,0:T(8,128)(2,1)}), bf16[1024,1536]{1,0:T(8,128)(2,1)}) %all-gather.26.cloned.1.call-update) | async-done | bytes 3145744 | tf_op jit(solution)/shard_map/all_gather | solution.py:187
  437.2 24.5 %all-gather.30.cloned.1.call-done = bf16[1536,1024]{1,0:T(8,128)(2,1)} async-done(((bf16[192,1024]{1,0:T(8,128)(2,1)}), bf16[1536,1024]{1,0:T(8,128)(2,1)}) %all-gather.30.cloned.1.call-update) | async-done | bytes 3145744 | tf_op jit(solution)/shard_map/all_gather | solution.py:190
  470.0 56.8 %all-gather.34.cloned.1.call-done = bf16[1,1024,1536]{2,1,0:T(8,128)(2,1)} async-done(((bf16[1,256,1536]{2,1,0:T(8,128)(2,1)}), bf16[1,1024,1536]{2,1,0:T(8,128)(2,1)}) %all-gather.34.cloned.1.call-update) | async-done | bytes 3145744 | tf_op jit(solution)/shard_map/all_gather | solution.py:207
  526.7 32.9 %all-gather.32.cloned.1.call-done = bf16[1536,1024]{1,0:T(8,128)(2,1)} async-done(((bf16[192,1024]{1,0:T(8,128)(2,1)}), bf16[1536,1024]{1,0:T(8,128)(2,1)}) %all-gather.32.cloned.1.call-update) | async-done | bytes 3145744 | tf_op jit(solution)/shard_map/all_gather | solution.py:191
  587.9 52.7 %reduce-scatter.16.cloned.1.call-done = bf16[256,1536]{1,0:T(8,128)(2,1)} async-done(((bf16[1024,1536]{1,0:T(8,128)(2,1)}), bf16[256,1536]{1,0:T(8,128)(2,1)}) %reduce-scatter.16.cloned.1.call-update) | async-done | bytes 786448 | tf_op jit(solution)/shard_map/reduce_scatter | solution.py:214
  642.8 60.5 %reduce-scatter.14.cloned.1.call-done = bf16[256,1536]{1,0:T(8,128)(2,1)} async-done(((bf16[1024,1536]{1,0:T(8,128)(2,1)}), bf16[256,1536]{1,0:T(8,128)(2,1)}) %reduce-scatter.14.cloned.1.call-update) | async-done | bytes 786448 | tf_op jit(solution)/shard_map/reduce_scatter | solution.py:198
  715.1 32.9 %while.47 = (s32[]{:T(128)}, f32[256,8,2,96]{0,3,2,1:T(8,128)}, f32[4,512,8,96]{1,3,2,0:T(8,128)}, bf16[4,512,8,96]{1,3,2,0:T(8,128)(2,1)}, s32[4]{0:T(128)S(1)}...) while((s32[]{:T(128)}, f32[256,8,2,96]{0,3,2,1:T(8,128)}, ...), condition=%wide.region_22.23_spmd.clone, body=%wide.region_18.22_spmd.clone.sunk | while | flops 2039350016 | bytes 68877632 | solution.py:274
  787.9 53.4 %reduce-scatter.18.cloned.1.call-done = bf16[256,768]{0,1:T(8,128)(2,1)} async-done(((bf16[2048,768]{0,1:T(8,128)(2,1)}), bf16[256,768]{0,1:T(8,128)(2,1)}) %reduce-scatter.18.cloned.1.call-update) | async-done | bytes 393232 | tf_op jit(solution)/shard_map/reduce_scatter | solution.py:286
  846.0 45.2 %reduce-scatter.20.cloned.1.call-done = bf16[256,768]{0,1:T(8,128)(2,1)} async-done(((bf16[2048,768]{0,1:T(8,128)(2,1)}), bf16[256,768]{0,1:T(8,128)(2,1)}) %reduce-scatter.20.cloned.1.call-update) | async-done | bytes 393232 | tf_op jit(solution)/shard_map/reduce_scatter | solution.py:289
  909.2 31.5 %reduce-scatter.34.cloned.1.call-done = bf16[192,1024]{1,0:T(8,128)(2,1)} async-done(((bf16[1536,1024]{1,0:T(8,128)(2,1)}), bf16[192,1024]{1,0:T(8,128)(2,1)}) %reduce-scatter.34.cloned.1.call-update) | async-done | bytes 393232
  942.9 47.6 %reduce-scatter.30.cloned.1.call-done = bf16[192,1024]{1,0:T(8,128)(2,1)} async-done(((bf16[1536,1024]{1,0:T(8,128)(2,1)}), bf16[192,1024]{1,0:T(8,128)(2,1)}) %reduce-scatter.30.cloned.1.call-update) | async-done | bytes 393232 | tf_op jit(solution)/shard_map/reduce_scatter | solution.py:221
  992.5 47.5 %reduce-scatter.32.cloned.1.call-done = bf16[192,1024]{1,0:T(8,128)(2,1)} async-done(((bf16[1536,1024]{1,0:T(8,128)(2,1)}), bf16[192,1024]{1,0:T(8,128)(2,1)}) %reduce-scatter.32.cloned.1.call-update) | async-done | bytes 393232 | tf_op jit(solution)/shard_map/reduce_scatter | solution.py:224
  1049.9 39.4 %all-reduce.4 = (f32[1536]{0:T(1024)S(1)}, f32[1536]{0:T(1024)S(1)}) all-reduce(f32[1536]{0:T(1024)S(1)} %get-tuple-element.579, f32[1536]{0:T(1024)S(1)} %copy-done.25), channel_id=8, replica_groups=mesh['seq'=8,'tp'=4] {'seq','tp'}, use_global_device_ids=true, to_apply=%region_27.28.clone | all-reduce | flops 3072 | bytes 24576
  1093.6 60.3 %reduce-scatter.24.cloned.1.call-done = f32[48,768]{1,0:T(8,128)} async-done(((f32[1536,768]{1,0:T(8,128)}), f32[48,768]{1,0:T(8,128)}) %reduce-scatter.24.cloned.1.call-update) | async-done | bytes 147472 | tf_op jit(solution)/shard_map/reduce_scatter | solution.py:320
  1153.9 112.0 %reduce-scatter.26.cloned.1.call-done = f32[48,768]{1,0:T(8,128)} async-done(((f32[1536,768]{1,0:T(8,128)}), f32[48,768]{1,0:T(8,128)}) %reduce-scatter.26.cloned.1.call-update) | async-done | bytes 147472 | tf_op jit(solution)/shard_map/reduce_scatter | solution.py:321
  1265.9 142.2 %reduce-scatter.28.cloned.1.call-done = f32[48,1536]{1,0:T(8,128)} async-done(((f32[1536,1536]{1,0:T(8,128)}), f32[48,1536]{1,0:T(8,128)}) %reduce-scatter.28.cloned.1.call-update) | async-done | bytes 294928 | tf_op jit(solution)/shard_map/reduce_scatter | solution.py:322
  1408.2 140.8 %reduce-scatter.22.cloned.1.call-done = f32[48,1536]{1,0:T(8,128)} async-done(((f32[1536,1536]{1,0:T(8,128)}), f32[48,1536]{1,0:T(8,128)}) %reduce-scatter.22.cloned.1.call-update) | async-done | bytes 294928 | tf_op jit(solution)/shard_map/reduce_scatter | solution.py:319
  (286 shorter events, 338.9 us)
Async XLA Ops:
  7.2 63.7 %all-gather.14.cloned.1.call-start = ((), (), s32[]{:S(2)}) async-start(), calls=%async_computation.11 | async-start | bytes 2433024 | tf_op jit(solution)/shard_map/all_gather | solution.py:80
  7.9 122.0 %all-gather.20.cloned.1.call-start = ((), (), s32[]{:S(2)}) async-start(), calls=%async_computation.14 | async-start | bytes 2433024 | tf_op jit(solution)/shard_map/all_gather | solution.py:81
  8.7 186.5 %all-gather.18.cloned.1.call-start = ((), (), s32[]{:S(2)}) async-start(), calls=%async_computation.13 | async-start | bytes 4866048 | tf_op jit(solution)/shard_map/all_gather | solution.py:79
  9.4 219.8 %all-gather.16.cloned.1.call-start = ((), (), s32[]{:S(2)}) async-start(), calls=%async_computation.12 | async-start | bytes 3538944 | tf_op jit(solution)/shard_map/all_gather | solution.py:108
  53.3 148.8 %copy-start.19 = (f32[1536]{0:T(1024)}, f32[1536]{0:T(1024)S(1)}, u32[]{:S(2)}) copy-start(f32[1536]{0:T(1024)S(1)} %convert_element_type.202) | copy-start | bytes 18436
  56.3 149.9 %copy-start.16 = (f32[256,48]{0,1:T(8,128)}, f32[256,48]{0,1:T(8,128)S(1)}, u32[]{:S(2)}) copy-start(f32[256,48]{0,1:T(8,128)S(1)} %get-tuple-element.676) | copy-start | bytes 147460
  78.6 185.2 %all-gather.22.cloned.1.call-start = ((), (), s32[]{:S(2)}) async-start(), calls=%async_computation.15 | async-start | bytes 3538944 | tf_op jit(solution)/shard_map/all_gather | solution.py:109
  133.2 197.0 %all-gather.24.cloned.1.call-start = ((), (), s32[]{:S(2)}) async-start(), calls=%async_computation.16 | async-start | bytes 4866048 | tf_op jit(solution)/shard_map/all_gather | solution.py:82
  133.8 229.4 %all-gather.28.cloned.1.call-start = ((), (), s32[]{:S(2)}) async-start(), calls=%async_computation.18 | async-start | bytes 3538944 | tf_op jit(solution)/shard_map/all_gather | solution.py:189
  134.5 294.4 %all-gather.26.cloned.1.call-start = ((), (), s32[]{:S(2)}) async-start(), calls=%async_computation.17 | async-start | bytes 3932160 | tf_op jit(solution)/shard_map/all_gather | solution.py:187
  335.4 126.4 %all-gather.30.cloned.1.call-start = ((), (), s32[]{:S(2)}) async-start(), calls=%async_computation.19 | async-start | bytes 3538944 | tf_op jit(solution)/shard_map/all_gather | solution.py:190
  336.1 190.6 %all-gather.34.cloned.1.call-start = ((), (), s32[]{:S(2)}) async-start(), calls=%async_computation.31 | async-start | bytes 3932160 | tf_op jit(solution)/shard_map/all_gather | solution.py:207
  336.7 222.9 %all-gather.32.cloned.1.call-start = ((), (), s32[]{:S(2)}) async-start(), calls=%async_computation.20 | async-start | bytes 3538944 | tf_op jit(solution)/shard_map/all_gather | solution.py:191
  337.4 303.2 %reduce-scatter.16.cloned.1.call-start = ((), (), s32[]{:S(2)}) async-start(), calls=%async_computation.22 | async-start | bytes 3932160 | tf_op jit(solution)/shard_map/reduce_scatter | solution.py:214
  580.2 123.1 %reduce-scatter.14.cloned.1.call-start = ((), (), s32[]{:S(2)}) async-start(), calls=%async_computation.21 | async-start | bytes 3932160 | tf_op jit(solution)/shard_map/reduce_scatter | solution.py:198
  587.9 253.4 %reduce-scatter.18.cloned.1.call-start = ((), (), s32[]{:S(2)}) async-start(), calls=%async_computation.23 | async-start | bytes 3538944 | tf_op jit(solution)/shard_map/reduce_scatter | solution.py:286
  756.9 134.3 %reduce-scatter.20.cloned.1.call-start = ((), (), s32[]{:S(2)}) async-start(), calls=%async_computation.24 | async-start | bytes 3538944 | tf_op jit(solution)/shard_map/reduce_scatter | solution.py:289
  763.9 176.8 %reduce-scatter.34.cloned.1.call-start = ((), (), s32[]{:S(2)}) async-start(), calls=%async_computation.32 | async-start | bytes 3538944
  772.8 217.7 %reduce-scatter.30.cloned.1.call-start = ((), (), s32[]{:S(2)}) async-start(), calls=%async_computation.29 | async-start | bytes 3538944 | tf_op jit(solution)/shard_map/reduce_scatter | solution.py:221
  781.2 258.8 %reduce-scatter.32.cloned.1.call-start = ((), (), s32[]{:S(2)}) async-start(), calls=%async_computation.30 | async-start | bytes 3538944 | tf_op jit(solution)/shard_map/reduce_scatter | solution.py:224
  787.8 366.1 %reduce-scatter.24.cloned.1.call-start = ((), (), s32[]{:S(2)}) async-start(), calls=%async_computation.26 | async-start | bytes 4866048 | tf_op jit(solution)/shard_map/reduce_scatter | solution.py:320
  845.7 420.2 %reduce-scatter.26.cloned.1.call-start = ((), (), s32[]{:S(2)}) async-start(), calls=%async_computation.27 | async-start | bytes 4866048 | tf_op jit(solution)/shard_map/reduce_scatter | solution.py:321
  895.3 512.9 %reduce-scatter.28.cloned.1.call-start = ((), (), s32[]{:S(2)}) async-start(), calls=%async_computation.28 | async-start | bytes 9732096 | tf_op jit(solution)/shard_map/reduce_scatter | solution.py:322
  902.0 647.0 %reduce-scatter.22.cloned.1.call-start = ((), (), s32[]{:S(2)}) async-start(), calls=%async_computation.25 | async-start | bytes 9732096 | tf_op jit(solution)/shard_map/reduce_scatter | solution.py:319
  (30 other events, 780.7 us)
Sparse Core Ops, SparseCore 0:
  10.8 60.0 all-gather.13
  73.7 56.2 all-gather.19
  132.7 62.4 all-gather.17
  197.5 31.6 all-gather.15
  231.5 32.3 all-gather.21
  266.5 63.6 all-gather.23
  332.1 31.1 all-gather.27
  365.4 63.4 all-gather.25
  430.8 30.9 all-gather.29
  463.2 63.4 all-gather.33
  528.6 30.9 all-gather.31
  580.3 60.2 reduce-scatter.15
  642.9 60.2 reduce-scatter.13
  757.0 84.2 reduce-scatter.17
  844.9 46.2 reduce-scatter.19
  894.4 46.1 reduce-scatter.33
  944.3 46.2 reduce-scatter.29
  993.8 46.1 reduce-scatter.31
  1047.0 106.8 reduce-scatter.23
  1159.8 106.0 reduce-scatter.25
  1273.4 134.7 reduce-scatter.27
  1414.7 134.3 reduce-scatter.21
where the time goes:
time: 1560 us
  waiting for transfers between devices  1190 us (76%)
  matrix products  127 us (8%)
  blocking collectives  90.4 us (6%)
  local copies, waits for them, and re-layouts  82.5 us (5%)
  other arithmetic  44 us (3%)
    reduce_scatter x1, waiting for transfers between devices, on_device(): lax.psum_scatter(output_term, ('seq', 'tp'), scatter_dimension=0, tiled=T...  142 us
    reduce_scatter x1, waiting for transfers between devices, on_device(): lax.psum_scatter(query_term, ('seq', 'tp'), scatter_dimension=0, tiled=True)  141 us
    reduce_scatter x1, waiting for transfers between devices, on_device(): lax.psum_scatter(value_term, ('seq', 'tp'), scatter_dimension=0, tiled=True)  112 us
    unnamed x2, blocking collectives  81.6 us
    all_gather x1, waiting for transfers between devices, on_device(): rows_all = lax.all_gather(normed_two, 'tp', axis=0, tiled=True)  65.7 us
    reduce_scatter x1, waiting for transfers between devices, on_device(): lax.psum_scatter(times_transpose(hidden, down_cols).astype(jnp.bfloat16),...  60.5 us
    reduce_scatter x1, waiting for transfers between devices, on_device(): lax.psum_scatter(key_term, ('seq', 'tp'), scatter_dimension=0, tiled=True)  60.3 us
    all_gather x1, waiting for transfers between devices, on_device(): grad_all = lax.all_gather(grad_low, 'tp', axis=0, tiled=True)  56.8 us
  transfers between devices with their start and end apart: 22, of which 22 were waited for; matrix products, arithmetic and copies ran while one was open for 11% of the time, Pallas kernels for 0%

commit v1 on v0

--- a/solution.py
+++ b/solution.py
@@ -1,8 +1,11 @@
+import functools
 import math
 
 import jax
 import jax.numpy as jnp
 from jax import lax
+from jax.experimental import pallas as pl
+from jax.experimental.pallas import tpu as pltpu
 from jax.sharding import PartitionSpec as P
 
 QUERY_HEADS = 16
@@ -337,9 +340,831 @@
     )
 
 
+MESH = pl.DeviceIdType.MESH
+ANY = pl.ANY
+HALF = HEAD_SIZE // 2
+LANES = 128
+SLOT = LANES // 2
+f32 = jnp.float32
+bf16 = jnp.bfloat16
+
+
+class Plane:
+    def __init__(self, n, m):
+        self.n, self.m, self.chips = n, m, n // 2
+        self.s = lax.axis_index("seq")
+        self.t = lax.axis_index("tp")
+        self.q = self.s // 2
+        self.c = lax.rem(self.s, 2)
+
+    def device(self, s):
+        return (s, self.t)
+
+    def sibling(self):
+        return (2 * self.q + 1 - self.c, self.t)
+
+    def ahead(self, k):
+        return lax.rem(self.q + k, self.chips)
+
+    def behind(self, k):
+        return lax.rem(self.q + self.chips - k, self.chips)
+
+    def seq_ahead(self, k):
+        return lax.rem(self.s + k, self.n)
+
+    def seq_behind(self, k):
+        return lax.rem(self.s + self.n - k, self.n)
+
+    def tp_ahead(self, k):
+        return (self.s, lax.rem(self.t + k, self.m))
+
+    def tp_behind(self, k):
+        return lax.rem(self.t + self.m - k, self.m)
+
+
+def enter_plane(plane, with_tp):
+    barrier = pltpu.get_barrier_semaphore()
+    for k in range(1, plane.n):
+        pl.semaphore_signal(
+            barrier, inc=1, device_id=plane.device(plane.seq_ahead(k)), device_id_type=MESH
+        )
+    count = plane.n - 1
+    if with_tp:
+        for k in range(1, plane.m):
+            pl.semaphore_signal(barrier, inc=1, device_id=plane.tp_ahead(k), device_id_type=MESH)
+        count += plane.m - 1
+    pl.semaphore_wait(barrier, count)
+
+
+def remote(src, dst, send, recv, device):
+    return pltpu.make_async_remote_copy(
+        src_ref=src,
+        dst_ref=dst,
+        send_sem=send,
+        recv_sem=recv,
+        device_id=device,
+        device_id_type=MESH,
+    )
+
+
+class Gather:
+    def __init__(self, plane, src, dst, send, recv, local):
+        chips = plane.chips
+        self.own = pltpu.make_async_copy(src, dst.at[plane.s], local)
+        self.out = [remote(src, dst.at[plane.s], send.at[0], recv.at[0], plane.sibling())]
+        self.forward = []
+        for k in range(1, chips):
+            peer = 2 * plane.ahead(k) + plane.c
+            self.out.append(
+                remote(src, dst.at[plane.s], send.at[k], recv.at[k], plane.device(peer))
+            )
+            came = 2 * plane.behind(k) + plane.c
+            self.forward.append(
+                remote(
+                    dst.at[came],
+                    dst.at[came],
+                    send.at[chips - 1 + k],
+                    recv.at[chips - 1 + k],
+                    plane.sibling(),
+                )
+            )
+
+    def start(self):
+        for copy in self.out[1:]:
+            copy.start()
+        self.out[0].start()
+        self.own.start()
+
+    def relay(self):
+        for copy, onward in zip(self.out[1:], self.forward):
+            copy.wait_recv()
+            onward.start()
+
+    def finish(self):
+        self.own.wait()
+        self.out[0].wait()
+        for copy in self.out[1:]:
+            copy.wait_send()
+        for onward in self.forward:
+            onward.wait()
+
+
+def exchange(plane, src_of, dst_of, send, recv, local):
+    own = pltpu.make_async_copy(src_of(plane.s), dst_of(plane.s), local)
+    copies = []
+    for k in range(1, plane.n):
+        peer = plane.seq_ahead(k)
+        copies.append(
+            remote(
+                src_of(peer), dst_of(plane.s), send.at[k - 1], recv.at[k - 1], plane.device(peer)
+            )
+        )
+    return [own] + copies
+
+
+def entry_body(
+    n, m, x, places, wqkv, wg, wu, wd, x_all, places_all, wqkv_all, ffn, sems_x, rem, loc
+):
+    plane = Plane(n, m)
+    enter_plane(plane, True)
+    width = wg.shape[1] // n
+    rows = wg.shape[0]
+    step = n - 1
+    mine = wqkv_all.at[plane.t]
+    a = exchange(
+        plane,
+        lambda i: wqkv.at[i],
+        lambda i: mine.at[i],
+        rem.at[0, 0],
+        rem.at[0, 1],
+        loc.at[0],
+    )
+    b = exchange(
+        plane,
+        lambda i: places,
+        lambda i: places_all.at[i],
+        rem.at[1, 0],
+        rem.at[1, 1],
+        loc.at[1],
+    )
+    gather = Gather(plane, x, x_all, sems_x.at[0], sems_x.at[1], loc.at[2])
+    for copy in a + b:
+        copy.start()
+    gather.start()
+    f = []
+    for j, w in enumerate((wg, wu, wd)):
+        f += exchange(
+            plane,
+            lambda i, w=w: w.at[:, pl.ds(pl.multiple_of(i * width, width), width)],
+            lambda i, j=j: ffn.at[j, pl.ds(pl.multiple_of(i * rows, rows), rows), :],
+            rem.at[2 + j, 0],
+            rem.at[2 + j, 1],
+            loc.at[3 + j],
+        )
+    for copy in f:
+        copy.start()
+    for copy in a:
+        copy.wait()
+    z = []
+    for k in range(1, m):
+        z.append(
+            remote(mine, mine, rem.at[5, 0].at[k - 1], rem.at[5, 1].at[k - 1], plane.tp_ahead(k))
+        )
+    for copy in z:
+        copy.start()
+    gather.relay()
+    for copy in b + f + z:
+        copy.wait()
+    gather.finish()
+
+
+def entry(n, m, x, places, wqkv, wg, wu, wd):
+    rows, width = wg.shape
+    return pl.pallas_call(
+        functools.partial(entry_body, n, m),
+        out_shape=(
+            jax.ShapeDtypeStruct((n,) + x.shape, x.dtype),
+            jax.ShapeDtypeStruct((n,) + places.shape, places.dtype),
+            jax.ShapeDtypeStruct((m,) + wqkv.shape, wqkv.dtype),
+            jax.ShapeDtypeStruct((3, rows * n, width // n), wg.dtype),
+        ),
+        in_specs=[pl.BlockSpec(memory_space=ANY)] * 6,
+        out_specs=[pl.BlockSpec(memory_space=ANY)] * 4,
+        scratch_shapes=[
+            pltpu.SemaphoreType.DMA((2, n)),
+            pltpu.SemaphoreType.DMA((6, 2, n - 1)),
+            pltpu.SemaphoreType.DMA((6,)),
+        ],
+        compiler_params=pltpu.CompilerParams(collective_id=0, has_side_effects=True),
+        cost_estimate=pl.CostEstimate(flops=0, transcendentals=0, bytes_accessed=150_000_000),
+        name="entry",
+    )(x, places, wqkv, wg, wu, wd)
+
+
+def gather_body(n, m, src, dst, sems, loc):
+    plane = Plane(n, m)
+    enter_plane(plane, False)
+    gather = Gather(plane, src, dst, sems.at[0], sems.at[1], loc.at[0])
+    gather.start()
+    gather.relay()
+    gather.finish()
+
+
+def plane_gather(n, m, block, ident):
+    return pl.pallas_call(
+        functools.partial(gather_body, n, m),
+        out_shape=jax.ShapeDtypeStruct((n,) + block.shape, block.dtype),
+        in_specs=[pl.BlockSpec(memory_space=ANY)],
+        out_specs=pl.BlockSpec(memory_space=ANY),
+        scratch_shapes=[pltpu.SemaphoreType.DMA((2, n)), pltpu.SemaphoreType.DMA((1,))],
+        compiler_params=pltpu.CompilerParams(collective_id=ident, has_side_effects=True),
+        cost_estimate=pl.CostEstimate(flops=0, transcendentals=0, bytes_accessed=120_000_000),
+        name="plane_gather",
+    )(block)
+
+
+def swap_body(n, m, src, dst, sems, loc):
+    plane = Plane(n, m)
+    enter_plane(plane, False)
+    copies = exchange(
+        plane, lambda i: src.at[i], lambda i: dst.at[i], sems.at[0], sems.at[1], loc.at[0]
+    )
+    for copy in copies:
+        copy.start()
+    for copy in copies:
+        copy.wait()
+
+
+def plane_swap(n, m, blocks, ident):
+    return pl.pallas_call(
+        functools.partial(swap_body, n, m),
+        out_shape=jax.ShapeDtypeStruct(blocks.shape, blocks.dtype),
+        in_specs=[pl.BlockSpec(memory_space=ANY)],
+        out_specs=pl.BlockSpec(memory_space=ANY),
+        scratch_shapes=[pltpu.SemaphoreType.DMA((2, n - 1)), pltpu.SemaphoreType.DMA((1,))],
+        compiler_params=pltpu.CompilerParams(collective_id=ident, has_side_effects=True),
+        cost_estimate=pl.CostEstimate(flops=0, transcendentals=0, bytes_accessed=40_000_000),
+        name="plane_swap",
+    )(blocks)
+
+
+def final_body(n, m, ffn, qkv, ffn_out, qkv_out, sems, loc):
+    plane = Plane(n, m)
+    enter_plane(plane, False)
+    rows = ffn_out.shape[1]
+    width = ffn.shape[2]
+    a = exchange(
+        plane,
+        lambda i: ffn.at[:, pl.ds(pl.multiple_of(i * rows, rows), rows), :],
+        lambda i: ffn_out.at[:, :, pl.ds(pl.multiple_of(i * width, width), width)],
+        sems.at[0],
+        sems.at[1],
+        loc.at[0],
+    )
+    b = exchange(
+        plane, lambda i: qkv.at[i], lambda i: qkv_out.at[i], sems.at[2], sems.at[3], loc.at[1]
+    )
+    for copy in a + b:
+        copy.start()
+    for copy in a + b:
+        copy.wait()
+
+
+def final_swap(n, m, ffn, qkv, ident):
+    return pl.pallas_call(
+        functools.partial(final_body, n, m),
+        out_shape=(
+            jax.ShapeDtypeStruct((3, ffn.shape[1] // n, ffn.shape[2] * n), ffn.dtype),
+            jax.ShapeDtypeStruct(qkv.shape, qkv.dtype),
+        ),
+        in_specs=[pl.BlockSpec(memory_space=ANY)] * 2,
+        out_specs=[pl.BlockSpec(memory_space=ANY)] * 2,
+        scratch_shapes=[pltpu.SemaphoreType.DMA((4, n - 1)), pltpu.SemaphoreType.DMA((2,))],
+        compiler_params=pltpu.CompilerParams(collective_id=ident, has_side_effects=True),
+        cost_estimate=pl.CostEstimate(flops=0, transcendentals=0, bytes_accessed=40_000_000),
+        name="final_swap",
+    )(ffn, qkv)
+
+
+def reduce_body(n, m, parts, total, pair, near, far, sems, loc):
+    plane = Plane(n, m)
+    enter_plane(plane, False)
+    chips = plane.chips
+    rows = parts.shape[1]
+    order = list(range(1, chips)) + [0]
+    loads, swaps, sends = {}, {}, {}
+    for k in order:
+        chip = plane.ahead(k)
+        swaps[k] = remote(
+            parts.at[2 * chip + 1 - plane.c],
+            near.at[k],
+            sems.at[0, k],
+            sems.at[1, k],
+            plane.sibling(),
+        )
+        loads[k] = pltpu.make_async_copy(parts.at[2 * chip + plane.c], pair.at[k], loc.at[k])
+        swaps[k].start()
+        loads[k].start()
+        if k:
+            sends[k] = remote(
+                pair.at[k],
+                far.at[k - 1],
+                sems.at[2, k],
+                sems.at[3, k],
+                plane.device(2 * chip + plane.c),
+            )
+    tile = 16
+
+    def spans(body):
+        def one(i, carry):
+            body(pl.ds(pl.multiple_of(i * tile, tile), tile))
+            return carry
+
+        lax.fori_loop(0, rows // tile, one, 0)
+
+    for k in order:
+        swaps[k].wait()
+        loads[k].wait()
+        if k:
+
+            def add(at, k=k):
+                both = pair[k, at, :].astype(f32) + near[k, at, :].astype(f32)
+                pair[k, at, :] = both.astype(bf16)
+
+            spans(add)
+            sends[k].start()
+        else:
+
+            def first(at):
+                total[at, :] = pair[0, at, :].astype(f32) + near[0, at, :].astype(f32)
+
+            spans(first)
+    for k in range(1, chips):
+        sends[k].wait()
+
+    def last(at):
+        value = total[at, :]
+        for k in range(1, chips):
+            value = value + far[k - 1, at, :].astype(f32)
+        total[at, :] = value
+
+    spans(last)
+
+
+def plane_reduce(n, m, parts, ident):
+    rows, width = parts.shape[1:]
+    chips = n // 2
+    return pl.pallas_call(
+        functools.partial(reduce_body, n, m),
+        out_shape=jax.ShapeDtypeStruct((rows, width), f32),
+        in_specs=[pl.BlockSpec(memory_space=ANY)],
+        out_specs=pl.BlockSpec(memory_space=pltpu.VMEM),
+        scratch_shapes=[
+            pltpu.VMEM((chips, rows, width), bf16),
+            pltpu.VMEM((chips, rows, width), bf16),
+            pltpu.VMEM((chips - 1, rows, width), bf16),
+            pltpu.SemaphoreType.DMA((4, chips)),
+            pltpu.SemaphoreType.DMA((chips,)),
+        ],
+        compiler_params=pltpu.CompilerParams(
+            collective_id=ident, has_side_effects=True, vmem_limit_bytes=32 << 20
+        ),
+        cost_estimate=pl.CostEstimate(flops=0, transcendentals=0, bytes_accessed=120_000_000),
+        name="plane_reduce",
+    )(parts)
+
+
+def project_body(heads, x, gain, w, cosine, sine, norm, q, k, v):
+    value = x[...].astype(f32)
+    scale = lax.rsqrt(jnp.mean(value * value, axis=1, keepdims=True) + norm_epsilon)
+    low = (value * scale * gain[...]).astype(bf16)
+    norm[...] = low
+    out = jnp.dot(low, w[...], preferred_element_type=f32)
+    cos, sin = cosine[...], sine[...]
+    for h in range(heads + 1):
+        part = out[:, h * LANES : (h + 1) * LANES]
+        turned = (part * cos + pltpu.roll(part, SLOT, 1) * sin).astype(bf16)
+        if h < heads:
+            q[h] = turned
+        else:
+            k[...] = turned
+    v[...] = out[:, (heads + 1) * LANES :].astype(bf16)
+
+
+def project(heads, x_all, gain, w, cosine, sine):
+    length, width = x_all.shape
+    tile = 256
+    wide = w.shape[1]
+    return pl.pallas_call(
+        functools.partial(project_body, heads),
+        grid=(length // tile,),
+        out_shape=(
+            jax.ShapeDtypeStruct((length, width), bf16),
+            jax.ShapeDtypeStruct((heads, length, LANES), bf16),
+            jax.ShapeDtypeStruct((length, LANES), bf16),
+            jax.ShapeDtypeStruct((length, LANES), bf16),
+        ),
+        in_specs=[
+            pl.BlockSpec((tile, width), lambda i: (i, 0)),
+            pl.BlockSpec((1, width), lambda i: (0, 0)),
+            pl.BlockSpec((width, wide), lambda i: (0, 0)),
+            pl.BlockSpec((tile, LANES), lambda i: (i, 0)),
+            pl.BlockSpec((tile, LANES), lambda i: (i, 0)),
+        ],
+        out_specs=[
+            pl.BlockSpec((tile, width), lambda i: (i, 0)),
+            pl.BlockSpec((heads, tile, LANES), lambda i: (0, i, 0)),
+            pl.BlockSpec((tile, LANES), lambda i: (i, 0)),
+            pl.BlockSpec((tile, LANES), lambda i: (i, 0)),
+        ],
+        cost_estimate=pl.CostEstimate(
+            flops=2 * length * width * wide, transcendentals=0, bytes_accessed=18_000_000
+        ),
+        name="project",
+    )(x_all, gain, w, cosine, sine)
+
+
+BLOCK = 512
+NT = (((1,), (1,)), ((), ()))
+LOG2E = 1.4426950408889634
+
+
+def allowed_block(first_key, first_query, begin, causal):
+    keys = first_key + lax.broadcasted_iota(jnp.int32, (BLOCK, BLOCK), 0)
+    ok = keys >= begin
+    if causal:
+        queries = first_query + lax.broadcasted_iota(jnp.int32, (BLOCK, BLOCK), 1)
+        ok = ok & (keys <= queries)
+    return ok
+
+
+def attend_body(factor, q, k, v, begin, o, low, lse, vt, top, total, acc):
+    i = pl.program_id(1)
+
+    @pl.when((i == 0) & (pl.program_id(0) == 0))
+    def _():
+        vt[...] = v[...].astype(f32).T.astype(bf16)
+
+    top[...] = jnp.full_like(top, mask_fill_value)
+    total[...] = jnp.zeros_like(total)
+    acc[...] = jnp.zeros_like(acc)
+    query = q[0]
+    start = begin[...]
+
+    def step(j, causal):
+        at = pl.ds(pl.multiple_of(j * BLOCK, BLOCK), BLOCK)
+        raw = lax.dot_general(k[at, :], query, NT, preferred_element_type=f32)
+        ok = allowed_block(j * BLOCK, i * BLOCK, start, causal)
+        scores = jnp.where(ok, raw * factor, mask_fill_value)
+        new_top = jnp.maximum(top[...], jnp.max(scores, axis=0, keepdims=True))
+        weights = jnp.exp2(scores - new_top)
+        keep = jnp.exp2(top[...] - new_top)
+        total[...] = total[...] * keep + jnp.sum(weights, axis=0, keepdims=True)
+        acc[...] = acc[...] * keep + jnp.dot(
+            vt[:, at], weights.astype(bf16), preferred_element_type=f32
+        )
+        top[...] = new_top
+
+    def loop(j, carry):
+        step(j, False)
+        return carry
+
+    lax.fori_loop(0, i, loop, 0)
+    step(i, True)
+    out = (acc[...] / total[...]).T
+    o[0] = out
+    low[...] = out.astype(bf16)
+    lse[0] = top[...] + jnp.log2(total[...])
+
+
+def attend(factor, q, k, v, begin):
+    heads, length, _ = q.shape
+    blocks = length // BLOCK
+    pairs = heads * BLOCK * BLOCK * blocks * (blocks + 1) // 2
+    return pl.pallas_call(
+        functools.partial(attend_body, factor),
+        grid=(heads, blocks),
+        out_shape=(
+            jax.ShapeDtypeStruct((heads, length, LANES), f32),
+            jax.ShapeDtypeStruct((length, heads * LANES), bf16),
+            jax.ShapeDtypeStruct((heads, 1, length), f32),
+        ),
+        in_specs=[
+            pl.BlockSpec((1, BLOCK, LANES), lambda h, i: (h, i, 0)),
+            pl.BlockSpec((length, LANES), lambda h, i: (0, 0)),
+            pl.BlockSpec((length, LANES), lambda h, i: (0, 0)),
+            pl.BlockSpec((1, BLOCK), lambda h, i: (0, i)),
+        ],
+        out_specs=[
+            pl.BlockSpec((1, BLOCK, LANES), lambda h, i: (h, i, 0)),
+            pl.BlockSpec((BLOCK, LANES), lambda h, i: (i, h)),
+            pl.BlockSpec((1, 1, BLOCK), lambda h, i: (h, 0, i)),
+        ],
+        scratch_shapes=[
+            pltpu.VMEM((LANES, length), bf16),
+            pltpu.VMEM((1, BLOCK), f32),
+            pltpu.VMEM((1, BLOCK), f32),
+            pltpu.VMEM((LANES, BLOCK), f32),
+        ],
+        cost_estimate=pl.CostEstimate(
+            flops=pairs * 4 * LANES * 3, transcendentals=pairs, bytes_accessed=6_000_000
+        ),
+        name="attend",
+    )(q, k, v, begin)
+
+
+def attend_back_body(
+    factor, scale, heads, q, k, v, go, o, lse, begin, cosine, sine, out, kt, dqt, dk, dv, delta
+):
+    h = pl.program_id(0)
+    j = pl.program_id(1)
+    blocks = pl.num_programs(1)
+
+    @pl.when((h == 0) & (j == 0))
+    def _():
+        kt[...] = k[...].astype(f32).T.astype(bf16)
+        dk[...] = jnp.zeros_like(dk)
+        dv[...] = jnp.zeros_like(dv)
+
+    @pl.when(j == 0)
+    def _():
+        dqt[...] = jnp.zeros_like(dqt)
+
+        def deltas(i, carry):
+            at = pl.ds(pl.multiple_of(i * BLOCK, BLOCK), BLOCK)
+            both = (go[at, :].astype(f32) * o[0, at, :]).T
+            delta[:, at] = jnp.sum(both, axis=0, keepdims=True)
+            return carry
+
+        lax.fori_loop(0, blocks, deltas, 0)
+
+    keys_at = pl.ds(pl.multiple_of(j * BLOCK, BLOCK), BLOCK)
+    key = k[keys_at, :]
+    value = v[keys_at, :]
+
+    def step(i, causal):
+        at = pl.ds(pl.multiple_of(i * BLOCK, BLOCK), BLOCK)
+        query = q[0, at, :]
+        raw = lax.dot_general(key, query, NT, preferred_element_type=f32)
+        ok = allowed_block(j * BLOCK, i * BLOCK, begin[:, at], causal)
+        probs = jnp.where(ok, jnp.exp2(raw * factor - lse[0, :, at]), 0.0)
+        grads = go[at, :]
+        dprob = lax.dot_general(value, grads, NT, preferred_element_type=f32)
+        dscore = (probs * (dprob - delta[:, at])).astype(bf16)
+        dv[keys_at, :] += jnp.dot(probs.astype(bf16), grads, preferred_element_type=f32)
+        dk[keys_at, :] += jnp.dot(dscore, query, preferred_element_type=f32)
+        dqt[:, at] += jnp.dot(kt[:, keys_at], dscore, preferred_element_type=f32)
+
+    step(j, True)
+
+    def loop(i, carry):
+        step(i, False)
+        return carry
+
+    lax.fori_loop(j + 1, blocks, loop, 0)
+
+    def unturn(value, at):
+        return value * cosine[at, :] - pltpu.roll(value, SLOT, 1) * sine[at, :]
+
+    @pl.when(j == blocks - 1)
+    def _():
+        def write(i, carry):
+            at = pl.ds(pl.multiple_of(i * BLOCK, BLOCK), BLOCK)
+            got = unturn(dqt[:, at].T * scale, at).astype(bf16)
+            for which in range(heads):
+
+                @pl.when(h == which)
+                def _(which=which):
+                    out[at, which * LANES : (which + 1) * LANES] = got
+
+            return carry
+
+        lax.fori_loop(0, blocks, write, 0)
+
+    @pl.when((h == heads - 1) & (j == blocks - 1))
+    def _():
+        def write(i, carry):
+            at = pl.ds(pl.multiple_of(i * BLOCK, BLOCK), BLOCK)
+            out[at, heads * LANES : (heads + 1) * LANES] = unturn(dk[at, :] * scale, at).astype(
+                bf16
+            )
+            out[at, (heads + 1) * LANES :] = dv[at, :].astype(bf16)
+            return carry
+
+        lax.fori_loop(0, blocks, write, 0)
+
+
+def attend_back(factor, scale, q, k, v, go, o, lse, begin, cosine, sine):
+    heads, length, _ = q.shape
+    blocks = length // BLOCK
+    pairs = heads * BLOCK * BLOCK * blocks * (blocks + 1) // 2
+    whole = pl.BlockSpec((length, LANES), lambda h, j: (0, 0))
+    one = pl.BlockSpec((1, length, LANES), lambda h, j: (h, 0, 0))
+    return pl.pallas_call(
+        functools.partial(attend_back_body, factor, scale, heads),
+        grid=(heads, blocks),
+        out_shape=jax.ShapeDtypeStruct((length, (heads + 2) * LANES), bf16),
+        in_specs=[
+            one,
+            whole,
+            whole,
+            pl.BlockSpec((length, LANES), lambda h, j: (0, h)),
+            one,
+            pl.BlockSpec((1, 1, length), lambda h, j: (h, 0, 0)),
+            pl.BlockSpec((1, length), lambda h, j: (0, 0)),
+            whole,
+            whole,
+        ],
+        out_specs=pl.BlockSpec((length, (heads + 2) * LANES), lambda h, j: (0, 0)),
+        scratch_shapes=[
+            pltpu.VMEM((LANES, length), bf16),
+            pltpu.VMEM((LANES, length), f32),
+            pltpu.VMEM((length, LANES), f32),
+            pltpu.VMEM((length, LANES), f32),
+            pltpu.VMEM((1, length), f32),
+        ],
+        cost_estimate=pl.CostEstimate(
+            flops=pairs * 10 * LANES * 2, transcendentals=pairs, bytes_accessed=12_000_000
+        ),
+        name="attend_back",
+    )(q, k, v, go, o, lse, begin, cosine, sine)
+
+
+def split_heads(w, groups):
+    rows = w.shape[0]
+    return w.reshape(rows, groups, -1).transpose(1, 0, 2)
+
+
+def spread(blocks):
+    lead = blocks.shape[:-1]
+    halves = blocks.reshape(lead + (-1, HALF))
+    pad = [(0, 0)] * len(lead) + [(0, 0), (0, SLOT - HALF)]
+    wide = jnp.pad(halves, pad)
+    return wide.reshape(lead + (-1,))
+
+
+def gathered(wide):
+    lead = wide.shape[:-1]
+    halves = wide.reshape(lead + (-1, SLOT))[..., :HALF]
+    return halves.reshape(lead + (-1,))
+
+
+def fast_layer(n, m):
+    def on_plane(
+        layer_input,
+        doc_ids,
+        positions,
+        first_gain,
+        query_weight,
+        key_weight,
+        value_weight,
+        output_weight,
+        second_gain,
+        gate_weight,
+        up_weight,
+        down_weight,
+        out_grad,
+    ):
+        x = layer_input[0]
+        rows, width = x.shape
+        length = rows * n
+        heads = QUERY_HEADS // n
+        scale = 1.0 / math.sqrt(HEAD_SIZE)
+        factor = scale * LOG2E
+        strip = query_weight.shape[0]
+        hid = gate_weight.shape[1] // n
+
+        packed = jnp.concatenate(
+            [split_heads(w, n) for w in (query_weight, key_weight, value_weight)], axis=2
+        )
+        cols = packed.shape[2]
+        gains = jnp.concatenate([first_gain, second_gain])
+        gain_rows = jnp.pad(gains[None, :], ((0, 7), (0, cols - 2 * strip)))
+        packed = jnp.concatenate(
+            [packed, jnp.broadcast_to(gain_rows[None], (n, 8, cols))], axis=1
+        )
+        places = jnp.concatenate([doc_ids, positions], axis=0)
+        output_full = lax.all_gather(output_weight, ("seq", "tp"), axis=0, tiled=True)
+
+        x_all, places_all, w_all, ffn_mine = entry(
+            n, m, x, places, packed, gate_weight, up_weight, down_weight
+        )
+        ffn_all = lax.all_gather(ffn_mine, "tp", axis=0, tiled=False)
+        x_all = x_all.reshape(length, width)
+        docs = places_all[:, 0].reshape(1, length)
+        places_seq = places_all[:, 1].reshape(length, 1).astype(f32)
+
+        ordered = w_all.transpose(1, 0, 2, 3)
+        wqkv = spread(ordered[:, :, :strip].reshape(width, cols))
+        gain_one = ordered[:, :, strip, :strip].reshape(1, width).astype(f32)
+        gain_two = ordered[:, :, strip, strip : 2 * strip].reshape(1, width).astype(f32)
+
+        lane = jnp.arange(SLOT)
+        inverse = jnp.where(
+            lane < HALF, rope_base ** (-(lane.astype(f32) * 2.0 / HEAD_SIZE)), 0.0
+        )
+        angles = places_seq * inverse[None, :]
+        cos, sin = jnp.cos(angles), jnp.sin(angles)
+        cosine = jnp.concatenate([cos, cos], axis=1)
+        sine = jnp.concatenate([-sin, sin], axis=1)
+        begin = jnp.zeros((1, length), jnp.int32)
+        for d in range(3):
+            begin = begin + jnp.where(docs > d, jnp.sum((docs == d).astype(jnp.int32)), 0)
+
+        norm_one, q, k, v = project(heads, x_all, gain_one, wqkv, cosine, sine)
+        o, low, lse = attend(factor, q, k, v, begin)
+        mine = plane_swap(n, m, low.reshape(n, rows, heads * LANES), 1)
+        attn_low = gathered(mine.transpose(1, 0, 2).reshape(rows, n * heads * LANES))
+
+        x_f = x.astype(f32)
+        resid = x_f + jnp.dot(attn_low, output_full, preferred_element_type=f32)
+        scale_two = lax.rsqrt(jnp.mean(resid * resid, axis=1, keepdims=True) + norm_epsilon)
+        norm_two = (resid * scale_two * gain_two).astype(bf16)
+        rows_all = plane_gather(n, m, norm_two, 2).reshape(length, width)
+        grad_low = out_grad[0]
+        grad_all = lax.all_gather(grad_low, "seq", axis=0, tiled=True)
+
+        gate_w, up_w, down_w = [
+            ffn_all[:, i].transpose(1, 0, 2).reshape(width, m * hid) for i in range(3)
+        ]
+        gate_pre = jnp.dot(rows_all, gate_w, preferred_element_type=f32)
+        up_pre = jnp.dot(rows_all, up_w, preferred_element_type=f32)
+        gate_sig = jax.nn.sigmoid(gate_pre)
+        gate_act = gate_pre * gate_sig
+        hidden = (gate_act * up_pre).astype(bf16)
+        mixed = times_transpose(hidden, down_w).astype(bf16)
+        dhidden = jnp.dot(grad_all, down_w, preferred_element_type=f32)
+        dgate = (dhidden * up_pre * gate_sig * (1.0 + gate_pre * (1.0 - gate_sig))).astype(bf16)
+        dup = (dhidden * gate_act).astype(bf16)
+        dnorm_part = (times_transpose(dgate, gate_w) + times_transpose(dup, up_w)).astype(bf16)
+        dnorm_two = plane_reduce(n, m, dnorm_part.reshape(n, rows, width), 3)
+
+        terms = [
+            outer_product(a, b).astype(bf16).reshape(width, m, hid).transpose(1, 0, 2)
+            for a, b in ((rows_all, dgate), (rows_all, dup), (grad_all, hidden))
+        ]
+        ffn_terms = jnp.stack(terms, axis=1)
+        ffn_sum = lax.psum_scatter(ffn_terms, "tp", scatter_dimension=0, tiled=False)
+
+        mixed_sum = plane_reduce(n, m, mixed.reshape(n, rows, width), 4)
+        layer_output = (resid + mixed_sum).astype(bf16)[None]
+
+        inner = gain_two * dnorm_two
+        moment = jnp.mean(resid * inner, axis=1, keepdims=True)
+        dresid = (
+            grad_low.astype(f32)
+            + scale_two * inner
+            - resid * scale_two * scale_two * scale_two * moment
+        )
+        dbranch = dresid.astype(bf16)
+        output_term = outer_product(attn_low, dbranch)
+        output_grad = lax.psum_scatter(
+            output_term.astype(bf16), ("seq", "tp"), scatter_dimension=0, tiled=True
+        ).astype(f32)
+        dheads = spread(times_transpose(dbranch, output_full).astype(bf16))
+        dheads = dheads.reshape(rows, n, heads * LANES).transpose(1, 0, 2)
+        go = plane_swap(n, m, dheads, 5).reshape(length, heads * LANES)
+
+        dqkv = attend_back(factor, scale, q, k, v, go, o, lse, begin, cosine, sine)
+        dnorm_one_part = times_transpose(dqkv, wqkv).astype(bf16)
+        qkv_term = gathered(outer_product(norm_one, dqkv).astype(bf16))
+        qkv_term = qkv_term.reshape(n, m, strip, cols).transpose(1, 0, 2, 3)
+        qkv_sum = lax.psum_scatter(qkv_term, "tp", scatter_dimension=0, tiled=False)
+        dnorm_one = plane_reduce(n, m, dnorm_one_part.reshape(n, rows, width), 6)
+
+        scale_one = lax.rsqrt(jnp.mean(x_f * x_f, axis=1, keepdims=True) + norm_epsilon)
+        inner = gain_one * dnorm_one
+        moment = jnp.mean(x_f * inner, axis=1, keepdims=True)
+        input_grad = (
+            dresid + scale_one * inner - x_f * scale_one * scale_one * scale_one * moment
+        )[None]
+
+        ffn_out, qkv_out = final_swap(n, m, ffn_sum, qkv_sum, 7)
+        gate_grad, up_grad, down_grad = [ffn_out[i].astype(f32) for i in range(3)]
+        kv = HEAD_SIZE * KEY_VALUE_HEADS // n
+        split = heads * HEAD_SIZE
+
+        def columns(a, b):
+            return qkv_out[:, :, a:b].transpose(1, 0, 2).reshape(strip, -1).astype(f32)
+
+        query_grad = columns(0, split)
+        key_grad = columns(split, split + kv)
+        value_grad = columns(split + kv, cols)
+
+        one = (
+            jnp.sum(query_weight.astype(f32) * query_grad, axis=1)
+            + jnp.sum(key_weight.astype(f32) * key_grad, axis=1)
+            + jnp.sum(value_weight.astype(f32) * value_grad, axis=1)
+        )
+        first_gain_grad = one / first_gain.astype(f32)
+        two = jnp.sum(
+            gate_weight.astype(f32) * gate_grad + up_weight.astype(f32) * up_grad, axis=1
+        )
+        second_gain_grad = lax.psum_scatter(
+            two, "tp", scatter_dimension=0, tiled=True
+        ) / second_gain.astype(f32)
+        return (
+            layer_output,
+            input_grad,
+            first_gain_grad,
+            query_grad,
+            key_grad,
+            value_grad,
+            output_grad,
+            second_gain_grad,
+            gate_grad,
+            up_grad,
+            down_grad,
+        )
+
+    return on_plane
+
+
 def solution(mesh):
+    n, m = mesh.shape["seq"], mesh.shape["tp"]
+    fits = KEY_VALUE_HEADS == n
     return jax.shard_map(
-        on_device,
+        fast_layer(n, m) if fits else on_device,
         mesh=mesh,
         in_specs=(
             P("tp", "seq", None),

time: 1560 us -> 694 us (0.44)
  waiting for transfers between devices: 1190 us -> 135 us
  Pallas kernels: 0 us -> 337 us
  blocking collectives: 90.4 us -> 11.2 us
  matrix products: 127 us -> 90.1 us
  local copies, waits for them, and re-layouts: 82.5 us -> 63.1 us
    reduce_scatter x10 -> x3, waiting for transfers between devices: 762 us -> 61.8 us  [the longest x1 61.8 us: on_plane(): lax.psum_scatter(ffn_terms, 'tp', scatter_dimension=0, tiled=False)]
    pallas_call x0 -> x11, Pallas kernels: none -> 337 us  [the longest x3 124 us: plane_reduce(): pl.pallas_call(functools.partial(reduce_body, n, m), out_shape=jax.ShapeD...]
    all_gather x11 -> x3, waiting for transfers between devices: 388 us -> 71.4 us  [the longest x1 53.5 us: on_plane(): lax.all_gather(output_weight, ('seq', 'tp'), axis=0, tiled=True)]
    unnamed x2 -> x1, blocking collectives: 81.6 us -> 11.2 us
    unnamed x23 -> x6, waiting for transfers between devices: 36.9 us -> 1.44 us
    dot_general x14 -> x4, matrix products: 62.2 us -> 28.8 us  [the longest x1 11.1 us: on_plane(): dhidden = jnp.dot(grad_all, down_w, preferred_element_type=f32)]
    unnamed x73 -> x57, local copies, waits for them, and re-layouts: 33.4 us -> 15.8 us
    dot_general x7 -> x5, matrix products: 36.4 us -> 34.8 us  [outer_product(): lax.dot_general(left, right, (((0,), (0,)), ((), ())), preferred_element_...]
  transfers between devices with their start and end apart: 22 -> 6, of which waited for: 22 -> 3; matrix products, arithmetic and copies ran while one was open for 11% -> 20% of each run, Pallas kernels for 0% -> 26%
where the time goes in v1:
time: 694 us; the launch traced here: 683 us
  Pallas kernels  337 us (49%)
  waiting for transfers between devices  135 us (19%)
  matrix products  90.1 us (13%)
  local copies, waits for them, and re-layouts  63.1 us (9%)
  other arithmetic  31.3 us (5%)
  between operations  15.7 us (2%)
  blocking collectives  11.2 us (2%)
    pallas_call x3, Pallas kernels, plane_reduce(): pl.pallas_call(functools.partial(reduce_body, n, m), out_shape=jax.ShapeD...  124 us
    reduce_scatter x1, waiting for transfers between devices, on_plane(): lax.psum_scatter(ffn_terms, 'tp', scatter_dimension=0, tiled=False)  61.8 us
    pallas_call x1, Pallas kernels, entry(): pl.pallas_call(functools.partial(entry_body, n, m), out_shape=(jax.ShapeD...  57.9 us
    all_gather x1, waiting for transfers between devices, on_plane(): lax.all_gather(output_weight, ('seq', 'tp'), axis=0, tiled=True)  53.5 us
    pallas_call x1, Pallas kernels, plane_gather(): pl.pallas_call(functools.partial(gather_body, n, m), out_shape=jax.ShapeD...  51.9 us
    dot_general x5, matrix products, outer_product(): lax.dot_general(left, right, (((0,), (0,)), ((), ())), preferred_element_...  34.8 us
    pallas_call x2, Pallas kernels, plane_swap(): pl.pallas_call(functools.partial(swap_body, n, m), out_shape=jax.ShapeDty...  28.3 us
    dot_general x5, matrix products, times_transpose(): lax.dot_general(left, right, (((1,), (1,)), ((), ())), preferred_element_...  26.4 us
  transfers between devices with their start and end apart: 6, of which 3 were waited for; matrix products, arithmetic and copies ran while one was open for 20% of the time, Pallas kernels for 26%

profile of v1, /device:TPU:0, one launch (start us, length us, event | category | flops | bytes accessed | tf_op | source)
XLA Modules:
  0.0 683.3 jit_solution(8343568927894721588)
XLA Ops:
  13.4 57.9 %entry.1 = (bf16[8,256,1536]{2,1,0:T(8,128)(2,1)}, s32[8,2,256]{2,1,0:T(2,128)}, bf16[4,8,56,384]{3,2,1,0:T(8,128)(2,1)}, bf16[3,1536,128]{2,1,0:T(8,128)(2,1)}) custom-call(bf16[256,1536]{1,0:T(8,128)(2,1)} %bitcast.149, s32[2,256]{1,0:T(2,128)} %pad_add_fusion.places, bf16[8,56,384]{2,1,0:T(8,128)(2,1)} %pad_maximum_fusion.3.wqkv, bf16[192,1024]{1,0:T(8,128)(2,1)} %wg.1, ...), custom_call_target="tpu_custom_call" | custom-call | bytes 150000000 | tf_op jit(solution)/shard_map/entry/pallas_call | solution.py:523
  79.6 6.4 reshape.284
  98.7 11.0 %project.1 = (bf16[2048,1536]{1,0:T(8,128)(2,1)}, bf16[2,2048,128]{2,1,0:T(8,128)(2,1)}, bf16[2048,128]{1,0:T(8,128)(2,1)}, bf16[2048,128]{1,0:T(8,128)(2,1)}) custom-call(bf16[2048,1536]{1,0:T(8,128)(2,1)} %bitcast.186, f32[1,1536]{1,0:T(1,128)} %reshape.271.gain, bf16[1536,512]{1,0:T(8,128)(2,1)} %copy.101.w, f32[2048,128]{1,0:T(8,128)} %pad_maximum_fusion.1.cosine, ...), custom_call_target="tpu_custom_call" | custom-call | flops 3221225472 | bytes 18000000 | tf_op jit(solution)/shard_map/project/pallas_call | solution.py:738
  109.7 17.8 %attend.1 = (f32[2,2048,128]{2,1,0:T(8,128)}, bf16[2048,256]{1,0:T(8,128)(2,1)}, f32[2,1,2048]{2,1,0:T(1,128)}) custom-call(bf16[2,2048,128]{2,1,0:T(8,128)(2,1)} %get-tuple-element.27.q, bf16[2048,128]{1,0:T(8,128)(2,1)} %get-tuple-element.28.k, bf16[2048,128]{1,0:T(8,128)(2,1)} %get-tuple-element.29.v, s32[1,2048]{1,0:T(1,128)} %bitcast.184), custom_call_target="tpu_custom_call" | custom-call | flops 8053063680 | bytes 6000000 | tf_op jit(solution)/shard_map/attend/pallas_call | solution.py:824
  127.6 13.7 %plane_swap.2 = bf16[8,256,256]{2,1,0:T(8,128)(2,1)} custom-call(bf16[8,256,256]{2,1,0:T(8,128)(2,1)} %bitcast.179), custom_call_target="tpu_custom_call" | custom-call | bytes 40000000 | tf_op jit(solution)/shard_map/plane_swap/pallas_call | solution.py:579
  142.8 17.9 %all-gather.8.cloned.1.call-done = bf16[12,1536,128]{2,1,0:T(8,128)(2,1)} async-done(((bf16[3,1536,128]{2,1,0:T(8,128)(2,1)}), bf16[12,1536,128]{2,1,0:T(8,128)(2,1)}) %all-gather.8.cloned.1.call-update) | async-done | bytes 4718608 | tf_op jit(solution)/shard_map/all_gather | solution.py:1032
  172.1 53.5 %all-gather.6.cloned.1.call-done = bf16[1536,1536]{1,0:T(8,128)(2,1)} async-done(((bf16[48,1536]{1,0:T(8,128)(2,1)}), bf16[1536,1536]{1,0:T(8,128)(2,1)}) %all-gather.6.cloned.1.call-update) | async-done | bytes 4718608 | tf_op jit(solution)/shard_map/all_gather | solution.py:1027
  230.5 51.9 %plane_gather.1 = bf16[8,256,1536]{2,1,0:T(8,128)(2,1)} custom-call(bf16[256,1536]{1,0:T(8,128)(2,1)} %multiply_convert_fusion.1.src), custom_call_target="tpu_custom_call" | custom-call | bytes 120000000 | tf_op jit(solution)/shard_map/plane_gather/pallas_call | solution.py:554
  282.4 8.9 %fusion.33 = f32[2048,512]{1,0:T(8,128)} fusion(bf16[2048,1536]{1,0:T(8,128)(2,1)} %bitcast.150, bf16[1536,512]{0,1:T(8,128)(2,1)} %bitcast.166), kind=kOutput, calls=%fused_computation.93 | convolution fusion | flops 3221225472 | bytes 12058624 | tf_op jit(solution)/shard_map/dot_general | solution.py:1071
  296.4 11.1 %fusion.7 = (bf16[2048,512]{1,0:T(8,128)(2,1)S(1)}, bf16[2048,512]{1,0:T(8,128)(2,1)S(1)}, bf16[2048,512]{1,0:T(8,128)(2,1)S(1)}) fusion(f32[2048,512]{1,0:T(8,128)} %fusion.32, f32[2048,512]{1,0:T(8,128)} %fusion.33, bf16[1536,512]{0,1:T(8,128)(2,1)} %bitcast.168, bf16[1,2048,1536]{2,1,0:T(8,128)(2,1)} %all-gather.10.cloned.1.call-done), kind=kOutput, calls=%fused_computation.14 | convolution fusion | flops 3236954112 | bytes 22544384 | tf_op jit(solution)/shard_map/dot_general | solution.py:1076
  311.2 41.2 %plane_reduce.3 = f32[256,1536]{1,0:T(8,128)S(1)} custom-call(bf16[8,256,1536]{2,1,0:T(8,128)(2,1)S(1)} %bitcast.146), custom_call_target="tpu_custom_call" | custom-call | bytes 120000000 | tf_op jit(solution)/shard_map/plane_reduce/pallas_call | solution.py:697
  352.4 6.3 fusion.34
  358.7 6.4 add_convert_fusion
  365.1 40.9 %plane_reduce.4 = f32[256,1536]{1,0:T(8,128)S(1)} custom-call(bf16[8,256,1536]{2,1,0:T(8,128)(2,1)S(1)} %bitcast.144), custom_call_target="tpu_custom_call" | custom-call | bytes 120000000 | tf_op jit(solution)/shard_map/plane_reduce/pallas_call | solution.py:697
  424.4 14.5 %plane_swap.3 = bf16[8,256,256]{2,1,0:T(8,128)(2,1)} custom-call(bf16[8,256,256]{2,1,0:T(8,128)(2,1)} %bitcast.163), custom_call_target="tpu_custom_call" | custom-call | bytes 40000000 | tf_op jit(solution)/shard_map/plane_swap/pallas_call | solution.py:579
  439.0 26.4 %attend_back.1 = bf16[2048,512]{1,0:T(8,128)(2,1)} custom-call(bf16[2,2048,128]{2,1,0:T(8,128)(2,1)} %get-tuple-element.27.q, bf16[2048,128]{1,0:T(8,128)(2,1)} %get-tuple-element.28.k, bf16[2048,128]{1,0:T(8,128)(2,1)} %get-tuple-element.29.v, bf16[2048,256]{1,0:T(8,128)(2,1)} %bitcast.178, f32[2,2048,128]{2,1,0:T(8,128)} %get-tuple-element.32.o, ...), custom_call_target="tpu_custom_call" | custom-call | flops 13421772800 | bytes 12000000 | tf_op jit(solution)/shard_map/attend_back/pallas_call | solution.py:943
  465.3 6.9 %convolution_convert_fusion.3 = bf16[1536,512]{0,1:T(8,128)(2,1)S(1)} fusion(bf16[2048,1536]{1,0:T(8,128)(2,1)} %get-tuple-element.34, bf16[2048,512]{1,0:T(8,128)(2,1)} %attend_back.1), kind=kOutput, calls=%fused_computation.19 | convolution fusion | flops 3222011904 | bytes 9961472 | tf_op jit(solution)/shard_map/dot_general | solution.py:40
  484.8 8.3 %fusion.9 = bf16[512,1536]{1,0:T(8,128)(2,1)} fusion(bf16[2048,512]{1,0:T(8,128)(2,1)} %copy-done.26, bf16[1,2048,1536]{2,1,0:T(8,128)(2,1)} %all-gather.10.cloned.1.call-done), kind=kOutput, calls=%fused_computation.18 | convolution fusion | flops 3222011904 | bytes 9961472 | tf_op jit(solution)/shard_map/dot_general | solution.py:40
  495.9 8.1 %convolution_convert_fusion.5 = bf16[1536,512]{0,1:T(8,128)(2,1)} fusion(bf16[2048,1536]{1,0:T(8,128)(2,1)} %bitcast.151, bf16[2048,512]{1,0:T(8,128)(2,1)} %copy-done.24), kind=kOutput, calls=%fused_computation.21 | convolution fusion | flops 3222011904 | bytes 9961472 | tf_op jit(solution)/shard_map/dot_general | solution.py:40
  506.6 8.0 %convolution_convert_fusion.4 = bf16[1536,512]{0,1:T(8,128)(2,1)} fusion(bf16[2048,1536]{1,0:T(8,128)(2,1)} %bitcast.152, bf16[2048,512]{1,0:T(8,128)(2,1)} %copy-done.25), kind=kOutput, calls=%fused_computation.20 | convolution fusion | flops 3222011904 | bytes 9961472 | tf_op jit(solution)/shard_map/dot_general | solution.py:40
  529.7 41.7 %plane_reduce.5 = f32[256,1536]{1,0:T(8,128)S(1)} custom-call(bf16[8,256,1536]{2,1,0:T(8,128)(2,1)S(1)} %bitcast.145), custom_call_target="tpu_custom_call" | custom-call | bytes 120000000 | tf_op jit(solution)/shard_map/plane_reduce/pallas_call | solution.py:697
  575.2 61.8 %reduce-scatter.4.cloned.1.call-done = bf16[1,3,1536,128]{3,2,1,0:T(8,128)(2,1)} async-done(((bf16[4,3,1536,128]{3,2,1,0:T(8,128)(2,1)}), bf16[1,3,1536,128]{3,2,1,0:T(8,128)(2,1)}) %reduce-scatter.4.cloned.1.call-update) | async-done | bytes 1179664 | tf_op jit(solution)/shard_map/reduce_scatter | solution.py:1087
  636.9 20.0 %final_swap.1 = (bf16[3,192,1024]{2,1,0:T(8,128)(2,1)}, bf16[8,48,384]{2,1,0:T(8,128)(2,1)}) custom-call(bf16[3,1536,128]{2,1,0:T(8,128)(2,1)} %bitcast.175, bf16[8,48,384]{2,1,0:T(8,128)(2,1)} %bitcast.182), custom_call_target="tpu_custom_call" | custom-call | bytes 40000000 | tf_op jit(solution)/shard_map/final_swap/pallas_call | solution.py:614
  663.8 11.2 %all-reduce.3 = f32[192]{0:T(256)S(1)} all-reduce(f32[192]{0:T(256)S(1)} %get-tuple-element.42), channel_id=7, replica_groups=mesh['seq'=8,'tp'=4] {'tp'}, use_global_device_ids=true, to_apply=%region_14.15.clone | all-reduce | flops 192 | bytes 1536
  (143 shorter events, 115.8 us)
Async XLA Ops:
  7.2 153.6 %all-gather.8.cloned.1.call-start = ((), (), s32[]{:S(2)}) async-start(), calls=%async_computation.7 | async-start | bytes 5898240 | tf_op jit(solution)/shard_map/all_gather | solution.py:1032
  71.4 154.2 %all-gather.6.cloned.1.call-start = ((), (), s32[]{:S(2)}) async-start(), calls=%async_computation.3 | async-start | bytes 4866048 | tf_op jit(solution)/shard_map/all_gather | solution.py:1027
  72.1 224.3 %all-gather.10.cloned.1.call-start = ((), (), s32[]{:S(2)}) async-start(), calls=%async_computation.8 | async-start | bytes 7077888 | tf_op jit(solution)/shard_map/all_gather | solution.py:1065
  72.9 500.6 %reduce-scatter.8.cloned.1.call-start = ((), (), s32[]{:S(2)}) async-start(), calls=%async_computation.6 | async-start | bytes 4866048 | tf_op jit(solution)/shard_map/reduce_scatter | solution.py:1101
  87.4 11.3 %copy-start.4 = (bf16[1536,8,64]{0,2,1:T(8,128)(2,1)}, bf16[1536,8,64]{0,2,1:T(8,128)(2,1)S(1)}, u32[]{:S(2)}) copy-start(bf16[1536,8,64]{0,2,1:T(8,128)(2,1)S(1)} %pad.13.clone) | copy-start | bytes 4718596
  170.3 55.3 %copy-start.2 = (bf16[1,256,1536]{2,1,0:T(8,128)(2,1)S(1)}, bf16[1,256,1536]{2,1,0:T(8,128)(2,1)}, u32[]{:S(2)}) copy-start(bf16[1,256,1536]{2,1,0:T(8,128)(2,1)} %param.13) | copy-start | bytes 2359300
  282.4 8.9 %copy-start.3 = (bf16[8,256,1536]{2,1,0:T(8,128)(2,1)S(1)}, bf16[8,256,1536]{2,1,0:T(8,128)(2,1)}, u32[]{:S(2)}) copy-start(bf16[8,256,1536]{2,1,0:T(8,128)(2,1)} %plane_gather.1) | copy-start | bytes 18874372
  282.4 8.9 %copy-start.8 = (bf16[1536,4,128]{0,2,1:T(8,128)(2,1)S(1)}, bf16[1536,4,128]{0,2,1:T(8,128)(2,1)}, u32[]{:S(2)}) copy-start(bf16[1536,4,128]{0,2,1:T(8,128)(2,1)} %copy.104) | copy-start | bytes 4718596
  296.4 11.1 %copy-start.7 = (bf16[1536,4,128]{0,2,1:T(8,128)(2,1)S(1)}, bf16[1536,4,128]{0,2,1:T(8,128)(2,1)}, u32[]{:S(2)}) copy-start(bf16[1536,4,128]{0,2,1:T(8,128)(2,1)} %copy.106) | copy-start | bytes 4718596
  307.5 3.7 copy-start.26
  307.5 44.9 %copy-start.24 = (bf16[2048,512]{1,0:T(8,128)(2,1)}, bf16[2048,512]{1,0:T(8,128)(2,1)S(1)}, u32[]{:S(2)}) copy-start(bf16[2048,512]{1,0:T(8,128)(2,1)S(1)} %get-tuple-element.46) | copy-start | bytes 6291460
  307.5 51.2 %copy-start.25 = (bf16[2048,512]{1,0:T(8,128)(2,1)}, bf16[2048,512]{1,0:T(8,128)(2,1)S(1)}, u32[]{:S(2)}) copy-start(bf16[2048,512]{1,0:T(8,128)(2,1)S(1)} %get-tuple-element.45) | copy-start | bytes 6291460
  311.2 41.2 %copy-start.9 = (bf16[1536,4,128]{0,2,1:T(8,128)(2,1)S(1)}, bf16[1536,4,128]{0,2,1:T(8,128)(2,1)}, u32[]{:S(2)}) copy-start(bf16[1536,4,128]{0,2,1:T(8,128)(2,1)} %copy.104) | copy-start | bytes 4718596
  352.4 6.3 copy-start.6
  413.5 161.7 %reduce-scatter.6.cloned.1.call-start = ((), (), s32[]{:S(2)}) async-start(), calls=%async_computation.5 | async-start | bytes 1474560 | tf_op jit(solution)/shard_map/reduce_scatter | solution.py:1112
  484.7 152.2 %reduce-scatter.4.cloned.1.call-start = ((), (), s32[]{:S(2)}) async-start(), calls=%async_computation.4 | async-start | bytes 5898240 | tf_op jit(solution)/shard_map/reduce_scatter | solution.py:1087
  636.9 24.2 %copy-start.10 = (bf16[192,1024]{1,0:T(8,128)(2,1)S(1)}, bf16[192,1024]{1,0:T(8,128)(2,1)}, u32[]{:S(2)}) copy-start(bf16[192,1024]{1,0:T(8,128)(2,1)} %wg.1) | copy-start | bytes 1179652
  636.9 24.2 %copy-start.11 = (bf16[192,1024]{1,0:T(8,128)(2,1)S(1)}, bf16[192,1024]{1,0:T(8,128)(2,1)}, u32[]{:S(2)}) copy-start(bf16[192,1024]{1,0:T(8,128)(2,1)} %wu.1) | copy-start | bytes 1179652
  656.9 4.1 copy-start.12
  662.7 12.3 %copy-start.22 = (bf16[48]{0:T(256)(128)(2,1)S(1)}, bf16[48]{0:T(256)(128)(2,1)}, u32[]{:S(2)}) copy-start(bf16[48]{0:T(256)(128)(2,1)} %param.21) | copy-start | bytes 292
  662.7 12.8 %copy-start.21 = (bf16[48]{0:T(256)(128)(2,1)S(1)}, bf16[48]{0:T(256)(128)(2,1)}, u32[]{:S(2)}) copy-start(bf16[48]{0:T(256)(128)(2,1)} %param.16) | copy-start | bytes 292
  662.9 13.2 %copy-start.13 = (f32[48,1536]{1,0:T(8,128)}, f32[48,1536]{1,0:T(8,128)S(1)}, u32[]{:S(2)}) copy-start(f32[48,1536]{1,0:T(8,128)S(1)} %reshape.274) | copy-start | bytes 884740
  663.3 12.7 %copy-start.15 = (f32[48,768]{1,0:T(8,128)}, f32[48,768]{1,0:T(8,128)S(1)}, u32[]{:S(2)}) copy-start(f32[48,768]{1,0:T(8,128)S(1)} %reshape.275) | copy-start | bytes 442372
  663.6 12.4 %copy-start.16 = (f32[48,768]{1,0:T(8,128)}, f32[48,768]{1,0:T(8,128)S(1)}, u32[]{:S(2)}) copy-start(f32[48,768]{1,0:T(8,128)S(1)} %reshape.276) | copy-start | bytes 442372
  (9 other events, 11.2 us)
Sparse Core Ops, SparseCore 0:
  71.5 89.1 all-gather.7
  163.5 61.9 all-gather.5
  227.5 67.9 all-gather.9
  413.6 106.4 reduce-scatter.7
  522.3 28.2 reduce-scatter.5
  552.9 83.9 reduce-scatter.3

commit v2 on v1

--- a/solution.py
+++ b/solution.py
@@ -357,8 +357,18 @@
         self.q = self.s // 2
         self.c = lax.rem(self.s, 2)
 
+        across = self.q + 1 - 2 * lax.rem(self.q, 2)
+        along = lax.rem(self.q + 2, 4)
+        self.to = across * (1 - self.c) + along * self.c
+        self.fro = across * self.c + along * (1 - self.c)
+        self.far = 3 - self.q
+        self.order = (self.q, self.to, self.fro, self.far)
+
     def device(self, s):
         return (s, self.t)
+
+    def same(self, chip):
+        return (2 * chip + self.c, self.t)
 
     def sibling(self):
         return (2 * self.q + 1 - self.c, self.t)
@@ -408,45 +418,71 @@
 
 
 class Gather:
+    COPIES = 7
+
     def __init__(self, plane, src, dst, send, recv, local):
-        chips = plane.chips
-        self.own = pltpu.make_async_copy(src, dst.at[plane.s], local)
-        self.out = [remote(src, dst.at[plane.s], send.at[0], recv.at[0], plane.sibling())]
-        self.forward = []
-        for k in range(1, chips):
-            peer = 2 * plane.ahead(k) + plane.c
-            self.out.append(
-                remote(src, dst.at[plane.s], send.at[k], recv.at[k], plane.device(peer))
-            )
-            came = 2 * plane.behind(k) + plane.c
-            self.forward.append(
-                remote(
-                    dst.at[came],
-                    dst.at[came],
-                    send.at[chips - 1 + k],
-                    recv.at[chips - 1 + k],
-                    plane.sibling(),
-                )
-            )
+        to, fro, far, c = plane.to, plane.fro, plane.far, plane.c
+        here = dst.at[plane.s]
+        self.own = pltpu.make_async_copy(src, here, local)
+
+        def block(chip):
+            return dst.at[2 * chip + c]
+
+        def copy(i, a, b, device):
+            return remote(a, b, send.at[i], recv.at[i], device)
+
+        sibling = plane.sibling()
+        self.swap = copy(0, src, here, sibling)
+        self.ahead = copy(1, src, here, plane.same(to))
+        self.back = copy(2, src, here, plane.same(fro))
+        self.relay = copy(3, block(fro), block(fro), plane.same(to))
+        self.share = [
+            copy(4, block(to), block(to), sibling),
+            copy(5, block(fro), block(fro), sibling),
+            copy(6, block(far), block(far), sibling),
+        ]
 
     def start(self):
-        for copy in self.out[1:]:
-            copy.start()
-        self.out[0].start()
+        self.back.start()
+        self.ahead.start()
+        self.swap.start()
         self.own.start()
 
-    def relay(self):
-        for copy, onward in zip(self.out[1:], self.forward):
-            copy.wait_recv()
-            onward.start()
+    def relay_near(self):
+        self.back.wait_recv()
+        self.relay.start()
+        self.share[1].start()
+        self.ahead.wait_recv()
+        self.share[0].start()
+
+    def relay_far(self):
+        self.relay.wait_recv()
+        self.share[2].start()
 
     def finish(self):
         self.own.wait()
-        self.out[0].wait()
-        for copy in self.out[1:]:
-            copy.wait_send()
-        for onward in self.forward:
-            onward.wait()
+        self.swap.wait()
+        self.ahead.wait_send()
+        self.back.wait_send()
+        self.relay.wait_send()
+        for copy in self.share:
+            copy.wait()
+
+    def run(self):
+        self.start()
+        self.relay_near()
+        self.relay_far()
+        self.finish()
+
+
+def fan(plane, src_of, dst_of, send, recv):
+    copies = []
+    for k in range(1, plane.m):
+        device = plane.tp_ahead(k)
+        copies.append(
+            remote(src_of(device[1]), dst_of(plane.t), send.at[k - 1], recv.at[k - 1], device)
+        )
+    return copies
 
 
 def exchange(plane, src_of, dst_of, send, recv, local):
@@ -462,265 +498,370 @@
     return [own] + copies
 
 
-def entry_body(
-    n, m, x, places, wqkv, wg, wu, wd, x_all, places_all, wqkv_all, ffn, sems_x, rem, loc
-):
+def entry_body(n, m, x, places, wqkv, gains, x_all, places_all, w_all, gains_all, sx, rem, sz, loc):
     plane = Plane(n, m)
     enter_plane(plane, True)
-    width = wg.shape[1] // n
-    rows = wg.shape[0]
-    step = n - 1
-    mine = wqkv_all.at[plane.t]
-    a = exchange(
+    gather = Gather(plane, x, x_all, sx.at[0], sx.at[1], loc.at[0])
+    copies = exchange(
         plane,
         lambda i: wqkv.at[i],
-        lambda i: mine.at[i],
+        lambda i: w_all.at[i, plane.t],
         rem.at[0, 0],
         rem.at[0, 1],
-        loc.at[0],
-    )
-    b = exchange(
+        loc.at[1],
+    )
+    copies += exchange(
         plane,
-        lambda i: places,
-        lambda i: places_all.at[i],
+        lambda i: gains,
+        lambda i: gains_all.at[i, plane.t],
         rem.at[1, 0],
         rem.at[1, 1],
-        loc.at[1],
-    )
-    gather = Gather(plane, x, x_all, sems_x.at[0], sems_x.at[1], loc.at[2])
-    for copy in a + b:
+        loc.at[2],
+    )
+    few = exchange(
+        plane, lambda i: places, lambda i: places_all.at[i], rem.at[2, 0], rem.at[2, 1], loc.at[3]
+    )
+    for copy in copies:
         copy.start()
     gather.start()
-    f = []
-    for j, w in enumerate((wg, wu, wd)):
-        f += exchange(
-            plane,
-            lambda i, w=w: w.at[:, pl.ds(pl.multiple_of(i * width, width), width)],
-            lambda i, j=j: ffn.at[j, pl.ds(pl.multiple_of(i * rows, rows), rows), :],
-            rem.at[2 + j, 0],
-            rem.at[2 + j, 1],
-            loc.at[3 + j],
-        )
-    for copy in f:
+    for copy in few:
         copy.start()
-    for copy in a:
+    for copy in copies:
         copy.wait()
-    z = []
-    for k in range(1, m):
-        z.append(
-            remote(mine, mine, rem.at[5, 0].at[k - 1], rem.at[5, 1].at[k - 1], plane.tp_ahead(k))
-        )
-    for copy in z:
+    across = []
+    for i, ref in enumerate((w_all, gains_all)):
+
+        def slot(t, ref=ref):
+            return ref.at[:, plane.t]
+
+        across += fan(plane, slot, slot, sz.at[i, 0], sz.at[i, 1])
+    for copy in across:
         copy.start()
-    gather.relay()
-    for copy in b + f + z:
+    gather.relay_near()
+    gather.relay_far()
+    for copy in few + across:
         copy.wait()
     gather.finish()
 
 
-def entry(n, m, x, places, wqkv, wg, wu, wd):
-    rows, width = wg.shape
+def entry(n, m, x, places, wqkv, gains):
     return pl.pallas_call(
         functools.partial(entry_body, n, m),
         out_shape=(
             jax.ShapeDtypeStruct((n,) + x.shape, x.dtype),
             jax.ShapeDtypeStruct((n,) + places.shape, places.dtype),
-            jax.ShapeDtypeStruct((m,) + wqkv.shape, wqkv.dtype),
-            jax.ShapeDtypeStruct((3, rows * n, width // n), wg.dtype),
+            jax.ShapeDtypeStruct((n, m) + wqkv.shape[1:], wqkv.dtype),
+            jax.ShapeDtypeStruct((n, m) + gains.shape, gains.dtype),
         ),
-        in_specs=[pl.BlockSpec(memory_space=ANY)] * 6,
+        in_specs=[pl.BlockSpec(memory_space=ANY)] * 4,
         out_specs=[pl.BlockSpec(memory_space=ANY)] * 4,
         scratch_shapes=[
-            pltpu.SemaphoreType.DMA((2, n)),
-            pltpu.SemaphoreType.DMA((6, 2, n - 1)),
-            pltpu.SemaphoreType.DMA((6,)),
+            pltpu.SemaphoreType.DMA((2, Gather.COPIES)),
+            pltpu.SemaphoreType.DMA((3, 2, n - 1)),
+            pltpu.SemaphoreType.DMA((2, 2, m - 1)),
+            pltpu.SemaphoreType.DMA((4,)),
         ],
         compiler_params=pltpu.CompilerParams(collective_id=0, has_side_effects=True),
-        cost_estimate=pl.CostEstimate(flops=0, transcendentals=0, bytes_accessed=150_000_000),
+        cost_estimate=pl.CostEstimate(flops=0, transcendentals=0, bytes_accessed=100_000_000),
         name="entry",
-    )(x, places, wqkv, wg, wu, wd)
-
-
-def gather_body(n, m, src, dst, sems, loc):
+    )(x, places, wqkv, gains)
+
+
+def swap_body(n, m, count, *refs):
     plane = Plane(n, m)
     enter_plane(plane, False)
-    gather = Gather(plane, src, dst, sems.at[0], sems.at[1], loc.at[0])
-    gather.start()
-    gather.relay()
-    gather.finish()
-
-
-def plane_gather(n, m, block, ident):
-    return pl.pallas_call(
-        functools.partial(gather_body, n, m),
-        out_shape=jax.ShapeDtypeStruct((n,) + block.shape, block.dtype),
-        in_specs=[pl.BlockSpec(memory_space=ANY)],
-        out_specs=pl.BlockSpec(memory_space=ANY),
-        scratch_shapes=[pltpu.SemaphoreType.DMA((2, n)), pltpu.SemaphoreType.DMA((1,))],
-        compiler_params=pltpu.CompilerParams(collective_id=ident, has_side_effects=True),
-        cost_estimate=pl.CostEstimate(flops=0, transcendentals=0, bytes_accessed=120_000_000),
-        name="plane_gather",
-    )(block)
-
-
-def swap_body(n, m, src, dst, sems, loc):
-    plane = Plane(n, m)
-    enter_plane(plane, False)
-    copies = exchange(
-        plane, lambda i: src.at[i], lambda i: dst.at[i], sems.at[0], sems.at[1], loc.at[0]
-    )
+    sems, loc = refs[2 * count :]
+    copies = []
+    for i in range(count):
+        src, dst = refs[i], refs[count + i]
+        copies += exchange(
+            plane,
+            lambda k, src=src: src.at[k],
+            lambda k, dst=dst: dst.at[k],
+            sems.at[i, 0],
+            sems.at[i, 1],
+            loc.at[i],
+        )
     for copy in copies:
         copy.start()
     for copy in copies:
         copy.wait()
 
 
-def plane_swap(n, m, blocks, ident):
+def plane_swap(n, m, ident, *arrays):
+    count = len(arrays)
     return pl.pallas_call(
-        functools.partial(swap_body, n, m),
-        out_shape=jax.ShapeDtypeStruct(blocks.shape, blocks.dtype),
-        in_specs=[pl.BlockSpec(memory_space=ANY)],
-        out_specs=pl.BlockSpec(memory_space=ANY),
-        scratch_shapes=[pltpu.SemaphoreType.DMA((2, n - 1)), pltpu.SemaphoreType.DMA((1,))],
+        functools.partial(swap_body, n, m, count),
+        out_shape=tuple(jax.ShapeDtypeStruct(a.shape, a.dtype) for a in arrays),
+        in_specs=[pl.BlockSpec(memory_space=ANY)] * count,
+        out_specs=[pl.BlockSpec(memory_space=ANY)] * count,
+        scratch_shapes=[
+            pltpu.SemaphoreType.DMA((count, 2, n - 1)),
+            pltpu.SemaphoreType.DMA((count,)),
+        ],
         compiler_params=pltpu.CompilerParams(collective_id=ident, has_side_effects=True),
         cost_estimate=pl.CostEstimate(flops=0, transcendentals=0, bytes_accessed=40_000_000),
         name="plane_swap",
-    )(blocks)
-
-
-def final_body(n, m, ffn, qkv, ffn_out, qkv_out, sems, loc):
+    )(*arrays)
+
+
+TILE = 16
+
+
+def in_tiles(rows, body):
+    def one(i, carry):
+        body(pl.ds(pl.multiple_of(i * TILE, TILE), TILE))
+        return carry
+
+    lax.fori_loop(0, rows // TILE, one, 0)
+
+
+class Reduce:
+    SLOTS = (4, 4, 3)
+
+    THEIRS = (0, 2, 1, 3)
+
+    def __init__(self, plane, part_of, pair, near, far, sems, loc, stage=None):
+        c = plane.c
+        self.pair, self.near, self.far = pair, near, far
+        self.rows = pair.shape[1]
+        self.swaps, self.loads = {}, {}
+        for k in range(4):
+            mine = self.THEIRS[k]
+            chip = plane.order[mine]
+            source = part_of(2 * chip + 1 - c) if stage is None else stage.at[mine]
+            self.swaps[k] = remote(
+                source, near.at[k], sems.at[0, k], sems.at[1, k], plane.sibling()
+            )
+            if stage is None:
+                self.loads[k] = pltpu.make_async_copy(
+                    part_of(2 * plane.order[k] + c), pair.at[k], loc.at[k]
+                )
+
+        def out(i, k, chip):
+            return remote(
+                pair.at[k], far.at[i], sems.at[2, i], sems.at[3, i], plane.same(chip)
+            )
+
+        self.out = [out(0, 3, plane.to), out(1, 1, plane.to), out(2, 2, plane.fro)]
+
+    def start(self):
+        for k in (3, 1, 2, 0):
+            self.swaps[k].start()
+            self.loads[k].start()
+
+    def landed(self, k):
+        self.swaps[k].wait()
+        if self.loads:
+            self.loads[k].wait()
+
+    def join(self, k):
+        pair, near = self.pair, self.near
+        self.landed(k)
+
+        def add(at):
+            both = pair[k, at, :].astype(f32) + near[k, at, :].astype(f32)
+            pair[k, at, :] = both.astype(bf16)
+
+        in_tiles(self.rows, add)
+
+    def send_to(self):
+        self.join(3)
+        self.out[0].start()
+        self.join(1)
+        self.out[1].start()
+
+    def ready(self):
+        self.landed(2)
+
+    def send_fro(self):
+        pair, near, far = self.pair, self.near, self.far
+        self.out[0].wait_recv()
+
+        def add(at):
+            both = pair[2, at, :].astype(f32) + near[2, at, :].astype(f32)
+            pair[2, at, :] = (both + far[0, at, :].astype(f32)).astype(bf16)
+
+        in_tiles(self.rows, add)
+        self.out[2].start()
+
+    def first(self, total):
+        pair, near = self.pair, self.near
+        self.landed(0)
+
+        def add(at):
+            total[at, :] = pair[0, at, :].astype(f32) + near[0, at, :].astype(f32)
+
+        in_tiles(self.rows, add)
+
+    def finish(self, total):
+        far = self.far
+        self.out[0].wait_send()
+        self.out[1].wait()
+        self.out[2].wait()
+
+        def add(at):
+            total[at, :] = (
+                total[at, :] + far[1, at, :].astype(f32) + far[2, at, :].astype(f32)
+            )
+
+        in_tiles(self.rows, add)
+
+    def run(self, total):
+        self.start()
+        self.send_to()
+        self.ready()
+        self.first(total)
+        self.send_fro()
+        self.finish(total)
+
+    @staticmethod
+    def scratch(rows, width):
+        return [pltpu.VMEM((slots, rows, width), bf16) for slots in Reduce.SLOTS] + [
+            pltpu.SemaphoreType.DMA((4, 4)),
+            pltpu.SemaphoreType.DMA((4,)),
+        ]
+
+
+def last_body(
+    n, m, parts, ffn, qkv, vec, total, ffn_out, qkv_out, vec_out,
+    pair, near, far, sr, lr, got, summed, sems, st, loc,
+):
     plane = Plane(n, m)
-    enter_plane(plane, False)
+    enter_plane(plane, True)
     rows = ffn_out.shape[1]
     width = ffn.shape[2]
+    across = fan(plane, lambda t: qkv.at[t], lambda t: got.at[t], st.at[0, 0], st.at[0, 1])
+    across_vec = fan(plane, lambda t: vec.at[t], lambda t: vec_out.at[t], st.at[1, 0], st.at[1, 1])
+    mine = [
+        pltpu.make_async_copy(qkv.at[plane.t], got.at[plane.t], loc.at[0]),
+        pltpu.make_async_copy(vec.at[plane.t], vec_out.at[plane.t], loc.at[1]),
+    ]
+    for copy in across + across_vec + mine:
+        copy.start()
+    reduce = Reduce(plane, lambda i: parts.at[i], pair, near, far, sr, lr)
+    reduce.start()
     a = exchange(
         plane,
         lambda i: ffn.at[:, pl.ds(pl.multiple_of(i * rows, rows), rows), :],
         lambda i: ffn_out.at[:, :, pl.ds(pl.multiple_of(i * width, width), width)],
-        sems.at[0],
-        sems.at[1],
-        loc.at[0],
-    )
+        sems.at[0, 0],
+        sems.at[0, 1],
+        loc.at[2],
+    )
+    for copy in a:
+        copy.start()
+    reduce.send_to()
+    reduce.ready()
+    reduce.first(total)
+    for copy in across + across_vec + mine:
+        copy.wait()
+    groups, strip, _ = summed.shape
+
+    for g in range(groups):
+
+        def add(at, g=g):
+            value = got[0, g, at, :].astype(f32)
+            for t in range(1, m):
+                value = value + got[t, g, at, :].astype(f32)
+            summed[g, at, :] = value.astype(bf16)
+
+        in_tiles(strip, add)
     b = exchange(
-        plane, lambda i: qkv.at[i], lambda i: qkv_out.at[i], sems.at[2], sems.at[3], loc.at[1]
-    )
-    for copy in a + b:
+        plane,
+        lambda i: summed.at[i],
+        lambda i: qkv_out.at[i],
+        sems.at[1, 0],
+        sems.at[1, 1],
+        loc.at[3],
+    )
+    for copy in b:
         copy.start()
+    reduce.send_fro()
+    reduce.finish(total)
     for copy in a + b:
         copy.wait()
 
 
-def final_swap(n, m, ffn, qkv, ident):
+def last(n, m, parts, ffn, qkv, vec, ident):
+    rows, width = parts.shape[1:]
     return pl.pallas_call(
-        functools.partial(final_body, n, m),
+        functools.partial(last_body, n, m),
         out_shape=(
+            jax.ShapeDtypeStruct((rows, width), f32),
             jax.ShapeDtypeStruct((3, ffn.shape[1] // n, ffn.shape[2] * n), ffn.dtype),
-            jax.ShapeDtypeStruct(qkv.shape, qkv.dtype),
+            jax.ShapeDtypeStruct(qkv.shape[1:], qkv.dtype),
+            jax.ShapeDtypeStruct(vec.shape, vec.dtype),
         ),
-        in_specs=[pl.BlockSpec(memory_space=ANY)] * 2,
-        out_specs=[pl.BlockSpec(memory_space=ANY)] * 2,
-        scratch_shapes=[pltpu.SemaphoreType.DMA((4, n - 1)), pltpu.SemaphoreType.DMA((2,))],
-        compiler_params=pltpu.CompilerParams(collective_id=ident, has_side_effects=True),
-        cost_estimate=pl.CostEstimate(flops=0, transcendentals=0, bytes_accessed=40_000_000),
-        name="final_swap",
-    )(ffn, qkv)
-
-
-def reduce_body(n, m, parts, total, pair, near, far, sems, loc):
-    plane = Plane(n, m)
-    enter_plane(plane, False)
-    chips = plane.chips
-    rows = parts.shape[1]
-    order = list(range(1, chips)) + [0]
-    loads, swaps, sends = {}, {}, {}
-    for k in order:
-        chip = plane.ahead(k)
-        swaps[k] = remote(
-            parts.at[2 * chip + 1 - plane.c],
-            near.at[k],
-            sems.at[0, k],
-            sems.at[1, k],
-            plane.sibling(),
-        )
-        loads[k] = pltpu.make_async_copy(parts.at[2 * chip + plane.c], pair.at[k], loc.at[k])
-        swaps[k].start()
-        loads[k].start()
-        if k:
-            sends[k] = remote(
-                pair.at[k],
-                far.at[k - 1],
-                sems.at[2, k],
-                sems.at[3, k],
-                plane.device(2 * chip + plane.c),
-            )
-    tile = 16
-
-    def spans(body):
-        def one(i, carry):
-            body(pl.ds(pl.multiple_of(i * tile, tile), tile))
-            return carry
-
-        lax.fori_loop(0, rows // tile, one, 0)
-
-    for k in order:
-        swaps[k].wait()
-        loads[k].wait()
-        if k:
-
-            def add(at, k=k):
-                both = pair[k, at, :].astype(f32) + near[k, at, :].astype(f32)
-                pair[k, at, :] = both.astype(bf16)
-
-            spans(add)
-            sends[k].start()
-        else:
-
-            def first(at):
-                total[at, :] = pair[0, at, :].astype(f32) + near[0, at, :].astype(f32)
-
-            spans(first)
-    for k in range(1, chips):
-        sends[k].wait()
-
-    def last(at):
-        value = total[at, :]
-        for k in range(1, chips):
-            value = value + far[k - 1, at, :].astype(f32)
-        total[at, :] = value
-
-    spans(last)
-
-
-def plane_reduce(n, m, parts, ident):
-    rows, width = parts.shape[1:]
-    chips = n // 2
-    return pl.pallas_call(
-        functools.partial(reduce_body, n, m),
-        out_shape=jax.ShapeDtypeStruct((rows, width), f32),
-        in_specs=[pl.BlockSpec(memory_space=ANY)],
-        out_specs=pl.BlockSpec(memory_space=pltpu.VMEM),
-        scratch_shapes=[
-            pltpu.VMEM((chips, rows, width), bf16),
-            pltpu.VMEM((chips, rows, width), bf16),
-            pltpu.VMEM((chips - 1, rows, width), bf16),
-            pltpu.SemaphoreType.DMA((4, chips)),
-            pltpu.SemaphoreType.DMA((chips,)),
+        in_specs=[pl.BlockSpec(memory_space=ANY)] * 4,
+        out_specs=[pl.BlockSpec(memory_space=pltpu.VMEM)]
+        + [pl.BlockSpec(memory_space=ANY)] * 3,
+        scratch_shapes=Reduce.scratch(rows, width)
+        + [
+            pltpu.VMEM(qkv.shape, bf16),
+            pltpu.VMEM(qkv.shape[1:], bf16),
+            pltpu.SemaphoreType.DMA((2, 2, n - 1)),
+            pltpu.SemaphoreType.DMA((2, 2, m - 1)),
+            pltpu.SemaphoreType.DMA((4,)),
         ],
         compiler_params=pltpu.CompilerParams(
-            collective_id=ident, has_side_effects=True, vmem_limit_bytes=32 << 20
+            collective_id=ident, has_side_effects=True, vmem_limit_bytes=40 << 20
         ),
-        cost_estimate=pl.CostEstimate(flops=0, transcendentals=0, bytes_accessed=120_000_000),
-        name="plane_reduce",
-    )(parts)
-
-
-def project_body(heads, x, gain, w, cosine, sine, norm, q, k, v):
-    value = x[...].astype(f32)
+        cost_estimate=pl.CostEstimate(flops=0, transcendentals=0, bytes_accessed=150_000_000),
+        name="last",
+    )(parts, ffn, qkv, vec)
+
+
+def column(row):
+    return jnp.broadcast_to(row, (8, row.shape[1])).T[:, :1]
+
+
+def project_body(
+    n, m, heads, x, gain, w, places, inverse, wg, wu, wd, wo, norm, q, k, v, cosine, sine, ffn, wo_z,
+    sems, loc, sz
+):
+    step = pl.program_id(0)
+    plane = Plane(n, m)
+    width, rows = wg.shape[1] // n, wg.shape[0]
+
+    def moves():
+        copies = []
+        for j, weight in enumerate((wg, wu, wd)):
+            copies += exchange(
+                plane,
+                lambda i, w=weight: w.at[:, pl.ds(pl.multiple_of(i * width, width), width)],
+                lambda i, j=j: ffn.at[j, pl.ds(pl.multiple_of(i * rows, rows), rows), :],
+                sems.at[j, 0],
+                sems.at[j, 1],
+                loc.at[j],
+            )
+        return copies
+
+    def spread_wo():
+        return fan(plane, lambda t: wo, lambda t: wo_z.at[t], sz.at[0], sz.at[1])
+
+    def own_wo():
+        return pltpu.make_async_copy(wo, wo_z.at[plane.t], loc.at[3])
+
+    @pl.when(step == 0)
+    def _():
+        own_wo().start()
+        enter_plane(plane, True)
+        for copy in moves() + spread_wo():
+            copy.start()
+
+    value = x[0].astype(f32)
     scale = lax.rsqrt(jnp.mean(value * value, axis=1, keepdims=True) + norm_epsilon)
     low = (value * scale * gain[...]).astype(bf16)
     norm[...] = low
     out = jnp.dot(low, w[...], preferred_element_type=f32)
-    cos, sin = cosine[...], sine[...]
+    angles = column(places[0, 1:2, :].astype(f32)) * inverse[...]
+    cos = jnp.cos(angles)
+    lanes = lax.broadcasted_iota(jnp.int32, angles.shape, 1)
+    sin = jnp.sin(angles)
+    sin = jnp.where(lanes < SLOT, -sin, sin)
+    cosine[...] = cos
+    sine[...] = sin
     for h in range(heads + 1):
         part = out[:, h * LANES : (h + 1) * LANES]
         turned = (part * cos + pltpu.roll(part, SLOT, 1) * sin).astype(bf16)
@@ -730,38 +871,61 @@
             k[...] = turned
     v[...] = out[:, (heads + 1) * LANES :].astype(bf16)
 
-
-def project(heads, x_all, gain, w, cosine, sine):
-    length, width = x_all.shape
-    tile = 256
+    @pl.when(step == pl.num_programs(0) - 1)
+    def _():
+        own_wo().wait()
+        for copy in moves() + spread_wo():
+            copy.wait()
+
+
+def project(n, m, heads, x_all, gain, w, places, inverse, wg, wu, wd, wo, ident):
+    tiles, tile, width = x_all.shape
+    length = tiles * tile
     wide = w.shape[1]
+    rows, cols = wg.shape
+    table = pl.BlockSpec((tile, LANES), lambda i: (i, 0))
     return pl.pallas_call(
-        functools.partial(project_body, heads),
-        grid=(length // tile,),
+        functools.partial(project_body, n, m, heads),
+        grid=(tiles,),
         out_shape=(
             jax.ShapeDtypeStruct((length, width), bf16),
             jax.ShapeDtypeStruct((heads, length, LANES), bf16),
             jax.ShapeDtypeStruct((length, LANES), bf16),
             jax.ShapeDtypeStruct((length, LANES), bf16),
+            jax.ShapeDtypeStruct((length, LANES), f32),
+            jax.ShapeDtypeStruct((length, LANES), f32),
+            jax.ShapeDtypeStruct((3, rows * n, cols // n), wg.dtype),
+            jax.ShapeDtypeStruct((m,) + wo.shape, wo.dtype),
         ),
         in_specs=[
-            pl.BlockSpec((tile, width), lambda i: (i, 0)),
+            pl.BlockSpec((1, tile, width), lambda i: (i, 0, 0)),
             pl.BlockSpec((1, width), lambda i: (0, 0)),
             pl.BlockSpec((width, wide), lambda i: (0, 0)),
-            pl.BlockSpec((tile, LANES), lambda i: (i, 0)),
-            pl.BlockSpec((tile, LANES), lambda i: (i, 0)),
-        ],
+            pl.BlockSpec((1,) + places.shape[1:], lambda i: (i, 0, 0)),
+            pl.BlockSpec((1, LANES), lambda i: (0, 0)),
+        ]
+        + [pl.BlockSpec(memory_space=ANY)] * 4,
         out_specs=[
             pl.BlockSpec((tile, width), lambda i: (i, 0)),
             pl.BlockSpec((heads, tile, LANES), lambda i: (0, i, 0)),
-            pl.BlockSpec((tile, LANES), lambda i: (i, 0)),
-            pl.BlockSpec((tile, LANES), lambda i: (i, 0)),
+            table,
+            table,
+            table,
+            table,
+            pl.BlockSpec(memory_space=ANY),
+            pl.BlockSpec(memory_space=ANY),
         ],
+        scratch_shapes=[
+            pltpu.SemaphoreType.DMA((3, 2, n - 1)),
+            pltpu.SemaphoreType.DMA((4,)),
+            pltpu.SemaphoreType.DMA((2, m - 1)),
+        ],
+        compiler_params=pltpu.CompilerParams(collective_id=ident, has_side_effects=True),
         cost_estimate=pl.CostEstimate(
-            flops=2 * length * width * wide, transcendentals=0, bytes_accessed=18_000_000
+            flops=2 * length * width * wide * 3, transcendentals=0, bytes_accessed=30_000_000
         ),
         name="project",
-    )(x_all, gain, w, cosine, sine)
+    )(x_all, gain, w, places, inverse, wg, wu, wd, wo)
 
 
 BLOCK = 512
@@ -778,23 +942,51 @@
     return ok
 
 
-def attend_body(factor, q, k, v, begin, o, low, lse, vt, top, total, acc):
-    i = pl.program_id(1)
-
-    @pl.when((i == 0) & (pl.program_id(0) == 0))
+def begins(docs):
+    begin = jnp.zeros(docs.shape, jnp.int32)
+    for d in range(3):
+        count = jnp.sum((docs == d).astype(f32), axis=1, keepdims=True).astype(jnp.int32)
+        begin = begin + jnp.where(docs > d, count, 0)
+    return begin
+
+
+def attend_body(
+    n, m, factor, q, k, v, docs, wo, go, o, low, lse, start, wo_all, go_all,
+    vt, top, total, acc, begin_row, sems, loc
+):
+    h, i = pl.program_id(0), pl.program_id(1)
+    plane = Plane(n, m)
+    first = Gather(plane, wo, wo_all, sems.at[0], sems.at[1], loc.at[0])
+    second = Gather(plane, go, go_all, sems.at[2], sems.at[3], loc.at[1])
+    at_step = h * pl.num_programs(1) + i
+
+    @pl.when(at_step == 0)
     def _():
-        vt[...] = v[...].astype(f32).T.astype(bf16)
+        enter_plane(plane, False)
+        first.start()
+        second.start()
+        vt[...] = v[...].T
+        begin_row[...] = begins(docs[...])
+        start[...] = begin_row[...]
+
+    @pl.when(at_step == 4)
+    def _():
+        first.relay_near()
+
+    @pl.when(at_step == 6)
+    def _():
+        first.relay_far()
 
     top[...] = jnp.full_like(top, mask_fill_value)
     total[...] = jnp.zeros_like(total)
     acc[...] = jnp.zeros_like(acc)
     query = q[0]
-    start = begin[...]
+    begin = begin_row[:, pl.ds(pl.multiple_of(i * BLOCK, BLOCK), BLOCK)]
 
     def step(j, causal):
         at = pl.ds(pl.multiple_of(j * BLOCK, BLOCK), BLOCK)
         raw = lax.dot_general(k[at, :], query, NT, preferred_element_type=f32)
-        ok = allowed_block(j * BLOCK, i * BLOCK, start, causal)
+        ok = allowed_block(j * BLOCK, i * BLOCK, begin, causal)
         scores = jnp.where(ok, raw * factor, mask_fill_value)
         new_top = jnp.maximum(top[...], jnp.max(scores, axis=0, keepdims=True))
         weights = jnp.exp2(scores - new_top)
@@ -816,53 +1008,103 @@
     low[...] = out.astype(bf16)
     lse[0] = top[...] + jnp.log2(total[...])
 
-
-def attend(factor, q, k, v, begin):
+    @pl.when(at_step == pl.num_programs(0) * pl.num_programs(1) - 1)
+    def _():
+        second.relay_near()
+        first.finish()
+        second.relay_far()
+        second.finish()
+
+
+def attend(n, m, factor, q, k, v, docs, wo, go, ident):
     heads, length, _ = q.shape
     blocks = length // BLOCK
     pairs = heads * BLOCK * BLOCK * blocks * (blocks + 1) // 2
     return pl.pallas_call(
-        functools.partial(attend_body, factor),
+        functools.partial(attend_body, n, m, factor),
         grid=(heads, blocks),
         out_shape=(
             jax.ShapeDtypeStruct((heads, length, LANES), f32),
             jax.ShapeDtypeStruct((length, heads * LANES), bf16),
             jax.ShapeDtypeStruct((heads, 1, length), f32),
+            jax.ShapeDtypeStruct((1, length), jnp.int32),
+            jax.ShapeDtypeStruct((n,) + wo.shape, wo.dtype),
+            jax.ShapeDtypeStruct((n,) + go.shape, go.dtype),
         ),
         in_specs=[
             pl.BlockSpec((1, BLOCK, LANES), lambda h, i: (h, i, 0)),
             pl.BlockSpec((length, LANES), lambda h, i: (0, 0)),
             pl.BlockSpec((length, LANES), lambda h, i: (0, 0)),
-            pl.BlockSpec((1, BLOCK), lambda h, i: (0, i)),
+            pl.BlockSpec((1, length), lambda h, i: (0, 0)),
+            pl.BlockSpec(memory_space=ANY),
+            pl.BlockSpec(memory_space=ANY),
         ],
         out_specs=[
             pl.BlockSpec((1, BLOCK, LANES), lambda h, i: (h, i, 0)),
             pl.BlockSpec((BLOCK, LANES), lambda h, i: (i, h)),
             pl.BlockSpec((1, 1, BLOCK), lambda h, i: (h, 0, i)),
+            pl.BlockSpec((1, length), lambda h, i: (0, 0)),
+            pl.BlockSpec(memory_space=ANY),
+            pl.BlockSpec(memory_space=ANY),
         ],
         scratch_shapes=[
             pltpu.VMEM((LANES, length), bf16),
             pltpu.VMEM((1, BLOCK), f32),
             pltpu.VMEM((1, BLOCK), f32),
             pltpu.VMEM((LANES, BLOCK), f32),
+            pltpu.VMEM((1, length), jnp.int32),
+            pltpu.SemaphoreType.DMA((4, Gather.COPIES)),
+            pltpu.SemaphoreType.DMA((2,)),
         ],
+        compiler_params=pltpu.CompilerParams(collective_id=ident, has_side_effects=True),
         cost_estimate=pl.CostEstimate(
-            flops=pairs * 4 * LANES * 3, transcendentals=pairs, bytes_accessed=6_000_000
+            flops=pairs * 4 * LANES * 3, transcendentals=pairs, bytes_accessed=120_000_000
         ),
         name="attend",
-    )(q, k, v, begin)
+    )(q, k, v, docs, wo, go)
 
 
 def attend_back_body(
-    factor, scale, heads, q, k, v, go, o, lse, begin, cosine, sine, out, kt, dqt, dk, dv, delta
+    n, m, factor, scale, heads, q, k, v, go, o, lse, begin, cosine, sine, mixed, terms,
+    out, mixed_sum, term_sum, kt, dqt, dk, dv, delta,
+    pair, near, far, sr, lr, pair2, near2, far2, sr2, lr2,
 ):
     h = pl.program_id(0)
     j = pl.program_id(1)
     blocks = pl.num_programs(1)
+    plane = Plane(n, m)
+    one = Reduce(plane, lambda i: mixed.at[i], pair, near, far, sr, lr)
+    two = Reduce(plane, lambda i: terms.at[i], pair2, near2, far2, sr2, lr2)
+    at_step = h * blocks + j
+
+    @pl.when(at_step == 0)
+    def _():
+        enter_plane(plane, False)
+        one.start()
+
+    @pl.when(at_step == 1)
+    def _():
+        one.send_to()
+        two.start()
+
+    @pl.when(at_step == 2)
+    def _():
+        one.ready()
+        one.first(mixed_sum)
+
+    @pl.when(at_step == 4)
+    def _():
+        one.send_fro()
+        two.send_to()
+
+    @pl.when(at_step == 5)
+    def _():
+        two.ready()
+        two.first(term_sum)
 
     @pl.when((h == 0) & (j == 0))
     def _():
-        kt[...] = k[...].astype(f32).T.astype(bf16)
+        kt[...] = k[...].T
         dk[...] = jnp.zeros_like(dk)
         dv[...] = jnp.zeros_like(dv)
 
@@ -932,18 +1174,25 @@
             return carry
 
         lax.fori_loop(0, blocks, write, 0)
-
-
-def attend_back(factor, scale, q, k, v, go, o, lse, begin, cosine, sine):
+        one.finish(mixed_sum)
+        two.send_fro()
+        two.finish(term_sum)
+
+
+def attend_back(n, m, factor, scale, q, k, v, go, o, lse, begin, cosine, sine, mixed, terms, ident):
     heads, length, _ = q.shape
     blocks = length // BLOCK
     pairs = heads * BLOCK * BLOCK * blocks * (blocks + 1) // 2
     whole = pl.BlockSpec((length, LANES), lambda h, j: (0, 0))
     one = pl.BlockSpec((1, length, LANES), lambda h, j: (h, 0, 0))
     return pl.pallas_call(
-        functools.partial(attend_back_body, factor, scale, heads),
+        functools.partial(attend_back_body, n, m, factor, scale, heads),
         grid=(heads, blocks),
-        out_shape=jax.ShapeDtypeStruct((length, (heads + 2) * LANES), bf16),
+        out_shape=(
+            jax.ShapeDtypeStruct((length, (heads + 2) * LANES), bf16),
+            jax.ShapeDtypeStruct(mixed.shape[1:], f32),
+            jax.ShapeDtypeStruct(terms.shape[1:], f32),
+        ),
         in_specs=[
             one,
             whole,
@@ -954,20 +1203,245 @@
             pl.BlockSpec((1, length), lambda h, j: (0, 0)),
             whole,
             whole,
+            pl.BlockSpec(memory_space=ANY),
+            pl.BlockSpec(memory_space=ANY),
         ],
-        out_specs=pl.BlockSpec((length, (heads + 2) * LANES), lambda h, j: (0, 0)),
+        out_specs=[
+            pl.BlockSpec((length, (heads + 2) * LANES), lambda h, j: (0, 0)),
+            pl.BlockSpec(mixed.shape[1:], lambda h, j: (0, 0)),
+            pl.BlockSpec(terms.shape[1:], lambda h, j: (0, 0)),
+        ],
         scratch_shapes=[
             pltpu.VMEM((LANES, length), bf16),
             pltpu.VMEM((LANES, length), f32),
             pltpu.VMEM((length, LANES), f32),
             pltpu.VMEM((length, LANES), f32),
             pltpu.VMEM((1, length), f32),
-        ],
+        ]
+        + Reduce.scratch(*mixed.shape[1:])
+        + Reduce.scratch(*terms.shape[1:]),
+        compiler_params=pltpu.CompilerParams(
+            collective_id=ident, has_side_effects=True, vmem_limit_bytes=56 << 20
+        ),
         cost_estimate=pl.CostEstimate(
-            flops=pairs * 10 * LANES * 2, transcendentals=pairs, bytes_accessed=12_000_000
+            flops=pairs * 10 * LANES * 2, transcendentals=pairs, bytes_accessed=150_000_000
         ),
         name="attend_back",
-    )(q, k, v, go, o, lse, begin, cosine, sine)
+    )(q, k, v, go, o, lse, begin, cosine, sine, mixed, terms)
+
+
+def feed_body(
+    n, m, mine, go, w_in, dnorm, grads, mixed,
+    rows, rows_t, go_t, go_two, w, h, mix_two, pair, near, far, stage,
+    sg, sr, loc, sw, so, sm, sd,
+):
+    plane = Plane(n, m)
+    c, q = plane.c, plane.q
+    tokens = rows.shape[1]
+    hid = w_in.shape[3]
+    enter_plane(plane, False)
+    gather = Gather(plane, mine, rows, sg.at[0], sg.at[1], loc.at[0])
+    reduce = Reduce(plane, None, pair, near, far, sr, None, stage)
+    gather.start()
+    weights = [
+        pltpu.make_async_copy(
+            w_in.at[t, j], w.at[j, :, t * hid : (t + 1) * hid], sw.at[j, t]
+        )
+        for j in range(3)
+        for t in range(m)
+    ]
+    for copy in weights:
+        copy.start()
+
+    def number(it):
+        k, other = it // 2, lax.rem(it, 2)
+        low, high = lax.rem(k, 2), k // 2
+        dx = low * (1 - c) + high * c
+        dy = high * (1 - c) + low * c
+        x, y = lax.rem(q, 2), q // 2
+        chip = 2 * (y + dy - 2 * y * dy) + x + dx - 2 * x * dx
+        return 2 * chip + c + other * (1 - 2 * c)
+
+    def load_go(it, slot):
+        return pltpu.make_async_copy(go.at[number(it)], go_two.at[slot], so.at[slot])
+
+    def store_mix(it, slot):
+        return pltpu.make_async_copy(mix_two.at[slot], mixed.at[number(it)], sm.at[slot])
+
+    load_go(0, 0).start()
+    gather.own.wait()
+    for copy in weights:
+        copy.wait()
+
+    def blocks(it, carry):
+        slot = lax.rem(it, 2)
+        k = it // 2
+        b = number(it)
+
+        @pl.when(it == 1)
+        def _():
+            gather.swap.wait_recv()
+
+        @pl.when(it == 2)
+        def _():
+            gather.relay_near()
+
+        @pl.when(it == 3)
+        def _():
+            gather.share[1].wait_recv()
+
+        @pl.when(it == 5)
+        def _():
+            gather.share[0].wait_recv()
+
+        @pl.when(it == 6)
+        def _():
+            reduce.join(1)
+            reduce.out[1].start()
+            gather.relay_far()
+
+        @pl.when(it == 7)
+        def _():
+            gather.share[2].wait_recv()
+
+        @pl.when(it < n - 1)
+        def _():
+            load_go(it + 1, 1 - slot).start()
+
+        load_go(it, slot).wait()
+
+        @pl.when(it >= 2)
+        def _():
+            store_mix(it - 2, slot).wait()
+
+        here = pl.ds(pl.multiple_of(b * tokens, tokens), tokens)
+        row = rows[b]
+        gate = jnp.dot(row, w[0], preferred_element_type=f32)
+        up = jnp.dot(row, w[1], preferred_element_type=f32)
+        grad = go_two[slot]
+        dhidden = jnp.dot(grad, w[2], preferred_element_type=f32)
+        sig = jax.nn.sigmoid(gate)
+        act = gate * sig
+        hidden = (act * up).astype(bf16)
+        dgate = (dhidden * up * sig * (1.0 + gate * (1.0 - sig))).astype(bf16)
+        dup = (dhidden * act).astype(bf16)
+        h[0, here, :] = dgate
+        h[1, here, :] = dup
+        h[2, here, :] = hidden
+        part = lax.dot_general(dgate, w[0], NT, preferred_element_type=f32)
+        part = part + lax.dot_general(dup, w[1], NT, preferred_element_type=f32)
+        part = part.astype(bf16)
+
+        @pl.when(lax.rem(it, 2) == 0)
+        def _():
+            pair[k] = part
+
+        @pl.when(lax.rem(it, 2) == 1)
+        def _():
+            stage[k] = part
+
+        for kk in range(4):
+
+            @pl.when(it == 2 * kk + 1)
+            def _(kk=kk):
+                reduce.swaps[Reduce.THEIRS[kk]].start()
+
+        mix_two[slot] = lax.dot_general(hidden, w[2], NT, preferred_element_type=f32).astype(bf16)
+        store_mix(it, slot).start()
+        rows_t[:, here] = row.T
+        go_t[:, here] = grad.T
+        return carry
+
+    lax.fori_loop(0, n, blocks, 0)
+    reduce.join(3)
+    reduce.out[0].start()
+    width = rows.shape[2]
+
+    def weight_grad(j, left):
+        def part(i, carry):
+            at = pl.ds(pl.multiple_of(i * 256, 256), 256)
+            value = jnp.dot(left[at, :], h[j], preferred_element_type=f32)
+            w[j, at, :] = value.astype(bf16)
+            return carry
+
+        lax.fori_loop(0, width // 256, part, 0)
+        outs = [
+            pltpu.make_async_copy(
+                w.at[j, :, t * hid : (t + 1) * hid], grads.at[t, j], sd.at[j, t]
+            )
+            for t in range(m)
+        ]
+        for copy in outs:
+            copy.start()
+        return outs
+
+    outs = weight_grad(0, rows_t)
+    reduce.ready()
+    reduce.first(dnorm)
+    reduce.send_fro()
+    outs += weight_grad(1, rows_t)
+    outs += weight_grad(2, go_t)
+    gather.swap.wait_send()
+    gather.ahead.wait_send()
+    gather.back.wait_send()
+    gather.relay.wait_send()
+    for copy in gather.share:
+        copy.wait_send()
+    store_mix(n - 2, 0).wait()
+    store_mix(n - 1, 1).wait()
+    reduce.finish(dnorm)
+    for copy in outs:
+        copy.wait()
+
+
+def feed(n, m, norm, go, w_in, ident):
+    tokens, width = norm.shape
+    hid = w_in.shape[3]
+    length = n * tokens
+    block = pltpu.VMEM((n, tokens, width), bf16)
+    return pl.pallas_call(
+        functools.partial(feed_body, n, m),
+        out_shape=(
+            jax.ShapeDtypeStruct((tokens, width), f32),
+            jax.ShapeDtypeStruct(w_in.shape, bf16),
+            jax.ShapeDtypeStruct((n, tokens, width), bf16),
+        ),
+        in_specs=[pl.BlockSpec(memory_space=ANY)] * 3,
+        out_specs=[
+            pl.BlockSpec(memory_space=pltpu.VMEM),
+            pl.BlockSpec(memory_space=ANY),
+            pl.BlockSpec(memory_space=ANY),
+        ],
+        scratch_shapes=[
+            block,
+            pltpu.VMEM((width, length), bf16),
+            pltpu.VMEM((width, length), bf16),
+            pltpu.VMEM((2, tokens, width), bf16),
+            pltpu.VMEM((3, width, m * hid), bf16),
+            pltpu.VMEM((3, length, m * hid), bf16),
+            pltpu.VMEM((2, tokens, width), bf16),
+        ]
+        + [pltpu.VMEM((slots, tokens, width), bf16) for slots in Reduce.SLOTS]
+        + [
+            pltpu.VMEM((4, tokens, width), bf16),
+            pltpu.SemaphoreType.DMA((2, Gather.COPIES)),
+            pltpu.SemaphoreType.DMA((4, 4)),
+            pltpu.SemaphoreType.DMA((1,)),
+            pltpu.SemaphoreType.DMA((3, m)),
+            pltpu.SemaphoreType.DMA((2,)),
+            pltpu.SemaphoreType.DMA((2,)),
+            pltpu.SemaphoreType.DMA((3, m)),
+        ],
+        compiler_params=pltpu.CompilerParams(
+            collective_id=ident, has_side_effects=True, vmem_limit_bytes=60 << 20
+        ),
+        cost_estimate=pl.CostEstimate(
+            flops=18 * length * width * m * hid,
+            transcendentals=length * m * hid,
+            bytes_accessed=60_000_000,
+        ),
+        name="feed",
+    )(norm, go, w_in)
 
 
 def split_heads(w, groups):
@@ -1014,80 +1488,46 @@
         strip = query_weight.shape[0]
         hid = gate_weight.shape[1] // n
 
-        packed = jnp.concatenate(
-            [split_heads(w, n) for w in (query_weight, key_weight, value_weight)], axis=2
+        packed = spread(
+            jnp.concatenate(
+                [split_heads(w, n) for w in (query_weight, key_weight, value_weight)], axis=2
+            )
         )
-        cols = packed.shape[2]
-        gains = jnp.concatenate([first_gain, second_gain])
-        gain_rows = jnp.pad(gains[None, :], ((0, 7), (0, cols - 2 * strip)))
-        packed = jnp.concatenate(
-            [packed, jnp.broadcast_to(gain_rows[None], (n, 8, cols))], axis=1
+        wide = packed.shape[2]
+        gains = jnp.pad(
+            jnp.stack([first_gain, second_gain]), ((0, 6), (0, LANES - strip))
         )
         places = jnp.concatenate([doc_ids, positions], axis=0)
-        output_full = lax.all_gather(output_weight, ("seq", "tp"), axis=0, tiled=True)
-
-        x_all, places_all, w_all, ffn_mine = entry(
-            n, m, x, places, packed, gate_weight, up_weight, down_weight
+        x_all, places_all, w_all, gains_all = entry(n, m, x, places, packed, gains)
+        docs = places_all[:, 0].reshape(1, length)
+        wqkv = w_all.reshape(width, wide)
+        gain_one, gain_two = [
+            gains_all[:, :, i, :strip].reshape(1, width).astype(f32) for i in range(2)
+        ]
+        lane = jnp.arange(LANES) % SLOT
+        inverse = jnp.where(
+            lane < HALF, rope_base ** (-(lane.astype(f32) * 2.0 / HEAD_SIZE)), 0.0
+        )[None]
+
+        norm_one, q, k, v, cosine, sine, ffn_mine, output_rows = project(
+            n, m, heads, x_all, gain_one, wqkv, places_all, inverse,
+            gate_weight, up_weight, down_weight, output_weight, 8,
         )
         ffn_all = lax.all_gather(ffn_mine, "tp", axis=0, tiled=False)
-        x_all = x_all.reshape(length, width)
-        docs = places_all[:, 0].reshape(1, length)
-        places_seq = places_all[:, 1].reshape(length, 1).astype(f32)
-
-        ordered = w_all.transpose(1, 0, 2, 3)
-        wqkv = spread(ordered[:, :, :strip].reshape(width, cols))
-        gain_one = ordered[:, :, strip, :strip].reshape(1, width).astype(f32)
-        gain_two = ordered[:, :, strip, strip : 2 * strip].reshape(1, width).astype(f32)
-
-        lane = jnp.arange(SLOT)
-        inverse = jnp.where(
-            lane < HALF, rope_base ** (-(lane.astype(f32) * 2.0 / HEAD_SIZE)), 0.0
+        o, low, lse, begin, output_full, grad_all = attend(
+            n, m, factor, q, k, v, docs, output_rows.reshape(m * strip, width), out_grad[0], 9
         )
-        angles = places_seq * inverse[None, :]
-        cos, sin = jnp.cos(angles), jnp.sin(angles)
-        cosine = jnp.concatenate([cos, cos], axis=1)
-        sine = jnp.concatenate([-sin, sin], axis=1)
-        begin = jnp.zeros((1, length), jnp.int32)
-        for d in range(3):
-            begin = begin + jnp.where(docs > d, jnp.sum((docs == d).astype(jnp.int32)), 0)
-
-        norm_one, q, k, v = project(heads, x_all, gain_one, wqkv, cosine, sine)
-        o, low, lse = attend(factor, q, k, v, begin)
-        mine = plane_swap(n, m, low.reshape(n, rows, heads * LANES), 1)
+        output_full = output_full.reshape(-1, width)
+        (mine,) = plane_swap(n, m, 1, low.reshape(n, rows, heads * LANES))
         attn_low = gathered(mine.transpose(1, 0, 2).reshape(rows, n * heads * LANES))
 
         x_f = x.astype(f32)
         resid = x_f + jnp.dot(attn_low, output_full, preferred_element_type=f32)
         scale_two = lax.rsqrt(jnp.mean(resid * resid, axis=1, keepdims=True) + norm_epsilon)
         norm_two = (resid * scale_two * gain_two).astype(bf16)
-        rows_all = plane_gather(n, m, norm_two, 2).reshape(length, width)
         grad_low = out_grad[0]
-        grad_all = lax.all_gather(grad_low, "seq", axis=0, tiled=True)
-
-        gate_w, up_w, down_w = [
-            ffn_all[:, i].transpose(1, 0, 2).reshape(width, m * hid) for i in range(3)
-        ]
-        gate_pre = jnp.dot(rows_all, gate_w, preferred_element_type=f32)
-        up_pre = jnp.dot(rows_all, up_w, preferred_element_type=f32)
-        gate_sig = jax.nn.sigmoid(gate_pre)
-        gate_act = gate_pre * gate_sig
-        hidden = (gate_act * up_pre).astype(bf16)
-        mixed = times_transpose(hidden, down_w).astype(bf16)
-        dhidden = jnp.dot(grad_all, down_w, preferred_element_type=f32)
-        dgate = (dhidden * up_pre * gate_sig * (1.0 + gate_pre * (1.0 - gate_sig))).astype(bf16)
-        dup = (dhidden * gate_act).astype(bf16)
-        dnorm_part = (times_transpose(dgate, gate_w) + times_transpose(dup, up_w)).astype(bf16)
-        dnorm_two = plane_reduce(n, m, dnorm_part.reshape(n, rows, width), 3)
-
-        terms = [
-            outer_product(a, b).astype(bf16).reshape(width, m, hid).transpose(1, 0, 2)
-            for a, b in ((rows_all, dgate), (rows_all, dup), (grad_all, hidden))
-        ]
-        ffn_terms = jnp.stack(terms, axis=1)
+        dnorm_two, ffn_terms, mixed = feed(n, m, norm_two, grad_all, ffn_all, 2)
         ffn_sum = lax.psum_scatter(ffn_terms, "tp", scatter_dimension=0, tiled=False)
-
-        mixed_sum = plane_reduce(n, m, mixed.reshape(n, rows, width), 4)
-        layer_output = (resid + mixed_sum).astype(bf16)[None]
 
         inner = gain_two * dnorm_two
         moment = jnp.mean(resid * inner, axis=1, keepdims=True)
@@ -1097,20 +1537,28 @@
             - resid * scale_two * scale_two * scale_two * moment
         )
         dbranch = dresid.astype(bf16)
-        output_term = outer_product(attn_low, dbranch)
-        output_grad = lax.psum_scatter(
-            output_term.astype(bf16), ("seq", "tp"), scatter_dimension=0, tiled=True
-        ).astype(f32)
+        output_term = outer_product(attn_low, dbranch).astype(bf16).reshape(n, m * strip, width)
         dheads = spread(times_transpose(dbranch, output_full).astype(bf16))
         dheads = dheads.reshape(rows, n, heads * LANES).transpose(1, 0, 2)
-        go = plane_swap(n, m, dheads, 5).reshape(length, heads * LANES)
-
-        dqkv = attend_back(factor, scale, q, k, v, go, o, lse, begin, cosine, sine)
+        gain_term = jnp.sum(dnorm_two * resid * scale_two, axis=0)
+        go, gain_parts = plane_swap(n, m, 5, dheads, gain_term.reshape(n, 1, m * strip))
+        go = go.reshape(length, heads * LANES)
+        gain_part = jnp.sum(gain_parts, axis=(0, 1)).reshape(m, 1, strip)
+
+        dqkv, mixed_sum, output_sum = attend_back(
+            n, m, factor, scale, q, k, v, go, o, lse, begin, cosine, sine, mixed, output_term, 3
+        )
+        layer_output = (resid + mixed_sum).astype(bf16)[None]
+        output_grad = lax.psum_scatter(
+            output_sum.astype(bf16), "tp", scatter_dimension=0, tiled=True
+        ).astype(f32)
         dnorm_one_part = times_transpose(dqkv, wqkv).astype(bf16)
         qkv_term = gathered(outer_product(norm_one, dqkv).astype(bf16))
+        cols = qkv_term.shape[1]
         qkv_term = qkv_term.reshape(n, m, strip, cols).transpose(1, 0, 2, 3)
-        qkv_sum = lax.psum_scatter(qkv_term, "tp", scatter_dimension=0, tiled=False)
-        dnorm_one = plane_reduce(n, m, dnorm_one_part.reshape(n, rows, width), 6)
+        dnorm_one, ffn_out, qkv_out, gain_sums = last(
+            n, m, dnorm_one_part.reshape(n, rows, width), ffn_sum, qkv_term, gain_part, 6
+        )
 
         scale_one = lax.rsqrt(jnp.mean(x_f * x_f, axis=1, keepdims=True) + norm_epsilon)
         inner = gain_one * dnorm_one
@@ -1119,7 +1567,6 @@
             dresid + scale_one * inner - x_f * scale_one * scale_one * scale_one * moment
         )[None]
 
-        ffn_out, qkv_out = final_swap(n, m, ffn_sum, qkv_sum, 7)
         gate_grad, up_grad, down_grad = [ffn_out[i].astype(f32) for i in range(3)]
         kv = HEAD_SIZE * KEY_VALUE_HEADS // n
         split = heads * HEAD_SIZE
@@ -1137,12 +1584,7 @@
             + jnp.sum(value_weight.astype(f32) * value_grad, axis=1)
         )
         first_gain_grad = one / first_gain.astype(f32)
-        two = jnp.sum(
-            gate_weight.astype(f32) * gate_grad + up_weight.astype(f32) * up_grad, axis=1
-        )
-        second_gain_grad = lax.psum_scatter(
-            two, "tp", scatter_dimension=0, tiled=True
-        ) / second_gain.astype(f32)
+        second_gain_grad = jnp.sum(gain_sums, axis=(0, 1))
         return (
             layer_output,
             input_grad,
@@ -1162,7 +1604,7 @@
 
 def solution(mesh):
     n, m = mesh.shape["seq"], mesh.shape["tp"]
-    fits = KEY_VALUE_HEADS == n
+    fits = n == KEY_VALUE_HEADS == 8
     return jax.shard_map(
         fast_layer(n, m) if fits else on_device,
         mesh=mesh,

time: 694 us -> 522 us (0.75); the launches traced: 683 us -> 521 us
  matrix products: 90.1 us -> 24.9 us
  waiting for transfers between devices: 135 us -> 85.3 us
  local copies, waits for them, and re-layouts: 63.1 us -> 40.3 us
  blocking collectives: 11.2 us -> 0 us
  other arithmetic: 31.3 us -> 21.4 us
    all_gather x2 -> x0, waiting for transfers between devices: 53.5 us -> none  [the longest x1 53.5 us: on_plane(): lax.all_gather(output_weight, ('seq', 'tp'), axis=0, tiled=True)]
    dot_general x3 -> x0, matrix products: 25 us -> none  [the longest x1 11.1 us: on_plane(): dhidden = jnp.dot(grad_all, down_w, preferred_element_type=f32)]
    dot_general x5 -> x2, matrix products: 34.8 us -> 10.5 us  [outer_product(): lax.dot_general(left, right, (((0,), (0,)), ((), ())), preferred_element_...]
    reduce_scatter x1, waiting for transfers between devices: 61.8 us -> 77.6 us  [on_plane(): lax.psum_scatter(ffn_terms, 'tp', scatter_dimension=0, tiled=False)]
    dot_general x5 -> x2, matrix products: 26.4 us -> 10.7 us  [times_transpose(): lax.dot_general(left, right, (((1,), (1,)), ((), ())), preferred_element_...]
    transpose x5 -> x0, local copies, waits for them, and re-layouts: 11.3 us -> none  [the longest x4 11.3 us: on_plane(): ffn_all[:, i].transpose(1, 0, 2).reshape(width, m * hid)]
    unnamed x1 -> x0, blocking collectives: 11.2 us -> none
    all_gather x1, waiting for transfers between devices: 17.9 us -> 6.99 us  [on_plane(): ffn_all = lax.all_gather(ffn_mine, 'tp', axis=0, tiled=False)]
  transfers between devices with their start and end apart: 6 -> 3, of which waited for: 3 -> 2; matrix products, arithmetic and copies ran while one was open for 20% -> 7% of each run, Pallas kernels for 26% -> 14%
where the time goes in v2:
time: 522 us; the launch traced here: 521 us
  Pallas kernels  335 us (64%)
  waiting for transfers between devices  85.3 us (16%)
  local copies, waits for them, and re-layouts  40.3 us (8%)
  matrix products  24.9 us (5%)
  other arithmetic  21.4 us (4%)
  between operations  14.1 us (3%)
    reduce_scatter x1, waiting for transfers between devices, on_plane(): lax.psum_scatter(ffn_terms, 'tp', scatter_dimension=0, tiled=False)  77.6 us
    pallas_call x1, Pallas kernels, feed(): pl.pallas_call(functools.partial(feed_body, n, m), out_shape=(jax.ShapeDt...  68.3 us
    pallas_call x1, Pallas kernels, attend(): pl.pallas_call(functools.partial(attend_body, n, m, factor), grid=(heads,...  61.5 us
    pallas_call x1, Pallas kernels, attend_back(): pl.pallas_call(functools.partial(attend_back_body, n, m, factor, scale, h...  58.4 us
    pallas_call x1, Pallas kernels, entry(): pl.pallas_call(functools.partial(entry_body, n, m), out_shape=(jax.ShapeD...  51.1 us
    pallas_call x1, Pallas kernels, last(): pl.pallas_call(functools.partial(last_body, n, m), out_shape=(jax.ShapeDt...  47.2 us
    pallas_call x2, Pallas kernels, plane_swap(): pl.pallas_call(functools.partial(swap_body, n, m, count), out_shape=tuple...  28.9 us
    pallas_call x1, Pallas kernels, project(): pl.pallas_call(functools.partial(project_body, n, m, heads), grid=(tiles,...  19.1 us
  transfers between devices with their start and end apart: 3, of which 2 were waited for; matrix products, arithmetic and copies ran while one was open for 7% of the time, Pallas kernels for 14%

profile of v2, /device:TPU:0, one launch (start us, length us, event | category | flops | bytes accessed | tf_op | source)
XLA Modules:
  0.0 521.0 jit_solution(27687583280810978)
XLA Ops:
  14.4 51.1 %entry.1 = (bf16[8,256,1536]{2,1,0:T(8,128)(2,1)}, s32[8,2,256]{2,1,0:T(2,128)}, bf16[8,4,48,512]{3,2,1,0:T(8,128)(2,1)}, bf16[8,4,8,128]{3,2,1,0:T(8,128)(2,1)}) custom-call(bf16[256,1536]{1,0:T(8,128)(2,1)} %bitcast.70, s32[2,256]{1,0:T(2,128)} %pad_add_fusion.places, bf16[8,48,512]{2,1,0:T(8,128)(2,1)} %reshape.182.wqkv, bf16[8,128]{1,0:T(8,128)(2,1)} %fusion.15.gains), custom_call_target="tpu_custom_call" | custom-call | bytes 100000000 | tf_op jit(solution)/shard_map/entry/pallas_call | solution.py:548
  67.3 19.1 %project.1 = (bf16[2048,1536]{1,0:T(8,128)(2,1)}, bf16[2,2048,128]{2,1,0:T(8,128)(2,1)}, bf16[2048,128]{1,0:T(8,128)(2,1)}, bf16[2048,128]{1,0:T(8,128)(2,1)}, f...) custom-call(bf16[8,256,1536]{2,1,0:T(8,128)(2,1)} %get-tuple-element.41., ...), custom_call_target="tpu_custom_call" | custom-call | flops 9663676416 | bytes 30000000 | tf_op jit(solution)/shard_map/project/pallas_call | solution.py:887
  87.4 61.5 %attend.1 = (f32[2,2048,128]{2,1,0:T(8,128)}, bf16[2048,256]{1,0:T(8,128)(2,1)}, f32[2,1,2048]{2,1,0:T(1,128)}, s32[1,2048]{1,0:T(1,128)}, bf16[8,192,1536]{2,1,0:T(8,128)(2,1)}, /*index=5*/bf16[8,256,1536]{2,1,0:T(8,128)(2,1)}) custom-call(bf16[2,2048,128]{2,1,0:T(8,128)(2,1)} %get-tuple-element.45.q, bf16[2048,128]{1,0:T(8,128)(2,1)} %get-tuple-element.46.k, ...), custom_call_target="tpu_custom_call" | custom-call | flops 8053063680 | bytes 120000000 | tf_op jit(solution)/shard_map/attend/pallas_call | solution.py:1023
  148.9 13.1 %plane_swap.2 = bf16[8,256,256]{2,1,0:T(8,128)(2,1)} custom-call(bf16[8,256,256]{2,1,0:T(8,128)(2,1)} %bitcast.76), custom_call_target="tpu_custom_call" | custom-call | bytes 40000000 | tf_op jit(solution)/shard_map/plane_swap/pallas_call | solution.py:593
  163.6 3.8 multiply_reduce_fusion.2
  168.5 7.0 %all-gather.3.cloned.1.call-done = bf16[12,1536,128]{2,1,0:T(8,128)(2,1)} async-done(((bf16[3,1536,128]{2,1,0:T(8,128)(2,1)}), bf16[12,1536,128]{2,1,0:T(8,128)(2,1)}) %all-gather.3.cloned.1.call-update) | async-done | bytes 4718608 | tf_op jit(solution)/shard_map/all_gather | solution.py:1516
  175.5 68.3 %feed.1 = (f32[256,1536]{1,0:T(8,128)}, bf16[4,3,1536,128]{3,2,1,0:T(8,128)(2,1)}, bf16[8,256,1536]{2,1,0:T(8,128)(2,1)}) custom-call(bf16[256,1536]{1,0:T(8,128)(2,1)} %multiply_convert_fusion.mine, bf16[8,256,1536]{2,1,0:T(8,128)(2,1)} %get-tuple-element.51.go, bf16[4,3,1536,128]{3,2,1,0:T(8,128)(2,1)} %bitcast.86), custom_call_target="tpu_custom_call" | custom-call | flops 28991029248 | bytes 60000000 | tf_op jit(solution)/shard_map/feed/pallas_call | solution.py:1402
  243.8 2.0 multiply_reduce_fusion
  246.5 5.2 convolution_convert_fusion.3
  251.7 3.5 convolution_convert_fusion.1
  255.8 2.3 copy.36
  260.7 15.9 %plane_swap.3 = (bf16[8,256,256]{2,1,0:T(8,128)(2,1)}, f32[8,1,192]{2,1,0:T(1,128)}) custom-call(bf16[8,256,256]{2,1,0:T(8,128)(2,1)} %bitcast.71, f32[8,1,192]{2,1,0:T(1,128)} %reshape.189.refs_1_), custom_call_target="tpu_custom_call" | custom-call | bytes 40000000 | tf_op jit(solution)/shard_map/plane_swap/pallas_call | solution.py:593
  276.6 58.4 %attend_back.1 = (bf16[2048,512]{1,0:T(8,128)(2,1)}, f32[256,1536]{1,0:T(8,128)}, f32[192,1536]{1,0:T(8,128)}) custom-call(bf16[2,2048,128]{2,1,0:T(8,128)(2,1)} %get-tuple-element.45.q, bf16[2048,128]{1,0:T(8,128)(2,1)} %get-tuple-element.46.k, bf16[2048,128]{1,0:T(8,128)(2,1)} %get-tuple-element.47.v, bf16[2048,256]{1,0:T(8,128)(2,1)} %bitcast.89, ...), custom_call_target="tpu_custom_call" | custom-call | flops 13421772800 | bytes 150000000 | tf_op jit(solution)/shard_map/attend_back/pallas_call | solution.py:1188
  335.0 2.1 convert_element_type.155
  339.0 7.0 %convolution_convert_fusion.2 = bf16[1536,512]{0,1:T(8,128)(2,1)S(1)} fusion(bf16[2048,1536]{1,0:T(8,128)(2,1)} %get-tuple-element.64, bf16[2048,512]{1,0:T(8,128)(2,1)} %get-tuple-element.62), kind=kOutput, calls=%fused_computation.2 | convolution fusion | flops 3222011904 | bytes 9961472 | tf_op jit(solution)/shard_map/dot_general | solution.py:40
  346.0 4.5 reshape.214
  350.5 4.9 copy.39
  355.5 2.6 fusion.7
  358.1 5.5 %convolution_convert_fusion = bf16[2048,1536]{1,0:T(8,128)(2,1)} fusion(bf16[2048,512]{1,0:T(8,128)(2,1)S(1)} %copy-done.21, bf16[1536,512]{1,0:T(8,128)(2,1)S(1)} %bitcast.88), kind=kOutput, calls=%fused_computation | convolution fusion | flops 3224371200 | bytes 9961472 | tf_op jit(solution)/shard_map/dot_general | solution.py:46
  365.3 77.6 %reduce-scatter.3.cloned.1.call-done = bf16[1,3,1536,128]{3,2,1,0:T(8,128)(2,1)} async-done(((bf16[4,3,1536,128]{3,2,1,0:T(8,128)(2,1)}), bf16[1,3,1536,128]{3,2,1,0:T(8,128)(2,1)}) %reduce-scatter.3.cloned.1.call-update) | async-done | bytes 1179664 | tf_op jit(solution)/shard_map/reduce_scatter | solution.py:1530
  442.9 2.8 copy-done
  446.9 47.2 %last.1 = (f32[256,1536]{1,0:T(8,128)S(1)}, bf16[3,192,1024]{2,1,0:T(8,128)(2,1)S(1)}, bf16[8,48,384]{2,1,0:T(8,128)(2,1)S(1)}, f32[4,1,48]{2,1,0:T(1,128)S(1)}) custom-call(bf16[8,256,1536]{2,1,0:T(8,128)(2,1)S(1)} %bitcast.62, bf16[3,1536,128]{2,1,0:T(8,128)(2,1)S(1)} %bitcast.64, bf16[4,8,48,384]{3,2,1,0:T(8,128)(2,1)S(1)} %bitcast.63, ...), custom_call_target="tpu_custom_call" | custom-call | bytes 150000000 | tf_op jit(solution)/shard_map/last/pallas_call | solution.py:788
  497.4 2.1 copy.40
  499.4 1.8 reshape.198
  (94 shorter events, 37.6 us)
Async XLA Ops:
  7.2 168.3 %all-gather.3.cloned.1.call-start = ((), (), s32[]{:S(2)}) async-start(), calls=%async_computation.4 | async-start | bytes 5898240 | tf_op jit(solution)/shard_map/all_gather | solution.py:1516
  11.8 1.4 copy-start.17
  11.8 1.4 copy-start.18
  11.8 2.0 copy-start.15
  11.8 2.0 copy-start.19
  67.3 19.4 %copy-start.14 = (s32[8,2,256]{2,1,0:T(2,128)S(1)}, s32[8,2,256]{2,1,0:T(2,128)}, u32[]{:S(2)}) copy-start(s32[8,2,256]{2,1,0:T(2,128)} %get-tuple-element.44.places) | copy-start | bytes 49156
  86.4 277.1 %reduce-scatter.5.cloned.1.call-start = ((), (), s32[]{:S(2)}) async-start(), calls=%async_computation.3 | async-start | bytes 737280 | tf_op jit(solution)/shard_map/reduce_scatter | solution.py:1552
  161.9 1.6 copy-start.6
  243.8 2.0 copy-start.7
  243.8 2.1 copy-start.8
  246.5 5.2 %copy-start.4 = (f32[256,1536]{1,0:T(8,128)}, f32[256,1536]{1,0:T(8,128)S(1)}, u32[]{:S(2)}) copy-start(f32[256,1536]{1,0:T(8,128)S(1)} %multiply_subtract_fusion) | copy-start | bytes 4718596
  337.2 105.7 %reduce-scatter.3.cloned.1.call-start = ((), (), s32[]{:S(2)}) async-start(), calls=%async_computation.2 | async-start | bytes 5898240 | tf_op jit(solution)/shard_map/reduce_scatter | solution.py:1530
  337.2 1.6 copy-start.13
  355.5 2.7 copy-start.20
  355.5 2.7 copy-start.21
  442.9 2.8 copy-start
  445.7 1.3 copy-start.1
  497.4 11.8 %copy-start.3 = (bf16[3,192,1024]{2,1,0:T(8,128)(2,1)S(1)}, bf16[3,192,1024]{2,1,0:T(8,128)(2,1)}, u32[]{:S(2)}) copy-start(bf16[3,192,1024]{2,1,0:T(8,128)(2,1)} %copy-done.2) | copy-start | bytes 3538948
  510.7 1.4 copy-start.5
  512.1 1.7 copy-start.9
  512.1 1.7 copy-start.10
  512.1 1.7 copy-start.11
  512.1 1.7 copy-start.12
  512.1 1.9 copy-start.16
  (1 other events, 1.0 us)
Sparse Core Ops, SparseCore 0:
  86.6 88.8 all-gather.2
  337.3 19.6 reduce-scatter.4
  359.3 83.5 reduce-scatter.2

commit v3 on v2

--- a/solution.py
+++ b/solution.py
@@ -347,6 +347,7 @@
 SLOT = LANES // 2
 f32 = jnp.float32
 bf16 = jnp.bfloat16
+COST = pl.CostEstimate(flops=1_000_000, transcendentals=0, bytes_accessed=100_000)
 
 
 class Plane:
@@ -369,6 +370,15 @@
 
     def same(self, chip):
         return (2 * chip + self.c, self.t)
+
+    def number(self, k, other):
+        c, q = self.c, self.q
+        low, high = lax.rem(k, 2), k // 2
+        dx = low * (1 - c) + high * c
+        dy = high * (1 - c) + low * c
+        x, y = lax.rem(q, 2), q // 2
+        chip = 2 * (y + dy - 2 * y * dy) + x + dx - 2 * x * dx
+        return 2 * chip + c + other * (1 - 2 * c)
 
     def sibling(self):
         return (2 * self.q + 1 - self.c, self.t)
@@ -496,75 +506,6 @@
             )
         )
     return [own] + copies
-
-
-def entry_body(n, m, x, places, wqkv, gains, x_all, places_all, w_all, gains_all, sx, rem, sz, loc):
-    plane = Plane(n, m)
-    enter_plane(plane, True)
-    gather = Gather(plane, x, x_all, sx.at[0], sx.at[1], loc.at[0])
-    copies = exchange(
-        plane,
-        lambda i: wqkv.at[i],
-        lambda i: w_all.at[i, plane.t],
-        rem.at[0, 0],
-        rem.at[0, 1],
-        loc.at[1],
-    )
-    copies += exchange(
-        plane,
-        lambda i: gains,
-        lambda i: gains_all.at[i, plane.t],
-        rem.at[1, 0],
-        rem.at[1, 1],
-        loc.at[2],
-    )
-    few = exchange(
-        plane, lambda i: places, lambda i: places_all.at[i], rem.at[2, 0], rem.at[2, 1], loc.at[3]
-    )
-    for copy in copies:
-        copy.start()
-    gather.start()
-    for copy in few:
-        copy.start()
-    for copy in copies:
-        copy.wait()
-    across = []
-    for i, ref in enumerate((w_all, gains_all)):
-
-        def slot(t, ref=ref):
-            return ref.at[:, plane.t]
-
-        across += fan(plane, slot, slot, sz.at[i, 0], sz.at[i, 1])
-    for copy in across:
-        copy.start()
-    gather.relay_near()
-    gather.relay_far()
-    for copy in few + across:
-        copy.wait()
-    gather.finish()
-
-
-def entry(n, m, x, places, wqkv, gains):
-    return pl.pallas_call(
-        functools.partial(entry_body, n, m),
-        out_shape=(
-            jax.ShapeDtypeStruct((n,) + x.shape, x.dtype),
-            jax.ShapeDtypeStruct((n,) + places.shape, places.dtype),
-            jax.ShapeDtypeStruct((n, m) + wqkv.shape[1:], wqkv.dtype),
-            jax.ShapeDtypeStruct((n, m) + gains.shape, gains.dtype),
-        ),
-        in_specs=[pl.BlockSpec(memory_space=ANY)] * 4,
-        out_specs=[pl.BlockSpec(memory_space=ANY)] * 4,
-        scratch_shapes=[
-            pltpu.SemaphoreType.DMA((2, Gather.COPIES)),
-            pltpu.SemaphoreType.DMA((3, 2, n - 1)),
-            pltpu.SemaphoreType.DMA((2, 2, m - 1)),
-            pltpu.SemaphoreType.DMA((4,)),
-        ],
-        compiler_params=pltpu.CompilerParams(collective_id=0, has_side_effects=True),
-        cost_estimate=pl.CostEstimate(flops=0, transcendentals=0, bytes_accessed=100_000_000),
-        name="entry",
-    )(x, places, wqkv, gains)
 
 
 def swap_body(n, m, count, *refs):
@@ -600,7 +541,7 @@
             pltpu.SemaphoreType.DMA((count,)),
         ],
         compiler_params=pltpu.CompilerParams(collective_id=ident, has_side_effects=True),
-        cost_estimate=pl.CostEstimate(flops=0, transcendentals=0, bytes_accessed=40_000_000),
+        cost_estimate=COST,
         name="plane_swap",
     )(*arrays)
 
@@ -694,16 +635,16 @@
 
         in_tiles(self.rows, add)
 
-    def finish(self, total):
+    def finish(self, total, out=None):
         far = self.far
+        out = total if out is None else out
         self.out[0].wait_send()
         self.out[1].wait()
         self.out[2].wait()
 
         def add(at):
-            total[at, :] = (
-                total[at, :] + far[1, at, :].astype(f32) + far[2, at, :].astype(f32)
-            )
+            value = total[at, :] + far[1, at, :].astype(f32) + far[2, at, :].astype(f32)
+            out[at, :] = value.astype(out.dtype)
 
         in_tiles(self.rows, add)
 
@@ -724,208 +665,367 @@
 
 
 def last_body(
-    n, m, parts, ffn, qkv, vec, total, ffn_out, qkv_out, vec_out,
-    pair, near, far, sr, lr, got, summed, sems, st, loc,
+    n, m, dqkv, w, narrow, norm_t, ffn, wo, vec, total, ffn_out, qkv_out, wo_out, vec_out,
+    pair, near, far, sr, lr, stage, norms, mine, got, summed, sems, st, loc,
 ):
     plane = Plane(n, m)
+    load = pltpu.make_async_copy(norm_t, norms, loc.at[0])
+    load.start()
     enter_plane(plane, True)
-    rows = ffn_out.shape[1]
-    width = ffn.shape[2]
-    across = fan(plane, lambda t: qkv.at[t], lambda t: got.at[t], st.at[0, 0], st.at[0, 1])
-    across_vec = fan(plane, lambda t: vec.at[t], lambda t: vec_out.at[t], st.at[1, 0], st.at[1, 1])
-    mine = [
-        pltpu.make_async_copy(qkv.at[plane.t], got.at[plane.t], loc.at[0]),
-        pltpu.make_async_copy(vec.at[plane.t], vec_out.at[plane.t], loc.at[1]),
+    rows, width = ffn_out.shape[1], ffn.shape[2]
+    across = fan(plane, lambda t: wo.at[t], lambda t: wo_out.at[t], st.at[1, 0], st.at[1, 1])
+    across += fan(plane, lambda t: vec.at[t], lambda t: vec_out.at[t], st.at[2, 0], st.at[2, 1])
+    across += [
+        pltpu.make_async_copy(wo.at[plane.t], wo_out.at[plane.t], loc.at[1]),
+        pltpu.make_async_copy(vec.at[plane.t], vec_out.at[plane.t], loc.at[2]),
     ]
-    for copy in across + across_vec + mine:
+    for copy in across:
         copy.start()
-    reduce = Reduce(plane, lambda i: parts.at[i], pair, near, far, sr, lr)
-    reduce.start()
     a = exchange(
         plane,
         lambda i: ffn.at[:, pl.ds(pl.multiple_of(i * rows, rows), rows), :],
         lambda i: ffn_out.at[:, :, pl.ds(pl.multiple_of(i * width, width), width)],
         sems.at[0, 0],
         sems.at[0, 1],
-        loc.at[2],
-    )
-    for copy in a:
+        loc.at[3],
+    )
+    reduce = Reduce(plane, None, pair, near, far, sr, lr, stage)
+    tokens = pair.shape[1]
+
+    def blocks(it, carry):
+        k = 3 - it // 2
+        other = 1 - lax.rem(it, 2)
+        b = plane.number(k, other)
+        here = pl.ds(pl.multiple_of(b * tokens, tokens), tokens)
+        part = lax.dot_general(dqkv[here, :], w[...], NT, preferred_element_type=f32).astype(bf16)
+
+        @pl.when(other == 0)
+        def _():
+            pair[k] = part
+
+        @pl.when(other == 1)
+        def _():
+            stage[k] = part
+
+        for kk in range(4):
+
+            @pl.when(it == 2 * (3 - kk))
+            def _(kk=kk):
+                reduce.swaps[Reduce.THEIRS[kk]].start()
+
+        @pl.when(it == 2)
+        def _():
+            for copy in a:
+                copy.start()
+
+        return carry
+
+    lax.fori_loop(0, n, blocks, 0)
+    reduce.send_to()
+    load.wait()
+    strip = summed.shape[1]
+
+    def weight_grads(s, carry):
+        at = pl.ds(pl.multiple_of(s * m * strip, m * strip), m * strip)
+        value = jnp.dot(norms[at, :], dqkv[...], preferred_element_type=f32).astype(bf16)
+        value = jnp.dot(value, narrow[...], preferred_element_type=f32).astype(bf16)
+        for t in range(m):
+            mine[s, t] = value[t * strip : (t + 1) * strip]
+        return carry
+
+    lax.fori_loop(0, n, weight_grads, 0)
+    over = fan(plane, lambda t: mine.at[:, t], lambda t: got.at[t], st.at[0, 0], st.at[0, 1])
+    for copy in over:
         copy.start()
-    reduce.send_to()
     reduce.ready()
     reduce.first(total)
-    for copy in across + across_vec + mine:
+    reduce.send_fro()
+    for copy in over:
         copy.wait()
-    groups, strip, _ = summed.shape
-
-    for g in range(groups):
-
-        def add(at, g=g):
-            value = got[0, g, at, :].astype(f32)
-            for t in range(1, m):
-                value = value + got[t, g, at, :].astype(f32)
-            summed[g, at, :] = value.astype(bf16)
-
-        in_tiles(strip, add)
+
+    def add(s, carry):
+        value = mine[s, plane.t].astype(f32)
+        for k in range(1, m):
+            value = value + got[plane.tp_behind(k), s].astype(f32)
+        summed[s] = value.astype(bf16)
+        return carry
+
+    lax.fori_loop(0, n, add, 0)
     b = exchange(
         plane,
         lambda i: summed.at[i],
         lambda i: qkv_out.at[i],
         sems.at[1, 0],
         sems.at[1, 1],
-        loc.at[3],
+        loc.at[4],
     )
     for copy in b:
         copy.start()
-    reduce.send_fro()
     reduce.finish(total)
-    for copy in a + b:
+    for copy in a + b + across:
         copy.wait()
 
 
-def last(n, m, parts, ffn, qkv, vec, ident):
-    rows, width = parts.shape[1:]
+def last(n, m, dqkv, w, narrow, norm_t, ffn, wo, vec, ident):
+    width, length = norm_t.shape
+    tokens = length // n
+    cols = narrow.shape[1]
+    strip = width // (n * m)
+    vmem = pl.BlockSpec(memory_space=pltpu.VMEM)
+    hbm = pl.BlockSpec(memory_space=ANY)
     return pl.pallas_call(
         functools.partial(last_body, n, m),
         out_shape=(
-            jax.ShapeDtypeStruct((rows, width), f32),
+            jax.ShapeDtypeStruct((tokens, width), f32),
             jax.ShapeDtypeStruct((3, ffn.shape[1] // n, ffn.shape[2] * n), ffn.dtype),
-            jax.ShapeDtypeStruct(qkv.shape[1:], qkv.dtype),
+            jax.ShapeDtypeStruct((n, strip, cols), bf16),
+            jax.ShapeDtypeStruct(wo.shape, wo.dtype),
             jax.ShapeDtypeStruct(vec.shape, vec.dtype),
         ),
-        in_specs=[pl.BlockSpec(memory_space=ANY)] * 4,
-        out_specs=[pl.BlockSpec(memory_space=pltpu.VMEM)]
-        + [pl.BlockSpec(memory_space=ANY)] * 3,
-        scratch_shapes=Reduce.scratch(rows, width)
+        in_specs=[vmem] * 3 + [hbm] * 4,
+        out_specs=[vmem] + [hbm] * 4,
+        scratch_shapes=Reduce.scratch(tokens, width)
         + [
-            pltpu.VMEM(qkv.shape, bf16),
-            pltpu.VMEM(qkv.shape[1:], bf16),
+            pltpu.VMEM((4, tokens, width), bf16),
+            pltpu.VMEM((width, length), bf16),
+            pltpu.VMEM((n, m, strip, cols), bf16),
+            pltpu.VMEM((m, n, strip, cols), bf16),
+            pltpu.VMEM((n, strip, cols), bf16),
             pltpu.SemaphoreType.DMA((2, 2, n - 1)),
-            pltpu.SemaphoreType.DMA((2, 2, m - 1)),
-            pltpu.SemaphoreType.DMA((4,)),
+            pltpu.SemaphoreType.DMA((3, 2, m - 1)),
+            pltpu.SemaphoreType.DMA((5,)),
         ],
         compiler_params=pltpu.CompilerParams(
-            collective_id=ident, has_side_effects=True, vmem_limit_bytes=40 << 20
+            collective_id=ident, has_side_effects=True, vmem_limit_bytes=50 << 20
         ),
-        cost_estimate=pl.CostEstimate(flops=0, transcendentals=0, bytes_accessed=150_000_000),
+        cost_estimate=COST,
         name="last",
-    )(parts, ffn, qkv, vec)
+    )(dqkv, w, narrow, norm_t, ffn, wo, vec)
 
 
 def column(row):
     return jnp.broadcast_to(row, (8, row.shape[1])).T[:, :1]
 
 
-def project_body(
-    n, m, heads, x, gain, w, places, inverse, wg, wu, wd, wo, norm, q, k, v, cosine, sine, ffn, wo_z,
-    sems, loc, sz
+def gain_row(tiles, which, strip):
+    stacked = tiles.reshape(-1, LANES).astype(bf16)
+    count = stacked.shape[0] // 8
+    shape = (LANES, count * strip)
+    lane = lax.broadcasted_iota(jnp.int32, shape, 1).astype(f32)
+    owner = jnp.floor((lane + 0.5) * (1.0 / strip))
+    inside = lane - owner * strip
+    pick = lax.broadcasted_iota(jnp.int32, shape, 0).astype(f32) == inside
+    spread_out = jnp.dot(
+        stacked, jnp.where(pick, 1.0, 0.0).astype(bf16), preferred_element_type=f32
+    )
+    shape = spread_out.shape
+    lane = lax.broadcasted_iota(jnp.int32, shape, 1).astype(f32)
+    owner = jnp.floor((lane + 0.5) * (1.0 / strip))
+    row = lax.broadcasted_iota(jnp.int32, shape, 0).astype(f32)
+    mine = row == owner * 8.0 + which
+    return jnp.sum(jnp.where(mine, spread_out, 0.0), axis=0, keepdims=True)
+
+
+def entry_body(
+    n, m, heads, strip, x, places, wqkv, gains, wg, wu, wd, wo, widen, inverse,
+    norm_t, q, k, v, cosine, sine, w, gain_rows, docs, ffn, wo_z,
+    blocks, norms, turned, places_all, w_all, gains_all,
+    sx, rem, sz, sn, loc,
 ):
-    step = pl.program_id(0)
     plane = Plane(n, m)
+    enter_plane(plane, True)
+    tokens = x.shape[0]
+    gather = Gather(plane, x, blocks, sx.at[0], sx.at[1], loc.at[0])
+    first = []
+    for i, (src, dst) in enumerate(((gains, gains_all), (wqkv, w_all))):
+        first += exchange(
+            plane,
+            lambda s, src=src, i=i: src.at[s] if i else src,
+            lambda s, dst=dst: dst.at[s, plane.t],
+            rem.at[i, 0],
+            rem.at[i, 1],
+            loc.at[1 + i],
+        )
+    few = exchange(
+        plane, lambda i: places, lambda i: places_all.at[i], rem.at[2, 0], rem.at[2, 1], loc.at[3]
+    )
+    for copy in first + few:
+        copy.start()
+    gather.start()
+    across = []
+    for i, ref in enumerate((gains_all, w_all)):
+
+        def slot(t, ref=ref):
+            return ref.at[:, plane.t]
+
+        across.append(fan(plane, slot, slot, sz.at[i, 0], sz.at[i, 1]))
+    across.append(fan(plane, lambda t: wo, lambda t: wo_z.at[t], sz.at[2, 0], sz.at[2, 1]))
+    own_wo = pltpu.make_async_copy(wo, wo_z.at[plane.t], loc.at[4])
+    own_wo.start()
+    for copy in first:
+        copy.wait()
+    for copy in across[0] + across[1] + across[2]:
+        copy.start()
+    moves = []
     width, rows = wg.shape[1] // n, wg.shape[0]
-
-    def moves():
-        copies = []
-        for j, weight in enumerate((wg, wu, wd)):
-            copies += exchange(
-                plane,
-                lambda i, w=weight: w.at[:, pl.ds(pl.multiple_of(i * width, width), width)],
-                lambda i, j=j: ffn.at[j, pl.ds(pl.multiple_of(i * rows, rows), rows), :],
-                sems.at[j, 0],
-                sems.at[j, 1],
-                loc.at[j],
-            )
-        return copies
-
-    def spread_wo():
-        return fan(plane, lambda t: wo, lambda t: wo_z.at[t], sz.at[0], sz.at[1])
-
-    def own_wo():
-        return pltpu.make_async_copy(wo, wo_z.at[plane.t], loc.at[3])
-
-    @pl.when(step == 0)
-    def _():
-        own_wo().start()
-        enter_plane(plane, True)
-        for copy in moves() + spread_wo():
-            copy.start()
-
-    value = x[0].astype(f32)
-    scale = lax.rsqrt(jnp.mean(value * value, axis=1, keepdims=True) + norm_epsilon)
-    low = (value * scale * gain[...]).astype(bf16)
-    norm[...] = low
-    out = jnp.dot(low, w[...], preferred_element_type=f32)
-    angles = column(places[0, 1:2, :].astype(f32)) * inverse[...]
-    cos = jnp.cos(angles)
-    lanes = lax.broadcasted_iota(jnp.int32, angles.shape, 1)
-    sin = jnp.sin(angles)
-    sin = jnp.where(lanes < SLOT, -sin, sin)
-    cosine[...] = cos
-    sine[...] = sin
-    for h in range(heads + 1):
-        part = out[:, h * LANES : (h + 1) * LANES]
-        turned = (part * cos + pltpu.roll(part, SLOT, 1) * sin).astype(bf16)
-        if h < heads:
-            q[h] = turned
-        else:
-            k[...] = turned
-    v[...] = out[:, (heads + 1) * LANES :].astype(bf16)
-
-    @pl.when(step == pl.num_programs(0) - 1)
-    def _():
-        own_wo().wait()
-        for copy in moves() + spread_wo():
-            copy.wait()
-
-
-def project(n, m, heads, x_all, gain, w, places, inverse, wg, wu, wd, wo, ident):
-    tiles, tile, width = x_all.shape
-    length = tiles * tile
-    wide = w.shape[1]
+    for j, weight in enumerate((wg, wu, wd)):
+        moves += exchange(
+            plane,
+            lambda i, weight=weight: weight.at[:, pl.ds(pl.multiple_of(i * width, width), width)],
+            lambda i, j=j: ffn.at[j, pl.ds(pl.multiple_of(i * rows, rows), rows), :],
+            rem.at[3 + j, 0],
+            rem.at[3 + j, 1],
+            loc.at[5 + j],
+        )
+    for copy in few + across[0]:
+        copy.wait()
+    tiles = gains_all[...]
+    for i in range(2):
+        gain_rows[i] = gain_row(tiles, i, strip)
+    gather.own.wait()
+
+    def number(it):
+        return plane.number(it // 2, lax.rem(it, 2))
+
+    def store(it, at):
+        span = pl.ds(pl.multiple_of(number(it) * tokens, tokens), tokens)
+        return pltpu.make_async_copy(turned.at[at], norm_t.at[:, span], sn.at[at])
+
+    def normalize(it, carry):
+        b = number(it)
+        at = lax.rem(it, 2)
+
+        @pl.when(it == 1)
+        def _():
+            gather.swap.wait_recv()
+
+        @pl.when(it == 2)
+        def _():
+            gather.relay_near()
+
+        @pl.when(it == 3)
+        def _():
+            gather.share[1].wait_recv()
+
+        @pl.when(it == 5)
+        def _():
+            gather.share[0].wait_recv()
+
+        @pl.when(it == 6)
+        def _():
+            gather.relay_far()
+            for copy in moves:
+                copy.start()
+
+        @pl.when(it == 7)
+        def _():
+            gather.share[2].wait_recv()
+
+        @pl.when(it >= 2)
+        def _():
+            store(it - 2, at).wait()
+
+        value = blocks[b].astype(f32)
+        scale = lax.rsqrt(jnp.mean(value * value, axis=1, keepdims=True) + norm_epsilon)
+        low = (value * scale * gain_rows[0]).astype(bf16)
+        norms[b] = low
+        turned[at] = low.T
+        store(it, at).start()
+        here = pl.ds(pl.multiple_of(b * tokens, tokens), tokens)
+        docs[:, here] = places_all[b, 0:1, :]
+        angles = column(places_all[b, 1:2, :].astype(f32)) * inverse[...]
+        lanes = lax.broadcasted_iota(jnp.int32, angles.shape, 1)
+        sin = jnp.sin(angles)
+        cosine[here, :] = jnp.cos(angles)
+        sine[here, :] = jnp.where(lanes < SLOT, -sin, sin)
+        return carry
+
+    lax.fori_loop(0, n, normalize, 0)
+    for copy in across[1]:
+        copy.wait()
+
+    def widened(s, carry):
+        for t in range(m):
+            at = pl.ds(pl.multiple_of((s * m + t) * strip, strip), strip)
+            w[at, :] = jnp.dot(
+                w_all[s, t], widen[...], preferred_element_type=f32
+            ).astype(bf16)
+        return carry
+
+    lax.fori_loop(0, n, widened, 0)
+
+    def project(b, carry):
+        here = pl.ds(pl.multiple_of(b * tokens, tokens), tokens)
+        out = jnp.dot(norms[b], w[...], preferred_element_type=f32)
+        cos, sin = cosine[here, :], sine[here, :]
+        for h in range(heads + 1):
+            part = out[:, h * LANES : (h + 1) * LANES]
+            rotated = (part * cos + pltpu.roll(part, SLOT, 1) * sin).astype(bf16)
+            if h < heads:
+                q[h, here, :] = rotated
+            else:
+                k[here, :] = rotated
+        v[here, :] = out[:, (heads + 1) * LANES :].astype(bf16)
+        return carry
+
+    lax.fori_loop(0, n, project, 0)
+    gather.swap.wait_send()
+    gather.ahead.wait_send()
+    gather.back.wait_send()
+    gather.relay.wait_send()
+    for copy in gather.share:
+        copy.wait_send()
+    store(n - 2, 0).wait()
+    store(n - 1, 1).wait()
+    own_wo.wait()
+    for copy in across[2] + moves:
+        copy.wait()
+
+
+def entry(n, m, heads, x, places, wqkv, gains, wg, wu, wd, wo, widen, inverse, ident):
+    tokens, width = x.shape
+    length = n * tokens
+    strip = wqkv.shape[1]
+    wide = widen.shape[1]
     rows, cols = wg.shape
-    table = pl.BlockSpec((tile, LANES), lambda i: (i, 0))
+    vmem = pl.BlockSpec(memory_space=pltpu.VMEM)
+    hbm = pl.BlockSpec(memory_space=ANY)
     return pl.pallas_call(
-        functools.partial(project_body, n, m, heads),
-        grid=(tiles,),
+        functools.partial(entry_body, n, m, heads, strip),
         out_shape=(
-            jax.ShapeDtypeStruct((length, width), bf16),
+            jax.ShapeDtypeStruct((width, length), bf16),
             jax.ShapeDtypeStruct((heads, length, LANES), bf16),
             jax.ShapeDtypeStruct((length, LANES), bf16),
             jax.ShapeDtypeStruct((length, LANES), bf16),
             jax.ShapeDtypeStruct((length, LANES), f32),
             jax.ShapeDtypeStruct((length, LANES), f32),
+            jax.ShapeDtypeStruct((width, wide), bf16),
+            jax.ShapeDtypeStruct((2, 1, width), f32),
+            jax.ShapeDtypeStruct((1, length), jnp.int32),
             jax.ShapeDtypeStruct((3, rows * n, cols // n), wg.dtype),
             jax.ShapeDtypeStruct((m,) + wo.shape, wo.dtype),
         ),
-        in_specs=[
-            pl.BlockSpec((1, tile, width), lambda i: (i, 0, 0)),
-            pl.BlockSpec((1, width), lambda i: (0, 0)),
-            pl.BlockSpec((width, wide), lambda i: (0, 0)),
-            pl.BlockSpec((1,) + places.shape[1:], lambda i: (i, 0, 0)),
-            pl.BlockSpec((1, LANES), lambda i: (0, 0)),
-        ]
-        + [pl.BlockSpec(memory_space=ANY)] * 4,
-        out_specs=[
-            pl.BlockSpec((tile, width), lambda i: (i, 0)),
-            pl.BlockSpec((heads, tile, LANES), lambda i: (0, i, 0)),
-            table,
-            table,
-            table,
-            table,
-            pl.BlockSpec(memory_space=ANY),
-            pl.BlockSpec(memory_space=ANY),
+        in_specs=[hbm] * 8 + [vmem] * 2,
+        out_specs=[hbm] + [vmem] * 8 + [hbm] * 2,
+        scratch_shapes=[
+            pltpu.VMEM((n, tokens, width), bf16),
+            pltpu.VMEM((n, tokens, width), bf16),
+            pltpu.VMEM((2, width, tokens), bf16),
+            pltpu.VMEM((n,) + places.shape, places.dtype),
+            pltpu.VMEM((n, m) + wqkv.shape[1:], wqkv.dtype),
+            pltpu.VMEM((n, m) + gains.shape, gains.dtype),
+            pltpu.SemaphoreType.DMA((2, Gather.COPIES)),
+            pltpu.SemaphoreType.DMA((6, 2, n - 1)),
+            pltpu.SemaphoreType.DMA((3, 2, m - 1)),
+            pltpu.SemaphoreType.DMA((2,)),
+            pltpu.SemaphoreType.DMA((8,)),
         ],
-        scratch_shapes=[
-            pltpu.SemaphoreType.DMA((3, 2, n - 1)),
-            pltpu.SemaphoreType.DMA((4,)),
-            pltpu.SemaphoreType.DMA((2, m - 1)),
-        ],
-        compiler_params=pltpu.CompilerParams(collective_id=ident, has_side_effects=True),
-        cost_estimate=pl.CostEstimate(
-            flops=2 * length * width * wide * 3, transcendentals=0, bytes_accessed=30_000_000
+        compiler_params=pltpu.CompilerParams(
+            collective_id=ident, has_side_effects=True, vmem_limit_bytes=50 << 20
         ),
-        name="project",
-    )(x_all, gain, w, places, inverse, wg, wu, wd, wo)
+        cost_estimate=COST,
+        name="entry",
+    )(x, places, wqkv, gains, wg, wu, wd, wo, widen, inverse)
 
 
 BLOCK = 512
@@ -1057,9 +1157,7 @@
             pltpu.SemaphoreType.DMA((2,)),
         ],
         compiler_params=pltpu.CompilerParams(collective_id=ident, has_side_effects=True),
-        cost_estimate=pl.CostEstimate(
-            flops=pairs * 4 * LANES * 3, transcendentals=pairs, bytes_accessed=120_000_000
-        ),
+        cost_estimate=COST,
         name="attend",
     )(q, k, v, docs, wo, go)
 
@@ -1067,7 +1165,7 @@
 def attend_back_body(
     n, m, factor, scale, heads, q, k, v, go, o, lse, begin, cosine, sine, mixed, terms,
     out, mixed_sum, term_sum, kt, dqt, dk, dv, delta,
-    pair, near, far, sr, lr, pair2, near2, far2, sr2, lr2,
+    pair, near, far, sr, lr, pair2, near2, far2, sr2, lr2, held,
 ):
     h = pl.program_id(0)
     j = pl.program_id(1)
@@ -1100,7 +1198,7 @@
     @pl.when(at_step == 5)
     def _():
         two.ready()
-        two.first(term_sum)
+        two.first(held)
 
     @pl.when((h == 0) & (j == 0))
     def _():
@@ -1176,7 +1274,7 @@
         lax.fori_loop(0, blocks, write, 0)
         one.finish(mixed_sum)
         two.send_fro()
-        two.finish(term_sum)
+        two.finish(held, term_sum)
 
 
 def attend_back(n, m, factor, scale, q, k, v, go, o, lse, begin, cosine, sine, mixed, terms, ident):
@@ -1191,7 +1289,7 @@
         out_shape=(
             jax.ShapeDtypeStruct((length, (heads + 2) * LANES), bf16),
             jax.ShapeDtypeStruct(mixed.shape[1:], f32),
-            jax.ShapeDtypeStruct(terms.shape[1:], f32),
+            jax.ShapeDtypeStruct(terms.shape[1:], bf16),
         ),
         in_specs=[
             one,
@@ -1219,13 +1317,12 @@
             pltpu.VMEM((1, length), f32),
         ]
         + Reduce.scratch(*mixed.shape[1:])
-        + Reduce.scratch(*terms.shape[1:]),
+        + Reduce.scratch(*terms.shape[1:])
+        + [pltpu.VMEM(terms.shape[1:], f32)],
         compiler_params=pltpu.CompilerParams(
             collective_id=ident, has_side_effects=True, vmem_limit_bytes=56 << 20
         ),
-        cost_estimate=pl.CostEstimate(
-            flops=pairs * 10 * LANES * 2, transcendentals=pairs, bytes_accessed=150_000_000
-        ),
+        cost_estimate=COST,
         name="attend_back",
     )(q, k, v, go, o, lse, begin, cosine, sine, mixed, terms)
 
@@ -1236,7 +1333,6 @@
     sg, sr, loc, sw, so, sm, sd,
 ):
     plane = Plane(n, m)
-    c, q = plane.c, plane.q
     tokens = rows.shape[1]
     hid = w_in.shape[3]
     enter_plane(plane, False)
@@ -1254,13 +1350,7 @@
         copy.start()
 
     def number(it):
-        k, other = it // 2, lax.rem(it, 2)
-        low, high = lax.rem(k, 2), k // 2
-        dx = low * (1 - c) + high * c
-        dy = high * (1 - c) + low * c
-        x, y = lax.rem(q, 2), q // 2
-        chip = 2 * (y + dy - 2 * y * dy) + x + dx - 2 * x * dx
-        return 2 * chip + c + other * (1 - 2 * c)
+        return plane.number(it // 2, lax.rem(it, 2))
 
     def load_go(it, slot):
         return pltpu.make_async_copy(go.at[number(it)], go_two.at[slot], so.at[slot])
@@ -1435,11 +1525,7 @@
         compiler_params=pltpu.CompilerParams(
             collective_id=ident, has_side_effects=True, vmem_limit_bytes=60 << 20
         ),
-        cost_estimate=pl.CostEstimate(
-            flops=18 * length * width * m * hid,
-            transcendentals=length * m * hid,
-            bytes_accessed=60_000_000,
-        ),
+        cost_estimate=COST,
         name="feed",
     )(norm, go, w_in)
 
@@ -1488,31 +1574,27 @@
         strip = query_weight.shape[0]
         hid = gate_weight.shape[1] // n
 
-        packed = spread(
-            jnp.concatenate(
-                [split_heads(w, n) for w in (query_weight, key_weight, value_weight)], axis=2
-            )
-        )
-        wide = packed.shape[2]
+        packed = jnp.concatenate(
+            [split_heads(w, n) for w in (query_weight, key_weight, value_weight)], axis=2
+        )
+        cols = packed.shape[2]
         gains = jnp.pad(
-            jnp.stack([first_gain, second_gain]), ((0, 6), (0, LANES - strip))
+            jnp.stack([first_gain, second_gain]).astype(f32), ((0, 6), (0, LANES - strip))
         )
         places = jnp.concatenate([doc_ids, positions], axis=0)
-        x_all, places_all, w_all, gains_all = entry(n, m, x, places, packed, gains)
-        docs = places_all[:, 0].reshape(1, length)
-        wqkv = w_all.reshape(width, wide)
-        gain_one, gain_two = [
-            gains_all[:, :, i, :strip].reshape(1, width).astype(f32) for i in range(2)
-        ]
         lane = jnp.arange(LANES) % SLOT
         inverse = jnp.where(
             lane < HALF, rope_base ** (-(lane.astype(f32) * 2.0 / HEAD_SIZE)), 0.0
         )[None]
-
-        norm_one, q, k, v, cosine, sine, ffn_mine, output_rows = project(
-            n, m, heads, x_all, gain_one, wqkv, places_all, inverse,
-            gate_weight, up_weight, down_weight, output_weight, 8,
-        )
+        from_col = jnp.arange(cols)
+        to_lane = from_col // HALF * SLOT + from_col % HALF
+        widen = (to_lane[:, None] == jnp.arange(cols // HALF * SLOT)[None, :]).astype(bf16)
+
+        norm_t, q, k, v, cosine, sine, wqkv, gain_rows, docs, ffn_mine, output_rows = entry(
+            n, m, heads, x, places, packed, gains,
+            gate_weight, up_weight, down_weight, output_weight, widen, inverse, 0,
+        )
+        gain_one, gain_two = gain_rows[0], gain_rows[1]
         ffn_all = lax.all_gather(ffn_mine, "tp", axis=0, tiled=False)
         o, low, lse, begin, output_full, grad_all = attend(
             n, m, factor, q, k, v, docs, output_rows.reshape(m * strip, width), out_grad[0], 9
@@ -1549,16 +1631,11 @@
             n, m, factor, scale, q, k, v, go, o, lse, begin, cosine, sine, mixed, output_term, 3
         )
         layer_output = (resid + mixed_sum).astype(bf16)[None]
-        output_grad = lax.psum_scatter(
-            output_sum.astype(bf16), "tp", scatter_dimension=0, tiled=True
-        ).astype(f32)
-        dnorm_one_part = times_transpose(dqkv, wqkv).astype(bf16)
-        qkv_term = gathered(outer_product(norm_one, dqkv).astype(bf16))
-        cols = qkv_term.shape[1]
-        qkv_term = qkv_term.reshape(n, m, strip, cols).transpose(1, 0, 2, 3)
-        dnorm_one, ffn_out, qkv_out, gain_sums = last(
-            n, m, dnorm_one_part.reshape(n, rows, width), ffn_sum, qkv_term, gain_part, 6
-        )
+        dnorm_one, ffn_out, qkv_out, output_parts, gain_sums = last(
+            n, m, dqkv, wqkv, widen.T, norm_t, ffn_sum,
+            output_sum.reshape(m, strip, width), gain_part, 6,
+        )
+        output_grad = jnp.sum(output_parts.astype(f32), axis=0)
 
         scale_one = lax.rsqrt(jnp.mean(x_f * x_f, axis=1, keepdims=True) + norm_epsilon)
         inner = gain_one * dnorm_one

time: 522 us -> 393 us (0.75)
  waiting for transfers between devices: 85.3 us -> 11.7 us
  local copies, waits for them, and re-layouts: 40.3 us -> 17.2 us
  matrix products: 24.9 us -> 11.1 us
  Pallas kernels: 335 us -> 322 us
  other arithmetic: 21.4 us -> 14.9 us
    reduce_scatter x1, waiting for transfers between devices: 77.6 us -> 0.01 us  [on_plane(): lax.psum_scatter(ffn_terms, 'tp', scatter_dimension=0, tiled=False)]
    pallas_call x2 -> x1, Pallas kernels: 70.3 us -> 54.7 us  [entry(): pl.pallas_call(functools.partial(entry_body, n, m, heads, strip), out_sha...]
    convert_element_type x6, local copies, waits for them, and re-layouts: 10.7 us -> 0.72 us  [columns(): return qkv_out[:, :, a:b].transpose(1, 0, 2).reshape(strip, -1).astype(f32)]
    another operation x2 -> x0, local copies, waits for them, and re-layouts: 9.4 us -> none  [on_plane(): qkv_term = qkv_term.reshape(n, m, strip, cols).transpose(1, 0, 2, 3)]
    dot_general x2 -> x1, matrix products: 10.5 us -> 3.49 us  [outer_product(): lax.dot_general(left, right, (((0,), (0,)), ((), ())), preferred_element_...]
    dot_general x2 -> x1, matrix products: 10.7 us -> 3.77 us  [times_transpose(): lax.dot_general(left, right, (((1,), (1,)), ((), ())), preferred_element_...]
    convert_element_type x4 -> x2, other arithmetic: 5.73 us -> 0.23 us  [on_plane(): (to_lane[:, None] == jnp.arange(cols // HALF * SLOT)[None, :]).astype(bf16)]
  transfers between devices with their start and end apart: 3 -> 2, of which waited for: 2 -> 1; matrix products, arithmetic and copies ran while one was open for 7% -> 6% of each run, Pallas kernels for 14% -> 38%
where the time goes in v3:
time: 393 us; the launch traced here: 392 us
  Pallas kernels  322 us (82%)
  local copies, waits for them, and re-layouts  17.2 us (4%)
  other arithmetic  14.9 us (4%)
  between operations  14.6 us (4%)
  waiting for transfers between devices  11.7 us (3%)
  matrix products  11.1 us (3%)
    pallas_call x1, Pallas kernels, feed(): pl.pallas_call(functools.partial(feed_body, n, m), out_shape=(jax.ShapeDt...  68.3 us
    pallas_call x1, Pallas kernels, attend(): pl.pallas_call(functools.partial(attend_body, n, m, factor), grid=(heads,...  61.5 us
    pallas_call x1, Pallas kernels, attend_back(): pl.pallas_call(functools.partial(attend_back_body, n, m, factor, scale, h...  58.3 us
    pallas_call x1, Pallas kernels, entry(): pl.pallas_call(functools.partial(entry_body, n, m, heads, strip), out_sha...  54.7 us
    pallas_call x1, Pallas kernels, last(): pl.pallas_call(functools.partial(last_body, n, m), out_shape=(jax.ShapeDt...  50.5 us
    pallas_call x2, Pallas kernels, plane_swap(): pl.pallas_call(functools.partial(swap_body, n, m, count), out_shape=tuple...  29 us
    all_gather x1, waiting for transfers between devices, on_plane(): ffn_all = lax.all_gather(ffn_mine, 'tp', axis=0, tiled=False)  11.7 us
  transfers between devices with their start and end apart: 2, of which 1 were waited for; matrix products, arithmetic and copies ran while one was open for 6% of the time, Pallas kernels for 38%

profile of v3, /device:TPU:0, one launch (start us, length us, event | category | flops | bytes accessed | tf_op | source)
XLA Modules:
  0.0 392.0 jit_solution(15372193122754178063)
XLA Ops:
  7.4 1.1 reshape.162
  8.5 1.0 reshape.163
  9.5 1.1 reshape.161
  11.1 54.7 %entry.1 = (bf16[1536,2048]{1,0:T(8,128)(2,1)}, bf16[2,2048,128]{2,1,0:T(8,128)(2,1)}, bf16[2048,128]{1,0:T(8,128)(2,1)S(1)}, bf16[2048,128]{1,0:T(8,128)(2,1)S(...) custom-call(bf16[256,1536]{1,0:T(8,128)(2,1)} %bitcast.60, ...), custom_call_target="tpu_custom_call" | custom-call | flops 1000000 | bytes 100000 | tf_op jit(solution)/shard_map/entry/pallas_call | solution.py:993
  69.1 61.5 %attend.1 = (f32[2,2048,128]{2,1,0:T(8,128)}, bf16[2048,256]{1,0:T(8,128)(2,1)}, f32[2,1,2048]{2,1,0:T(1,128)}, s32[1,2048]{1,0:T(1,128)}, bf16[8,192,1536]{2,1,0:T(8,128)(2,1)}, /*index=5*/bf16[8,256,1536]{2,1,0:T(8,128)(2,1)}) custom-call(bf16[2,2048,128]{2,1,0:T(8,128)(2,1)} %get-tuple-element.41.q, bf16[2048,128]{1,0:T(8,128)(2,1)} %copy-done, ...), custom_call_target="tpu_custom_call" | custom-call | flops 1000000 | bytes 100000 | tf_op jit(solution)/shard_map/attend/pallas_call | solution.py:1123
  130.6 13.1 %plane_swap.2 = bf16[8,256,256]{2,1,0:T(8,128)(2,1)} custom-call(bf16[8,256,256]{2,1,0:T(8,128)(2,1)} %bitcast.70), custom_call_target="tpu_custom_call" | custom-call | flops 1000000 | bytes 100000 | tf_op jit(solution)/shard_map/plane_swap/pallas_call | solution.py:534
  143.7 1.6 copy.36
  145.4 3.8 multiply_reduce_fusion.2
  149.2 1.3 multiply_convert_fusion.mine
  150.5 11.7 %all-gather.3.cloned.1.call-done = bf16[12,1536,128]{2,1,0:T(8,128)(2,1)} async-done(((bf16[3,1536,128]{2,1,0:T(8,128)(2,1)}), bf16[12,1536,128]{2,1,0:T(8,128)(2,1)}) %all-gather.3.cloned.1.call-update) | async-done | bytes 4718608 | tf_op jit(solution)/shard_map/all_gather | solution.py:1598
  162.1 68.3 %feed.1 = (f32[256,1536]{1,0:T(8,128)}, bf16[4,3,1536,128]{3,2,1,0:T(8,128)(2,1)}, bf16[8,256,1536]{2,1,0:T(8,128)(2,1)}) custom-call(bf16[256,1536]{1,0:T(8,128)(2,1)} %multiply_convert_fusion.mine, bf16[8,256,1536]{2,1,0:T(8,128)(2,1)} %get-tuple-element.49.go, bf16[4,3,1536,128]{3,2,1,0:T(8,128)(2,1)} %bitcast.61), custom_call_target="tpu_custom_call" | custom-call | flops 1000000 | bytes 100000 | tf_op jit(solution)/shard_map/feed/pallas_call | solution.py:1492
  231.3 2.0 multiply_reduce_fusion
  233.9 1.2 copy-done.11
  235.1 3.8 convolution_convert_fusion.1
  239.1 1.2 pad.12
  240.3 2.4 copy.38
  243.4 15.9 %plane_swap.3 = (bf16[8,256,256]{2,1,0:T(8,128)(2,1)}, f32[8,1,192]{2,1,0:T(1,128)}) custom-call(bf16[8,256,256]{2,1,0:T(8,128)(2,1)} %bitcast.62, f32[8,1,192]{2,1,0:T(1,128)} %reshape.169.refs_1_), custom_call_target="tpu_custom_call" | custom-call | flops 1000000 | bytes 100000 | tf_op jit(solution)/shard_map/plane_swap/pallas_call | solution.py:534
  260.2 3.5 convolution_convert_fusion
  263.6 58.3 %attend_back.1 = (bf16[2048,512]{1,0:T(8,128)(2,1)}, f32[256,1536]{1,0:T(8,128)}, bf16[192,1536]{1,0:T(8,128)(2,1)}) custom-call(bf16[2,2048,128]{2,1,0:T(8,128)(2,1)} %get-tuple-element.41.q, bf16[2048,128]{1,0:T(8,128)(2,1)} %copy-done, bf16[2048,128]{1,0:T(8,128)(2,1)} %copy-done.1, bf16[2048,256]{1,0:T(8,128)(2,1)} %bitcast.69, ...), custom_call_target="tpu_custom_call" | custom-call | flops 1000000 | bytes 100000 | tf_op jit(solution)/shard_map/attend_back/pallas_call | solution.py:1286
  322.0 2.5 fusion.7
  324.5 50.5 %last.1 = (f32[256,1536]{1,0:T(8,128)}, bf16[3,192,1024]{2,1,0:T(8,128)(2,1)S(1)}, bf16[8,48,384]{2,1,0:T(8,128)(2,1)S(1)}, bf16[4,48,1536]{2,1,0:T(8,128)(2,1)S(1)}, f32[4,1,48]{2,1,0:T(1,128)S(1)}) custom-call(bf16[2048,512]{1,0:T(8,128)(2,1)} %get-tuple-element.60.dqkv, bf16[1536,512]{1,0:T(8,128)(2,1)} %get-tuple-element.61.w, ...), custom_call_target="tpu_custom_call" | custom-call | flops 1000000 | bytes 100000 | tf_op jit(solution)/shard_map/last/pallas_call | solution.py:776
  377.2 1.5 bitcast_convert_fusion
  378.7 1.0 copy-done.16
  381.5 3.1 fusion.5
  (102 shorter events, 11.5 us)
Async XLA Ops:
  7.2 3.7 copy-start.27
  7.2 3.7 copy-start.31
  7.2 3.7 copy-start.30
  7.2 3.7 copy-start.29
  7.2 3.9 copy-start.7
  7.2 3.9 copy-start.4
  7.2 3.9 copy-start.5
  7.3 3.9 copy-start.6
  7.3 154.9 %all-gather.3.cloned.1.call-start = ((), (), s32[]{:S(2)}) async-start(), calls=%async_computation.2 | async-start | bytes 5898240 | tf_op jit(solution)/shard_map/all_gather | solution.py:1598
  7.3 3.5 copy-start.25
  68.9 255.7 %reduce-scatter.2.cloned.1.call-start = ((), (), s32[]{:S(2)}) async-start(), calls=%async_computation.1 | async-start | bytes 5898240 | tf_op jit(solution)/shard_map/reduce_scatter | solution.py:1612
  143.7 1.7 copy-start.14
  149.2 84.0 %copy-start.9 = (f32[256,1536]{1,0:T(8,128)}, f32[256,1536]{1,0:T(8,128)S(1)}, u32[]{:S(2)}) copy-start(f32[256,1536]{1,0:T(8,128)S(1)} %get-tuple-element.83) | copy-start | bytes 4718596
  231.3 2.0 copy-start.17
  231.3 2.1 copy-start.18
  240.3 19.8 %copy-start.12 = (f32[256,1536]{1,0:T(8,128)S(1)}, f32[256,1536]{1,0:T(8,128)}, u32[]{:S(2)}) copy-start(f32[256,1536]{1,0:T(8,128)} %copy-done.11) | copy-start | bytes 4718596
  263.6 58.3 %copy-start.10 = (f32[256,1536]{1,0:T(8,128)S(1)}, f32[256,1536]{1,0:T(8,128)}, u32[]{:S(2)}) copy-start(f32[256,1536]{1,0:T(8,128)} %copy-done.9) | copy-start | bytes 4718596
  322.0 2.5 copy-start.2
  375.9 2.8 copy-start.19
  377.1 1.6 copy-start.21
  377.2 1.5 copy-start.15
  377.2 2.5 copy-start.16
  379.7 1.8 copy-start.13
  381.5 3.1 copy-start.28
  (10 other events, 8.8 us)
Sparse Core Ops, SparseCore 0:
  69.0 93.1 all-gather.2
  230.6 82.7 reduce-scatter.1

commit v4 on v3

--- a/solution.py
+++ b/solution.py
@@ -347,6 +347,7 @@
 SLOT = LANES // 2
 f32 = jnp.float32
 bf16 = jnp.bfloat16
+VMEM_LIMIT = 62 << 20
 COST = pl.CostEstimate(flops=1_000_000, transcendentals=0, bytes_accessed=100_000)
 
 
@@ -430,13 +431,13 @@
 class Gather:
     COPIES = 7
 
-    def __init__(self, plane, src, dst, send, recv, local):
+    def __init__(self, plane, src, dst_of, send, recv, local):
         to, fro, far, c = plane.to, plane.fro, plane.far, plane.c
-        here = dst.at[plane.s]
+        here = dst_of(plane.s)
         self.own = pltpu.make_async_copy(src, here, local)
 
         def block(chip):
-            return dst.at[2 * chip + c]
+            return dst_of(2 * chip + c)
 
         def copy(i, a, b, device):
             return remote(a, b, send.at[i], recv.at[i], device)
@@ -455,6 +456,8 @@
     def start(self):
         self.back.start()
         self.ahead.start()
+
+    def start_here(self):
         self.swap.start()
         self.own.start()
 
@@ -469,20 +472,133 @@
         self.relay.wait_recv()
         self.share[2].start()
 
+    def wait_sends(self):
+        for copy in [self.swap, self.ahead, self.back, self.relay] + self.share:
+            copy.wait_send()
+
+
+class Gathers:
+    def __init__(self, plane, src, dst_of, sems, local, pieces):
+        rows = src.shape[0] // pieces
+        self.parts = []
+        for i in range(pieces):
+            at = pl.ds(i * rows, rows)
+            self.parts.append(
+                Gather(
+                    plane,
+                    src.at[at],
+                    lambda d, at=at: dst_of(d).at[at],
+                    sems.at[i, 0],
+                    sems.at[i, 1],
+                    local.at[i],
+                )
+            )
+
+    def start(self):
+        for part in self.parts:
+            part.start()
+        for part in self.parts:
+            part.start_here()
+
+    def relay_near(self):
+        for part in self.parts:
+            part.relay_near()
+
+    def relay_far(self):
+        for part in self.parts:
+            part.relay_far()
+
+    def wait_own(self):
+        for part in self.parts:
+            part.own.wait()
+
+    def wait_swap(self):
+        for part in self.parts:
+            part.swap.wait_recv()
+
+    def wait_share(self, i):
+        for part in self.parts:
+            part.share[i].wait_recv()
+
+    def wait_sends(self):
+        for part in self.parts:
+            part.wait_sends()
+
     def finish(self):
-        self.own.wait()
-        self.swap.wait()
-        self.ahead.wait_send()
-        self.back.wait_send()
-        self.relay.wait_send()
-        for copy in self.share:
-            copy.wait()
-
-    def run(self):
-        self.start()
-        self.relay_near()
-        self.relay_far()
-        self.finish()
+        self.wait_own()
+        self.wait_swap()
+        for i in range(3):
+            self.wait_share(i)
+        self.wait_sends()
+
+    @staticmethod
+    def scratch(pieces):
+        return [
+            pltpu.SemaphoreType.DMA((pieces, 2, Gather.COPIES)),
+            pltpu.SemaphoreType.DMA((pieces,)),
+        ]
+
+
+class Chain:
+    def __init__(self, plane, mine, slot_of, sems):
+        self.plane, self.mine, self.slot_of, self.sems = plane, mine, slot_of, sems
+
+    def copy(self, way, hop, to):
+        plane, row = self.plane, 0 if way > 0 else 2
+        slot = self.slot_of(plane.t - way * hop)
+        return remote(
+            self.mine if hop == 0 else slot,
+            slot,
+            self.sems.at[row, hop],
+            self.sems.at[row + 1, hop],
+            (plane.s, to),
+        )
+
+    def inside(self, way, hop):
+        t, m = self.plane.t, self.plane.m
+        holds = t >= hop if way > 0 else t < m - hop
+        passes = t < m - 1 if way > 0 else t > 0
+        return holds, passes
+
+    def start(self):
+        self.pass_on(0)
+
+    def pass_on(self, hop):
+        for way in (1, -1):
+            holds, passes = self.inside(way, hop)
+
+            @pl.when(holds & passes)
+            def _(way=way):
+                self.copy(way, hop, self.plane.t + way).start()
+
+    def step(self, hop):
+        plane = self.plane
+        for way in (1, -1):
+            holds, _ = self.inside(way, hop)
+
+            @pl.when(holds)
+            def _(way=way):
+                row = 0 if way > 0 else 2
+                slot = self.slot_of(plane.t - way * hop)
+                remote(
+                    slot,
+                    slot,
+                    self.sems.at[row, hop - 1],
+                    self.sems.at[row + 1, hop - 1],
+                    (plane.s, plane.t - way),
+                ).wait_recv()
+
+        if hop < plane.m - 1:
+            self.pass_on(hop)
+
+    def wait_sends(self):
+        for hop in range(self.plane.m - 1):
+            for way in (1, -1):
+                holds, passes = self.inside(way, hop)
+
+                @pl.when(holds & passes)
+                def _(way=way, hop=hop):
+                    self.copy(way, hop, self.plane.t + way).wait_send()
 
 
 def fan(plane, src_of, dst_of, send, recv):
@@ -506,44 +622,6 @@
             )
         )
     return [own] + copies
-
-
-def swap_body(n, m, count, *refs):
-    plane = Plane(n, m)
-    enter_plane(plane, False)
-    sems, loc = refs[2 * count :]
-    copies = []
-    for i in range(count):
-        src, dst = refs[i], refs[count + i]
-        copies += exchange(
-            plane,
-            lambda k, src=src: src.at[k],
-            lambda k, dst=dst: dst.at[k],
-            sems.at[i, 0],
-            sems.at[i, 1],
-            loc.at[i],
-        )
-    for copy in copies:
-        copy.start()
-    for copy in copies:
-        copy.wait()
-
-
-def plane_swap(n, m, ident, *arrays):
-    count = len(arrays)
-    return pl.pallas_call(
-        functools.partial(swap_body, n, m, count),
-        out_shape=tuple(jax.ShapeDtypeStruct(a.shape, a.dtype) for a in arrays),
-        in_specs=[pl.BlockSpec(memory_space=ANY)] * count,
-        out_specs=[pl.BlockSpec(memory_space=ANY)] * count,
-        scratch_shapes=[
-            pltpu.SemaphoreType.DMA((count, 2, n - 1)),
-            pltpu.SemaphoreType.DMA((count,)),
-        ],
-        compiler_params=pltpu.CompilerParams(collective_id=ident, has_side_effects=True),
-        cost_estimate=COST,
-        name="plane_swap",
-    )(*arrays)
 
 
 TILE = 16
@@ -586,8 +664,8 @@
 
         self.out = [out(0, 3, plane.to), out(1, 1, plane.to), out(2, 2, plane.fro)]
 
-    def start(self):
-        for k in (3, 1, 2, 0):
+    def start(self, *which):
+        for k in which:
             self.swaps[k].start()
             self.loads[k].start()
 
@@ -626,12 +704,13 @@
         in_tiles(self.rows, add)
         self.out[2].start()
 
-    def first(self, total):
+    def first(self, total, more=None):
         pair, near = self.pair, self.near
         self.landed(0)
 
         def add(at):
-            total[at, :] = pair[0, at, :].astype(f32) + near[0, at, :].astype(f32)
+            value = pair[0, at, :].astype(f32) + near[0, at, :].astype(f32)
+            total[at, :] = value if more is None else value + more[at, :]
 
         in_tiles(self.rows, add)
 
@@ -648,14 +727,6 @@
 
         in_tiles(self.rows, add)
 
-    def run(self, total):
-        self.start()
-        self.send_to()
-        self.ready()
-        self.first(total)
-        self.send_fro()
-        self.finish(total)
-
     @staticmethod
     def scratch(rows, width):
         return [pltpu.VMEM((slots, rows, width), bf16) for slots in Reduce.SLOTS] + [
@@ -665,12 +736,20 @@
 
 
 def last_body(
-    n, m, dqkv, w, narrow, norm_t, ffn, wo, vec, total, ffn_out, qkv_out, wo_out, vec_out,
-    pair, near, far, sr, lr, stage, norms, mine, got, summed, sems, st, loc,
+    n, m, dqkv_in, w_in, narrow, x_in, dresid_in, gain, norm_t, ffn, wo, vec,
+    input_grad, ffn_out, qkv_out, wo_out, vec_out,
+    dqkv, w, x, dresid, pair, near, far, sr, lr, total, stage, norms, mine, got, summed, sems, st, loc,
 ):
     plane = Plane(n, m)
+    loads = [
+        pltpu.make_async_copy(a, b, loc.at[5 + i])
+        for i, (a, b) in enumerate(
+            ((dqkv_in, dqkv), (w_in, w), (x_in, x), (dresid_in, dresid))
+        )
+    ]
     load = pltpu.make_async_copy(norm_t, norms, loc.at[0])
-    load.start()
+    for copy in loads + [load]:
+        copy.start()
     enter_plane(plane, True)
     rows, width = ffn_out.shape[1], ffn.shape[2]
     across = fan(plane, lambda t: wo.at[t], lambda t: wo_out.at[t], st.at[1, 0], st.at[1, 1])
@@ -691,6 +770,8 @@
     )
     reduce = Reduce(plane, None, pair, near, far, sr, lr, stage)
     tokens = pair.shape[1]
+    for copy in loads[:2]:
+        copy.wait()
 
     def blocks(it, carry):
         k = 3 - it // 2
@@ -761,12 +842,25 @@
     )
     for copy in b:
         copy.start()
+    for copy in loads[2:]:
+        copy.wait()
     reduce.finish(total)
+
+    def into_input(at):
+        value = x[at, :].astype(f32)
+        scale = lax.rsqrt(jnp.mean(value * value, axis=1, keepdims=True) + norm_epsilon)
+        inner = gain[...] * total[at, :]
+        moment = jnp.mean(value * inner, axis=1, keepdims=True)
+        input_grad[at, :] = (
+            dresid[at, :] + scale * inner - value * scale * (scale * scale * moment)
+        )
+
+    in_tiles(tokens, into_input)
     for copy in a + b + across:
         copy.wait()
 
 
-def last(n, m, dqkv, w, narrow, norm_t, ffn, wo, vec, ident):
+def last(n, m, dqkv, w, narrow, x, dresid, gain, norm_t, ffn, wo, vec, ident):
     width, length = norm_t.shape
     tokens = length // n
     cols = narrow.shape[1]
@@ -782,10 +876,17 @@
             jax.ShapeDtypeStruct(wo.shape, wo.dtype),
             jax.ShapeDtypeStruct(vec.shape, vec.dtype),
         ),
-        in_specs=[vmem] * 3 + [hbm] * 4,
+        in_specs=[hbm, hbm, vmem, hbm, hbm, vmem] + [hbm] * 4,
         out_specs=[vmem] + [hbm] * 4,
-        scratch_shapes=Reduce.scratch(tokens, width)
+        scratch_shapes=[
+            pltpu.VMEM(dqkv.shape, bf16),
+            pltpu.VMEM(w.shape, bf16),
+            pltpu.VMEM(x.shape, bf16),
+            pltpu.VMEM(dresid.shape, f32),
+        ]
+        + Reduce.scratch(tokens, width)
         + [
+            pltpu.VMEM((tokens, width), f32),
             pltpu.VMEM((4, tokens, width), bf16),
             pltpu.VMEM((width, length), bf16),
             pltpu.VMEM((n, m, strip, cols), bf16),
@@ -793,14 +894,14 @@
             pltpu.VMEM((n, strip, cols), bf16),
             pltpu.SemaphoreType.DMA((2, 2, n - 1)),
             pltpu.SemaphoreType.DMA((3, 2, m - 1)),
-            pltpu.SemaphoreType.DMA((5,)),
+            pltpu.SemaphoreType.DMA((9,)),
         ],
         compiler_params=pltpu.CompilerParams(
-            collective_id=ident, has_side_effects=True, vmem_limit_bytes=50 << 20
+            collective_id=ident, has_side_effects=True, vmem_limit_bytes=VMEM_LIMIT
         ),
         cost_estimate=COST,
         name="last",
-    )(dqkv, w, narrow, norm_t, ffn, wo, vec)
+    )(dqkv, w, narrow, x, dresid, gain, norm_t, ffn, wo, vec)
 
 
 def column(row):
@@ -828,14 +929,14 @@
 
 def entry_body(
     n, m, heads, strip, x, places, wqkv, gains, wg, wu, wd, wo, widen, inverse,
-    norm_t, q, k, v, cosine, sine, w, gain_rows, docs, ffn, wo_z,
-    blocks, norms, turned, places_all, w_all, gains_all,
-    sx, rem, sz, sn, loc,
+    norm_t, q, k, v, cosine, sine, w, gain_rows, docs, ffn, down, wo_z,
+    blocks, norms, turned, places_all, w_all, gains_all, q_here, k_here, v_here, cos_here, sin_here,
+    sx, lx, rem, sz, sn, loc,
 ):
     plane = Plane(n, m)
     enter_plane(plane, True)
     tokens = x.shape[0]
-    gather = Gather(plane, x, blocks, sx.at[0], sx.at[1], loc.at[0])
+    gather = Gathers(plane, x, lambda i: blocks.at[i], sx, lx, 2)
     first = []
     for i, (src, dst) in enumerate(((gains, gains_all), (wqkv, w_all))):
         first += exchange(
@@ -864,7 +965,7 @@
     own_wo.start()
     for copy in first:
         copy.wait()
-    for copy in across[0] + across[1] + across[2]:
+    for copy in across[0] + across[1]:
         copy.start()
     moves = []
     width, rows = wg.shape[1] // n, wg.shape[0]
@@ -872,7 +973,9 @@
         moves += exchange(
             plane,
             lambda i, weight=weight: weight.at[:, pl.ds(pl.multiple_of(i * width, width), width)],
-            lambda i, j=j: ffn.at[j, pl.ds(pl.multiple_of(i * rows, rows), rows), :],
+            lambda i, dst=ffn.at[j] if j < 2 else down: dst.at[
+                pl.ds(pl.multiple_of(i * rows, rows), rows), :
+            ],
             rem.at[3 + j, 0],
             rem.at[3 + j, 1],
             loc.at[5 + j],
@@ -882,7 +985,7 @@
     tiles = gains_all[...]
     for i in range(2):
         gain_rows[i] = gain_row(tiles, i, strip)
-    gather.own.wait()
+    gather.wait_own()
 
     def number(it):
         return plane.number(it // 2, lax.rem(it, 2))
@@ -897,7 +1000,7 @@
 
         @pl.when(it == 1)
         def _():
-            gather.swap.wait_recv()
+            gather.wait_swap()
 
         @pl.when(it == 2)
         def _():
@@ -905,21 +1008,21 @@
 
         @pl.when(it == 3)
         def _():
-            gather.share[1].wait_recv()
+            gather.wait_share(1)
 
         @pl.when(it == 5)
         def _():
-            gather.share[0].wait_recv()
+            gather.wait_share(0)
 
         @pl.when(it == 6)
         def _():
             gather.relay_far()
-            for copy in moves:
+            for copy in moves + across[2]:
                 copy.start()
 
         @pl.when(it == 7)
         def _():
-            gather.share[2].wait_recv()
+            gather.wait_share(2)
 
         @pl.when(it >= 2)
         def _():
@@ -936,20 +1039,27 @@
         angles = column(places_all[b, 1:2, :].astype(f32)) * inverse[...]
         lanes = lax.broadcasted_iota(jnp.int32, angles.shape, 1)
         sin = jnp.sin(angles)
-        cosine[here, :] = jnp.cos(angles)
-        sine[here, :] = jnp.where(lanes < SLOT, -sin, sin)
+        cos_here[here, :] = jnp.cos(angles)
+        sin_here[here, :] = jnp.where(lanes < SLOT, -sin, sin)
         return carry
 
     lax.fori_loop(0, n, normalize, 0)
+    outs = [
+        pltpu.make_async_copy(cos_here, cosine, loc.at[8]),
+        pltpu.make_async_copy(sin_here, sine, loc.at[9]),
+        pltpu.make_async_copy(q_here, q, loc.at[10]),
+        pltpu.make_async_copy(k_here, k, loc.at[11]),
+        pltpu.make_async_copy(v_here, v, loc.at[12]),
+    ]
+    for copy in outs[:2]:
+        copy.start()
     for copy in across[1]:
         copy.wait()
 
     def widened(s, carry):
-        for t in range(m):
-            at = pl.ds(pl.multiple_of((s * m + t) * strip, strip), strip)
-            w[at, :] = jnp.dot(
-                w_all[s, t], widen[...], preferred_element_type=f32
-            ).astype(bf16)
+        at = pl.ds(pl.multiple_of(s * m * strip, m * strip), m * strip)
+        narrow = w_all[s].reshape(m * strip, w_all.shape[3])
+        w[at, :] = jnp.dot(narrow, widen[...], preferred_element_type=f32).astype(bf16)
         return carry
 
     lax.fori_loop(0, n, widened, 0)
@@ -957,28 +1067,25 @@
     def project(b, carry):
         here = pl.ds(pl.multiple_of(b * tokens, tokens), tokens)
         out = jnp.dot(norms[b], w[...], preferred_element_type=f32)
-        cos, sin = cosine[here, :], sine[here, :]
+        cos, sin = cos_here[here, :], sin_here[here, :]
         for h in range(heads + 1):
             part = out[:, h * LANES : (h + 1) * LANES]
             rotated = (part * cos + pltpu.roll(part, SLOT, 1) * sin).astype(bf16)
             if h < heads:
-                q[h, here, :] = rotated
+                q_here[h, here, :] = rotated
             else:
-                k[here, :] = rotated
-        v[here, :] = out[:, (heads + 1) * LANES :].astype(bf16)
+                k_here[here, :] = rotated
+        v_here[here, :] = out[:, (heads + 1) * LANES :].astype(bf16)
         return carry
 
     lax.fori_loop(0, n, project, 0)
-    gather.swap.wait_send()
-    gather.ahead.wait_send()
-    gather.back.wait_send()
-    gather.relay.wait_send()
-    for copy in gather.share:
-        copy.wait_send()
+    for copy in outs[2:]:
+        copy.start()
+    gather.wait_sends()
     store(n - 2, 0).wait()
     store(n - 1, 1).wait()
     own_wo.wait()
-    for copy in across[2] + moves:
+    for copy in across[2] + moves + outs:
         copy.wait()
 
 
@@ -1002,11 +1109,12 @@
             jax.ShapeDtypeStruct((width, wide), bf16),
             jax.ShapeDtypeStruct((2, 1, width), f32),
             jax.ShapeDtypeStruct((1, length), jnp.int32),
-            jax.ShapeDtypeStruct((3, rows * n, cols // n), wg.dtype),
+            jax.ShapeDtypeStruct((2, rows * n, cols // n), wg.dtype),
+            jax.ShapeDtypeStruct((rows * n, cols // n), wg.dtype),
             jax.ShapeDtypeStruct((m,) + wo.shape, wo.dtype),
         ),
         in_specs=[hbm] * 8 + [vmem] * 2,
-        out_specs=[hbm] + [vmem] * 8 + [hbm] * 2,
+        out_specs=[hbm] * 6 + [vmem] * 3 + [hbm] * 3,
         scratch_shapes=[
             pltpu.VMEM((n, tokens, width), bf16),
             pltpu.VMEM((n, tokens, width), bf16),
@@ -1014,14 +1122,19 @@
             pltpu.VMEM((n,) + places.shape, places.dtype),
             pltpu.VMEM((n, m) + wqkv.shape[1:], wqkv.dtype),
             pltpu.VMEM((n, m) + gains.shape, gains.dtype),
-            pltpu.SemaphoreType.DMA((2, Gather.COPIES)),
+            pltpu.VMEM((heads, length, LANES), bf16),
+            pltpu.VMEM((length, LANES), bf16),
+            pltpu.VMEM((length, LANES), bf16),
+            pltpu.VMEM((length, LANES), f32),
+            pltpu.VMEM((length, LANES), f32),
+            *Gathers.scratch(2),
             pltpu.SemaphoreType.DMA((6, 2, n - 1)),
             pltpu.SemaphoreType.DMA((3, 2, m - 1)),
             pltpu.SemaphoreType.DMA((2,)),
-            pltpu.SemaphoreType.DMA((8,)),
+            pltpu.SemaphoreType.DMA((13,)),
         ],
         compiler_params=pltpu.CompilerParams(
-            collective_id=ident, has_side_effects=True, vmem_limit_bytes=50 << 20
+            collective_id=ident, has_side_effects=True, vmem_limit_bytes=VMEM_LIMIT
         ),
         cost_estimate=COST,
         name="entry",
@@ -1051,31 +1164,38 @@
 
 
 def attend_body(
-    n, m, factor, q, k, v, docs, wo, go, o, low, lse, start, wo_all, go_all,
-    vt, top, total, acc, begin_row, sems, loc
+    n, m, factor, q, k, v, docs, wo, go, x, gain,
+    o, lse, start, mine_all, wo_all, go_all, resid, norm,
+    mine, vt, top, total, acc, begin_row, low, wo_here, go_here, sems, so, sl, loc,
 ):
     h, i = pl.program_id(0), pl.program_id(1)
+    heads, blocks = pl.num_programs(0), pl.num_programs(1)
     plane = Plane(n, m)
-    first = Gather(plane, wo, wo_all, sems.at[0], sems.at[1], loc.at[0])
-    second = Gather(plane, go, go_all, sems.at[2], sems.at[3], loc.at[1])
-    at_step = h * pl.num_programs(1) + i
+    filled = wo.shape[1]
+
+    def wo_at(i):
+        return wo_here.at[i, :, pl.ds(0, filled), :]
+
+    first = Gathers(plane, wo, wo_at, sems.at[0], loc.at[0], 2)
+    second = Gathers(plane, go, lambda i: go_here.at[i], sems.at[1], loc.at[1], 2)
+    at_step = h * blocks + i
+    rows = go.shape[0]
+    each = BLOCK // rows
 
     @pl.when(at_step == 0)
     def _():
         enter_plane(plane, False)
         first.start()
-        second.start()
+        gap = (n, wo_here.shape[1], SLOT - filled, wo_here.shape[3])
+        wo_here[:, :, filled:, :] = jnp.zeros(gap, bf16)
         vt[...] = v[...].T
         begin_row[...] = begins(docs[...])
         start[...] = begin_row[...]
 
-    @pl.when(at_step == 4)
-    def _():
-        first.relay_near()
-
     @pl.when(at_step == 6)
     def _():
-        first.relay_far()
+        second.start()
+        first.relay_near()
 
     top[...] = jnp.full_like(top, mask_fill_value)
     total[...] = jnp.zeros_like(total)
@@ -1105,100 +1225,287 @@
     step(i, True)
     out = (acc[...] / total[...]).T
     o[0] = out
-    low[...] = out.astype(bf16)
+    low[h, pl.ds(pl.multiple_of(i * BLOCK, BLOCK), BLOCK), :] = out.astype(bf16)
     lse[0] = top[...] + jnp.log2(total[...])
 
-    @pl.when(at_step == pl.num_programs(0) * pl.num_programs(1) - 1)
+    def part(hh, owner):
+        return low.at[hh, pl.ds(pl.multiple_of(owner * rows, rows), rows), :]
+
+    def place(hh, source):
+        return mine.at[source, :, pl.ds(pl.multiple_of(hh * LANES, LANES), LANES)]
+
+    def send(hh, owner):
+        return remote(
+            part(hh, owner),
+            place(hh, plane.s),
+            so.at[0, hh, owner],
+            so.at[1, hh, plane.s],
+            plane.device(owner),
+        )
+
+    def keep_own(hh):
+        return pltpu.make_async_copy(part(hh, plane.s), place(hh, plane.s), sl.at[hh])
+
+    for r in range(each):
+        owner = i * each + r
+
+        @pl.when(owner != plane.s)
+        def _(owner=owner):
+            send(h, owner).start()
+
+        @pl.when(owner == plane.s)
+        def _():
+            keep_own(h).start()
+
+    @pl.when(at_step == heads * blocks - 1)
     def _():
+        first.relay_far()
         second.relay_near()
+        for hh in range(low.shape[0]):
+            keep_own(hh).wait()
+            for owner in range(n):
+
+                @pl.when(owner != plane.s)
+                def _(hh=hh, owner=owner):
+                    send(hh, owner).wait_send()
+                    remote(
+                        part(hh, owner),
+                        place(hh, owner),
+                        so.at[0, hh, owner],
+                        so.at[1, hh, owner],
+                        plane.device(owner),
+                    ).wait_recv()
+
         first.finish()
+        whole = [
+            pltpu.make_async_copy(wo_here, wo_all, loc.at[2, 0]),
+            pltpu.make_async_copy(mine, mine_all, loc.at[2, 1]),
+        ]
+        for copy in whole:
+            copy.start()
+        resid[...] = x[...].astype(f32)
+        width = resid.shape[1]
+
+        def branch(s, carry):
+            rhs = wo_here[s].reshape(-1, width)
+            resid[...] += jnp.dot(mine[s], rhs, preferred_element_type=f32)
+            return carry
+
+        lax.fori_loop(0, n, branch, 0)
         second.relay_far()
+
+        def normalize(at):
+            value = resid[at, :]
+            scale = lax.rsqrt(jnp.mean(value * value, axis=1, keepdims=True) + norm_epsilon)
+            norm[at, :] = (value * scale * gain[...]).astype(bf16)
+
+        in_tiles(rows, normalize)
         second.finish()
-
-
-def attend(n, m, factor, q, k, v, docs, wo, go, ident):
+        rest = pltpu.make_async_copy(go_here, go_all, loc.at[3, 0])
+        rest.start()
+        for copy in whole + [rest]:
+            copy.wait()
+
+
+def attend(n, m, factor, q, k, v, docs, wo, go, x, gain, ident):
     heads, length, _ = q.shape
     blocks = length // BLOCK
-    pairs = heads * BLOCK * BLOCK * blocks * (blocks + 1) // 2
+    rows, width = x.shape
+    hbm = pl.BlockSpec(memory_space=ANY)
+
+    def fixed(*shape):
+        return pl.BlockSpec(
+            shape, lambda h, i: (0,) * len(shape), pipeline_mode=pl.Buffered(buffer_count=1)
+        )
+
     return pl.pallas_call(
         functools.partial(attend_body, n, m, factor),
         grid=(heads, blocks),
         out_shape=(
             jax.ShapeDtypeStruct((heads, length, LANES), f32),
-            jax.ShapeDtypeStruct((length, heads * LANES), bf16),
             jax.ShapeDtypeStruct((heads, 1, length), f32),
             jax.ShapeDtypeStruct((1, length), jnp.int32),
-            jax.ShapeDtypeStruct((n,) + wo.shape, wo.dtype),
+            jax.ShapeDtypeStruct((n, rows, heads * LANES), bf16),
+            jax.ShapeDtypeStruct((n, wo.shape[0], SLOT, width), wo.dtype),
             jax.ShapeDtypeStruct((n,) + go.shape, go.dtype),
+            jax.ShapeDtypeStruct((rows, width), f32),
+            jax.ShapeDtypeStruct((rows, width), bf16),
         ),
         in_specs=[
             pl.BlockSpec((1, BLOCK, LANES), lambda h, i: (h, i, 0)),
-            pl.BlockSpec((length, LANES), lambda h, i: (0, 0)),
-            pl.BlockSpec((length, LANES), lambda h, i: (0, 0)),
-            pl.BlockSpec((1, length), lambda h, i: (0, 0)),
-            pl.BlockSpec(memory_space=ANY),
-            pl.BlockSpec(memory_space=ANY),
+            fixed(length, LANES),
+            fixed(length, LANES),
+            fixed(1, length),
+            hbm,
+            hbm,
+            fixed(rows, width),
+            fixed(1, width),
         ],
         out_specs=[
             pl.BlockSpec((1, BLOCK, LANES), lambda h, i: (h, i, 0)),
-            pl.BlockSpec((BLOCK, LANES), lambda h, i: (i, h)),
             pl.BlockSpec((1, 1, BLOCK), lambda h, i: (h, 0, i)),
-            pl.BlockSpec((1, length), lambda h, i: (0, 0)),
-            pl.BlockSpec(memory_space=ANY),
-            pl.BlockSpec(memory_space=ANY),
+            fixed(1, length),
+            hbm,
+            hbm,
+            hbm,
+            fixed(rows, width),
+            fixed(rows, width),
         ],
         scratch_shapes=[
+            pltpu.VMEM((n, rows, heads * LANES), bf16),
             pltpu.VMEM((LANES, length), bf16),
             pltpu.VMEM((1, BLOCK), f32),
             pltpu.VMEM((1, BLOCK), f32),
             pltpu.VMEM((LANES, BLOCK), f32),
             pltpu.VMEM((1, length), jnp.int32),
-            pltpu.SemaphoreType.DMA((4, Gather.COPIES)),
-            pltpu.SemaphoreType.DMA((2,)),
+            pltpu.VMEM((heads, length, LANES), bf16),
+            pltpu.VMEM((n, wo.shape[0], SLOT, width), wo.dtype),
+            pltpu.VMEM((n,) + go.shape, go.dtype),
+            pltpu.SemaphoreType.DMA((2, 2, 2, Gather.COPIES)),
+            pltpu.SemaphoreType.DMA((2, heads, n)),
+            pltpu.SemaphoreType.DMA((heads,)),
+            pltpu.SemaphoreType.DMA((4, 2)),
         ],
-        compiler_params=pltpu.CompilerParams(collective_id=ident, has_side_effects=True),
+        compiler_params=pltpu.CompilerParams(
+            collective_id=ident, has_side_effects=True, vmem_limit_bytes=VMEM_LIMIT
+        ),
         cost_estimate=COST,
         name="attend",
-    )(q, k, v, docs, wo, go)
+    )(q, k, v, docs, wo, go, x, gain)
 
 
 def attend_back_body(
-    n, m, factor, scale, heads, q, k, v, go, o, lse, begin, cosine, sine, mixed, terms,
-    out, mixed_sum, term_sum, kt, dqt, dk, dv, delta,
-    pair, near, far, sr, lr, pair2, near2, far2, sr2, lr2, held,
+    n, m, factor, scale, heads, q, k, v, o, lse, begin, cosine, sine,
+    mixed, wo, mine, dnorm, resid, grad, gain,
+    out, layer, term_sum, dresid, gain_out,
+    kt, dqt, dk, dv, delta, pair, near, far, sr, lr, pair2, near2, far2, sr2, lr2, stage2,
+    held, held2, wo_here, dbranch, go_out, go, gain_sum, gain_cut, gain_got, sg, sv, loc,
 ):
     h = pl.program_id(0)
     j = pl.program_id(1)
     blocks = pl.num_programs(1)
     plane = Plane(n, m)
     one = Reduce(plane, lambda i: mixed.at[i], pair, near, far, sr, lr)
-    two = Reduce(plane, lambda i: terms.at[i], pair2, near2, far2, sr2, lr2)
+    two = Reduce(plane, None, pair2, near2, far2, sr2, lr2, stage2)
     at_step = h * blocks + j
+    rows, width = dnorm.shape
+    strip = gain_out.shape[2]
+    gain_copies = exchange(
+        plane, lambda i: gain_cut.at[i], lambda i: gain_got.at[i], sv.at[0], sv.at[1], loc.at[1]
+    )
+
+    def own_heads():
+        return pltpu.make_async_copy(go_out.at[plane.s], go.at[plane.s], loc.at[2])
+
+    def send_heads(r):
+        peer = plane.seq_ahead(r)
+        return remote(
+            go_out.at[peer], go.at[plane.s], sg.at[0, r], sg.at[1, r], plane.device(peer)
+        )
 
     @pl.when(at_step == 0)
     def _():
+        load = pltpu.make_async_copy(wo, wo_here, loc.at[0])
+        load.start()
         enter_plane(plane, False)
-        one.start()
+        one.start(3, 1)
+        gain_sum[...] = jnp.zeros_like(gain_sum)
+
+        def into_branch(at):
+            value, up = resid[at, :], dnorm[at, :]
+            scale_two = lax.rsqrt(jnp.mean(value * value, axis=1, keepdims=True) + norm_epsilon)
+            inner = gain[...] * up
+            moment = jnp.mean(value * inner, axis=1, keepdims=True)
+            turned = value * scale_two
+            got = (
+                grad[at, :].astype(f32)
+                + scale_two * inner
+                - turned * (scale_two * scale_two * moment)
+            )
+            dresid[at, :] = got
+            dbranch[at, :] = got.astype(bf16)
+            gain_sum[...] += up * turned
+
+        in_tiles(rows, into_branch)
+        one.send_to()
+        one.start(2, 0)
+        total_gain = jnp.sum(gain_sum[...], axis=0, keepdims=True)
+        for i in range(n):
+            gain_cut[i] = total_gain[:, i * (width // n) : (i + 1) * (width // n)]
+        for copy in gain_copies:
+            copy.start()
+        load.wait()
+
+        def into_heads(r, carry):
+            peer = plane.seq_ahead(r)
+            value = lax.dot_general(
+                dbranch[...], wo_here[peer], NT, preferred_element_type=f32
+            ).astype(bf16)
+            for hh in range(heads):
+                go_out[peer, hh] = value[:, hh * LANES : (hh + 1) * LANES]
+
+            @pl.when(r == 0)
+            def _():
+                own_heads().start()
+
+            @pl.when(r > 0)
+            def _():
+                send_heads(r).start()
+
+            return carry
+
+        lax.fori_loop(0, n, into_heads, 0)
+
+        def into_terms(it, carry):
+            kk = 3 - it // 2
+            other = 1 - lax.rem(it, 2)
+            b = plane.number(kk, other)
+            value = lax.dot_general(
+                mine[b], dbranch[...], (((0,), (0,)), ((), ())), preferred_element_type=f32
+            ).astype(bf16)
+            for half in range(2 * heads):
+                cut = value[half * SLOT : half * SLOT + HALF]
+                at = slice(half * HALF, (half + 1) * HALF)
+
+                @pl.when(other == 0)
+                def _(cut=cut, at=at):
+                    pair2[kk, at, :] = cut
+
+                @pl.when(other == 1)
+                def _(cut=cut, at=at):
+                    stage2[kk, at, :] = cut
+
+            for which in range(4):
+
+                @pl.when(it == 2 * (3 - which))
+                def _(which=which):
+                    two.swaps[Reduce.THEIRS[which]].start()
+
+            return carry
+
+        lax.fori_loop(0, n, into_terms, 0)
+        own_heads().wait()
+        for r in range(1, n):
+            send_heads(r).wait()
 
     @pl.when(at_step == 1)
     def _():
-        one.send_to()
-        two.start()
-
-    @pl.when(at_step == 2)
+        two.send_to()
+        one.ready()
+        one.first(held, resid)
+
+    @pl.when(at_step == 3)
     def _():
-        one.ready()
-        one.first(mixed_sum)
+        one.send_fro()
 
     @pl.when(at_step == 4)
     def _():
-        one.send_fro()
-        two.send_to()
-
-    @pl.when(at_step == 5)
-    def _():
         two.ready()
-        two.first(held)
+        two.first(held2)
+
+    def heads_grad(i):
+        each = BLOCK // rows
+        return go[pl.ds(i * each, each), h].reshape(BLOCK, LANES)
 
     @pl.when((h == 0) & (j == 0))
     def _():
@@ -1212,7 +1519,7 @@
 
         def deltas(i, carry):
             at = pl.ds(pl.multiple_of(i * BLOCK, BLOCK), BLOCK)
-            both = (go[at, :].astype(f32) * o[0, at, :]).T
+            both = (heads_grad(i).astype(f32) * o[0, at, :]).T
             delta[:, at] = jnp.sum(both, axis=0, keepdims=True)
             return carry
 
@@ -1228,7 +1535,7 @@
         raw = lax.dot_general(key, query, NT, preferred_element_type=f32)
         ok = allowed_block(j * BLOCK, i * BLOCK, begin[:, at], causal)
         probs = jnp.where(ok, jnp.exp2(raw * factor - lse[0, :, at]), 0.0)
-        grads = go[at, :]
+        grads = heads_grad(i)
         dprob = lax.dot_general(value, grads, NT, preferred_element_type=f32)
         dscore = (probs * (dprob - delta[:, at])).astype(bf16)
         dv[keys_at, :] += jnp.dot(probs.astype(bf16), grads, preferred_element_type=f32)
@@ -1272,42 +1579,67 @@
             return carry
 
         lax.fori_loop(0, blocks, write, 0)
-        one.finish(mixed_sum)
         two.send_fro()
-        two.finish(held, term_sum)
-
-
-def attend_back(n, m, factor, scale, q, k, v, go, o, lse, begin, cosine, sine, mixed, terms, ident):
+        one.finish(held, layer)
+        for copy in gain_copies:
+            copy.wait()
+        got = gain_got[0]
+        for i in range(1, n):
+            got = got + gain_got[i]
+        for t in range(m):
+            gain_out[t] = got[:, t * strip : (t + 1) * strip]
+        two.finish(held2, term_sum)
+
+
+def attend_back(
+    n, m, factor, scale, q, k, v, o, lse, begin, cosine, sine,
+    mixed, wo, mine, dnorm, resid, grad, gain, ident,
+):
     heads, length, _ = q.shape
     blocks = length // BLOCK
-    pairs = heads * BLOCK * BLOCK * blocks * (blocks + 1) // 2
-    whole = pl.BlockSpec((length, LANES), lambda h, j: (0, 0))
+    rows, width = dnorm.shape
+    strip = width // (n * m)
+
+    def fixed(*shape):
+        return pl.BlockSpec(
+            shape, lambda h, j: (0,) * len(shape), pipeline_mode=pl.Buffered(buffer_count=1)
+        )
+
+    hbm = pl.BlockSpec(memory_space=ANY)
     one = pl.BlockSpec((1, length, LANES), lambda h, j: (h, 0, 0))
     return pl.pallas_call(
         functools.partial(attend_back_body, n, m, factor, scale, heads),
         grid=(heads, blocks),
         out_shape=(
             jax.ShapeDtypeStruct((length, (heads + 2) * LANES), bf16),
-            jax.ShapeDtypeStruct(mixed.shape[1:], f32),
-            jax.ShapeDtypeStruct(terms.shape[1:], bf16),
+            jax.ShapeDtypeStruct((rows, width), bf16),
+            jax.ShapeDtypeStruct((width // n, width), bf16),
+            jax.ShapeDtypeStruct((rows, width), f32),
+            jax.ShapeDtypeStruct((m, 1, strip), f32),
         ),
         in_specs=[
             one,
-            whole,
-            whole,
-            pl.BlockSpec((length, LANES), lambda h, j: (0, h)),
+            fixed(length, LANES),
+            fixed(length, LANES),
             one,
             pl.BlockSpec((1, 1, length), lambda h, j: (h, 0, 0)),
-            pl.BlockSpec((1, length), lambda h, j: (0, 0)),
-            whole,
-            whole,
-            pl.BlockSpec(memory_space=ANY),
-            pl.BlockSpec(memory_space=ANY),
+            fixed(1, length),
+            fixed(length, LANES),
+            fixed(length, LANES),
+            hbm,
+            hbm,
+            fixed(*mine.shape),
+            fixed(rows, width),
+            fixed(rows, width),
+            fixed(rows, width),
+            fixed(1, width),
         ],
         out_specs=[
-            pl.BlockSpec((length, (heads + 2) * LANES), lambda h, j: (0, 0)),
-            pl.BlockSpec(mixed.shape[1:], lambda h, j: (0, 0)),
-            pl.BlockSpec(terms.shape[1:], lambda h, j: (0, 0)),
+            fixed(length, (heads + 2) * LANES),
+            fixed(rows, width),
+            fixed(width // n, width),
+            fixed(rows, width),
+            fixed(m, 1, strip),
         ],
         scratch_shapes=[
             pltpu.VMEM((LANES, length), bf16),
@@ -1316,148 +1648,146 @@
             pltpu.VMEM((length, LANES), f32),
             pltpu.VMEM((1, length), f32),
         ]
-        + Reduce.scratch(*mixed.shape[1:])
-        + Reduce.scratch(*terms.shape[1:])
-        + [pltpu.VMEM(terms.shape[1:], f32)],
+        + Reduce.scratch(rows, width)
+        + Reduce.scratch(width // n, width)
+        + [
+            pltpu.VMEM((4, width // n, width), bf16),
+            pltpu.VMEM((rows, width), f32),
+            pltpu.VMEM((width // n, width), f32),
+            pltpu.VMEM(wo.shape, bf16),
+            pltpu.VMEM((rows, width), bf16),
+            pltpu.VMEM((n, heads, rows, LANES), bf16),
+            pltpu.VMEM((n, heads, rows, LANES), bf16),
+            pltpu.VMEM((TILE, width), f32),
+            pltpu.VMEM((n, 1, width // n), f32),
+            pltpu.VMEM((n, 1, width // n), f32),
+            pltpu.SemaphoreType.DMA((2, n)),
+            pltpu.SemaphoreType.DMA((2, n - 1)),
+            pltpu.SemaphoreType.DMA((3,)),
+        ],
         compiler_params=pltpu.CompilerParams(
-            collective_id=ident, has_side_effects=True, vmem_limit_bytes=56 << 20
+            collective_id=ident, has_side_effects=True, vmem_limit_bytes=VMEM_LIMIT
         ),
         cost_estimate=COST,
         name="attend_back",
-    )(q, k, v, go, o, lse, begin, cosine, sine, mixed, terms)
+    )(q, k, v, o, lse, begin, cosine, sine, mixed, wo, mine, dnorm, resid, grad, gain)
 
 
 def feed_body(
-    n, m, mine, go, w_in, dnorm, grads, mixed,
-    rows, rows_t, go_t, go_two, w, h, mix_two, pair, near, far, stage,
-    sg, sr, loc, sw, so, sm, sd,
+    n, m, mine, go, w_in, down, dnorm, grads, mixed,
+    rows, rows_t, go_t, go_two, w, gates, h, mix_two, down_held, pair, near, far, stage,
+    sg, lg, sr, loc, sw, so, sm, sd, sz,
 ):
     plane = Plane(n, m)
     tokens = rows.shape[1]
-    hid = w_in.shape[3]
-    enter_plane(plane, False)
-    gather = Gather(plane, mine, rows, sg.at[0], sg.at[1], loc.at[0])
+    hid = down.shape[1]
+    enter_plane(plane, True)
+    gather = Gathers(plane, mine, lambda i: rows.at[i], sg, lg, 2)
     reduce = Reduce(plane, None, pair, near, far, sr, None, stage)
     gather.start()
+
+    def down_at(t):
+        return w.at[2, :, pl.ds(pl.multiple_of(t * hid, hid), hid)]
+
+    chain = Chain(plane, down, down_at, sz)
+    chain.start()
+    own_down = pltpu.make_async_copy(down, down_at(plane.t), loc.at[0])
+    own_down.start()
     weights = [
         pltpu.make_async_copy(
             w_in.at[t, j], w.at[j, :, t * hid : (t + 1) * hid], sw.at[j, t]
         )
-        for j in range(3)
+        for j in range(2)
         for t in range(m)
     ]
     for copy in weights:
         copy.start()
 
-    def number(it):
-        return plane.number(it // 2, lax.rem(it, 2))
-
-    def load_go(it, slot):
-        return pltpu.make_async_copy(go.at[number(it)], go_two.at[slot], so.at[slot])
-
-    def store_mix(it, slot):
-        return pltpu.make_async_copy(mix_two.at[slot], mixed.at[number(it)], sm.at[slot])
-
-    load_go(0, 0).start()
-    gather.own.wait()
+    gather.wait_own()
     for copy in weights:
         copy.wait()
 
-    def blocks(it, carry):
+    def span(b):
+        return pl.ds(pl.multiple_of(b * tokens, tokens), tokens)
+
+    def forward(it, carry):
+        b = plane.number(it // 2, lax.rem(it, 2))
+
+        @pl.when(it == 1)
+        def _():
+            gather.wait_swap()
+
+        @pl.when(it == 2)
+        def _():
+            chain.step(1)
+            gather.relay_near()
+
+        @pl.when(it == 3)
+        def _():
+            gather.wait_share(1)
+
+        @pl.when(it == 4)
+        def _():
+            chain.step(2)
+
+        @pl.when(it == 5)
+        def _():
+            gather.wait_share(0)
+
+        @pl.when(it == 6)
+        def _():
+            gather.relay_far()
+
+        @pl.when(it == 7)
+        def _():
+            gather.wait_share(2)
+
         slot = lax.rem(it, 2)
-        k = it // 2
-        b = number(it)
-
-        @pl.when(it == 1)
-        def _():
-            gather.swap.wait_recv()
-
-        @pl.when(it == 2)
-        def _():
-            gather.relay_near()
-
-        @pl.when(it == 3)
-        def _():
-            gather.share[1].wait_recv()
-
-        @pl.when(it == 5)
-        def _():
-            gather.share[0].wait_recv()
-
-        @pl.when(it == 6)
-        def _():
-            reduce.join(1)
-            reduce.out[1].start()
-            gather.relay_far()
-
-        @pl.when(it == 7)
-        def _():
-            gather.share[2].wait_recv()
 
         @pl.when(it < n - 1)
         def _():
-            load_go(it + 1, 1 - slot).start()
-
-        load_go(it, slot).wait()
-
-        @pl.when(it >= 2)
-        def _():
-            store_mix(it - 2, slot).wait()
-
-        here = pl.ds(pl.multiple_of(b * tokens, tokens), tokens)
+            early_go(it + 1, 1 - slot).start()
+
         row = rows[b]
         gate = jnp.dot(row, w[0], preferred_element_type=f32)
         up = jnp.dot(row, w[1], preferred_element_type=f32)
-        grad = go_two[slot]
-        dhidden = jnp.dot(grad, w[2], preferred_element_type=f32)
-        sig = jax.nn.sigmoid(gate)
-        act = gate * sig
-        hidden = (act * up).astype(bf16)
-        dgate = (dhidden * up * sig * (1.0 + gate * (1.0 - sig))).astype(bf16)
-        dup = (dhidden * act).astype(bf16)
-        h[0, here, :] = dgate
-        h[1, here, :] = dup
-        h[2, here, :] = hidden
-        part = lax.dot_general(dgate, w[0], NT, preferred_element_type=f32)
-        part = part + lax.dot_general(dup, w[1], NT, preferred_element_type=f32)
-        part = part.astype(bf16)
-
-        @pl.when(lax.rem(it, 2) == 0)
-        def _():
-            pair[k] = part
-
-        @pl.when(lax.rem(it, 2) == 1)
-        def _():
-            stage[k] = part
-
-        for kk in range(4):
-
-            @pl.when(it == 2 * kk + 1)
-            def _(kk=kk):
-                reduce.swaps[Reduce.THEIRS[kk]].start()
-
-        mix_two[slot] = lax.dot_general(hidden, w[2], NT, preferred_element_type=f32).astype(bf16)
-        store_mix(it, slot).start()
-        rows_t[:, here] = row.T
-        go_t[:, here] = grad.T
+        gates[0, span(b), :] = gate
+        gates[1, span(b), :] = up
+        h[2, span(b), :] = (gate * jax.nn.sigmoid(gate) * up).astype(bf16)
+        rows_t[:, span(b)] = row.T
+        early_go(it, slot).wait()
+        go_t[:, span(b)] = go_two[slot].T
         return carry
 
-    lax.fori_loop(0, n, blocks, 0)
-    reduce.join(3)
-    reduce.out[0].start()
+    def early_go(it, slot):
+        b = plane.number(it // 2, lax.rem(it, 2))
+        return pltpu.make_async_copy(go.at[b], go_two.at[slot], so.at[slot])
+
+    early_go(0, 0).start()
+    lax.fori_loop(0, n, forward, 0)
+
+    def number(it):
+        return plane.number(3 - it // 2, 1 - lax.rem(it, 2))
+
+    def load_go(it, slot):
+        return pltpu.make_async_copy(go.at[number(it)], go_two.at[slot], so.at[slot])
+
+    def store_mix(it, slot):
+        return pltpu.make_async_copy(mix_two.at[slot], mixed.at[number(it)], sm.at[slot])
+
     width = rows.shape[2]
 
-    def weight_grad(j, left):
+    def weight_grad(j, left, held):
         def part(i, carry):
             at = pl.ds(pl.multiple_of(i * 256, 256), 256)
             value = jnp.dot(left[at, :], h[j], preferred_element_type=f32)
-            w[j, at, :] = value.astype(bf16)
+            held[at, :] = value.astype(bf16)
             return carry
 
         lax.fori_loop(0, width // 256, part, 0)
         outs = [
             pltpu.make_async_copy(
-                w.at[j, :, t * hid : (t + 1) * hid], grads.at[t, j], sd.at[j, t]
+                held.at[:, t * hid : (t + 1) * hid], grads.at[t, j], sd.at[j, t]
             )
             for t in range(m)
         ]
@@ -1465,88 +1795,135 @@
             copy.start()
         return outs
 
-    outs = weight_grad(0, rows_t)
-    reduce.ready()
-    reduce.first(dnorm)
-    reduce.send_fro()
-    outs += weight_grad(1, rows_t)
-    outs += weight_grad(2, go_t)
-    gather.swap.wait_send()
-    gather.ahead.wait_send()
-    gather.back.wait_send()
-    gather.relay.wait_send()
-    for copy in gather.share:
-        copy.wait_send()
+    load_go(0, 0).start()
+    outs = weight_grad(2, go_t, down_held)
+    for hop in range(3, m):
+        chain.step(hop)
+    own_down.wait()
+
+    def backward(it, carry):
+        slot = lax.rem(it, 2)
+        k = 3 - it // 2
+        b = number(it)
+
+        @pl.when(it == 3)
+        def _():
+            reduce.join(3)
+            reduce.out[0].start()
+
+        @pl.when(it == 6)
+        def _():
+            reduce.join(1)
+            reduce.out[1].start()
+
+        @pl.when(it < n - 1)
+        def _():
+            load_go(it + 1, 1 - slot).start()
+
+        load_go(it, slot).wait()
+
+        @pl.when(it >= 2)
+        def _():
+            store_mix(it - 2, slot).wait()
+
+        gate = gates[0, span(b), :]
+        up = gates[1, span(b), :]
+        grad = go_two[slot]
+        dhidden = jnp.dot(grad, w[2], preferred_element_type=f32)
+        sig = jax.nn.sigmoid(gate)
+        hidden = h[2, span(b), :]
+        dgate = (dhidden * up * sig * (1.0 + gate * (1.0 - sig))).astype(bf16)
+        dup = (dhidden * gate * sig).astype(bf16)
+        h[0, span(b), :] = dgate
+        h[1, span(b), :] = dup
+        part = lax.dot_general(dgate, w[0], NT, preferred_element_type=f32)
+        part = part + lax.dot_general(dup, w[1], NT, preferred_element_type=f32)
+        part = part.astype(bf16)
+
+        @pl.when(lax.rem(it, 2) == 1)
+        def _():
+            pair[k] = part
+
+        @pl.when(lax.rem(it, 2) == 0)
+        def _():
+            stage[k] = part
+
+        for kk in range(4):
+
+            @pl.when(it == 2 * (3 - kk))
+            def _(kk=kk):
+                reduce.swaps[Reduce.THEIRS[kk]].start()
+
+        mix_two[slot] = lax.dot_general(hidden, w[2], NT, preferred_element_type=f32).astype(bf16)
+        store_mix(it, slot).start()
+        return carry
+
+    lax.fori_loop(0, n, backward, 0)
     store_mix(n - 2, 0).wait()
     store_mix(n - 1, 1).wait()
+    reduce.ready()
+    reduce.send_fro()
+    outs += weight_grad(0, rows_t, w.at[0])
+    reduce.first(dnorm)
+    outs += weight_grad(1, rows_t, w.at[1])
+    gather.wait_sends()
+    chain.wait_sends()
     reduce.finish(dnorm)
     for copy in outs:
         copy.wait()
 
 
-def feed(n, m, norm, go, w_in, ident):
+def feed(n, m, norm, go, w_in, down, ident):
     tokens, width = norm.shape
-    hid = w_in.shape[3]
+    hid = down.shape[1]
     length = n * tokens
-    block = pltpu.VMEM((n, tokens, width), bf16)
     return pl.pallas_call(
         functools.partial(feed_body, n, m),
         out_shape=(
             jax.ShapeDtypeStruct((tokens, width), f32),
-            jax.ShapeDtypeStruct(w_in.shape, bf16),
+            jax.ShapeDtypeStruct((m, 3, width, hid), bf16),
             jax.ShapeDtypeStruct((n, tokens, width), bf16),
         ),
-        in_specs=[pl.BlockSpec(memory_space=ANY)] * 3,
+        in_specs=[pl.BlockSpec(memory_space=ANY)] * 4,
         out_specs=[
             pl.BlockSpec(memory_space=pltpu.VMEM),
             pl.BlockSpec(memory_space=ANY),
             pl.BlockSpec(memory_space=ANY),
         ],
         scratch_shapes=[
-            block,
+            pltpu.VMEM((n, tokens, width), bf16),
             pltpu.VMEM((width, length), bf16),
             pltpu.VMEM((width, length), bf16),
             pltpu.VMEM((2, tokens, width), bf16),
             pltpu.VMEM((3, width, m * hid), bf16),
+            pltpu.VMEM((2, length, m * hid), f32),
             pltpu.VMEM((3, length, m * hid), bf16),
             pltpu.VMEM((2, tokens, width), bf16),
+            pltpu.VMEM((width, m * hid), bf16),
         ]
         + [pltpu.VMEM((slots, tokens, width), bf16) for slots in Reduce.SLOTS]
         + [
             pltpu.VMEM((4, tokens, width), bf16),
-            pltpu.SemaphoreType.DMA((2, Gather.COPIES)),
+            *Gathers.scratch(2),
             pltpu.SemaphoreType.DMA((4, 4)),
             pltpu.SemaphoreType.DMA((1,)),
-            pltpu.SemaphoreType.DMA((3, m)),
+            pltpu.SemaphoreType.DMA((2, m)),
             pltpu.SemaphoreType.DMA((2,)),
             pltpu.SemaphoreType.DMA((2,)),
             pltpu.SemaphoreType.DMA((3, m)),
+            pltpu.SemaphoreType.DMA((4, m)),
         ],
         compiler_params=pltpu.CompilerParams(
-            collective_id=ident, has_side_effects=True, vmem_limit_bytes=60 << 20
+            collective_id=ident, has_side_effects=True, vmem_limit_bytes=VMEM_LIMIT
         ),
         cost_estimate=COST,
         name="feed",
-    )(norm, go, w_in)
+    )(norm, go, w_in, down)
 
 
 def split_heads(w, groups):
     rows = w.shape[0]
     return w.reshape(rows, groups, -1).transpose(1, 0, 2)
-
-
-def spread(blocks):
-    lead = blocks.shape[:-1]
-    halves = blocks.reshape(lead + (-1, HALF))
-    pad = [(0, 0)] * len(lead) + [(0, 0), (0, SLOT - HALF)]
-    wide = jnp.pad(halves, pad)
-    return wide.reshape(lead + (-1,))
-
-
-def gathered(wide):
-    lead = wide.shape[:-1]
-    halves = wide.reshape(lead + (-1, SLOT))[..., :HALF]
-    return halves.reshape(lead + (-1,))
 
 
 def fast_layer(n, m):
@@ -1590,59 +1967,27 @@
         to_lane = from_col // HALF * SLOT + from_col % HALF
         widen = (to_lane[:, None] == jnp.arange(cols // HALF * SLOT)[None, :]).astype(bf16)
 
-        norm_t, q, k, v, cosine, sine, wqkv, gain_rows, docs, ffn_mine, output_rows = entry(
+        norm_t, q, k, v, cosine, sine, wqkv, gain_rows, docs, ffn_mine, down_mine, output_rows = entry(
             n, m, heads, x, places, packed, gains,
             gate_weight, up_weight, down_weight, output_weight, widen, inverse, 0,
         )
         gain_one, gain_two = gain_rows[0], gain_rows[1]
         ffn_all = lax.all_gather(ffn_mine, "tp", axis=0, tiled=False)
-        o, low, lse, begin, output_full, grad_all = attend(
-            n, m, factor, q, k, v, docs, output_rows.reshape(m * strip, width), out_grad[0], 9
-        )
-        output_full = output_full.reshape(-1, width)
-        (mine,) = plane_swap(n, m, 1, low.reshape(n, rows, heads * LANES))
-        attn_low = gathered(mine.transpose(1, 0, 2).reshape(rows, n * heads * LANES))
-
-        x_f = x.astype(f32)
-        resid = x_f + jnp.dot(attn_low, output_full, preferred_element_type=f32)
-        scale_two = lax.rsqrt(jnp.mean(resid * resid, axis=1, keepdims=True) + norm_epsilon)
-        norm_two = (resid * scale_two * gain_two).astype(bf16)
-        grad_low = out_grad[0]
-        dnorm_two, ffn_terms, mixed = feed(n, m, norm_two, grad_all, ffn_all, 2)
+        o, lse, begin, mine, output_full, grad_all, resid, norm_two = attend(
+            n, m, factor, q, k, v, docs,
+            output_rows.reshape(-1, HALF, width), out_grad[0], x, gain_two, 9,
+        )
+        dnorm_two, ffn_terms, mixed = feed(n, m, norm_two, grad_all, ffn_all, down_mine, 2)
         ffn_sum = lax.psum_scatter(ffn_terms, "tp", scatter_dimension=0, tiled=False)
-
-        inner = gain_two * dnorm_two
-        moment = jnp.mean(resid * inner, axis=1, keepdims=True)
-        dresid = (
-            grad_low.astype(f32)
-            + scale_two * inner
-            - resid * scale_two * scale_two * scale_two * moment
-        )
-        dbranch = dresid.astype(bf16)
-        output_term = outer_product(attn_low, dbranch).astype(bf16).reshape(n, m * strip, width)
-        dheads = spread(times_transpose(dbranch, output_full).astype(bf16))
-        dheads = dheads.reshape(rows, n, heads * LANES).transpose(1, 0, 2)
-        gain_term = jnp.sum(dnorm_two * resid * scale_two, axis=0)
-        go, gain_parts = plane_swap(n, m, 5, dheads, gain_term.reshape(n, 1, m * strip))
-        go = go.reshape(length, heads * LANES)
-        gain_part = jnp.sum(gain_parts, axis=(0, 1)).reshape(m, 1, strip)
-
-        dqkv, mixed_sum, output_sum = attend_back(
-            n, m, factor, scale, q, k, v, go, o, lse, begin, cosine, sine, mixed, output_term, 3
-        )
-        layer_output = (resid + mixed_sum).astype(bf16)[None]
-        dnorm_one, ffn_out, qkv_out, output_parts, gain_sums = last(
-            n, m, dqkv, wqkv, widen.T, norm_t, ffn_sum,
+        dqkv, layer_output, output_sum, dresid, gain_part = attend_back(
+            n, m, factor, scale, q, k, v, o, lse, begin, cosine, sine, mixed,
+            output_full.reshape(n, -1, width), mine, dnorm_two, resid, out_grad[0], gain_two, 3,
+        )
+        input_grad, ffn_out, qkv_out, output_parts, gain_sums = last(
+            n, m, dqkv, wqkv, widen.T, x, dresid, gain_one, norm_t, ffn_sum,
             output_sum.reshape(m, strip, width), gain_part, 6,
         )
         output_grad = jnp.sum(output_parts.astype(f32), axis=0)
-
-        scale_one = lax.rsqrt(jnp.mean(x_f * x_f, axis=1, keepdims=True) + norm_epsilon)
-        inner = gain_one * dnorm_one
-        moment = jnp.mean(x_f * inner, axis=1, keepdims=True)
-        input_grad = (
-            dresid + scale_one * inner - x_f * scale_one * scale_one * scale_one * moment
-        )[None]
 
         gate_grad, up_grad, down_grad = [ffn_out[i].astype(f32) for i in range(3)]
         kv = HEAD_SIZE * KEY_VALUE_HEADS // n
@@ -1663,8 +2008,8 @@
         first_gain_grad = one / first_gain.astype(f32)
         second_gain_grad = jnp.sum(gain_sums, axis=(0, 1))
         return (
-            layer_output,
-            input_grad,
+            layer_output[None],
+            input_grad[None],
             first_gain_grad,
             query_grad,
             key_grad,

time: 393 us -> 373 us (0.949)
  matrix products: 11.1 us -> 0 us
  Pallas kernels: 322 us -> 332 us
  local copies, waits for them, and re-layouts: 17.2 us -> 7.8 us
  other arithmetic: 14.9 us -> 10.2 us
  waiting for transfers between devices: 11.7 us -> 7.36 us
    pallas_call x2 -> x0, Pallas kernels: 29 us -> none  [plane_swap(): pl.pallas_call(functools.partial(swap_body, n, m, count), out_shape=tuple...]
    pallas_call x1, Pallas kernels: 58.3 us -> 76.1 us  [attend_back(): pl.pallas_call(functools.partial(attend_back_body, n, m, factor, scale, h...]
    all_gather x1, waiting for transfers between devices: 11.7 us -> 0.02 us  [on_plane(): ffn_all = lax.all_gather(ffn_mine, 'tp', axis=0, tiled=False)]
    pallas_call x1, Pallas kernels: 68.3 us -> 79.9 us  [feed(): pl.pallas_call(functools.partial(feed_body, n, m), out_shape=(jax.ShapeDt...]
    dot_general x3 -> x0, matrix products: 11.1 us -> none  [the longest x1 3.82 us: on_plane(): resid = x_f + jnp.dot(attn_low, output_full, preferred_element_type=f32)]
    pallas_call x1, Pallas kernels: 61.5 us -> 70.4 us  [attend(): pl.pallas_call(functools.partial(attend_body, n, m, factor), grid=(heads,...]
    reduce_scatter x1, waiting for transfers between devices: 0.01 us -> 7.31 us  [on_plane(): lax.psum_scatter(ffn_terms, 'tp', scatter_dimension=0, tiled=False)]
    broadcast_in_dim x2 -> x0, other arithmetic: 5.67 us -> none  [the longest x1 3.14 us: on_plane(): (dresid + scale_one * inner - x_f * scale_one * scale_one * scale_one * m...]
  transfers between devices with their start and end apart: 2 -> 2, of which waited for: 1 -> 1; matrix products, arithmetic and copies ran while one was open for 6% -> 1% of each run, Pallas kernels for 38% -> 39%
where the time goes in v4:
time: 373 us; the launch traced here: 372 us
  Pallas kernels  332 us (89%)
  between operations  14.3 us (4%)
  other arithmetic  10.2 us (3%)
  local copies, waits for them, and re-layouts  7.8 us (2%)
  waiting for transfers between devices  7.36 us (2%)
    pallas_call x1, Pallas kernels, feed(): pl.pallas_call(functools.partial(feed_body, n, m), out_shape=(jax.ShapeDt...  79.9 us
    pallas_call x1, Pallas kernels, attend_back(): pl.pallas_call(functools.partial(attend_back_body, n, m, factor, scale, h...  76.1 us
    pallas_call x1, Pallas kernels, attend(): pl.pallas_call(functools.partial(attend_body, n, m, factor), grid=(heads,...  70.4 us
    pallas_call x1, Pallas kernels, entry(): pl.pallas_call(functools.partial(entry_body, n, m, heads, strip), out_sha...  54.3 us
    pallas_call x1, Pallas kernels, last(): pl.pallas_call(functools.partial(last_body, n, m), out_shape=(jax.ShapeDt...  51.8 us
  transfers between devices with their start and end apart: 2, of which 1 were waited for; matrix products, arithmetic and copies ran while one was open for 1% of the time, Pallas kernels for 39%

profile of v4, /device:TPU:0, one launch (start us, length us, event | category | flops | bytes accessed | tf_op | source)
XLA Modules:
  0.0 372.3 jit_solution(4543770570408705861)
XLA Ops:
  7.3 0.5 compare_select_fusion.inverse
  7.8 1.0 reshape.112
  8.8 1.0 reshape.113
  9.9 1.1 reshape.111
  11.0 0.9 fusion.widen
  12.0 0.6 fusion.14.gains
  12.6 0.6 pad_add_fusion.places
  13.1 0.9 pad_maximum_fusion.wqkv
  14.0 54.3 %entry.1 = (bf16[1536,2048]{1,0:T(8,128)(2,1)}, bf16[2,2048,128]{2,1,0:T(8,128)(2,1)}, bf16[2048,128]{1,0:T(8,128)(2,1)}, bf16[2048,128]{1,0:T(8,128)(2,1)}, f32...) custom-call(bf16[256,1536]{1,0:T(8,128)(2,1)} %bitcast.36, ...), custom_call_target="tpu_custom_call" | custom-call | flops 1000000 | bytes 100000 | tf_op jit(solution)/shard_map/entry/pallas_call | solution.py:1100
  68.6 1.3 slice_bitcast_fusion
  69.9 70.4 %attend.1 = (f32[2,2048,128]{2,1,0:T(8,128)}, f32[2,1,2048]{2,1,0:T(1,128)}, s32[1,2048]{1,0:T(1,128)}, bf16[8,256,256]{2,1,0:T(8,128)(2,1)}, bf16[8,4,64,1536]{...) custom-call(bf16[2,2048,128]{2,1,0:T(8,128)(2,1)} %get-tuple-element.44.q, ...), custom_call_target="tpu_custom_call" | custom-call | flops 1000000 | bytes 100000 | tf_op jit(solution)/shard_map/attend/pallas_call | solution.py:1321
  140.3 79.9 %feed.1 = (f32[256,1536]{1,0:T(8,128)}, bf16[4,3,1536,128]{3,2,1,0:T(8,128)(2,1)}, bf16[8,256,1536]{2,1,0:T(8,128)(2,1)}) custom-call(bf16[256,1536]{1,0:T(8,128)(2,1)} %get-tuple-element.55.mine, bf16[8,256,1536]{2,1,0:T(8,128)(2,1)} %get-tuple-element.56.go, bf16[4,2,1536,128]{3,2,1,0:T(8,128)(2,1)} %bitcast.42, bf16[1536,128]{1,0:T(8,128)(2,1)} %get-tuple-element.58.down), custom_call_target="tpu_custom_call" | custom-call | flops 1000000 | bytes 100000 | tf_op jit(solution)/shard_map/feed/pallas_call | solution.py:1880
  220.3 0.8 fusion.1.narrow
  221.1 76.1 %attend_back.1 = (bf16[2048,512]{1,0:T(8,128)(2,1)}, bf16[256,1536]{1,0:T(8,128)(2,1)}, bf16[192,1536]{1,0:T(8,128)(2,1)}, f32[256,1536]{1,0:T(8,128)}, f32[4,1,48]{2,1,0:T(1,128)}) custom-call(bf16[2,2048,128]{2,1,0:T(8,128)(2,1)} %get-tuple-element.44.q, bf16[2048,128]{1,0:T(8,128)(2,1)} %get-tuple-element.45.k, bf16[2048,128]{1,0:T(8,128)(2,1)} %get-tuple-element.46.v, ...), custom_call_target="tpu_custom_call" | custom-call | flops 1000000 | bytes 100000 | tf_op jit(solution)/shard_map/attend_back/pallas_call | solution.py:1610
  297.2 7.3 %reduce-scatter.2.cloned.1.call-done = bf16[1,3,1536,128]{3,2,1,0:T(8,128)(2,1)} async-done(((bf16[4,3,1536,128]{3,2,1,0:T(8,128)(2,1)}), bf16[1,3,1536,128]{3,2,1,0:T(8,128)(2,1)}) %reduce-scatter.2.cloned.1.call-update) | async-done | bytes 1179664 | tf_op jit(solution)/shard_map/reduce_scatter | solution.py:1981
  304.5 51.8 %last.1 = (f32[256,1536]{1,0:T(8,128)}, bf16[3,192,1024]{2,1,0:T(8,128)(2,1)}, bf16[8,48,384]{2,1,0:T(8,128)(2,1)}, bf16[4,48,1536]{2,1,0:T(8,128)(2,1)}, f32[4,1,48]{2,1,0:T(1,128)}) custom-call(bf16[2048,512]{1,0:T(8,128)(2,1)} %get-tuple-element.65.dqkv_in, bf16[1536,512]{1,0:T(8,128)(2,1)} %get-tuple-element.66.w_in, bf16[512,384]{1,0:T(8,128)(2,1)} %fusion.1.narrow, ...), custom_call_target="tpu_custom_call" | custom-call | flops 1000000 | bytes 100000 | tf_op jit(solution)/shard_map/last/pallas_call | solution.py:870
  356.3 1.0 convert_bitcast_fusion
  357.3 1.1 convert_bitcast_fusion.2
  360.1 1.5 bitcast_convert_fusion
  361.6 0.8 convert_reduce_fusion
  362.4 0.5 reduce_sum.49
  363.0 0.5 convert_divide_fusion
  363.5 0.9 copy.42
  364.4 1.1 copy.43
  (47 shorter events, 2.0 us)
Async XLA Ops:
  7.2 4.8 %copy-start.10 = (bf16[48]{0:T(256)(128)(2,1)S(1)}, bf16[48]{0:T(256)(128)(2,1)}, u32[]{:S(2)}) copy-start(bf16[48]{0:T(256)(128)(2,1)} %param.16) | copy-start | bytes 292
  7.2 4.8 %copy-start.14 = (bf16[48]{0:T(256)(128)(2,1)S(1)}, bf16[48]{0:T(256)(128)(2,1)}, u32[]{:S(2)}) copy-start(bf16[48]{0:T(256)(128)(2,1)} %param.21) | copy-start | bytes 292
  7.2 5.4 %copy-start.13 = (s32[1,256]{1,0:T(1,128)S(1)}, s32[1,256]{1,0:T(1,128)}, u32[]{:S(2)}) copy-start(s32[1,256]{1,0:T(1,128)} %param.14) | copy-start | bytes 3076
  7.2 5.4 %copy-start.12 = (s32[1,256]{1,0:T(1,128)S(1)}, s32[1,256]{1,0:T(1,128)}, u32[]{:S(2)}) copy-start(s32[1,256]{1,0:T(1,128)} %param.15) | copy-start | bytes 3076
  7.2 133.1 %all-gather.3.cloned.1.call-start = ((), (), s32[]{:S(2)}) async-start(), calls=%async_computation.2 | async-start | bytes 3932160 | tf_op jit(solution)/shard_map/all_gather | solution.py:1975
  68.4 236.1 %reduce-scatter.2.cloned.1.call-start = ((), (), s32[]{:S(2)}) async-start(), calls=%async_computation.1 | async-start | bytes 5898240 | tf_op jit(solution)/shard_map/reduce_scatter | solution.py:1981
  356.3 2.6 copy-start.7
  357.3 1.9 copy-start.8
  358.7 0.9 copy-start.9
  358.7 1.4 copy-start.1
  358.8 2.7 copy-start.2
  359.2 2.4 copy-start.5
  359.6 2.0 copy-start.6
  360.1 1.5 copy-start.4
  360.1 2.3 copy-start.11
  360.1 3.4 copy-start.3
  361.6 2.8 copy-start
Sparse Core Ops, SparseCore 0:
  68.5 68.9 all-gather.2
  220.4 84.0 reduce-scatter.1

commit v5 on v4

--- a/solution.py
+++ b/solution.py
@@ -710,7 +710,7 @@
 
         def add(at):
             value = pair[0, at, :].astype(f32) + near[0, at, :].astype(f32)
-            total[at, :] = value if more is None else value + more[at, :]
+            total[at, :] = value if more is None else value + more[at, :].astype(f32)
 
         in_tiles(self.rows, add)
 
@@ -736,15 +736,15 @@
 
 
 def last_body(
-    n, m, dqkv_in, w_in, narrow, x_in, dresid_in, gain, norm_t, ffn, wo, vec,
+    n, m, dqkv_in, w_in, narrow, x_in, dresid_in, gain, norm_t, ffn, downs, wo, vec,
     input_grad, ffn_out, qkv_out, wo_out, vec_out,
-    dqkv, w, x, dresid, pair, near, far, sr, lr, total, stage, norms, mine, got, summed, sems, st, loc,
+    dqkv, w, x, dresid, down_here, down_sum, pair, near, far, sr, lr, total, stage, norms, mine, got, summed, sems, st, loc,
 ):
     plane = Plane(n, m)
     loads = [
         pltpu.make_async_copy(a, b, loc.at[5 + i])
         for i, (a, b) in enumerate(
-            ((dqkv_in, dqkv), (w_in, w), (x_in, x), (dresid_in, dresid))
+            ((dqkv_in, dqkv), (w_in, w), (downs, down_here), (x_in, x), (dresid_in, dresid))
         )
     ]
     load = pltpu.make_async_copy(norm_t, norms, loc.at[0])
@@ -763,10 +763,20 @@
     a = exchange(
         plane,
         lambda i: ffn.at[:, pl.ds(pl.multiple_of(i * rows, rows), rows), :],
-        lambda i: ffn_out.at[:, :, pl.ds(pl.multiple_of(i * width, width), width)],
+        lambda i: ffn_out.at[
+            pl.ds(0, 2), :, pl.ds(pl.multiple_of(i * width, width), width)
+        ],
         sems.at[0, 0],
         sems.at[0, 1],
         loc.at[3],
+    )
+    a_down = exchange(
+        plane,
+        lambda i: down_sum.at[pl.ds(pl.multiple_of(i * rows, rows), rows), :],
+        lambda i: ffn_out.at[2, :, pl.ds(pl.multiple_of(i * width, width), width)],
+        sems.at[2, 0],
+        sems.at[2, 1],
+        loc.at[10],
     )
     reduce = Reduce(plane, None, pair, near, far, sr, lr, stage)
     tokens = pair.shape[1]
@@ -803,6 +813,17 @@
 
     lax.fori_loop(0, n, blocks, 0)
     reduce.send_to()
+    loads[2].wait()
+
+    def add_down(at):
+        value = down_here[0, at, :].astype(f32)
+        for t in range(1, m):
+            value = value + down_here[t, at, :].astype(f32)
+        down_sum[at, :] = value.astype(bf16)
+
+    in_tiles(down_sum.shape[0], add_down)
+    for copy in a_down:
+        copy.start()
     load.wait()
     strip = summed.shape[1]
 
@@ -842,7 +863,7 @@
     )
     for copy in b:
         copy.start()
-    for copy in loads[2:]:
+    for copy in loads[3:]:
         copy.wait()
     reduce.finish(total)
 
@@ -856,11 +877,11 @@
         )
 
     in_tiles(tokens, into_input)
-    for copy in a + b + across:
+    for copy in a + a_down + b + across:
         copy.wait()
 
 
-def last(n, m, dqkv, w, narrow, x, dresid, gain, norm_t, ffn, wo, vec, ident):
+def last(n, m, dqkv, w, narrow, x, dresid, gain, norm_t, ffn, downs, wo, vec, ident):
     width, length = norm_t.shape
     tokens = length // n
     cols = narrow.shape[1]
@@ -876,13 +897,15 @@
             jax.ShapeDtypeStruct(wo.shape, wo.dtype),
             jax.ShapeDtypeStruct(vec.shape, vec.dtype),
         ),
-        in_specs=[hbm, hbm, vmem, hbm, hbm, vmem] + [hbm] * 4,
+        in_specs=[hbm, hbm, vmem, hbm, hbm, vmem] + [hbm] * 5,
         out_specs=[vmem] + [hbm] * 4,
         scratch_shapes=[
             pltpu.VMEM(dqkv.shape, bf16),
             pltpu.VMEM(w.shape, bf16),
             pltpu.VMEM(x.shape, bf16),
             pltpu.VMEM(dresid.shape, f32),
+            pltpu.VMEM(downs.shape, bf16),
+            pltpu.VMEM(downs.shape[1:], bf16),
         ]
         + Reduce.scratch(tokens, width)
         + [
@@ -892,16 +915,16 @@
             pltpu.VMEM((n, m, strip, cols), bf16),
             pltpu.VMEM((m, n, strip, cols), bf16),
             pltpu.VMEM((n, strip, cols), bf16),
-            pltpu.SemaphoreType.DMA((2, 2, n - 1)),
+            pltpu.SemaphoreType.DMA((3, 2, n - 1)),
             pltpu.SemaphoreType.DMA((3, 2, m - 1)),
-            pltpu.SemaphoreType.DMA((9,)),
+            pltpu.SemaphoreType.DMA((11,)),
         ],
         compiler_params=pltpu.CompilerParams(
             collective_id=ident, has_side_effects=True, vmem_limit_bytes=VMEM_LIMIT
         ),
         cost_estimate=COST,
         name="last",
-    )(dqkv, w, narrow, x, dresid, gain, norm_t, ffn, wo, vec)
+    )(dqkv, w, narrow, x, dresid, gain, norm_t, ffn, downs, wo, vec)
 
 
 def column(row):
@@ -1163,209 +1186,155 @@
     return begin
 
 
+def spread_rows(wo, wo_here):
+    halves, filled, width = wo.shape
+    for i in range(halves):
+        wo_here[i * SLOT : i * SLOT + filled, :] = wo[i]
+        wo_here[i * SLOT + filled : (i + 1) * SLOT, :] = jnp.zeros((SLOT - filled, width), bf16)
+
+
 def attend_body(
     n, m, factor, q, k, v, docs, wo, go, x, gain,
-    o, lse, start, mine_all, wo_all, go_all, resid, norm,
-    mine, vt, top, total, acc, begin_row, low, wo_here, go_here, sems, so, sl, loc,
+    o_out, lse, start, low_out, go_all, resid, norm,
+    o, low, vt, top, total, acc, wo_here, go_here,
+    pair, near, far, sr, lr, stage, sg, lg, loc,
 ):
-    h, i = pl.program_id(0), pl.program_id(1)
-    heads, blocks = pl.num_programs(0), pl.num_programs(1)
     plane = Plane(n, m)
-    filled = wo.shape[1]
-
-    def wo_at(i):
-        return wo_here.at[i, :, pl.ds(0, filled), :]
-
-    first = Gathers(plane, wo, wo_at, sems.at[0], loc.at[0], 2)
-    second = Gathers(plane, go, lambda i: go_here.at[i], sems.at[1], loc.at[1], 2)
-    at_step = h * blocks + i
-    rows = go.shape[0]
-    each = BLOCK // rows
-
-    @pl.when(at_step == 0)
-    def _():
-        enter_plane(plane, False)
-        first.start()
-        gap = (n, wo_here.shape[1], SLOT - filled, wo_here.shape[3])
-        wo_here[:, :, filled:, :] = jnp.zeros(gap, bf16)
-        vt[...] = v[...].T
-        begin_row[...] = begins(docs[...])
-        start[...] = begin_row[...]
-
-    @pl.when(at_step == 6)
-    def _():
-        second.start()
-        first.relay_near()
-
-    top[...] = jnp.full_like(top, mask_fill_value)
-    total[...] = jnp.zeros_like(total)
-    acc[...] = jnp.zeros_like(acc)
-    query = q[0]
-    begin = begin_row[:, pl.ds(pl.multiple_of(i * BLOCK, BLOCK), BLOCK)]
-
-    def step(j, causal):
-        at = pl.ds(pl.multiple_of(j * BLOCK, BLOCK), BLOCK)
-        raw = lax.dot_general(k[at, :], query, NT, preferred_element_type=f32)
-        ok = allowed_block(j * BLOCK, i * BLOCK, begin, causal)
-        scores = jnp.where(ok, raw * factor, mask_fill_value)
-        new_top = jnp.maximum(top[...], jnp.max(scores, axis=0, keepdims=True))
-        weights = jnp.exp2(scores - new_top)
-        keep = jnp.exp2(top[...] - new_top)
-        total[...] = total[...] * keep + jnp.sum(weights, axis=0, keepdims=True)
-        acc[...] = acc[...] * keep + jnp.dot(
-            vt[:, at], weights.astype(bf16), preferred_element_type=f32
-        )
-        top[...] = new_top
-
-    def loop(j, carry):
-        step(j, False)
+    rows = x.shape[0]
+    heads = q.shape[0]
+    enter_plane(plane, False)
+    gather = Gathers(plane, go, lambda i: go_here.at[i], sg, lg, 2)
+    reduce = Reduce(plane, None, pair, near, far, sr, None, stage)
+    gather.start()
+    spread_rows(wo, wo_here)
+    vt[...] = v[...].T
+    start[...] = begins(docs[...])
+
+    def chips(step, carry):
+        kk = 3 - step
+        i = plane.number(kk, 0) // 2
+        here = pl.ds(pl.multiple_of(i * BLOCK, BLOCK), BLOCK)
+        begin = start[:, here]
+
+        def head(h, carry):
+            query = q[h, here, :]
+            top[...] = jnp.full_like(top, mask_fill_value)
+            total[...] = jnp.zeros_like(total)
+            acc[...] = jnp.zeros_like(acc)
+
+            def keys(j, causal):
+                at = pl.ds(pl.multiple_of(j * BLOCK, BLOCK), BLOCK)
+                raw = lax.dot_general(k[at, :], query, NT, preferred_element_type=f32)
+                ok = allowed_block(j * BLOCK, i * BLOCK, begin, causal)
+                scores = jnp.where(ok, raw * factor, mask_fill_value)
+                new_top = jnp.maximum(top[...], jnp.max(scores, axis=0, keepdims=True))
+                weights = jnp.exp2(scores - new_top)
+                keep = jnp.exp2(top[...] - new_top)
+                total[...] = total[...] * keep + jnp.sum(weights, axis=0, keepdims=True)
+                acc[...] = acc[...] * keep + jnp.dot(
+                    vt[:, at], weights.astype(bf16), preferred_element_type=f32
+                )
+                top[...] = new_top
+
+            def loop(j, carry):
+                keys(j, False)
+                return carry
+
+            lax.fori_loop(0, i, loop, 0)
+            keys(i, True)
+            out = (acc[...] / total[...]).T
+            o[h, here, :] = out
+            low[here, pl.ds(pl.multiple_of(h * LANES, LANES), LANES)] = out.astype(bf16)
+            lse[h, :, here] = top[...] + jnp.log2(total[...])
+            return carry
+
+        lax.fori_loop(0, heads, head, 0)
+
+        @pl.when(step == 1)
+        def _():
+            reduce.join(3)
+            reduce.out[0].start()
+
+        @pl.when(step == 3)
+        def _():
+            reduce.join(1)
+            reduce.out[1].start()
+
+        for other in (1, 0):
+            b = plane.number(kk, other)
+            at = pl.ds(pl.multiple_of(b * rows, rows), rows)
+            part = jnp.dot(low[at, :], wo_here[...], preferred_element_type=f32).astype(bf16)
+            if other:
+                stage[kk] = part
+                for which in range(4):
+
+                    @pl.when(kk == which)
+                    def _(which=which):
+                        reduce.swaps[Reduce.THEIRS[which]].start()
+
+            else:
+                pair[kk] = part
         return carry
 
-    lax.fori_loop(0, i, loop, 0)
-    step(i, True)
-    out = (acc[...] / total[...]).T
-    o[0] = out
-    low[h, pl.ds(pl.multiple_of(i * BLOCK, BLOCK), BLOCK), :] = out.astype(bf16)
-    lse[0] = top[...] + jnp.log2(total[...])
-
-    def part(hh, owner):
-        return low.at[hh, pl.ds(pl.multiple_of(owner * rows, rows), rows), :]
-
-    def place(hh, source):
-        return mine.at[source, :, pl.ds(pl.multiple_of(hh * LANES, LANES), LANES)]
-
-    def send(hh, owner):
-        return remote(
-            part(hh, owner),
-            place(hh, plane.s),
-            so.at[0, hh, owner],
-            so.at[1, hh, plane.s],
-            plane.device(owner),
-        )
-
-    def keep_own(hh):
-        return pltpu.make_async_copy(part(hh, plane.s), place(hh, plane.s), sl.at[hh])
-
-    for r in range(each):
-        owner = i * each + r
-
-        @pl.when(owner != plane.s)
-        def _(owner=owner):
-            send(h, owner).start()
-
-        @pl.when(owner == plane.s)
-        def _():
-            keep_own(h).start()
-
-    @pl.when(at_step == heads * blocks - 1)
-    def _():
-        first.relay_far()
-        second.relay_near()
-        for hh in range(low.shape[0]):
-            keep_own(hh).wait()
-            for owner in range(n):
-
-                @pl.when(owner != plane.s)
-                def _(hh=hh, owner=owner):
-                    send(hh, owner).wait_send()
-                    remote(
-                        part(hh, owner),
-                        place(hh, owner),
-                        so.at[0, hh, owner],
-                        so.at[1, hh, owner],
-                        plane.device(owner),
-                    ).wait_recv()
-
-        first.finish()
-        whole = [
-            pltpu.make_async_copy(wo_here, wo_all, loc.at[2, 0]),
-            pltpu.make_async_copy(mine, mine_all, loc.at[2, 1]),
-        ]
-        for copy in whole:
-            copy.start()
-        resid[...] = x[...].astype(f32)
-        width = resid.shape[1]
-
-        def branch(s, carry):
-            rhs = wo_here[s].reshape(-1, width)
-            resid[...] += jnp.dot(mine[s], rhs, preferred_element_type=f32)
-            return carry
-
-        lax.fori_loop(0, n, branch, 0)
-        second.relay_far()
-
-        def normalize(at):
-            value = resid[at, :]
-            scale = lax.rsqrt(jnp.mean(value * value, axis=1, keepdims=True) + norm_epsilon)
-            norm[at, :] = (value * scale * gain[...]).astype(bf16)
-
-        in_tiles(rows, normalize)
-        second.finish()
-        rest = pltpu.make_async_copy(go_here, go_all, loc.at[3, 0])
-        rest.start()
-        for copy in whole + [rest]:
-            copy.wait()
+    lax.fori_loop(0, 4, chips, 0)
+    outs = [
+        pltpu.make_async_copy(o, o_out, loc.at[0]),
+        pltpu.make_async_copy(low, low_out, loc.at[1]),
+    ]
+    for copy in outs:
+        copy.start()
+    gather.relay_near()
+    reduce.ready()
+    reduce.first(resid, x)
+    reduce.send_fro()
+    gather.relay_far()
+    reduce.finish(resid)
+
+    def normalize(at):
+        value = resid[at, :]
+        scale = lax.rsqrt(jnp.mean(value * value, axis=1, keepdims=True) + norm_epsilon)
+        norm[at, :] = (value * scale * gain[...]).astype(bf16)
+
+    in_tiles(rows, normalize)
+    gather.finish()
+    outs.append(pltpu.make_async_copy(go_here, go_all, loc.at[2]))
+    outs[-1].start()
+    for copy in outs:
+        copy.wait()
 
 
 def attend(n, m, factor, q, k, v, docs, wo, go, x, gain, ident):
     heads, length, _ = q.shape
-    blocks = length // BLOCK
     rows, width = x.shape
     hbm = pl.BlockSpec(memory_space=ANY)
-
-    def fixed(*shape):
-        return pl.BlockSpec(
-            shape, lambda h, i: (0,) * len(shape), pipeline_mode=pl.Buffered(buffer_count=1)
-        )
-
+    vmem = pl.BlockSpec(memory_space=pltpu.VMEM)
     return pl.pallas_call(
         functools.partial(attend_body, n, m, factor),
-        grid=(heads, blocks),
         out_shape=(
             jax.ShapeDtypeStruct((heads, length, LANES), f32),
             jax.ShapeDtypeStruct((heads, 1, length), f32),
             jax.ShapeDtypeStruct((1, length), jnp.int32),
-            jax.ShapeDtypeStruct((n, rows, heads * LANES), bf16),
-            jax.ShapeDtypeStruct((n, wo.shape[0], SLOT, width), wo.dtype),
+            jax.ShapeDtypeStruct((length, heads * LANES), bf16),
             jax.ShapeDtypeStruct((n,) + go.shape, go.dtype),
             jax.ShapeDtypeStruct((rows, width), f32),
             jax.ShapeDtypeStruct((rows, width), bf16),
         ),
-        in_specs=[
-            pl.BlockSpec((1, BLOCK, LANES), lambda h, i: (h, i, 0)),
-            fixed(length, LANES),
-            fixed(length, LANES),
-            fixed(1, length),
-            hbm,
-            hbm,
-            fixed(rows, width),
-            fixed(1, width),
-        ],
-        out_specs=[
-            pl.BlockSpec((1, BLOCK, LANES), lambda h, i: (h, i, 0)),
-            pl.BlockSpec((1, 1, BLOCK), lambda h, i: (h, 0, i)),
-            fixed(1, length),
-            hbm,
-            hbm,
-            hbm,
-            fixed(rows, width),
-            fixed(rows, width),
-        ],
+        in_specs=[vmem] * 5 + [hbm] + [vmem] * 2,
+        out_specs=[hbm, vmem, vmem, hbm, hbm, vmem, vmem],
         scratch_shapes=[
-            pltpu.VMEM((n, rows, heads * LANES), bf16),
+            pltpu.VMEM((heads, length, LANES), f32),
+            pltpu.VMEM((length, heads * LANES), bf16),
             pltpu.VMEM((LANES, length), bf16),
             pltpu.VMEM((1, BLOCK), f32),
             pltpu.VMEM((1, BLOCK), f32),
             pltpu.VMEM((LANES, BLOCK), f32),
-            pltpu.VMEM((1, length), jnp.int32),
-            pltpu.VMEM((heads, length, LANES), bf16),
-            pltpu.VMEM((n, wo.shape[0], SLOT, width), wo.dtype),
+            pltpu.VMEM((heads * LANES, width), bf16),
             pltpu.VMEM((n,) + go.shape, go.dtype),
-            pltpu.SemaphoreType.DMA((2, 2, 2, Gather.COPIES)),
-            pltpu.SemaphoreType.DMA((2, heads, n)),
-            pltpu.SemaphoreType.DMA((heads,)),
-            pltpu.SemaphoreType.DMA((4, 2)),
-        ],
+        ]
+        + Reduce.scratch(rows, width)
+        + [pltpu.VMEM((4, rows, width), bf16)]
+        + Gathers.scratch(2)
+        + [pltpu.SemaphoreType.DMA((3,))],
         compiler_params=pltpu.CompilerParams(
             collective_id=ident, has_side_effects=True, vmem_limit_bytes=VMEM_LIMIT
         ),
@@ -1375,308 +1344,223 @@
 
 
 def attend_back_body(
-    n, m, factor, scale, heads, q, k, v, o, lse, begin, cosine, sine,
-    mixed, wo, mine, dnorm, resid, grad, gain,
-    out, layer, term_sum, dresid, gain_out,
-    kt, dqt, dk, dv, delta, pair, near, far, sr, lr, pair2, near2, far2, sr2, lr2, stage2,
-    held, held2, wo_here, dbranch, go_out, go, gain_sum, gain_cut, gain_got, sg, sv, loc,
+    n, m, factor, scale, q_in, k_in, v_in, o_in, lse, begin, cos_in, sin_in, low_in,
+    mixed, wo, dnorm, resid, grad, gain,
+    out, layer, terms, dresid, gain_out,
+    q, k, v, o, cosine, sine, low, kt, dqt, dk, dv, delta, go, every, dbranch, wo_here,
+    pair, near, far, sr, lr, held, gain_sum, gain_cut, gain_got, sg, lg, sv, loc,
 ):
-    h = pl.program_id(0)
-    j = pl.program_id(1)
-    blocks = pl.num_programs(1)
     plane = Plane(n, m)
-    one = Reduce(plane, lambda i: mixed.at[i], pair, near, far, sr, lr)
-    two = Reduce(plane, None, pair2, near2, far2, sr2, lr2, stage2)
-    at_step = h * blocks + j
+    heads, length, _ = q.shape
     rows, width = dnorm.shape
     strip = gain_out.shape[2]
+    loads = [
+        pltpu.make_async_copy(a, b, loc.at[i])
+        for i, (a, b) in enumerate(
+            (
+                (q_in, q), (k_in, k), (v_in, v), (o_in, o),
+                (cos_in, cosine), (sin_in, sine), (low_in, low),
+            )
+        )
+    ]
+    for copy in loads:
+        copy.start()
+    enter_plane(plane, False)
+    one = Reduce(plane, lambda i: mixed.at[i], pair, near, far, sr, lr)
+    one.start(3, 1)
+    gather = Gathers(plane, dbranch, lambda i: every.at[i], sg, lg, 2)
     gain_copies = exchange(
-        plane, lambda i: gain_cut.at[i], lambda i: gain_got.at[i], sv.at[0], sv.at[1], loc.at[1]
-    )
-
-    def own_heads():
-        return pltpu.make_async_copy(go_out.at[plane.s], go.at[plane.s], loc.at[2])
-
-    def send_heads(r):
-        peer = plane.seq_ahead(r)
-        return remote(
-            go_out.at[peer], go.at[plane.s], sg.at[0, r], sg.at[1, r], plane.device(peer)
-        )
-
-    @pl.when(at_step == 0)
-    def _():
-        load = pltpu.make_async_copy(wo, wo_here, loc.at[0])
-        load.start()
-        enter_plane(plane, False)
-        one.start(3, 1)
-        gain_sum[...] = jnp.zeros_like(gain_sum)
-
-        def into_branch(at):
-            value, up = resid[at, :], dnorm[at, :]
-            scale_two = lax.rsqrt(jnp.mean(value * value, axis=1, keepdims=True) + norm_epsilon)
-            inner = gain[...] * up
-            moment = jnp.mean(value * inner, axis=1, keepdims=True)
-            turned = value * scale_two
-            got = (
-                grad[at, :].astype(f32)
-                + scale_two * inner
-                - turned * (scale_two * scale_two * moment)
-            )
-            dresid[at, :] = got
-            dbranch[at, :] = got.astype(bf16)
-            gain_sum[...] += up * turned
-
-        in_tiles(rows, into_branch)
-        one.send_to()
-        one.start(2, 0)
-        total_gain = jnp.sum(gain_sum[...], axis=0, keepdims=True)
-        for i in range(n):
-            gain_cut[i] = total_gain[:, i * (width // n) : (i + 1) * (width // n)]
-        for copy in gain_copies:
-            copy.start()
-        load.wait()
-
-        def into_heads(r, carry):
-            peer = plane.seq_ahead(r)
-            value = lax.dot_general(
-                dbranch[...], wo_here[peer], NT, preferred_element_type=f32
-            ).astype(bf16)
-            for hh in range(heads):
-                go_out[peer, hh] = value[:, hh * LANES : (hh + 1) * LANES]
-
-            @pl.when(r == 0)
-            def _():
-                own_heads().start()
-
-            @pl.when(r > 0)
-            def _():
-                send_heads(r).start()
-
-            return carry
-
-        lax.fori_loop(0, n, into_heads, 0)
-
-        def into_terms(it, carry):
-            kk = 3 - it // 2
-            other = 1 - lax.rem(it, 2)
-            b = plane.number(kk, other)
-            value = lax.dot_general(
-                mine[b], dbranch[...], (((0,), (0,)), ((), ())), preferred_element_type=f32
-            ).astype(bf16)
-            for half in range(2 * heads):
-                cut = value[half * SLOT : half * SLOT + HALF]
-                at = slice(half * HALF, (half + 1) * HALF)
-
-                @pl.when(other == 0)
-                def _(cut=cut, at=at):
-                    pair2[kk, at, :] = cut
-
-                @pl.when(other == 1)
-                def _(cut=cut, at=at):
-                    stage2[kk, at, :] = cut
-
-            for which in range(4):
-
-                @pl.when(it == 2 * (3 - which))
-                def _(which=which):
-                    two.swaps[Reduce.THEIRS[which]].start()
-
-            return carry
-
-        lax.fori_loop(0, n, into_terms, 0)
-        own_heads().wait()
-        for r in range(1, n):
-            send_heads(r).wait()
-
-    @pl.when(at_step == 1)
-    def _():
-        two.send_to()
-        one.ready()
-        one.first(held, resid)
-
-    @pl.when(at_step == 3)
-    def _():
-        one.send_fro()
-
-    @pl.when(at_step == 4)
-    def _():
-        two.ready()
-        two.first(held2)
-
-    def heads_grad(i):
-        each = BLOCK // rows
-        return go[pl.ds(i * each, each), h].reshape(BLOCK, LANES)
-
-    @pl.when((h == 0) & (j == 0))
-    def _():
-        kt[...] = k[...].T
-        dk[...] = jnp.zeros_like(dk)
-        dv[...] = jnp.zeros_like(dv)
-
-    @pl.when(j == 0)
-    def _():
-        dqt[...] = jnp.zeros_like(dqt)
-
-        def deltas(i, carry):
-            at = pl.ds(pl.multiple_of(i * BLOCK, BLOCK), BLOCK)
-            both = (heads_grad(i).astype(f32) * o[0, at, :]).T
-            delta[:, at] = jnp.sum(both, axis=0, keepdims=True)
-            return carry
-
-        lax.fori_loop(0, blocks, deltas, 0)
-
-    keys_at = pl.ds(pl.multiple_of(j * BLOCK, BLOCK), BLOCK)
-    key = k[keys_at, :]
-    value = v[keys_at, :]
-
-    def step(i, causal):
-        at = pl.ds(pl.multiple_of(i * BLOCK, BLOCK), BLOCK)
-        query = q[0, at, :]
-        raw = lax.dot_general(key, query, NT, preferred_element_type=f32)
-        ok = allowed_block(j * BLOCK, i * BLOCK, begin[:, at], causal)
-        probs = jnp.where(ok, jnp.exp2(raw * factor - lse[0, :, at]), 0.0)
-        grads = heads_grad(i)
-        dprob = lax.dot_general(value, grads, NT, preferred_element_type=f32)
-        dscore = (probs * (dprob - delta[:, at])).astype(bf16)
-        dv[keys_at, :] += jnp.dot(probs.astype(bf16), grads, preferred_element_type=f32)
-        dk[keys_at, :] += jnp.dot(dscore, query, preferred_element_type=f32)
-        dqt[:, at] += jnp.dot(kt[:, keys_at], dscore, preferred_element_type=f32)
-
-    step(j, True)
-
-    def loop(i, carry):
-        step(i, False)
-        return carry
-
-    lax.fori_loop(j + 1, blocks, loop, 0)
+        plane, lambda i: gain_cut.at[i], lambda i: gain_got.at[i], sv.at[0], sv.at[1], loc.at[7]
+    )
+    gain_sum[...] = jnp.zeros_like(gain_sum)
+
+    def into_branch(at):
+        value, up = resid[at, :], dnorm[at, :]
+        scale_two = lax.rsqrt(jnp.mean(value * value, axis=1, keepdims=True) + norm_epsilon)
+        inner = gain[...] * up
+        moment = jnp.mean(value * inner, axis=1, keepdims=True)
+        turned = value * scale_two
+        got = (
+            grad[at, :].astype(f32) + scale_two * inner - turned * (scale_two * scale_two * moment)
+        )
+        dresid[at, :] = got
+        dbranch[at, :] = got.astype(bf16)
+        gain_sum[...] += up * turned
+
+    in_tiles(rows, into_branch)
+    gather.start()
+    one.start(2, 0)
+    total_gain = jnp.sum(gain_sum[...], axis=0, keepdims=True)
+    for i in range(n):
+        gain_cut[i] = total_gain[:, i * (width // n) : (i + 1) * (width // n)]
+    for copy in gain_copies:
+        copy.start()
+    spread_rows(wo, wo_here)
+    for copy in loads:
+        copy.wait()
+    kt[...] = k[...].T
+    dk[...] = jnp.zeros_like(dk)
+    dv[...] = jnp.zeros_like(dv)
 
     def unturn(value, at):
         return value * cosine[at, :] - pltpu.roll(value, SLOT, 1) * sine[at, :]
 
-    @pl.when(j == blocks - 1)
-    def _():
-        def write(i, carry):
-            at = pl.ds(pl.multiple_of(i * BLOCK, BLOCK), BLOCK)
-            got = unturn(dqt[:, at].T * scale, at).astype(bf16)
-            for which in range(heads):
-
-                @pl.when(h == which)
-                def _(which=which):
-                    out[at, which * LANES : (which + 1) * LANES] = got
-
+    def chips(kk, carry):
+        @pl.when(kk == 0)
+        def _():
+            gather.wait_own()
+            gather.wait_swap()
+
+        @pl.when(kk == 1)
+        def _():
+            gather.relay_near()
+            gather.wait_share(1)
+
+        @pl.when(kk == 2)
+        def _():
+            one.send_to()
+            gather.wait_share(0)
+
+        @pl.when(kk == 3)
+        def _():
+            one.ready()
+            one.first(held, resid)
+            gather.relay_far()
+            gather.wait_share(2)
+
+        i = plane.number(kk, 0) // 2
+        here = pl.ds(pl.multiple_of(i * BLOCK, BLOCK), BLOCK)
+        for other in range(2):
+            b = plane.number(kk, other)
+            at = pl.ds(pl.multiple_of(b * rows, rows), rows)
+            value = lax.dot_general(every[b], wo_here[...], NT, preferred_element_type=f32)
+            for h in range(heads):
+                go[h, at, :] = value[:, h * LANES : (h + 1) * LANES].astype(bf16)
+
+        def head(h, carry):
+            query = q[h, here, :]
+            grads = go[h, here, :]
+            delta[...] = jnp.sum((grads.astype(f32) * o[h, here, :]).T, axis=0, keepdims=True)
+            dqt[...] = jnp.zeros_like(dqt)
+
+            def keys(j, causal):
+                at = pl.ds(pl.multiple_of(j * BLOCK, BLOCK), BLOCK)
+                raw = lax.dot_general(k[at, :], query, NT, preferred_element_type=f32)
+                ok = allowed_block(j * BLOCK, i * BLOCK, begin[:, here], causal)
+                probs = jnp.where(ok, jnp.exp2(raw * factor - lse[h, :, here]), 0.0)
+                dprob = lax.dot_general(v[at, :], grads, NT, preferred_element_type=f32)
+                dscore = (probs * (dprob - delta[...])).astype(bf16)
+                dv[at, :] += jnp.dot(probs.astype(bf16), grads, preferred_element_type=f32)
+                dk[at, :] += jnp.dot(dscore, query, preferred_element_type=f32)
+                dqt[...] += jnp.dot(kt[:, at], dscore, preferred_element_type=f32)
+
+            def loop(j, carry):
+                keys(j, False)
+                return carry
+
+            lax.fori_loop(0, i, loop, 0)
+            keys(i, True)
+            got = unturn(dqt[...].T * scale, here).astype(bf16)
+            out[here, pl.ds(pl.multiple_of(h * LANES, LANES), LANES)] = got
             return carry
 
-        lax.fori_loop(0, blocks, write, 0)
-
-    @pl.when((h == heads - 1) & (j == blocks - 1))
-    def _():
-        def write(i, carry):
-            at = pl.ds(pl.multiple_of(i * BLOCK, BLOCK), BLOCK)
-            out[at, heads * LANES : (heads + 1) * LANES] = unturn(dk[at, :] * scale, at).astype(
-                bf16
-            )
-            out[at, (heads + 1) * LANES :] = dv[at, :].astype(bf16)
-            return carry
-
-        lax.fori_loop(0, blocks, write, 0)
-        two.send_fro()
-        one.finish(held, layer)
-        for copy in gain_copies:
-            copy.wait()
-        got = gain_got[0]
-        for i in range(1, n):
-            got = got + gain_got[i]
-        for t in range(m):
-            gain_out[t] = got[:, t * strip : (t + 1) * strip]
-        two.finish(held2, term_sum)
+        lax.fori_loop(0, heads, head, 0)
+        return carry
+
+    lax.fori_loop(0, 4, chips, 0)
+
+    def write(i, carry):
+        at = pl.ds(pl.multiple_of(i * BLOCK, BLOCK), BLOCK)
+        turned = unturn(dk[at, :] * scale, at).astype(bf16)
+        out[at, heads * LANES : (heads + 1) * LANES] = turned
+        out[at, (heads + 1) * LANES :] = dv[at, :].astype(bf16)
+        return carry
+
+    lax.fori_loop(0, length // BLOCK, write, 0)
+    one.send_fro()
+    across = every.reshape(length, width)
+    part = 512
+
+    def into_terms(i, carry):
+        at = pl.ds(pl.multiple_of(i * part, part), part)
+        value = lax.dot_general(
+            low[...], across[:, at], (((0,), (0,)), ((), ())), preferred_element_type=f32
+        ).astype(bf16)
+        for half in range(terms.shape[0]):
+            terms[half, :, at] = value[half * SLOT : half * SLOT + HALF]
+        return carry
+
+    lax.fori_loop(0, width // part, into_terms, 0)
+    for copy in gain_copies:
+        copy.wait()
+    got = gain_got[0]
+    for i in range(1, n):
+        got = got + gain_got[i]
+    for t in range(m):
+        gain_out[t] = got[:, t * strip : (t + 1) * strip]
+    gather.wait_sends()
+    one.finish(held, layer)
 
 
 def attend_back(
-    n, m, factor, scale, q, k, v, o, lse, begin, cosine, sine,
-    mixed, wo, mine, dnorm, resid, grad, gain, ident,
+    n, m, factor, scale, q, k, v, o, lse, begin, cosine, sine, low,
+    mixed, wo, dnorm, resid, grad, gain, ident,
 ):
     heads, length, _ = q.shape
-    blocks = length // BLOCK
     rows, width = dnorm.shape
     strip = width // (n * m)
-
-    def fixed(*shape):
-        return pl.BlockSpec(
-            shape, lambda h, j: (0,) * len(shape), pipeline_mode=pl.Buffered(buffer_count=1)
-        )
-
     hbm = pl.BlockSpec(memory_space=ANY)
-    one = pl.BlockSpec((1, length, LANES), lambda h, j: (h, 0, 0))
+    vmem = pl.BlockSpec(memory_space=pltpu.VMEM)
     return pl.pallas_call(
-        functools.partial(attend_back_body, n, m, factor, scale, heads),
-        grid=(heads, blocks),
+        functools.partial(attend_back_body, n, m, factor, scale),
         out_shape=(
             jax.ShapeDtypeStruct((length, (heads + 2) * LANES), bf16),
             jax.ShapeDtypeStruct((rows, width), bf16),
-            jax.ShapeDtypeStruct((width // n, width), bf16),
+            jax.ShapeDtypeStruct(wo.shape, bf16),
             jax.ShapeDtypeStruct((rows, width), f32),
             jax.ShapeDtypeStruct((m, 1, strip), f32),
         ),
-        in_specs=[
-            one,
-            fixed(length, LANES),
-            fixed(length, LANES),
-            one,
-            pl.BlockSpec((1, 1, length), lambda h, j: (h, 0, 0)),
-            fixed(1, length),
-            fixed(length, LANES),
-            fixed(length, LANES),
-            hbm,
-            hbm,
-            fixed(*mine.shape),
-            fixed(rows, width),
-            fixed(rows, width),
-            fixed(rows, width),
-            fixed(1, width),
-        ],
-        out_specs=[
-            fixed(length, (heads + 2) * LANES),
-            fixed(rows, width),
-            fixed(width // n, width),
-            fixed(rows, width),
-            fixed(m, 1, strip),
-        ],
+        in_specs=[hbm] * 4 + [vmem] * 2 + [hbm] * 4 + [vmem] * 5,
+        out_specs=[vmem] * 5,
         scratch_shapes=[
+            pltpu.VMEM(q.shape, bf16),
+            pltpu.VMEM(k.shape, bf16),
+            pltpu.VMEM(v.shape, bf16),
+            pltpu.VMEM(o.shape, f32),
+            pltpu.VMEM(cosine.shape, f32),
+            pltpu.VMEM(sine.shape, f32),
+            pltpu.VMEM(low.shape, bf16),
             pltpu.VMEM((LANES, length), bf16),
-            pltpu.VMEM((LANES, length), f32),
+            pltpu.VMEM((LANES, BLOCK), f32),
             pltpu.VMEM((length, LANES), f32),
             pltpu.VMEM((length, LANES), f32),
-            pltpu.VMEM((1, length), f32),
+            pltpu.VMEM((1, BLOCK), f32),
+            pltpu.VMEM((heads, length, LANES), bf16),
+            pltpu.VMEM((n, rows, width), bf16),
+            pltpu.VMEM((rows, width), bf16),
+            pltpu.VMEM((heads * LANES, width), bf16),
         ]
         + Reduce.scratch(rows, width)
-        + Reduce.scratch(width // n, width)
         + [
-            pltpu.VMEM((4, width // n, width), bf16),
             pltpu.VMEM((rows, width), f32),
-            pltpu.VMEM((width // n, width), f32),
-            pltpu.VMEM(wo.shape, bf16),
-            pltpu.VMEM((rows, width), bf16),
-            pltpu.VMEM((n, heads, rows, LANES), bf16),
-            pltpu.VMEM((n, heads, rows, LANES), bf16),
             pltpu.VMEM((TILE, width), f32),
             pltpu.VMEM((n, 1, width // n), f32),
             pltpu.VMEM((n, 1, width // n), f32),
-            pltpu.SemaphoreType.DMA((2, n)),
-            pltpu.SemaphoreType.DMA((2, n - 1)),
-            pltpu.SemaphoreType.DMA((3,)),
-        ],
+        ]
+        + Gathers.scratch(2)
+        + [pltpu.SemaphoreType.DMA((2, n - 1)), pltpu.SemaphoreType.DMA((8,))],
         compiler_params=pltpu.CompilerParams(
             collective_id=ident, has_side_effects=True, vmem_limit_bytes=VMEM_LIMIT
         ),
         cost_estimate=COST,
         name="attend_back",
-    )(q, k, v, o, lse, begin, cosine, sine, mixed, wo, mine, dnorm, resid, grad, gain)
+    )(q, k, v, o, lse, begin, cosine, sine, low, mixed, wo, dnorm, resid, grad, gain)
 
 
 def feed_body(
-    n, m, mine, go, w_in, down, dnorm, grads, mixed,
+    n, m, mine, go, w_in, down, dnorm, grads, mixed, down_parts,
     rows, rows_t, go_t, go_two, w, gates, h, mix_two, down_held, pair, near, far, stage,
-    sg, lg, sr, loc, sw, so, sm, sd, sz,
+    sg, lg, sr, loc, sw, so, sm, sd, sz, sf,
 ):
     plane = Plane(n, m)
     tokens = rows.shape[1]
@@ -1785,6 +1669,8 @@
             return carry
 
         lax.fori_loop(0, width // 256, part, 0)
+        if j == 2:
+            return []
         outs = [
             pltpu.make_async_copy(
                 held.at[:, t * hid : (t + 1) * hid], grads.at[t, j], sd.at[j, t]
@@ -1797,6 +1683,16 @@
 
     load_go(0, 0).start()
     outs = weight_grad(2, go_t, down_held)
+
+    def down_part(t):
+        return down_held.at[:, pl.ds(pl.multiple_of(t * hid, hid), hid)]
+
+    outs += fan(plane, down_part, lambda t: down_parts.at[t], sf.at[0], sf.at[1])
+    outs.append(
+        pltpu.make_async_copy(down_part(plane.t), down_parts.at[plane.t], loc.at[1])
+    )
+    for copy in outs:
+        copy.start()
     for hop in range(3, m):
         chain.step(hop)
     own_down.wait()
@@ -1881,12 +1777,14 @@
         functools.partial(feed_body, n, m),
         out_shape=(
             jax.ShapeDtypeStruct((tokens, width), f32),
-            jax.ShapeDtypeStruct((m, 3, width, hid), bf16),
+            jax.ShapeDtypeStruct((m, 2, width, hid), bf16),
             jax.ShapeDtypeStruct((n, tokens, width), bf16),
+            jax.ShapeDtypeStruct((m, width, hid), bf16),
         ),
         in_specs=[pl.BlockSpec(memory_space=ANY)] * 4,
         out_specs=[
             pl.BlockSpec(memory_space=pltpu.VMEM),
+            pl.BlockSpec(memory_space=ANY),
             pl.BlockSpec(memory_space=ANY),
             pl.BlockSpec(memory_space=ANY),
         ],
@@ -1906,12 +1804,13 @@
             pltpu.VMEM((4, tokens, width), bf16),
             *Gathers.scratch(2),
             pltpu.SemaphoreType.DMA((4, 4)),
-            pltpu.SemaphoreType.DMA((1,)),
+            pltpu.SemaphoreType.DMA((2,)),
             pltpu.SemaphoreType.DMA((2, m)),
             pltpu.SemaphoreType.DMA((2,)),
             pltpu.SemaphoreType.DMA((2,)),
             pltpu.SemaphoreType.DMA((3, m)),
             pltpu.SemaphoreType.DMA((4, m)),
+            pltpu.SemaphoreType.DMA((2, m - 1)),
         ],
         compiler_params=pltpu.CompilerParams(
             collective_id=ident, has_side_effects=True, vmem_limit_bytes=VMEM_LIMIT
@@ -1973,19 +1872,20 @@
         )
         gain_one, gain_two = gain_rows[0], gain_rows[1]
         ffn_all = lax.all_gather(ffn_mine, "tp", axis=0, tiled=False)
-        o, lse, begin, mine, output_full, grad_all, resid, norm_two = attend(
-            n, m, factor, q, k, v, docs,
-            output_rows.reshape(-1, HALF, width), out_grad[0], x, gain_two, 9,
-        )
-        dnorm_two, ffn_terms, mixed = feed(n, m, norm_two, grad_all, ffn_all, down_mine, 2)
+        o, lse, begin, low, grad_all, resid, norm_two = attend(
+            n, m, factor, q, k, v, docs, output_rows, out_grad[0], x, gain_two, 9
+        )
+        dnorm_two, ffn_terms, mixed, down_parts = feed(
+            n, m, norm_two, grad_all, ffn_all, down_mine, 2
+        )
         ffn_sum = lax.psum_scatter(ffn_terms, "tp", scatter_dimension=0, tiled=False)
-        dqkv, layer_output, output_sum, dresid, gain_part = attend_back(
-            n, m, factor, scale, q, k, v, o, lse, begin, cosine, sine, mixed,
-            output_full.reshape(n, -1, width), mine, dnorm_two, resid, out_grad[0], gain_two, 3,
+        dqkv, layer_output, output_terms, dresid, gain_part = attend_back(
+            n, m, factor, scale, q, k, v, o, lse, begin, cosine, sine, low, mixed,
+            output_rows, dnorm_two, resid, out_grad[0], gain_two, 3,
         )
         input_grad, ffn_out, qkv_out, output_parts, gain_sums = last(
-            n, m, dqkv, wqkv, widen.T, x, dresid, gain_one, norm_t, ffn_sum,
-            output_sum.reshape(m, strip, width), gain_part, 6,
+            n, m, dqkv, wqkv, widen.T, x, dresid, gain_one, norm_t, ffn_sum, down_parts,
+            output_terms, gain_part, 6,
         )
         output_grad = jnp.sum(output_parts.astype(f32), axis=0)
 

time: 373 us -> 348 us (0.933)
  Pallas kernels: 332 us -> 312 us
    pallas_call x2, Pallas kernels: 146 us -> 128 us  [the longest x1 64 us: attend(): pl.pallas_call(functools.partial(attend_body, n, m, factor), out_shape=(j...]
    reduce_scatter x1, waiting for transfers between devices: 7.31 us -> 0.02 us  [on_plane(): lax.psum_scatter(ffn_terms, 'tp', scatter_dimension=0, tiled=False)]
    pallas_call x1, Pallas kernels: 79.9 us -> 75.7 us  [feed(): pl.pallas_call(functools.partial(feed_body, n, m), out_shape=(jax.ShapeDt...]
    all_gather x1, waiting for transfers between devices: 0.02 us -> 3.78 us  [on_plane(): ffn_all = lax.all_gather(ffn_mine, 'tp', axis=0, tiled=False)]
  transfers between devices with their start and end apart: 2 -> 2, of which waited for: 1 -> 1; matrix products, arithmetic and copies ran while one was open for 1% -> 1% of each run, Pallas kernels for 39% -> 37%
where the time goes in v5:
time: 348 us
  Pallas kernels  312 us (90%)
  between operations  14.3 us (4%)
  other arithmetic  10.2 us (3%)
  local copies, waits for them, and re-layouts  7.8 us (2%)
  waiting for transfers between devices  3.84 us (1%)
    pallas_call x1, Pallas kernels, feed(): pl.pallas_call(functools.partial(feed_body, n, m), out_shape=(jax.ShapeDt...  75.7 us
    pallas_call x1, Pallas kernels, attend(): pl.pallas_call(functools.partial(attend_body, n, m, factor), out_shape=(j...  64 us
    pallas_call x1, Pallas kernels, attend_back(): pl.pallas_call(functools.partial(attend_back_body, n, m, factor, scale),...  63.9 us
    pallas_call x1, Pallas kernels, entry(): pl.pallas_call(functools.partial(entry_body, n, m, heads, strip), out_sha...  54.3 us
    pallas_call x1, Pallas kernels, last(): pl.pallas_call(functools.partial(last_body, n, m), out_shape=(jax.ShapeDt...  53.6 us
  transfers between devices with their start and end apart: 2, of which 1 were waited for; matrix products, arithmetic and copies ran while one was open for 1% of the time, Pallas kernels for 37%

profile of v5, /device:TPU:0, one launch (start us, length us, event | category | flops | bytes accessed | tf_op | source)
XLA Modules:
  0.0 347.8 jit_solution(10612873773827589254)
XLA Ops:
  7.3 0.5 compare_select_fusion.inverse
  7.8 1.0 reshape.106
  8.8 1.0 reshape.107
  9.9 1.1 reshape.105
  11.0 0.9 fusion.widen
  12.0 0.6 fusion.14.gains
  12.6 0.6 pad_add_fusion.places
  13.1 0.9 pad_maximum_fusion.wqkv
  14.0 54.3 %entry.1 = (bf16[1536,2048]{1,0:T(8,128)(2,1)}, bf16[2,2048,128]{2,1,0:T(8,128)(2,1)}, bf16[2048,128]{1,0:T(8,128)(2,1)}, bf16[2048,128]{1,0:T(8,128)(2,1)}, f32...) custom-call(bf16[256,1536]{1,0:T(8,128)(2,1)} %bitcast.34, ...), custom_call_target="tpu_custom_call" | custom-call | flops 1000000 | bytes 100000 | tf_op jit(solution)/shard_map/entry/pallas_call | solution.py:1123
  68.4 1.3 slice_bitcast_fusion
  69.7 64.0 %attend.1 = (f32[2,2048,128]{2,1,0:T(8,128)}, f32[2,1,2048]{2,1,0:T(1,128)}, s32[1,2048]{1,0:T(1,128)}, bf16[2048,256]{1,0:T(8,128)(2,1)}, bf16[8,256,1536]{2,1,...) custom-call(bf16[2,2048,128]{2,1,0:T(8,128)(2,1)} %get-tuple-element.44.q.q_in, ...), custom_call_target="tpu_custom_call" | custom-call | flops 1000000 | bytes 100000 | tf_op jit(solution)/shard_map/attend/pallas_call | solution.py:1311
  133.7 3.8 %all-gather.3.cloned.1.call-done = bf16[8,1536,128]{2,1,0:T(8,128)(2,1)} async-done(((bf16[2,1536,128]{2,1,0:T(8,128)(2,1)}), bf16[8,1536,128]{2,1,0:T(8,128)(2,1)}) %all-gather.3.cloned.1.call-update) | async-done | bytes 3145744 | tf_op jit(solution)/shard_map/all_gather | solution.py:1874
  137.5 75.7 %feed.1 = (f32[256,1536]{1,0:T(8,128)}, bf16[4,2,1536,128]{3,2,1,0:T(8,128)(2,1)}, bf16[8,256,1536]{2,1,0:T(8,128)(2,1)}, bf16[4,1536,128]{2,1,0:T(8,128)(2,1)}) custom-call(bf16[256,1536]{1,0:T(8,128)(2,1)} %get-tuple-element.56.mine, bf16[8,256,1536]{2,1,0:T(8,128)(2,1)} %get-tuple-element.57.go, bf16[4,2,1536,128]{3,2,1,0:T(8,128)(2,1)} %bitcast.39, ...), custom_call_target="tpu_custom_call" | custom-call | flops 1000000 | bytes 100000 | tf_op jit(solution)/shard_map/feed/pallas_call | solution.py:1776
  213.3 0.8 fusion.1.narrow
  214.2 63.9 %attend_back.1 = (bf16[2048,512]{1,0:T(8,128)(2,1)}, bf16[256,1536]{1,0:T(8,128)(2,1)}, bf16[4,48,1536]{2,1,0:T(8,128)(2,1)}, f32[256,1536]{1,0:T(8,128)}, f32[4,1,48]{2,1,0:T(1,128)}) custom-call(bf16[2,2048,128]{2,1,0:T(8,128)(2,1)} %get-tuple-element.44.q.q_in, bf16[2048,128]{1,0:T(8,128)(2,1)} %get-tuple-element.45.k.k_in, ...), custom_call_target="tpu_custom_call" | custom-call | flops 1000000 | bytes 100000 | tf_op jit(solution)/shard_map/attend_back/pallas_call | solution.py:1514
  278.1 53.6 %last.1 = (f32[256,1536]{1,0:T(8,128)}, bf16[3,192,1024]{2,1,0:T(8,128)(2,1)}, bf16[8,48,384]{2,1,0:T(8,128)(2,1)}, bf16[4,48,1536]{2,1,0:T(8,128)(2,1)}, f32[4,1,48]{2,1,0:T(1,128)}) custom-call(bf16[2048,512]{1,0:T(8,128)(2,1)} %get-tuple-element.64.dqkv_in, bf16[1536,512]{1,0:T(8,128)(2,1)} %get-tuple-element.65.w_in, bf16[512,384]{1,0:T(8,128)(2,1)} %fusion.1.narrow, ...), custom_call_target="tpu_custom_call" | custom-call | flops 1000000 | bytes 100000 | tf_op jit(solution)/shard_map/last/pallas_call | solution.py:891
  331.7 1.0 convert_bitcast_fusion
  332.7 1.1 convert_bitcast_fusion.2
  335.6 1.5 bitcast_convert_fusion
  337.1 0.8 convert_reduce_fusion
  337.9 0.5 reduce_sum.49
  338.4 0.5 convert_divide_fusion
  338.9 0.9 copy.42
  339.8 1.1 copy.43
  (47 shorter events, 1.8 us)
Async XLA Ops:
  7.2 4.8 %copy-start.10 = (bf16[48]{0:T(256)(128)(2,1)S(1)}, bf16[48]{0:T(256)(128)(2,1)}, u32[]{:S(2)}) copy-start(bf16[48]{0:T(256)(128)(2,1)} %param.16) | copy-start | bytes 292
  7.2 4.8 %copy-start.14 = (bf16[48]{0:T(256)(128)(2,1)S(1)}, bf16[48]{0:T(256)(128)(2,1)}, u32[]{:S(2)}) copy-start(bf16[48]{0:T(256)(128)(2,1)} %param.21) | copy-start | bytes 292
  7.2 5.4 %copy-start.13 = (s32[1,256]{1,0:T(1,128)S(1)}, s32[1,256]{1,0:T(1,128)}, u32[]{:S(2)}) copy-start(s32[1,256]{1,0:T(1,128)} %param.14) | copy-start | bytes 3076
  7.2 5.4 %copy-start.12 = (s32[1,256]{1,0:T(1,128)S(1)}, s32[1,256]{1,0:T(1,128)}, u32[]{:S(2)}) copy-start(s32[1,256]{1,0:T(1,128)} %param.15) | copy-start | bytes 3076
  7.2 130.3 %all-gather.3.cloned.1.call-start = ((), (), s32[]{:S(2)}) async-start(), calls=%async_computation.2 | async-start | bytes 3932160 | tf_op jit(solution)/shard_map/all_gather | solution.py:1874
  68.4 209.7 %reduce-scatter.2.cloned.1.call-start = ((), (), s32[]{:S(2)}) async-start(), calls=%async_computation.1 | async-start | bytes 3932160 | tf_op jit(solution)/shard_map/reduce_scatter | solution.py:1881
  331.7 2.6 copy-start.7
  332.7 1.9 copy-start.8
  334.1 0.9 copy-start.9
  334.1 1.4 copy-start.1
  334.3 2.7 copy-start.2
  334.7 2.4 copy-start.5
  335.0 2.0 copy-start.6
  335.6 1.5 copy-start.4
  335.6 2.3 copy-start.11
  335.6 3.4 copy-start.3
  337.1 2.8 copy-start
Sparse Core Ops, SparseCore 0:
  68.5 68.9 all-gather.2
  213.4 61.0 reduce-scatter.1

commit v6 on v5

--- a/solution.py
+++ b/solution.py
@@ -3,6 +3,7 @@
 
 import jax
 import jax.numpy as jnp
+import numpy as np
 from jax import lax
 from jax.experimental import pallas as pl
 from jax.experimental.pallas import tpu as pltpu
@@ -403,18 +404,20 @@
         return lax.rem(self.t + self.m - k, self.m)
 
 
-def enter_plane(plane, with_tp):
+def greet(plane, with_tp):
     barrier = pltpu.get_barrier_semaphore()
     for k in range(1, plane.n):
         pl.semaphore_signal(
             barrier, inc=1, device_id=plane.device(plane.seq_ahead(k)), device_id_type=MESH
         )
-    count = plane.n - 1
     if with_tp:
         for k in range(1, plane.m):
             pl.semaphore_signal(barrier, inc=1, device_id=plane.tp_ahead(k), device_id_type=MESH)
-        count += plane.m - 1
-    pl.semaphore_wait(barrier, count)
+
+
+def meet(plane, with_tp):
+    count = plane.n - 1 + (plane.m - 1 if with_tp else 0)
+    pl.semaphore_wait(pltpu.get_barrier_semaphore(), count)
 
 
 def remote(src, dst, send, recv, device):
@@ -736,11 +739,12 @@
 
 
 def last_body(
-    n, m, dqkv_in, w_in, narrow, x_in, dresid_in, gain, norm_t, ffn, downs, wo, vec,
+    n, m, dqkv_in, w_in, x_in, dresid_in, gain, norm_t, ffn, downs, wo, vec,
     input_grad, ffn_out, qkv_out, wo_out, vec_out,
-    dqkv, w, x, dresid, down_here, down_sum, pair, near, far, sr, lr, total, stage, norms, mine, got, summed, sems, st, loc,
+    dqkv, w, x, dresid, down_here, down_sum, narrow, pair, near, far, sr, lr, total, stage, norms, mine, got, summed, sems, st, loc,
 ):
     plane = Plane(n, m)
+    greet(plane, True)
     loads = [
         pltpu.make_async_copy(a, b, loc.at[5 + i])
         for i, (a, b) in enumerate(
@@ -750,7 +754,8 @@
     load = pltpu.make_async_copy(norm_t, norms, loc.at[0])
     for copy in loads + [load]:
         copy.start()
-    enter_plane(plane, True)
+    narrow[...] = lanes_of_columns(narrow.shape, 1)
+    meet(plane, True)
     rows, width = ffn_out.shape[1], ffn.shape[2]
     across = fan(plane, lambda t: wo.at[t], lambda t: wo_out.at[t], st.at[1, 0], st.at[1, 1])
     across += fan(plane, lambda t: vec.at[t], lambda t: vec_out.at[t], st.at[2, 0], st.at[2, 1])
@@ -778,6 +783,8 @@
         sems.at[2, 1],
         loc.at[10],
     )
+    for copy in a:
+        copy.start()
     reduce = Reduce(plane, None, pair, near, far, sr, lr, stage)
     tokens = pair.shape[1]
     for copy in loads[:2]:
@@ -803,11 +810,6 @@
             @pl.when(it == 2 * (3 - kk))
             def _(kk=kk):
                 reduce.swaps[Reduce.THEIRS[kk]].start()
-
-        @pl.when(it == 2)
-        def _():
-            for copy in a:
-                copy.start()
 
         return carry
 
@@ -881,10 +883,10 @@
         copy.wait()
 
 
-def last(n, m, dqkv, w, narrow, x, dresid, gain, norm_t, ffn, downs, wo, vec, ident):
+def last(n, m, dqkv, w, x, dresid, gain, norm_t, ffn, downs, wo, vec, ident):
     width, length = norm_t.shape
     tokens = length // n
-    cols = narrow.shape[1]
+    cols = w.shape[1] // SLOT * HALF
     strip = width // (n * m)
     vmem = pl.BlockSpec(memory_space=pltpu.VMEM)
     hbm = pl.BlockSpec(memory_space=ANY)
@@ -897,7 +899,7 @@
             jax.ShapeDtypeStruct(wo.shape, wo.dtype),
             jax.ShapeDtypeStruct(vec.shape, vec.dtype),
         ),
-        in_specs=[hbm, hbm, vmem, hbm, hbm, vmem] + [hbm] * 5,
+        in_specs=[hbm] * 4 + [vmem] + [hbm] * 5,
         out_specs=[vmem] + [hbm] * 4,
         scratch_shapes=[
             pltpu.VMEM(dqkv.shape, bf16),
@@ -906,6 +908,7 @@
             pltpu.VMEM(dresid.shape, f32),
             pltpu.VMEM(downs.shape, bf16),
             pltpu.VMEM(downs.shape[1:], bf16),
+            pltpu.VMEM((w.shape[1], cols), bf16),
         ]
         + Reduce.scratch(tokens, width)
         + [
@@ -924,11 +927,18 @@
         ),
         cost_estimate=COST,
         name="last",
-    )(dqkv, w, narrow, x, dresid, gain, norm_t, ffn, downs, wo, vec)
+    )(dqkv, w, x, dresid, gain, norm_t, ffn, downs, wo, vec)
 
 
 def column(row):
     return jnp.broadcast_to(row, (8, row.shape[1])).T[:, :1]
+
+
+def lanes_of_columns(shape, of):
+    column = lax.broadcasted_iota(jnp.int32, shape, of).astype(f32)
+    lane = lax.broadcasted_iota(jnp.int32, shape, 1 - of).astype(f32)
+    half = jnp.floor((column + 0.5) * (1.0 / HALF))
+    return jnp.where(lane == column + half * (SLOT - HALF), 1.0, 0.0).astype(bf16)
 
 
 def gain_row(tiles, which, strip):
@@ -951,14 +961,26 @@
 
 
 def entry_body(
-    n, m, heads, strip, x, places, wqkv, gains, wg, wu, wd, wo, widen, inverse,
-    norm_t, q, k, v, cosine, sine, w, gain_rows, docs, ffn, down, wo_z,
+    n, m, heads, strip, x, doc_ids, positions, wq, wk, wv, one, two, wg, wu, wd, wo, inverse,
+    norm_t, q, k, v, cosine, sine, w, gain_one, gain_two, docs, ffn, down, wo_z,
     blocks, norms, turned, places_all, w_all, gains_all, q_here, k_here, v_here, cos_here, sin_here,
-    sx, lx, rem, sz, sn, loc,
+    places, wqkv, gains, widen, sx, lx, rem, sz, sn, loc,
 ):
     plane = Plane(n, m)
-    enter_plane(plane, True)
+    greet(plane, True)
     tokens = x.shape[0]
+    start = 0
+    for weight in (wq, wk, wv):
+        each = weight.shape[1] // n
+        for i in range(n):
+            wqkv[i, :, start : start + each] = weight[:, i * each : (i + 1) * each]
+        start += each
+    gains[...] = jnp.zeros_like(gains)
+    gains[0:1, :strip] = one[...].astype(f32)
+    gains[1:2, :strip] = two[...].astype(f32)
+    places[0:1, :] = doc_ids[...]
+    places[1:2, :] = positions[...]
+    meet(plane, True)
     gather = Gathers(plane, x, lambda i: blocks.at[i], sx, lx, 2)
     first = []
     for i, (src, dst) in enumerate(((gains, gains_all), (wqkv, w_all))):
@@ -990,6 +1012,7 @@
         copy.wait()
     for copy in across[0] + across[1]:
         copy.start()
+    widen[...] = lanes_of_columns(widen.shape, 0)
     moves = []
     width, rows = wg.shape[1] // n, wg.shape[0]
     for j, weight in enumerate((wg, wu, wd)):
@@ -1006,8 +1029,8 @@
     for copy in few + across[0]:
         copy.wait()
     tiles = gains_all[...]
-    for i in range(2):
-        gain_rows[i] = gain_row(tiles, i, strip)
+    gain_one[...] = gain_row(tiles, 0, strip)
+    gain_two[...] = gain_row(tiles, 1, strip)
     gather.wait_own()
 
     def number(it):
@@ -1053,7 +1076,7 @@
 
         value = blocks[b].astype(f32)
         scale = lax.rsqrt(jnp.mean(value * value, axis=1, keepdims=True) + norm_epsilon)
-        low = (value * scale * gain_rows[0]).astype(bf16)
+        low = (value * scale * gain_one[...]).astype(bf16)
         norms[b] = low
         turned[at] = low.T
         store(it, at).start()
@@ -1112,11 +1135,12 @@
         copy.wait()
 
 
-def entry(n, m, heads, x, places, wqkv, gains, wg, wu, wd, wo, widen, inverse, ident):
+def entry(n, m, heads, x, docs, positions, wq, wk, wv, one, two, wg, wu, wd, wo, inverse, ident):
     tokens, width = x.shape
     length = n * tokens
-    strip = wqkv.shape[1]
-    wide = widen.shape[1]
+    strip = wq.shape[0]
+    each = (wq.shape[1] + wk.shape[1] + wv.shape[1]) // n
+    wide = each // HALF * SLOT
     rows, cols = wg.shape
     vmem = pl.BlockSpec(memory_space=pltpu.VMEM)
     hbm = pl.BlockSpec(memory_space=ANY)
@@ -1130,26 +1154,31 @@
             jax.ShapeDtypeStruct((length, LANES), f32),
             jax.ShapeDtypeStruct((length, LANES), f32),
             jax.ShapeDtypeStruct((width, wide), bf16),
-            jax.ShapeDtypeStruct((2, 1, width), f32),
+            jax.ShapeDtypeStruct((1, width), f32),
+            jax.ShapeDtypeStruct((1, width), f32),
             jax.ShapeDtypeStruct((1, length), jnp.int32),
             jax.ShapeDtypeStruct((2, rows * n, cols // n), wg.dtype),
             jax.ShapeDtypeStruct((rows * n, cols // n), wg.dtype),
             jax.ShapeDtypeStruct((m,) + wo.shape, wo.dtype),
         ),
-        in_specs=[hbm] * 8 + [vmem] * 2,
-        out_specs=[hbm] * 6 + [vmem] * 3 + [hbm] * 3,
+        in_specs=[hbm] + [vmem] * 7 + [hbm] * 4 + [vmem],
+        out_specs=[hbm] * 6 + [vmem] * 4 + [hbm] * 3,
         scratch_shapes=[
             pltpu.VMEM((n, tokens, width), bf16),
             pltpu.VMEM((n, tokens, width), bf16),
             pltpu.VMEM((2, width, tokens), bf16),
-            pltpu.VMEM((n,) + places.shape, places.dtype),
-            pltpu.VMEM((n, m) + wqkv.shape[1:], wqkv.dtype),
-            pltpu.VMEM((n, m) + gains.shape, gains.dtype),
+            pltpu.VMEM((n, 2, tokens), jnp.int32),
+            pltpu.VMEM((n, m, strip, each), bf16),
+            pltpu.VMEM((n, m, 8, LANES), f32),
             pltpu.VMEM((heads, length, LANES), bf16),
             pltpu.VMEM((length, LANES), bf16),
             pltpu.VMEM((length, LANES), bf16),
             pltpu.VMEM((length, LANES), f32),
             pltpu.VMEM((length, LANES), f32),
+            pltpu.VMEM((2, tokens), jnp.int32),
+            pltpu.VMEM((n, strip, each), bf16),
+            pltpu.VMEM((8, LANES), f32),
+            pltpu.VMEM((each, wide), bf16),
             *Gathers.scratch(2),
             pltpu.SemaphoreType.DMA((6, 2, n - 1)),
             pltpu.SemaphoreType.DMA((3, 2, m - 1)),
@@ -1161,7 +1190,7 @@
         ),
         cost_estimate=COST,
         name="entry",
-    )(x, places, wqkv, gains, wg, wu, wd, wo, widen, inverse)
+    )(x, docs, positions, wq, wk, wv, one, two, wg, wu, wd, wo, inverse)
 
 
 BLOCK = 512
@@ -1194,21 +1223,26 @@
 
 
 def attend_body(
-    n, m, factor, q, k, v, docs, wo, go, x, gain,
-    o_out, lse, start, low_out, go_all, resid, norm,
+    n, m, factor, q, k, v, docs, wo, go, x, gain, ffn,
+    o_out, lse, start, low_out, go_all, resid, norm, ffn_all,
     o, low, vt, top, total, acc, wo_here, go_here,
-    pair, near, far, sr, lr, stage, sg, lg, loc,
+    pair, near, far, sr, lr, stage, sg, lg, sz, loc,
 ):
     plane = Plane(n, m)
     rows = x.shape[0]
     heads = q.shape[0]
-    enter_plane(plane, False)
+    greet(plane, True)
     gather = Gathers(plane, go, lambda i: go_here.at[i], sg, lg, 2)
     reduce = Reduce(plane, None, pair, near, far, sr, None, stage)
-    gather.start()
     spread_rows(wo, wo_here)
     vt[...] = v[...].T
     start[...] = begins(docs[...])
+    meet(plane, True)
+    gather.start()
+    chain = Chain(plane, ffn, lambda t: ffn_all.at[t], sz)
+    chain.start()
+    own_ffn = pltpu.make_async_copy(ffn, ffn_all.at[plane.t], loc.at[3])
+    own_ffn.start()
 
     def chips(step, carry):
         kk = 3 - step
@@ -1284,9 +1318,12 @@
     for copy in outs:
         copy.start()
     gather.relay_near()
+    chain.step(1)
     reduce.ready()
     reduce.first(resid, x)
     reduce.send_fro()
+    for hop in range(2, m - 1):
+        chain.step(hop)
     gather.relay_far()
     reduce.finish(resid)
 
@@ -1299,11 +1336,14 @@
     gather.finish()
     outs.append(pltpu.make_async_copy(go_here, go_all, loc.at[2]))
     outs[-1].start()
+    chain.step(m - 1)
+    chain.wait_sends()
+    own_ffn.wait()
     for copy in outs:
         copy.wait()
 
 
-def attend(n, m, factor, q, k, v, docs, wo, go, x, gain, ident):
+def attend(n, m, factor, q, k, v, docs, wo, go, x, gain, ffn, ident):
     heads, length, _ = q.shape
     rows, width = x.shape
     hbm = pl.BlockSpec(memory_space=ANY)
@@ -1318,9 +1358,10 @@
             jax.ShapeDtypeStruct((n,) + go.shape, go.dtype),
             jax.ShapeDtypeStruct((rows, width), f32),
             jax.ShapeDtypeStruct((rows, width), bf16),
+            jax.ShapeDtypeStruct((m,) + ffn.shape, bf16),
         ),
-        in_specs=[vmem] * 5 + [hbm] + [vmem] * 2,
-        out_specs=[hbm, vmem, vmem, hbm, hbm, vmem, vmem],
+        in_specs=[vmem] * 5 + [hbm] + [vmem] * 2 + [hbm],
+        out_specs=[hbm, vmem, vmem, hbm, hbm, vmem, vmem, hbm],
         scratch_shapes=[
             pltpu.VMEM((heads, length, LANES), f32),
             pltpu.VMEM((length, heads * LANES), bf16),
@@ -1334,21 +1375,21 @@
         + Reduce.scratch(rows, width)
         + [pltpu.VMEM((4, rows, width), bf16)]
         + Gathers.scratch(2)
-        + [pltpu.SemaphoreType.DMA((3,))],
+        + [pltpu.SemaphoreType.DMA((4, m)), pltpu.SemaphoreType.DMA((4,))],
         compiler_params=pltpu.CompilerParams(
             collective_id=ident, has_side_effects=True, vmem_limit_bytes=VMEM_LIMIT
         ),
         cost_estimate=COST,
         name="attend",
-    )(q, k, v, docs, wo, go, x, gain)
+    )(q, k, v, docs, wo, go, x, gain, ffn)
 
 
 def attend_back_body(
     n, m, factor, scale, q_in, k_in, v_in, o_in, lse, begin, cos_in, sin_in, low_in,
-    mixed, wo, dnorm, resid, grad, gain,
+    hid_in, down_in, wo, dnorm, resid, grad, gain,
     out, layer, terms, dresid, gain_out,
     q, k, v, o, cosine, sine, low, kt, dqt, dk, dv, delta, go, every, dbranch, wo_here,
-    pair, near, far, sr, lr, held, gain_sum, gain_cut, gain_got, sg, lg, sv, loc,
+    hid_low, w_down, stage, pair, near, far, sr, lr, held, gain_sum, gain_cut, gain_got, sg, lg, sv, loc,
 ):
     plane = Plane(n, m)
     heads, length, _ = q.shape
@@ -1365,9 +1406,14 @@
     ]
     for copy in loads:
         copy.start()
-    enter_plane(plane, False)
-    one = Reduce(plane, lambda i: mixed.at[i], pair, near, far, sr, lr)
-    one.start(3, 1)
+    greet(plane, False)
+    moves = [
+        pltpu.make_async_copy(hid_in, hid_low, loc.at[8]),
+        pltpu.make_async_copy(down_in, w_down, loc.at[9]),
+    ]
+    for copy in moves:
+        copy.start()
+    one = Reduce(plane, None, pair, near, far, sr, None, stage)
     gather = Gathers(plane, dbranch, lambda i: every.at[i], sg, lg, 2)
     gain_copies = exchange(
         plane, lambda i: gain_cut.at[i], lambda i: gain_got.at[i], sv.at[0], sv.at[1], loc.at[7]
@@ -1388,14 +1434,43 @@
         gain_sum[...] += up * turned
 
     in_tiles(rows, into_branch)
+    meet(plane, False)
     gather.start()
-    one.start(2, 0)
     total_gain = jnp.sum(gain_sum[...], axis=0, keepdims=True)
     for i in range(n):
         gain_cut[i] = total_gain[:, i * (width // n) : (i + 1) * (width // n)]
     for copy in gain_copies:
         copy.start()
     spread_rows(wo, wo_here)
+    for copy in moves:
+        copy.wait()
+
+    def mix(it, carry):
+        kk = 3 - it // 2
+        other = 1 - lax.rem(it, 2)
+        b = plane.number(kk, other)
+        at = pl.ds(pl.multiple_of(b * rows, rows), rows)
+        part = lax.dot_general(
+            hid_low[at, :], w_down[...], NT, preferred_element_type=f32
+        ).astype(bf16)
+
+        @pl.when(other == 0)
+        def _():
+            pair[kk] = part
+
+        @pl.when(other == 1)
+        def _():
+            stage[kk] = part
+
+        for which in range(4):
+
+            @pl.when(it == 2 * (3 - which))
+            def _(which=which):
+                one.swaps[Reduce.THEIRS[which]].start()
+
+        return carry
+
+    lax.fori_loop(0, n, mix, 0)
     for copy in loads:
         copy.wait()
     kt[...] = k[...].T
@@ -1504,7 +1579,7 @@
 
 def attend_back(
     n, m, factor, scale, q, k, v, o, lse, begin, cosine, sine, low,
-    mixed, wo, dnorm, resid, grad, gain, ident,
+    hid_low, w_down, wo, dnorm, resid, grad, gain, ident,
 ):
     heads, length, _ = q.shape
     rows, width = dnorm.shape
@@ -1520,7 +1595,7 @@
             jax.ShapeDtypeStruct((rows, width), f32),
             jax.ShapeDtypeStruct((m, 1, strip), f32),
         ),
-        in_specs=[hbm] * 4 + [vmem] * 2 + [hbm] * 4 + [vmem] * 5,
+        in_specs=[hbm] * 4 + [vmem] * 2 + [hbm] * 5 + [vmem] * 5,
         out_specs=[vmem] * 5,
         scratch_shapes=[
             pltpu.VMEM(q.shape, bf16),
@@ -1539,6 +1614,9 @@
             pltpu.VMEM((n, rows, width), bf16),
             pltpu.VMEM((rows, width), bf16),
             pltpu.VMEM((heads * LANES, width), bf16),
+            pltpu.VMEM(hid_low.shape, bf16),
+            pltpu.VMEM(w_down.shape, bf16),
+            pltpu.VMEM((4, rows, width), bf16),
         ]
         + Reduce.scratch(rows, width)
         + [
@@ -1548,45 +1626,49 @@
             pltpu.VMEM((n, 1, width // n), f32),
         ]
         + Gathers.scratch(2)
-        + [pltpu.SemaphoreType.DMA((2, n - 1)), pltpu.SemaphoreType.DMA((8,))],
+        + [pltpu.SemaphoreType.DMA((2, n - 1)), pltpu.SemaphoreType.DMA((10,))],
         compiler_params=pltpu.CompilerParams(
             collective_id=ident, has_side_effects=True, vmem_limit_bytes=VMEM_LIMIT
         ),
         cost_estimate=COST,
         name="attend_back",
-    )(q, k, v, o, lse, begin, cosine, sine, low, mixed, wo, dnorm, resid, grad, gain)
+    )(q, k, v, o, lse, begin, cosine, sine, low, hid_low, w_down, wo, dnorm, resid, grad, gain)
 
 
 def feed_body(
-    n, m, mine, go, w_in, down, dnorm, grads, mixed, down_parts,
-    rows, rows_t, go_t, go_two, w, gates, h, mix_two, down_held, pair, near, far, stage,
-    sg, lg, sr, loc, sw, so, sm, sd, sz, sf,
+    n, m, mine, go, w_in, down, dnorm, grads, hid_out, down_out, down_parts,
+    rows, rows_t, go_t, go_two, w, w_down, gates, h, hid_low, down_held, down_sum,
+    pair, near, far, stage,
+    sg, lg, sr, loc, sw, so, sd, sz, sf,
 ):
     plane = Plane(n, m)
-    tokens = rows.shape[1]
+    tokens, width = rows.shape[1:]
     hid = down.shape[1]
-    enter_plane(plane, True)
+    half = m * hid
+    greet(plane, True)
     gather = Gathers(plane, mine, lambda i: rows.at[i], sg, lg, 2)
     reduce = Reduce(plane, None, pair, near, far, sr, None, stage)
-    gather.start()
-
-    def down_at(t):
-        return w.at[2, :, pl.ds(pl.multiple_of(t * hid, hid), hid)]
-
-    chain = Chain(plane, down, down_at, sz)
-    chain.start()
-    own_down = pltpu.make_async_copy(down, down_at(plane.t), loc.at[0])
-    own_down.start()
+
+    def columns(ref, j, t):
+        return ref.at[:, j * half + t * hid : j * half + (t + 1) * hid]
+
     weights = [
-        pltpu.make_async_copy(
-            w_in.at[t, j], w.at[j, :, t * hid : (t + 1) * hid], sw.at[j, t]
-        )
+        pltpu.make_async_copy(w_in.at[t, j], columns(w, j, t), sw.at[j, t])
         for j in range(2)
         for t in range(m)
     ]
     for copy in weights:
         copy.start()
-
+    meet(plane, True)
+    gather.start()
+
+    def down_at(ref, t):
+        return ref.at[:, pl.ds(pl.multiple_of(t * hid, hid), hid)]
+
+    chain = Chain(plane, down, lambda t: down_at(w_down, t), sz)
+    chain.start()
+    own_down = pltpu.make_async_copy(down, down_at(w_down, plane.t), loc.at[0])
+    own_down.start()
     gather.wait_own()
     for copy in weights:
         copy.wait()
@@ -1594,6 +1676,31 @@
     def span(b):
         return pl.ds(pl.multiple_of(b * tokens, tokens), tokens)
 
+    def down_grad(kk, keep):
+        chip = plane.number(kk, 0) // 2
+        at = pl.ds(pl.multiple_of(chip * 2 * tokens, 2 * tokens), 2 * tokens)
+
+        def part(i, carry):
+            line = pl.ds(pl.multiple_of(i * 256, 256), 256)
+            value = jnp.dot(go_t[line, at], hid_low[at, :], preferred_element_type=f32)
+            keep(line, value)
+            return carry
+
+        lax.fori_loop(0, width // 256, part, 0)
+
+    def set_down(line, value):
+        down_sum[line, :] = value
+
+    def add_down(line, value):
+        down_sum[line, :] += value
+
+    def hold_down(line, value):
+        down_held[line, :] = (down_sum[line, :] + value).astype(bf16)
+
+    def early_go(it, slot):
+        b = plane.number(it // 2, lax.rem(it, 2))
+        return pltpu.make_async_copy(go.at[b], go_two.at[slot], so.at[slot])
+
     def forward(it, carry):
         b = plane.number(it // 2, lax.rem(it, 2))
 
@@ -1603,6 +1710,7 @@
 
         @pl.when(it == 2)
         def _():
+            down_grad(0, set_down)
             chain.step(1)
             gather.relay_near()
 
@@ -1620,6 +1728,8 @@
 
         @pl.when(it == 6)
         def _():
+            down_grad(1, add_down)
+            down_grad(2, add_down)
             gather.relay_far()
 
         @pl.when(it == 7)
@@ -1633,20 +1743,15 @@
             early_go(it + 1, 1 - slot).start()
 
         row = rows[b]
-        gate = jnp.dot(row, w[0], preferred_element_type=f32)
-        up = jnp.dot(row, w[1], preferred_element_type=f32)
-        gates[0, span(b), :] = gate
-        gates[1, span(b), :] = up
-        h[2, span(b), :] = (gate * jax.nn.sigmoid(gate) * up).astype(bf16)
+        both = jnp.dot(row, w[...], preferred_element_type=f32)
+        gates[span(b), :] = both
+        gate, up = both[:, :half], both[:, half:]
+        hid_low[span(b), :] = (gate * jax.nn.sigmoid(gate) * up).astype(bf16)
         rows_t[:, span(b)] = row.T
         early_go(it, slot).wait()
         go_t[:, span(b)] = go_two[slot].T
         return carry
 
-    def early_go(it, slot):
-        b = plane.number(it // 2, lax.rem(it, 2))
-        return pltpu.make_async_copy(go.at[b], go_two.at[slot], so.at[slot])
-
     early_go(0, 0).start()
     lax.fori_loop(0, n, forward, 0)
 
@@ -1656,46 +1761,22 @@
     def load_go(it, slot):
         return pltpu.make_async_copy(go.at[number(it)], go_two.at[slot], so.at[slot])
 
-    def store_mix(it, slot):
-        return pltpu.make_async_copy(mix_two.at[slot], mixed.at[number(it)], sm.at[slot])
-
-    width = rows.shape[2]
-
-    def weight_grad(j, left, held):
-        def part(i, carry):
-            at = pl.ds(pl.multiple_of(i * 256, 256), 256)
-            value = jnp.dot(left[at, :], h[j], preferred_element_type=f32)
-            held[at, :] = value.astype(bf16)
-            return carry
-
-        lax.fori_loop(0, width // 256, part, 0)
-        if j == 2:
-            return []
-        outs = [
-            pltpu.make_async_copy(
-                held.at[:, t * hid : (t + 1) * hid], grads.at[t, j], sd.at[j, t]
-            )
-            for t in range(m)
-        ]
-        for copy in outs:
-            copy.start()
-        return outs
-
     load_go(0, 0).start()
-    outs = weight_grad(2, go_t, down_held)
-
-    def down_part(t):
-        return down_held.at[:, pl.ds(pl.multiple_of(t * hid, hid), hid)]
-
-    outs += fan(plane, down_part, lambda t: down_parts.at[t], sf.at[0], sf.at[1])
+    down_grad(3, hold_down)
+    outs = fan(
+        plane, lambda t: down_at(down_held, t), lambda t: down_parts.at[t], sf.at[0], sf.at[1]
+    )
     outs.append(
-        pltpu.make_async_copy(down_part(plane.t), down_parts.at[plane.t], loc.at[1])
-    )
+        pltpu.make_async_copy(down_at(down_held, plane.t), down_parts.at[plane.t], loc.at[1])
+    )
+    outs.append(pltpu.make_async_copy(hid_low, hid_out, loc.at[2]))
     for copy in outs:
         copy.start()
     for hop in range(3, m):
         chain.step(hop)
     own_down.wait()
+    outs.append(pltpu.make_async_copy(w_down, down_out, loc.at[3]))
+    outs[-1].start()
 
     def backward(it, carry):
         slot = lax.rem(it, 2)
@@ -1712,28 +1793,26 @@
             reduce.join(1)
             reduce.out[1].start()
 
+        @pl.when(it == 7)
+        def _():
+            reduce.ready()
+            reduce.send_fro()
+
         @pl.when(it < n - 1)
         def _():
             load_go(it + 1, 1 - slot).start()
 
         load_go(it, slot).wait()
 
-        @pl.when(it >= 2)
-        def _():
-            store_mix(it - 2, slot).wait()
-
-        gate = gates[0, span(b), :]
-        up = gates[1, span(b), :]
-        grad = go_two[slot]
-        dhidden = jnp.dot(grad, w[2], preferred_element_type=f32)
+        gate = gates[span(b), :half]
+        up = gates[span(b), half:]
+        dhidden = jnp.dot(go_two[slot], w_down[...], preferred_element_type=f32)
         sig = jax.nn.sigmoid(gate)
-        hidden = h[2, span(b), :]
         dgate = (dhidden * up * sig * (1.0 + gate * (1.0 - sig))).astype(bf16)
         dup = (dhidden * gate * sig).astype(bf16)
-        h[0, span(b), :] = dgate
-        h[1, span(b), :] = dup
-        part = lax.dot_general(dgate, w[0], NT, preferred_element_type=f32)
-        part = part + lax.dot_general(dup, w[1], NT, preferred_element_type=f32)
+        h[span(b), :half] = dgate
+        h[span(b), half:] = dup
+        part = lax.dot_general(h[span(b), :], w[...], NT, preferred_element_type=f32)
         part = part.astype(bf16)
 
         @pl.when(lax.rem(it, 2) == 1)
@@ -1750,22 +1829,29 @@
             def _(kk=kk):
                 reduce.swaps[Reduce.THEIRS[kk]].start()
 
-        mix_two[slot] = lax.dot_general(hidden, w[2], NT, preferred_element_type=f32).astype(bf16)
-        store_mix(it, slot).start()
         return carry
 
     lax.fori_loop(0, n, backward, 0)
-    store_mix(n - 2, 0).wait()
-    store_mix(n - 1, 1).wait()
-    reduce.ready()
-    reduce.send_fro()
-    outs += weight_grad(0, rows_t, w.at[0])
+
+    def weight_grad(i, carry):
+        at = pl.ds(pl.multiple_of(i * 256, 256), 256)
+        value = jnp.dot(rows_t[at, :], h[...], preferred_element_type=f32)
+        w[at, :] = value.astype(bf16)
+        return carry
+
+    lax.fori_loop(0, width // 256, weight_grad, 0)
+    ends = [
+        pltpu.make_async_copy(columns(w, j, t), grads.at[t, j], sd.at[j, t])
+        for j in range(2)
+        for t in range(m)
+    ]
+    for copy in ends:
+        copy.start()
     reduce.first(dnorm)
-    outs += weight_grad(1, rows_t, w.at[1])
     gather.wait_sends()
     chain.wait_sends()
     reduce.finish(dnorm)
-    for copy in outs:
+    for copy in outs + ends:
         copy.wait()
 
 
@@ -1773,42 +1859,41 @@
     tokens, width = norm.shape
     hid = down.shape[1]
     length = n * tokens
+    half = m * hid
+    hbm = pl.BlockSpec(memory_space=ANY)
     return pl.pallas_call(
         functools.partial(feed_body, n, m),
         out_shape=(
             jax.ShapeDtypeStruct((tokens, width), f32),
             jax.ShapeDtypeStruct((m, 2, width, hid), bf16),
-            jax.ShapeDtypeStruct((n, tokens, width), bf16),
+            jax.ShapeDtypeStruct((length, half), bf16),
+            jax.ShapeDtypeStruct((width, half), bf16),
             jax.ShapeDtypeStruct((m, width, hid), bf16),
         ),
-        in_specs=[pl.BlockSpec(memory_space=ANY)] * 4,
-        out_specs=[
-            pl.BlockSpec(memory_space=pltpu.VMEM),
-            pl.BlockSpec(memory_space=ANY),
-            pl.BlockSpec(memory_space=ANY),
-            pl.BlockSpec(memory_space=ANY),
-        ],
+        in_specs=[hbm] * 4,
+        out_specs=[pl.BlockSpec(memory_space=pltpu.VMEM)] + [hbm] * 4,
         scratch_shapes=[
             pltpu.VMEM((n, tokens, width), bf16),
             pltpu.VMEM((width, length), bf16),
             pltpu.VMEM((width, length), bf16),
             pltpu.VMEM((2, tokens, width), bf16),
-            pltpu.VMEM((3, width, m * hid), bf16),
-            pltpu.VMEM((2, length, m * hid), f32),
-            pltpu.VMEM((3, length, m * hid), bf16),
-            pltpu.VMEM((2, tokens, width), bf16),
-            pltpu.VMEM((width, m * hid), bf16),
+            pltpu.VMEM((width, 2 * half), bf16),
+            pltpu.VMEM((width, half), bf16),
+            pltpu.VMEM((length, 2 * half), f32),
+            pltpu.VMEM((length, 2 * half), bf16),
+            pltpu.VMEM((length, half), bf16),
+            pltpu.VMEM((width, half), bf16),
+            pltpu.VMEM((width, half), f32),
         ]
         + [pltpu.VMEM((slots, tokens, width), bf16) for slots in Reduce.SLOTS]
         + [
             pltpu.VMEM((4, tokens, width), bf16),
             *Gathers.scratch(2),
             pltpu.SemaphoreType.DMA((4, 4)),
+            pltpu.SemaphoreType.DMA((4,)),
+            pltpu.SemaphoreType.DMA((2, m)),
             pltpu.SemaphoreType.DMA((2,)),
             pltpu.SemaphoreType.DMA((2, m)),
-            pltpu.SemaphoreType.DMA((2,)),
-            pltpu.SemaphoreType.DMA((2,)),
-            pltpu.SemaphoreType.DMA((3, m)),
             pltpu.SemaphoreType.DMA((4, m)),
             pltpu.SemaphoreType.DMA((2, m - 1)),
         ],
@@ -1818,11 +1903,6 @@
         cost_estimate=COST,
         name="feed",
     )(norm, go, w_in, down)
-
-
-def split_heads(w, groups):
-    rows = w.shape[0]
-    return w.reshape(rows, groups, -1).transpose(1, 0, 2)
 
 
 def fast_layer(n, m):
@@ -1842,49 +1922,36 @@
         out_grad,
     ):
         x = layer_input[0]
-        rows, width = x.shape
-        length = rows * n
+        width = x.shape[1]
         heads = QUERY_HEADS // n
         scale = 1.0 / math.sqrt(HEAD_SIZE)
         factor = scale * LOG2E
         strip = query_weight.shape[0]
-        hid = gate_weight.shape[1] // n
-
-        packed = jnp.concatenate(
-            [split_heads(w, n) for w in (query_weight, key_weight, value_weight)], axis=2
+
+        lane = np.arange(LANES) % SLOT
+        inverse = np.where(lane < HALF, rope_base ** (-(lane * 2.0 / HEAD_SIZE)), 0.0)
+        (
+            norm_t, q, k, v, cosine, sine, wqkv, gain_one, gain_two, docs,
+            ffn_mine, down_mine, output_rows,
+        ) = entry(
+            n, m, heads, x, doc_ids, positions, query_weight, key_weight, value_weight,
+            first_gain.reshape(1, strip), second_gain.reshape(1, strip),
+            gate_weight, up_weight, down_weight, output_weight,
+            jnp.asarray(inverse[None], f32), 0,
         )
-        cols = packed.shape[2]
-        gains = jnp.pad(
-            jnp.stack([first_gain, second_gain]).astype(f32), ((0, 6), (0, LANES - strip))
+        o, lse, begin, low, grad_all, resid, norm_two, ffn_all = attend(
+            n, m, factor, q, k, v, docs, output_rows, out_grad[0], x, gain_two, ffn_mine, 9
         )
-        places = jnp.concatenate([doc_ids, positions], axis=0)
-        lane = jnp.arange(LANES) % SLOT
-        inverse = jnp.where(
-            lane < HALF, rope_base ** (-(lane.astype(f32) * 2.0 / HEAD_SIZE)), 0.0
-        )[None]
-        from_col = jnp.arange(cols)
-        to_lane = from_col // HALF * SLOT + from_col % HALF
-        widen = (to_lane[:, None] == jnp.arange(cols // HALF * SLOT)[None, :]).astype(bf16)
-
-        norm_t, q, k, v, cosine, sine, wqkv, gain_rows, docs, ffn_mine, down_mine, output_rows = entry(
-            n, m, heads, x, places, packed, gains,
-            gate_weight, up_weight, down_weight, output_weight, widen, inverse, 0,
-        )
-        gain_one, gain_two = gain_rows[0], gain_rows[1]
-        ffn_all = lax.all_gather(ffn_mine, "tp", axis=0, tiled=False)
-        o, lse, begin, low, grad_all, resid, norm_two = attend(
-            n, m, factor, q, k, v, docs, output_rows, out_grad[0], x, gain_two, 9
-        )
-        dnorm_two, ffn_terms, mixed, down_parts = feed(
+        dnorm_two, ffn_terms, hid_low, w_down, down_parts = feed(
             n, m, norm_two, grad_all, ffn_all, down_mine, 2
         )
         ffn_sum = lax.psum_scatter(ffn_terms, "tp", scatter_dimension=0, tiled=False)
         dqkv, layer_output, output_terms, dresid, gain_part = attend_back(
-            n, m, factor, scale, q, k, v, o, lse, begin, cosine, sine, low, mixed,
+            n, m, factor, scale, q, k, v, o, lse, begin, cosine, sine, low, hid_low, w_down,
             output_rows, dnorm_two, resid, out_grad[0], gain_two, 3,
         )
         input_grad, ffn_out, qkv_out, output_parts, gain_sums = last(
-            n, m, dqkv, wqkv, widen.T, x, dresid, gain_one, norm_t, ffn_sum, down_parts,
+            n, m, dqkv, wqkv, x, dresid, gain_one, norm_t, ffn_sum, down_parts,
             output_terms, gain_part, 6,
         )
         output_grad = jnp.sum(output_parts.astype(f32), axis=0)
@@ -1898,7 +1965,7 @@
 
         query_grad = columns(0, split)
         key_grad = columns(split, split + kv)
-        value_grad = columns(split + kv, cols)
+        value_grad = columns(split + kv, split + 2 * kv)
 
         one = (
             jnp.sum(query_weight.astype(f32) * query_grad, axis=1)

time: 348 us -> 333 us (0.957)
  local copies, waits for them, and re-layouts: 7.8 us -> 3.13 us
  other arithmetic: 10.2 us -> 5.77 us
    pallas_call x1, Pallas kernels: 64 us -> 69.9 us  [attend(): pl.pallas_call(functools.partial(attend_body, n, m, factor), out_shape=(j...]
    pallas_call x1, Pallas kernels: 75.7 us -> 71.8 us  [feed(): pl.pallas_call(functools.partial(feed_body, n, m), out_shape=(jax.ShapeDt...]
    all_gather x1 -> x0, waiting for transfers between devices: 3.78 us -> none  [on_plane(): ffn_all = lax.all_gather(ffn_mine, 'tp', axis=0, tiled=False)]
  transfers between devices with their start and end apart: 2 -> 1, of which waited for: 1 -> 1; matrix products, arithmetic and copies ran while one was open for 1% -> 0% of each run, Pallas kernels for 37% -> 19%
where the time goes in v6:
time: 333 us
  Pallas kernels  309 us (93%)
  between operations  14.2 us (4%)
  other arithmetic  5.77 us (2%)
    pallas_call x1, Pallas kernels, feed(): pl.pallas_call(functools.partial(feed_body, n, m), out_shape=(jax.ShapeDt...  71.8 us
    pallas_call x1, Pallas kernels, attend(): pl.pallas_call(functools.partial(attend_body, n, m, factor), out_shape=(j...  69.9 us
    pallas_call x1, Pallas kernels, attend_back(): pl.pallas_call(functools.partial(attend_back_body, n, m, factor, scale),...  62.5 us
    pallas_call x1, Pallas kernels, entry(): pl.pallas_call(functools.partial(entry_body, n, m, heads, strip), out_sha...  53.7 us
    pallas_call x1, Pallas kernels, last(): pl.pallas_call(functools.partial(last_body, n, m), out_shape=(jax.ShapeDt...  51.5 us
  transfers between devices with their start and end apart: 1, of which 1 were waited for; matrix products, arithmetic and copies ran while one was open for 0% of the time, Pallas kernels for 19%

profile of v6, /device:TPU:0, one launch (start us, length us, event | category | flops | bytes accessed | tf_op | source)
XLA Modules:
  0.0 333.1 jit_solution(4181240018375572912)
XLA Ops:
  7.2 0.0 reduce-scatter.2.cloned.1.call-start
  7.2 53.7 %entry.1 = (bf16[1536,2048]{1,0:T(8,128)(2,1)}, bf16[2,2048,128]{2,1,0:T(8,128)(2,1)}, bf16[2048,128]{1,0:T(8,128)(2,1)}, bf16[2048,128]{1,0:T(8,128)(2,1)}, f32...) custom-call(bf16[256,1536]{1,0:T(8,128)(2,1)} %bitcast.22, ...), custom_call_target="tpu_custom_call" | custom-call | flops 1000000 | bytes 100000 | tf_op jit(solution)/shard_map/entry/pallas_call | solution.py:1147
  61.0 69.9 %attend.1 = (f32[2,2048,128]{2,1,0:T(8,128)}, f32[2,1,2048]{2,1,0:T(1,128)}, s32[1,2048]{1,0:T(1,128)}, bf16[2048,256]{1,0:T(8,128)(2,1)}, bf16[8,256,1536]{2,1,...) custom-call(bf16[2,2048,128]{2,1,0:T(8,128)(2,1)} %get-tuple-element.47.q.q_in, ...), custom_call_target="tpu_custom_call" | custom-call | flops 1000000 | bytes 100000 | tf_op jit(solution)/shard_map/attend/pallas_call | solution.py:1351
  130.9 71.8 %feed.1 = (f32[256,1536]{1,0:T(8,128)}, bf16[4,2,1536,128]{3,2,1,0:T(8,128)(2,1)}, bf16[2048,512]{1,0:T(8,128)(2,1)}, bf16[1536,512]{1,0:T(8,128)(2,1)}, bf16[4,1536,128]{2,1,0:T(8,128)(2,1)}) custom-call(bf16[256,1536]{1,0:T(8,128)(2,1)} %get-tuple-element.60.mine, bf16[8,256,1536]{2,1,0:T(8,128)(2,1)} %get-tuple-element.61.go, ...), custom_call_target="tpu_custom_call" | custom-call | flops 1000000 | bytes 100000 | tf_op jit(solution)/shard_map/feed/pallas_call | solution.py:1864
  202.8 62.5 %attend_back.1 = (bf16[2048,512]{1,0:T(8,128)(2,1)}, bf16[256,1536]{1,0:T(8,128)(2,1)}, bf16[4,48,1536]{2,1,0:T(8,128)(2,1)}, f32[256,1536]{1,0:T(8,128)}, f32[4,1,48]{2,1,0:T(1,128)}) custom-call(bf16[2,2048,128]{2,1,0:T(8,128)(2,1)} %get-tuple-element.47.q.q_in, bf16[2048,128]{1,0:T(8,128)(2,1)} %get-tuple-element.48.k.k_in, ...), custom_call_target="tpu_custom_call" | custom-call | flops 1000000 | bytes 100000 | tf_op jit(solution)/shard_map/attend_back/pallas_call | solution.py:1589
  265.3 0.4 reduce-scatter.2.cloned.1.call-done
  265.7 51.5 %last.1 = (f32[256,1536]{1,0:T(8,128)}, bf16[3,192,1024]{2,1,0:T(8,128)(2,1)}, bf16[8,48,384]{2,1,0:T(8,128)(2,1)}, bf16[4,48,1536]{2,1,0:T(8,128)(2,1)}, f32[4,1,48]{2,1,0:T(1,128)}) custom-call(bf16[2048,512]{1,0:T(8,128)(2,1)} %get-tuple-element.69.dqkv_in, bf16[1536,512]{1,0:T(8,128)(2,1)} %get-tuple-element.70.w_in, bf16[256,1536]{1,0:T(8,128)(2,1)} %bitcast.24, ...), custom_call_target="tpu_custom_call" | custom-call | flops 1000000 | bytes 100000 | tf_op jit(solution)/shard_map/last/pallas_call | solution.py:893
  317.2 1.0 convert_bitcast_fusion
  318.2 1.1 convert_bitcast_fusion.2
  319.4 0.8 convert_reduce_fusion
  320.2 0.2 copy.25
  320.4 0.1 reshape.45
  320.6 0.1 multiply_reduce_fusion
  320.7 0.1 copy.26
  320.8 0.1 reshape.46
  320.9 0.1 copy.27
  321.0 0.1 reshape.47
  321.1 0.3 copy-done.1
  321.5 1.5 bitcast_convert_fusion
  323.0 0.5 reduce_sum.49
  323.5 0.1 multiply_reduce_fusion.1
  323.7 0.5 convert_divide_fusion
  324.2 0.9 copy.30
  325.1 1.1 copy.31
  (24 shorter events, 0.1 us)
Async XLA Ops:
  7.2 258.6 %reduce-scatter.2.cloned.1.call-start = ((), (), s32[]{:S(2)}) async-start(), calls=%async_computation.1 | async-start | bytes 3932160 | tf_op jit(solution)/shard_map/reduce_scatter | solution.py:1948
  317.2 2.2 copy-start.5
  318.2 2.4 copy-start.4
  320.2 1.3 copy-start.1
  320.6 2.4 copy-start.2
  320.9 2.6 copy-start.6
  321.1 2.4 copy-start.7
  321.5 1.5 copy-start.10
  321.5 2.0 copy-start.8
  321.5 2.0 copy-start.9
  321.5 2.2 copy-start.11
  321.5 2.7 copy-start.3
  323.0 2.1 copy-start
Sparse Core Ops, SparseCore 0:
  202.9 62.8 reduce-scatter.1

commit v7 on v6

--- a/solution.py
+++ b/solution.py
@@ -604,6 +604,116 @@
                     self.copy(way, hop, self.plane.t + way).wait_send()
 
 
+class Scatter:
+    def __init__(self, plane, parts, total, add, own, got, sems, loc):
+        t = plane.t
+        self.plane, self.total = plane, total
+        self.add, self.own, self.got, self.loc = add, own, got, loc
+        self.inner = (t == 1) | (t == 2)
+        self.outer = (t == 0) | (t == 3)
+        up = t // 2
+        self.near = t + 1 - 2 * lax.rem(t, 2)
+        self.far_outer = 3 - 3 * up
+        self.far_inner = 2 - up
+        self.parts, self.sems = parts, sems
+
+    def copy(self, i, j, src, dst, to):
+        return remote(
+            src, dst, self.sems.at[0, i, j], self.sems.at[1, i, j], (self.plane.s, to)
+        )
+
+    def first(self, i, j):
+        chunk = (self.far_outer, self.far_inner, self.near)[i]
+        dst = self.got.at[0, j] if i == 2 else self.add.at[i, j]
+        return self.copy(i, j, self.parts.at[chunk, j], dst, self.near)
+
+    def back(self, j):
+        return self.copy(2, j, self.parts.at[self.near, j], self.got.at[0, j], self.near)
+
+    def sent(self, i, j):
+        to = self.far_inner if i else self.far_outer
+        return remote(
+            self.add.at[i, j],
+            self.got.at[1, j],
+            self.sems.at[0, 3 + i, j],
+            self.sems.at[1, 3, j],
+            (self.plane.s, to),
+        )
+
+    def load(self, i, j):
+        chunk = (self.far_outer, self.far_inner, self.plane.t)[i]
+        dst = self.total.at[j] if i == 2 else self.own.at[i, j]
+        return pltpu.make_async_copy(self.parts.at[chunk, j], dst, self.loc.at[i, j])
+
+    def start(self):
+        for j in range(2):
+            self.load(2, j).start()
+
+        @pl.when(self.outer)
+        def _():
+            for i in range(3):
+                for j in range(2):
+                    self.first(i, j).start()
+
+        @pl.when(self.inner)
+        def _():
+            for j in range(2):
+                self.back(j).start()
+            for i in range(2):
+                for j in range(2):
+                    self.load(i, j).start()
+
+    def relay(self, i, j):
+        @pl.when(self.inner)
+        def _():
+            self.first(i, j).wait_recv()
+            self.load(i, j).wait()
+            add, own = self.add, self.own
+
+            def both(at):
+                value = add[i, j, at, :].astype(f32) + own[i, j, at, :].astype(f32)
+                add[i, j, at, :] = value.astype(bf16)
+
+            in_tiles(add.shape[2], both, 256)
+            self.sent(i, j).start()
+
+    def finish(self):
+        total, got = self.total, self.got
+        for j in range(2):
+            self.load(2, j).wait()
+            self.back(j).wait_recv()
+            self.sent(0, j).wait_recv()
+
+            def sums(at, j=j):
+                value = total[j, at, :].astype(f32) + got[0, j, at, :].astype(f32)
+                total[j, at, :] = (value + got[1, j, at, :].astype(f32)).astype(bf16)
+
+            in_tiles(total.shape[1], sums, 256)
+
+        @pl.when(self.outer)
+        def _():
+            for i in range(3):
+                for j in range(2):
+                    self.first(i, j).wait_send()
+
+        @pl.when(self.inner)
+        def _():
+            for j in range(2):
+                self.back(j).wait_send()
+                for i in range(2):
+                    self.sent(i, j).wait_send()
+
+    @staticmethod
+    def scratch(shape):
+        return [
+            pltpu.VMEM((2,) + shape, bf16),
+            pltpu.VMEM((2,) + shape, bf16),
+            pltpu.VMEM((2,) + shape, bf16),
+            pltpu.SemaphoreType.DMA((2, 5, 2)),
+            pltpu.SemaphoreType.DMA((3, 2)),
+        ]
+
+
 def fan(plane, src_of, dst_of, send, recv):
     copies = []
     for k in range(1, plane.m):
@@ -630,12 +740,12 @@
 TILE = 16
 
 
-def in_tiles(rows, body):
+def in_tiles(rows, body, tile=TILE):
     def one(i, carry):
-        body(pl.ds(pl.multiple_of(i * TILE, TILE), TILE))
+        body(pl.ds(pl.multiple_of(i * tile, tile), tile))
         return carry
 
-    lax.fori_loop(0, rows // TILE, one, 0)
+    lax.fori_loop(0, rows // tile, one, 0)
 
 
 class Reduce:
@@ -1386,10 +1496,11 @@
 
 def attend_back_body(
     n, m, factor, scale, q_in, k_in, v_in, o_in, lse, begin, cos_in, sin_in, low_in,
-    hid_in, down_in, wo, dnorm, resid, grad, gain,
-    out, layer, terms, dresid, gain_out,
+    hid_in, down_in, ffn, wo, dnorm, resid, grad, gain,
+    out, layer, terms, dresid, gain_out, ffn_sum,
     q, k, v, o, cosine, sine, low, kt, dqt, dk, dv, delta, go, every, dbranch, wo_here,
-    hid_low, w_down, stage, pair, near, far, sr, lr, held, gain_sum, gain_cut, gain_got, sg, lg, sv, loc,
+    hid_low, w_down, stage, pair, near, far, sr, lr, held, gain_sum, gain_cut, gain_got,
+    sums, add, own, got, ss, ls, sg, lg, sv, loc,
 ):
     plane = Plane(n, m)
     heads, length, _ = q.shape
@@ -1406,7 +1517,7 @@
     ]
     for copy in loads:
         copy.start()
-    greet(plane, False)
+    greet(plane, True)
     moves = [
         pltpu.make_async_copy(hid_in, hid_low, loc.at[8]),
         pltpu.make_async_copy(down_in, w_down, loc.at[9]),
@@ -1434,8 +1545,10 @@
         gain_sum[...] += up * turned
 
     in_tiles(rows, into_branch)
-    meet(plane, False)
+    meet(plane, True)
     gather.start()
+    scatter = Scatter(plane, ffn, sums, add, own, got, ss, ls)
+    scatter.start()
     total_gain = jnp.sum(gain_sum[...], axis=0, keepdims=True)
     for i in range(n):
         gain_cut[i] = total_gain[:, i * (width // n) : (i + 1) * (width // n)]
@@ -1490,11 +1603,13 @@
         def _():
             gather.relay_near()
             gather.wait_share(1)
+            scatter.relay(0, 0)
 
         @pl.when(kk == 2)
         def _():
             one.send_to()
             gather.wait_share(0)
+            scatter.relay(0, 1)
 
         @pl.when(kk == 3)
         def _():
@@ -1502,6 +1617,7 @@
             one.first(held, resid)
             gather.relay_far()
             gather.wait_share(2)
+            scatter.relay(1, 0)
 
         i = plane.number(kk, 0) // 2
         here = pl.ds(pl.multiple_of(i * BLOCK, BLOCK), BLOCK)
@@ -1543,6 +1659,7 @@
         return carry
 
     lax.fori_loop(0, 4, chips, 0)
+    scatter.relay(1, 1)
 
     def write(i, carry):
         at = pl.ds(pl.multiple_of(i * BLOCK, BLOCK), BLOCK)
@@ -1568,18 +1685,22 @@
     lax.fori_loop(0, width // part, into_terms, 0)
     for copy in gain_copies:
         copy.wait()
-    got = gain_got[0]
+    all_gain = gain_got[0]
     for i in range(1, n):
-        got = got + gain_got[i]
+        all_gain = all_gain + gain_got[i]
     for t in range(m):
-        gain_out[t] = got[:, t * strip : (t + 1) * strip]
+        gain_out[t] = all_gain[:, t * strip : (t + 1) * strip]
     gather.wait_sends()
     one.finish(held, layer)
+    scatter.finish()
+    back = pltpu.make_async_copy(sums, ffn_sum, loc.at[10])
+    back.start()
+    back.wait()
 
 
 def attend_back(
     n, m, factor, scale, q, k, v, o, lse, begin, cosine, sine, low,
-    hid_low, w_down, wo, dnorm, resid, grad, gain, ident,
+    hid_low, w_down, ffn, wo, dnorm, resid, grad, gain, ident,
 ):
     heads, length, _ = q.shape
     rows, width = dnorm.shape
@@ -1594,9 +1715,10 @@
             jax.ShapeDtypeStruct(wo.shape, bf16),
             jax.ShapeDtypeStruct((rows, width), f32),
             jax.ShapeDtypeStruct((m, 1, strip), f32),
+            jax.ShapeDtypeStruct(ffn.shape[1:], bf16),
         ),
-        in_specs=[hbm] * 4 + [vmem] * 2 + [hbm] * 5 + [vmem] * 5,
-        out_specs=[vmem] * 5,
+        in_specs=[hbm] * 4 + [vmem] * 2 + [hbm] * 6 + [vmem] * 5,
+        out_specs=[vmem] * 5 + [hbm],
         scratch_shapes=[
             pltpu.VMEM(q.shape, bf16),
             pltpu.VMEM(k.shape, bf16),
@@ -1624,15 +1746,19 @@
             pltpu.VMEM((TILE, width), f32),
             pltpu.VMEM((n, 1, width // n), f32),
             pltpu.VMEM((n, 1, width // n), f32),
+            pltpu.VMEM(ffn.shape[1:], bf16),
         ]
+        + Scatter.scratch(ffn.shape[1:])
         + Gathers.scratch(2)
-        + [pltpu.SemaphoreType.DMA((2, n - 1)), pltpu.SemaphoreType.DMA((10,))],
+        + [pltpu.SemaphoreType.DMA((2, n - 1)), pltpu.SemaphoreType.DMA((11,))],
         compiler_params=pltpu.CompilerParams(
             collective_id=ident, has_side_effects=True, vmem_limit_bytes=VMEM_LIMIT
         ),
         cost_estimate=COST,
         name="attend_back",
-    )(q, k, v, o, lse, begin, cosine, sine, low, hid_low, w_down, wo, dnorm, resid, grad, gain)
+    )(
+        q, k, v, o, lse, begin, cosine, sine, low, hid_low, w_down, ffn, wo, dnorm, resid, grad, gain
+    )
 
 
 def feed_body(
@@ -1783,7 +1909,7 @@
         k = 3 - it // 2
         b = number(it)
 
-        @pl.when(it == 3)
+        @pl.when(it == 2)
         def _():
             reduce.join(3)
             reduce.out[0].start()
@@ -1945,9 +2071,8 @@
         dnorm_two, ffn_terms, hid_low, w_down, down_parts = feed(
             n, m, norm_two, grad_all, ffn_all, down_mine, 2
         )
-        ffn_sum = lax.psum_scatter(ffn_terms, "tp", scatter_dimension=0, tiled=False)
-        dqkv, layer_output, output_terms, dresid, gain_part = attend_back(
-            n, m, factor, scale, q, k, v, o, lse, begin, cosine, sine, low, hid_low, w_down,
+        dqkv, layer_output, output_terms, dresid, gain_part, ffn_sum = attend_back(
+            n, m, factor, scale, q, k, v, o, lse, begin, cosine, sine, low, hid_low, w_down, ffn_terms,
             output_rows, dnorm_two, resid, out_grad[0], gain_two, 3,
         )
         input_grad, ffn_out, qkv_out, output_parts, gain_sums = last(
@@ -1993,7 +2118,7 @@
 
 def solution(mesh):
     n, m = mesh.shape["seq"], mesh.shape["tp"]
-    fits = n == KEY_VALUE_HEADS == 8
+    fits = n == KEY_VALUE_HEADS == 8 and m == 4
     return jax.shard_map(
         fast_layer(n, m) if fits else on_device,
         mesh=mesh,

time: 333 us -> 325 us (0.976)
  between operations: 14.2 us -> 0.83 us
  Pallas kernels: 309 us -> 313 us
    pallas_call x1, Pallas kernels: 62.5 us -> 68.4 us  [attend_back(): pl.pallas_call(functools.partial(attend_back_body, n, m, factor, scale),...]
  transfers between devices with their start and end apart: 1 -> 0, of which waited for: 1 -> 0; matrix products, arithmetic and copies ran while one was open for 0% -> 0% of each run, Pallas kernels for 19% -> 0%
where the time goes in v7:
time: 325 us; the launch traced here: 324 us
  Pallas kernels  313 us (96%)
  other arithmetic  6.52 us (2%)
  local copies, waits for them, and re-layouts  3.65 us (1%)
    pallas_call x1, Pallas kernels, feed(): pl.pallas_call(functools.partial(feed_body, n, m), out_shape=(jax.ShapeDt...  70.5 us
    pallas_call x1, Pallas kernels, attend(): pl.pallas_call(functools.partial(attend_body, n, m, factor), out_shape=(j...  69.9 us
    pallas_call x1, Pallas kernels, attend_back(): pl.pallas_call(functools.partial(attend_back_body, n, m, factor, scale),...  68.4 us
    pallas_call x1, Pallas kernels, entry(): pl.pallas_call(functools.partial(entry_body, n, m, heads, strip), out_sha...  53.7 us
    pallas_call x1, Pallas kernels, last(): pl.pallas_call(functools.partial(last_body, n, m), out_shape=(jax.ShapeDt...  50.6 us

profile of v7, /device:TPU:0, one launch (start us, length us, event | category | flops | bytes accessed | tf_op | source)
XLA Modules:
  0.0 324.1 jit_solution(14444515878706419042)
XLA Ops:
  0.6 53.7 %entry.1 = (bf16[1536,2048]{1,0:T(8,128)(2,1)}, bf16[2,2048,128]{2,1,0:T(8,128)(2,1)}, bf16[2048,128]{1,0:T(8,128)(2,1)}, bf16[2048,128]{1,0:T(8,128)(2,1)}, f32...) custom-call(bf16[256,1536]{1,0:T(8,128)(2,1)} %bitcast.21, ...), custom_call_target="tpu_custom_call" | custom-call | flops 1000000 | bytes 100000 | tf_op jit(solution)/shard_map/entry/pallas_call | solution.py:1257
  54.4 69.9 %attend.1 = (f32[2,2048,128]{2,1,0:T(8,128)}, f32[2,1,2048]{2,1,0:T(1,128)}, s32[1,2048]{1,0:T(1,128)}, bf16[2048,256]{1,0:T(8,128)(2,1)}, bf16[8,256,1536]{2,1,...) custom-call(bf16[2,2048,128]{2,1,0:T(8,128)(2,1)} %get-tuple-element.48.q.q_in, ...), custom_call_target="tpu_custom_call" | custom-call | flops 1000000 | bytes 100000 | tf_op jit(solution)/shard_map/attend/pallas_call | solution.py:1461
  124.3 70.5 %feed.1 = (f32[256,1536]{1,0:T(8,128)}, bf16[4,2,1536,128]{3,2,1,0:T(8,128)(2,1)}, bf16[2048,512]{1,0:T(8,128)(2,1)}, bf16[1536,512]{1,0:T(8,128)(2,1)}, bf16[4,1536,128]{2,1,0:T(8,128)(2,1)}) custom-call(bf16[256,1536]{1,0:T(8,128)(2,1)} %get-tuple-element.61.mine, bf16[8,256,1536]{2,1,0:T(8,128)(2,1)} %get-tuple-element.62.go, ...), custom_call_target="tpu_custom_call" | custom-call | flops 1000000 | bytes 100000 | tf_op jit(solution)/shard_map/feed/pallas_call | solution.py:1990
  194.8 68.4 %attend_back.1 = (bf16[2048,512]{1,0:T(8,128)(2,1)}, bf16[256,1536]{1,0:T(8,128)(2,1)}, bf16[4,48,1536]{2,1,0:T(8,128)(2,1)}, f32[256,1536]{1,0:T(8,128)}, f32[4...) custom-call(bf16[2,2048,128]{2,1,0:T(8,128)(2,1)} %get-tuple-element.48.q.q_in, ...), custom_call_target="tpu_custom_call" | custom-call | flops 1000000 | bytes 100000 | tf_op jit(solution)/shard_map/attend_back/pallas_call | solution.py:1710
  263.2 50.6 %last.1 = (f32[256,1536]{1,0:T(8,128)}, bf16[3,192,1024]{2,1,0:T(8,128)(2,1)}, bf16[8,48,384]{2,1,0:T(8,128)(2,1)}, bf16[4,48,1536]{2,1,0:T(8,128)(2,1)}, f32[4,1,48]{2,1,0:T(1,128)}) custom-call(bf16[2048,512]{1,0:T(8,128)(2,1)} %get-tuple-element.71.dqkv_in, bf16[1536,512]{1,0:T(8,128)(2,1)} %get-tuple-element.72.w_in, bf16[256,1536]{1,0:T(8,128)(2,1)} %bitcast.23, ...), custom_call_target="tpu_custom_call" | custom-call | flops 1000000 | bytes 100000 | tf_op jit(solution)/shard_map/last/pallas_call | solution.py:1003
  313.8 1.2 reduce_sum.49
  315.1 1.9 convert_reduce_fusion
  317.0 1.0 convert_bitcast_fusion
  317.9 0.2 copy.25
  318.2 0.1 reshape.45
  318.4 0.1 multiply_reduce_fusion
  318.5 0.1 convert_bitcast_fusion.2
  318.7 0.1 copy.26
  318.7 0.1 reshape.46
  318.9 0.1 copy.27
  318.9 0.1 reshape.47
  319.1 0.0 copy-done.9
  319.1 0.1 multiply_reduce_fusion.1
  319.3 0.5 convert_divide_fusion
  319.8 0.0 copy-done.1
  319.8 1.5 bitcast_convert_fusion
  321.3 0.9 copy.30
  322.2 0.8 copy-done
  323.0 1.1 copy.31
  (19 shorter events, 0.1 us)
Async XLA Ops:
  313.8 4.5 %copy-start.4 = (bf16[48,1536]{1,0:T(8,128)(2,1)S(1)}, bf16[48,1536]{1,0:T(8,128)(2,1)}, u32[]{:S(2)}) copy-start(bf16[48,1536]{1,0:T(8,128)(2,1)} %wq.1) | copy-start | bytes 442372
  315.1 3.5 %copy-start.7 = (bf16[8,48,384]{2,1,0:T(8,128)(2,1)S(1)}, bf16[8,48,384]{2,1,0:T(8,128)(2,1)}, u32[]{:S(2)}) copy-start(bf16[8,48,384]{2,1,0:T(8,128)(2,1)} %get-tuple-element.81) | copy-start | bytes 884740
  318.2 0.9 copy-start.8
  318.2 0.9 copy-start.9
  318.4 2.9 copy-start.2
  318.4 0.9 copy-start.10
  318.4 1.4 copy-start.1
  318.9 2.4 copy-start.5
  319.1 2.2 copy-start.6
  319.8 1.5 copy-start.3
  321.3 1.7 copy-start

commit v8 on v7

--- a/solution.py
+++ b/solution.py
@@ -849,16 +849,16 @@
 
 
 def last_body(
-    n, m, dqkv_in, w_in, x_in, dresid_in, gain, norm_t, ffn, downs, wo, vec,
-    input_grad, ffn_out, qkv_out, wo_out, vec_out,
-    dqkv, w, x, dresid, down_here, down_sum, narrow, pair, near, far, sr, lr, total, stage, norms, mine, got, summed, sems, st, loc,
+    n, m, dqkv_in, w_in, norm_t, ffn, downs, wo, vec,
+    total, ffn_out, qkv_out, wo_out, vec_out,
+    dqkv, w, down_here, down_sum, narrow, pair, near, far, sr, lr, stage, norms, mine, got, summed, sems, st, loc,
 ):
     plane = Plane(n, m)
     greet(plane, True)
     loads = [
         pltpu.make_async_copy(a, b, loc.at[5 + i])
         for i, (a, b) in enumerate(
-            ((dqkv_in, dqkv), (w_in, w), (downs, down_here), (x_in, x), (dresid_in, dresid))
+            ((dqkv_in, dqkv), (w_in, w), (downs, down_here))
         )
     ]
     load = pltpu.make_async_copy(norm_t, norms, loc.at[0])
@@ -975,25 +975,12 @@
     )
     for copy in b:
         copy.start()
-    for copy in loads[3:]:
-        copy.wait()
     reduce.finish(total)
-
-    def into_input(at):
-        value = x[at, :].astype(f32)
-        scale = lax.rsqrt(jnp.mean(value * value, axis=1, keepdims=True) + norm_epsilon)
-        inner = gain[...] * total[at, :]
-        moment = jnp.mean(value * inner, axis=1, keepdims=True)
-        input_grad[at, :] = (
-            dresid[at, :] + scale * inner - value * scale * (scale * scale * moment)
-        )
-
-    in_tiles(tokens, into_input)
     for copy in a + a_down + b + across:
         copy.wait()
 
 
-def last(n, m, dqkv, w, x, dresid, gain, norm_t, ffn, downs, wo, vec, ident):
+def last(n, m, dqkv, w, norm_t, ffn, downs, wo, vec, ident):
     width, length = norm_t.shape
     tokens = length // n
     cols = w.shape[1] // SLOT * HALF
@@ -1009,20 +996,17 @@
             jax.ShapeDtypeStruct(wo.shape, wo.dtype),
             jax.ShapeDtypeStruct(vec.shape, vec.dtype),
         ),
-        in_specs=[hbm] * 4 + [vmem] + [hbm] * 5,
+        in_specs=[hbm] * 7,
         out_specs=[vmem] + [hbm] * 4,
         scratch_shapes=[
             pltpu.VMEM(dqkv.shape, bf16),
             pltpu.VMEM(w.shape, bf16),
-            pltpu.VMEM(x.shape, bf16),
-            pltpu.VMEM(dresid.shape, f32),
             pltpu.VMEM(downs.shape, bf16),
             pltpu.VMEM(downs.shape[1:], bf16),
             pltpu.VMEM((w.shape[1], cols), bf16),
         ]
         + Reduce.scratch(tokens, width)
         + [
-            pltpu.VMEM((tokens, width), f32),
             pltpu.VMEM((4, tokens, width), bf16),
             pltpu.VMEM((width, length), bf16),
             pltpu.VMEM((n, m, strip, cols), bf16),
@@ -1037,7 +1021,7 @@
         ),
         cost_estimate=COST,
         name="last",
-    )(dqkv, w, x, dresid, gain, norm_t, ffn, downs, wo, vec)
+    )(dqkv, w, norm_t, ffn, downs, wo, vec)
 
 
 def column(row):
@@ -1091,7 +1075,7 @@
     places[0:1, :] = doc_ids[...]
     places[1:2, :] = positions[...]
     meet(plane, True)
-    gather = Gathers(plane, x, lambda i: blocks.at[i], sx, lx, 2)
+    gather = Gathers(plane, x, lambda i: blocks.at[i], sx, lx, 1)
     first = []
     for i, (src, dst) in enumerate(((gains, gains_all), (wqkv, w_all))):
         first += exchange(
@@ -1289,7 +1273,7 @@
             pltpu.VMEM((n, strip, each), bf16),
             pltpu.VMEM((8, LANES), f32),
             pltpu.VMEM((each, wide), bf16),
-            *Gathers.scratch(2),
+            *Gathers.scratch(1),
             pltpu.SemaphoreType.DMA((6, 2, n - 1)),
             pltpu.SemaphoreType.DMA((3, 2, m - 1)),
             pltpu.SemaphoreType.DMA((2,)),
@@ -2031,6 +2015,110 @@
     )(norm, go, w_in, down)
 
 
+def results_body(
+    dnorm, dresid, x, gain, layer_in, ffn, qkv, wo, vec, wq, wk, wv, one,
+    layer, input_grad, first, query, key, value, output, second, gate, up, down,
+):
+    step = pl.program_id(0)
+
+    def into_input(at):
+        token = x[at, :].astype(f32)
+        scale = lax.rsqrt(jnp.mean(token * token, axis=1, keepdims=True) + norm_epsilon)
+        inner = gain[...] * dnorm[at, :]
+        moment = jnp.mean(token * inner, axis=1, keepdims=True)
+        input_grad[at, :] = (
+            dresid[at, :] + scale * inner - token * scale * (scale * scale * moment)
+        )
+        layer[at, :] = layer_in[at, :]
+
+    in_tiles(x.shape[0], into_input)
+    for i, ref in enumerate((gate, up, down)):
+        ref[...] = ffn[i].astype(f32)
+
+    @pl.when(step == 0)
+    def _():
+        groups, strip, _ = qkv.shape
+        start = 0
+        sums = jnp.zeros((strip, 1), f32)
+        for ref, weight in ((query, wq), (key, wk), (value, wv)):
+            each = ref.shape[1] // groups
+            for g in range(groups):
+                ref[:, g * each : (g + 1) * each] = qkv[g, :, start : start + each].astype(f32)
+            start += each
+            sums += jnp.sum(weight[...].astype(f32) * ref[...], axis=1, keepdims=True)
+        row = jnp.broadcast_to(sums, (strip, LANES)).T[0:1, :strip]
+        first[...] = row / one[...].astype(f32)
+        total = wo[0].astype(f32)
+        gains = vec[0]
+        for t in range(1, wo.shape[0]):
+            total += wo[t].astype(f32)
+            gains += vec[t]
+        output[...] = total
+        second[...] = gains
+
+
+def results(dnorm, dresid, x, gain, layer, ffn, qkv, wo, vec, wq, wk, wv, one):
+    tokens, width = x.shape
+    rows, cols = ffn.shape[1:]
+    strip = wq.shape[0]
+    steps = 2
+
+    def tiled(count, columns):
+        return pl.BlockSpec((count // steps, columns), lambda i: (i, 0))
+
+    def fixed(*shape):
+        return pl.BlockSpec(shape, lambda i: (0,) * len(shape))
+
+    return pl.pallas_call(
+        results_body,
+        grid=(steps,),
+        out_shape=(
+            jax.ShapeDtypeStruct((tokens, width), bf16),
+            jax.ShapeDtypeStruct((tokens, width), f32),
+            jax.ShapeDtypeStruct((1, strip), f32),
+            jax.ShapeDtypeStruct(wq.shape, f32),
+            jax.ShapeDtypeStruct(wk.shape, f32),
+            jax.ShapeDtypeStruct(wv.shape, f32),
+            jax.ShapeDtypeStruct((strip, width), f32),
+            jax.ShapeDtypeStruct((1, strip), f32),
+            jax.ShapeDtypeStruct((rows, cols), f32),
+            jax.ShapeDtypeStruct((rows, cols), f32),
+            jax.ShapeDtypeStruct((rows, cols), f32),
+        ),
+        in_specs=[
+            tiled(tokens, width),
+            tiled(tokens, width),
+            tiled(tokens, width),
+            fixed(1, width),
+            tiled(tokens, width),
+            pl.BlockSpec((3, rows // steps, cols), lambda i: (0, i, 0)),
+            fixed(*qkv.shape),
+            fixed(*wo.shape),
+            fixed(*vec.shape),
+            fixed(*wq.shape),
+            fixed(*wk.shape),
+            fixed(*wv.shape),
+            fixed(1, strip),
+        ],
+        out_specs=[
+            tiled(tokens, width),
+            tiled(tokens, width),
+            fixed(1, strip),
+            fixed(*wq.shape),
+            fixed(*wk.shape),
+            fixed(*wv.shape),
+            fixed(strip, width),
+            fixed(1, strip),
+            tiled(rows, cols),
+            tiled(rows, cols),
+            tiled(rows, cols),
+        ],
+        compiler_params=pltpu.CompilerParams(vmem_limit_bytes=VMEM_LIMIT),
+        cost_estimate=COST,
+        name="results",
+    )(dnorm, dresid, x, gain, layer, ffn, qkv, wo, vec, wq, wk, wv, one)
+
+
 def fast_layer(n, m):
     def on_plane(
         layer_input,
@@ -2075,39 +2163,25 @@
             n, m, factor, scale, q, k, v, o, lse, begin, cosine, sine, low, hid_low, w_down, ffn_terms,
             output_rows, dnorm_two, resid, out_grad[0], gain_two, 3,
         )
-        input_grad, ffn_out, qkv_out, output_parts, gain_sums = last(
-            n, m, dqkv, wqkv, x, dresid, gain_one, norm_t, ffn_sum, down_parts,
-            output_terms, gain_part, 6,
+        dnorm_one, ffn_out, qkv_out, output_parts, gain_sums = last(
+            n, m, dqkv, wqkv, norm_t, ffn_sum, down_parts, output_terms, gain_part, 6
         )
-        output_grad = jnp.sum(output_parts.astype(f32), axis=0)
-
-        gate_grad, up_grad, down_grad = [ffn_out[i].astype(f32) for i in range(3)]
-        kv = HEAD_SIZE * KEY_VALUE_HEADS // n
-        split = heads * HEAD_SIZE
-
-        def columns(a, b):
-            return qkv_out[:, :, a:b].transpose(1, 0, 2).reshape(strip, -1).astype(f32)
-
-        query_grad = columns(0, split)
-        key_grad = columns(split, split + kv)
-        value_grad = columns(split + kv, split + 2 * kv)
-
-        one = (
-            jnp.sum(query_weight.astype(f32) * query_grad, axis=1)
-            + jnp.sum(key_weight.astype(f32) * key_grad, axis=1)
-            + jnp.sum(value_weight.astype(f32) * value_grad, axis=1)
+        (
+            layer_output, input_grad, first_gain_grad, query_grad, key_grad, value_grad,
+            output_grad, second_gain_grad, gate_grad, up_grad, down_grad,
+        ) = results(
+            dnorm_one, dresid, x, gain_one, layer_output, ffn_out, qkv_out, output_parts,
+            gain_sums, query_weight, key_weight, value_weight, first_gain.reshape(1, strip),
         )
-        first_gain_grad = one / first_gain.astype(f32)
-        second_gain_grad = jnp.sum(gain_sums, axis=(0, 1))
         return (
             layer_output[None],
             input_grad[None],
-            first_gain_grad,
+            first_gain_grad.reshape(strip),
             query_grad,
             key_grad,
             value_grad,
             output_grad,
-            second_gain_grad,
+            second_gain_grad.reshape(strip),
             gate_grad,
             up_grad,
             down_grad,

time: 325 us -> 315 us (0.969)
  other arithmetic: 6.52 us -> 0 us
  local copies, waits for them, and re-layouts: 3.65 us -> 0 us
    pallas_call x0 -> x1, Pallas kernels: none -> 6.38 us  [results(): pl.pallas_call(results_body, grid=(steps,), out_shape=(jax.ShapeDtypeStru...]
    reduce_sum x4 -> x0, other arithmetic: 3.44 us -> none  [the longest x1 1.93 us: on_plane(): output_grad = jnp.sum(output_parts.astype(f32), axis=0)]
where the time goes in v8:
time: 315 us
  Pallas kernels  314 us (100%)
    pallas_call x1, Pallas kernels, feed(): pl.pallas_call(functools.partial(feed_body, n, m), out_shape=(jax.ShapeDt...  69.7 us
    pallas_call x1, Pallas kernels, attend_back(): pl.pallas_call(functools.partial(attend_back_body, n, m, factor, scale),...  67.8 us
    pallas_call x1, Pallas kernels, attend(): pl.pallas_call(functools.partial(attend_body, n, m, factor), out_shape=(j...  66.7 us
    pallas_call x1, Pallas kernels, entry(): pl.pallas_call(functools.partial(entry_body, n, m, heads, strip), out_sha...  54.8 us
    pallas_call x1, Pallas kernels, last(): pl.pallas_call(functools.partial(last_body, n, m), out_shape=(jax.ShapeDt...  48.8 us
    pallas_call x1, Pallas kernels, results(): pl.pallas_call(results_body, grid=(steps,), out_shape=(jax.ShapeDtypeStru...  6.38 us

profile of v8, /device:TPU:0, one launch (start us, length us, event | category | flops | bytes accessed | tf_op | source)
XLA Modules:
  0.0 315.0 jit_solution(18310379878071066408)
XLA Ops:
  0.6 54.8 %entry.1 = (bf16[1536,2048]{1,0:T(8,128)(2,1)}, bf16[2,2048,128]{2,1,0:T(8,128)(2,1)}, bf16[2048,128]{1,0:T(8,128)(2,1)}, bf16[2048,128]{1,0:T(8,128)(2,1)}, f32...) custom-call(bf16[256,1536]{1,0:T(8,128)(2,1)} %bitcast.8, ...), custom_call_target="tpu_custom_call" | custom-call | flops 1000000 | bytes 100000 | tf_op jit(solution)/shard_map/entry/pallas_call | solution.py:1241
  55.4 66.7 %attend.1 = (f32[2,2048,128]{2,1,0:T(8,128)}, f32[2,1,2048]{2,1,0:T(1,128)}, s32[1,2048]{1,0:T(1,128)}, bf16[2048,256]{1,0:T(8,128)(2,1)}, bf16[8,256,1536]{2,1,...) custom-call(bf16[2,2048,128]{2,1,0:T(8,128)(2,1)} %get-tuple-element.59.q.q_in, ...), custom_call_target="tpu_custom_call" | custom-call | flops 1000000 | bytes 100000 | tf_op jit(solution)/shard_map/attend/pallas_call | solution.py:1445
  122.2 69.7 %feed.1 = (f32[256,1536]{1,0:T(8,128)}, bf16[4,2,1536,128]{3,2,1,0:T(8,128)(2,1)}, bf16[2048,512]{1,0:T(8,128)(2,1)}, bf16[1536,512]{1,0:T(8,128)(2,1)}, bf16[4,1536,128]{2,1,0:T(8,128)(2,1)}) custom-call(bf16[256,1536]{1,0:T(8,128)(2,1)} %get-tuple-element.72.mine, bf16[8,256,1536]{2,1,0:T(8,128)(2,1)} %get-tuple-element.73.go, ...), custom_call_target="tpu_custom_call" | custom-call | flops 1000000 | bytes 100000 | tf_op jit(solution)/shard_map/feed/pallas_call | solution.py:1974
  191.9 67.8 %attend_back.1 = (bf16[2048,512]{1,0:T(8,128)(2,1)}, bf16[256,1536]{1,0:T(8,128)(2,1)}, bf16[4,48,1536]{2,1,0:T(8,128)(2,1)}, f32[256,1536]{1,0:T(8,128)}, f32[4...) custom-call(bf16[2,2048,128]{2,1,0:T(8,128)(2,1)} %get-tuple-element.59.q.q_in, ...), custom_call_target="tpu_custom_call" | custom-call | flops 1000000 | bytes 100000 | tf_op jit(solution)/shard_map/attend_back/pallas_call | solution.py:1694
  259.7 48.8 %last.1 = (f32[256,1536]{1,0:T(8,128)}, bf16[3,192,1024]{2,1,0:T(8,128)(2,1)}, bf16[8,48,384]{2,1,0:T(8,128)(2,1)}, bf16[4,48,1536]{2,1,0:T(8,128)(2,1)}, f32[4,1,48]{2,1,0:T(1,128)}) custom-call(bf16[2048,512]{1,0:T(8,128)(2,1)} %get-tuple-element.81.dqkv_in, bf16[1536,512]{1,0:T(8,128)(2,1)} %get-tuple-element.82.w_in, ...), custom_call_target="tpu_custom_call" | custom-call | flops 1000000 | bytes 100000 | tf_op jit(solution)/shard_map/last/pallas_call | solution.py:990
  308.5 6.4 %results.1 = (bf16[256,1536]{1,0:T(8,128)(2,1)}, f32[256,1536]{1,0:T(8,128)}, f32[1,48]{1,0:T(1,128)}, f32[48,1536]{1,0:T(8,128)}, f32[48,768]{1,0:T(8,128)}, /*...) custom-call(f32[256,1536]{1,0:T(8,128)} %get-tuple-element.88.dnorm,, ...), custom_call_target="tpu_custom_call" | custom-call | flops 1000000 | bytes 100000 | tf_op jit(solution)/shard_map/results/pallas_call | solution.py:2072

commit v9 on v8

--- a/solution.py
+++ b/solution.py
@@ -737,7 +737,7 @@
     return [own] + copies
 
 
-TILE = 16
+TILE = 32
 
 
 def in_tiles(rows, body, tile=TILE):
@@ -1586,12 +1586,12 @@
         @pl.when(kk == 1)
         def _():
             gather.relay_near()
+            one.send_to()
             gather.wait_share(1)
             scatter.relay(0, 0)
 
         @pl.when(kk == 2)
         def _():
-            one.send_to()
             gather.wait_share(0)
             scatter.relay(0, 1)
 

time: 315 us -> 313 us (level)
  no operation moved by 1% of the time
where the time goes in v9:
time: 313 us; the launch traced here: 312 us
  Pallas kernels  311 us (99%)
    pallas_call x1, Pallas kernels, feed(): pl.pallas_call(functools.partial(feed_body, n, m), out_shape=(jax.ShapeDt...  69.8 us
    pallas_call x1, Pallas kernels, attend_back(): pl.pallas_call(functools.partial(attend_back_body, n, m, factor, scale),...  66.9 us
    pallas_call x1, Pallas kernels, attend(): pl.pallas_call(functools.partial(attend_body, n, m, factor), out_shape=(j...  66.2 us
    pallas_call x1, Pallas kernels, entry(): pl.pallas_call(functools.partial(entry_body, n, m, heads, strip), out_sha...  54.8 us
    pallas_call x1, Pallas kernels, last(): pl.pallas_call(functools.partial(last_body, n, m), out_shape=(jax.ShapeDt...  47.8 us

profile of v9, /device:TPU:0, one launch (start us, length us, event | category | flops | bytes accessed | tf_op | source)
XLA Modules:
  0.0 312.0 jit_solution(10655888357388334902)
XLA Ops:
  0.6 54.8 %entry.1 = (bf16[1536,2048]{1,0:T(8,128)(2,1)}, bf16[2,2048,128]{2,1,0:T(8,128)(2,1)}, bf16[2048,128]{1,0:T(8,128)(2,1)}, bf16[2048,128]{1,0:T(8,128)(2,1)}, f32...) custom-call(bf16[256,1536]{1,0:T(8,128)(2,1)} %bitcast.8, ...), custom_call_target="tpu_custom_call" | custom-call | flops 1000000 | bytes 100000 | tf_op jit(solution)/shard_map/entry/pallas_call | solution.py:1241
  55.4 66.2 %attend.1 = (f32[2,2048,128]{2,1,0:T(8,128)}, f32[2,1,2048]{2,1,0:T(1,128)}, s32[1,2048]{1,0:T(1,128)}, bf16[2048,256]{1,0:T(8,128)(2,1)}, bf16[8,256,1536]{2,1,...) custom-call(bf16[2,2048,128]{2,1,0:T(8,128)(2,1)} %get-tuple-element.59.q.q_in, ...), custom_call_target="tpu_custom_call" | custom-call | flops 1000000 | bytes 100000 | tf_op jit(solution)/shard_map/attend/pallas_call | solution.py:1445
  121.6 69.8 %feed.1 = (f32[256,1536]{1,0:T(8,128)}, bf16[4,2,1536,128]{3,2,1,0:T(8,128)(2,1)}, bf16[2048,512]{1,0:T(8,128)(2,1)}, bf16[1536,512]{1,0:T(8,128)(2,1)}, bf16[4,1536,128]{2,1,0:T(8,128)(2,1)}) custom-call(bf16[256,1536]{1,0:T(8,128)(2,1)} %get-tuple-element.72.mine, bf16[8,256,1536]{2,1,0:T(8,128)(2,1)} %get-tuple-element.73.go, ...), custom_call_target="tpu_custom_call" | custom-call | flops 1000000 | bytes 100000 | tf_op jit(solution)/shard_map/feed/pallas_call | solution.py:1974
  191.4 66.9 %attend_back.1 = (bf16[2048,512]{1,0:T(8,128)(2,1)}, bf16[256,1536]{1,0:T(8,128)(2,1)}, bf16[4,48,1536]{2,1,0:T(8,128)(2,1)}, f32[256,1536]{1,0:T(8,128)}, f32[4...) custom-call(bf16[2,2048,128]{2,1,0:T(8,128)(2,1)} %get-tuple-element.59.q.q_in, ...), custom_call_target="tpu_custom_call" | custom-call | flops 1000000 | bytes 100000 | tf_op jit(solution)/shard_map/attend_back/pallas_call | solution.py:1694
  258.4 47.8 %last.1 = (f32[256,1536]{1,0:T(8,128)}, bf16[3,192,1024]{2,1,0:T(8,128)(2,1)}, bf16[8,48,384]{2,1,0:T(8,128)(2,1)}, bf16[4,48,1536]{2,1,0:T(8,128)(2,1)}, f32[4,1,48]{2,1,0:T(1,128)}) custom-call(bf16[2048,512]{1,0:T(8,128)(2,1)} %get-tuple-element.81.dqkv_in, bf16[1536,512]{1,0:T(8,128)(2,1)} %get-tuple-element.82.w_in, ...), custom_call_target="tpu_custom_call" | custom-call | flops 1000000 | bytes 100000 | tf_op jit(solution)/shard_map/last/pallas_call | solution.py:990
  306.2 5.7 %results.1 = (bf16[256,1536]{1,0:T(8,128)(2,1)}, f32[256,1536]{1,0:T(8,128)}, f32[1,48]{1,0:T(1,128)}, f32[48,1536]{1,0:T(8,128)}, f32[48,768]{1,0:T(8,128)}, /*...) custom-call(f32[256,1536]{1,0:T(8,128)} %get-tuple-element.88.dnorm,, ...), custom_call_target="tpu_custom_call" | custom-call | flops 1000000 | bytes 100000 | tf_op jit(solution)/shard_map/results/pallas_call | solution.py:2072

commit v10 on v9

--- a/solution.py
+++ b/solution.py
@@ -2031,7 +2031,7 @@
         )
         layer[at, :] = layer_in[at, :]
 
-    in_tiles(x.shape[0], into_input)
+    in_tiles(x.shape[0], into_input, 64)
     for i, ref in enumerate((gate, up, down)):
         ref[...] = ffn[i].astype(f32)
 
@@ -2067,7 +2067,9 @@
         return pl.BlockSpec((count // steps, columns), lambda i: (i, 0))
 
     def fixed(*shape):
-        return pl.BlockSpec(shape, lambda i: (0,) * len(shape))
+        return pl.BlockSpec(
+            shape, lambda i: (0,) * len(shape), pipeline_mode=pl.Buffered(buffer_count=1)
+        )
 
     return pl.pallas_call(
         results_body,

time: 313 us -> 313 us (level)
  no operation moved by 1% of the time
where the time goes in v10:
time: 313 us; the launch traced here: 312 us
  Pallas kernels  311 us (99%)
    pallas_call x1, Pallas kernels, feed(): pl.pallas_call(functools.partial(feed_body, n, m), out_shape=(jax.ShapeDt...  69.8 us
    pallas_call x1, Pallas kernels, attend_back(): pl.pallas_call(functools.partial(attend_back_body, n, m, factor, scale),...  66.9 us
    pallas_call x1, Pallas kernels, attend(): pl.pallas_call(functools.partial(attend_body, n, m, factor), out_shape=(j...  66.2 us
    pallas_call x1, Pallas kernels, entry(): pl.pallas_call(functools.partial(entry_body, n, m, heads, strip), out_sha...  54.8 us
    pallas_call x1, Pallas kernels, last(): pl.pallas_call(functools.partial(last_body, n, m), out_shape=(jax.ShapeDt...  47.8 us

profile of v10, /device:TPU:0, one launch (start us, length us, event | category | flops | bytes accessed | tf_op | source)
XLA Modules:
  0.0 311.8 jit_solution(16470600289598145915)
XLA Ops:
  0.6 54.8 %entry.1 = (bf16[1536,2048]{1,0:T(8,128)(2,1)}, bf16[2,2048,128]{2,1,0:T(8,128)(2,1)}, bf16[2048,128]{1,0:T(8,128)(2,1)}, bf16[2048,128]{1,0:T(8,128)(2,1)}, f32...) custom-call(bf16[256,1536]{1,0:T(8,128)(2,1)} %bitcast.8, ...), custom_call_target="tpu_custom_call" | custom-call | flops 1000000 | bytes 100000 | tf_op jit(solution)/shard_map/entry/pallas_call | solution.py:1241
  55.4 66.2 %attend.1 = (f32[2,2048,128]{2,1,0:T(8,128)}, f32[2,1,2048]{2,1,0:T(1,128)}, s32[1,2048]{1,0:T(1,128)}, bf16[2048,256]{1,0:T(8,128)(2,1)}, bf16[8,256,1536]{2,1,...) custom-call(bf16[2,2048,128]{2,1,0:T(8,128)(2,1)} %get-tuple-element.59.q.q_in, ...), custom_call_target="tpu_custom_call" | custom-call | flops 1000000 | bytes 100000 | tf_op jit(solution)/shard_map/attend/pallas_call | solution.py:1445
  121.6 69.8 %feed.1 = (f32[256,1536]{1,0:T(8,128)}, bf16[4,2,1536,128]{3,2,1,0:T(8,128)(2,1)}, bf16[2048,512]{1,0:T(8,128)(2,1)}, bf16[1536,512]{1,0:T(8,128)(2,1)}, bf16[4,1536,128]{2,1,0:T(8,128)(2,1)}) custom-call(bf16[256,1536]{1,0:T(8,128)(2,1)} %get-tuple-element.72.mine, bf16[8,256,1536]{2,1,0:T(8,128)(2,1)} %get-tuple-element.73.go, ...), custom_call_target="tpu_custom_call" | custom-call | flops 1000000 | bytes 100000 | tf_op jit(solution)/shard_map/feed/pallas_call | solution.py:1974
  191.4 66.9 %attend_back.1 = (bf16[2048,512]{1,0:T(8,128)(2,1)}, bf16[256,1536]{1,0:T(8,128)(2,1)}, bf16[4,48,1536]{2,1,0:T(8,128)(2,1)}, f32[256,1536]{1,0:T(8,128)}, f32[4...) custom-call(bf16[2,2048,128]{2,1,0:T(8,128)(2,1)} %get-tuple-element.59.q.q_in, ...), custom_call_target="tpu_custom_call" | custom-call | flops 1000000 | bytes 100000 | tf_op jit(solution)/shard_map/attend_back/pallas_call | solution.py:1694
  258.4 47.8 %last.1 = (f32[256,1536]{1,0:T(8,128)}, bf16[3,192,1024]{2,1,0:T(8,128)(2,1)}, bf16[8,48,384]{2,1,0:T(8,128)(2,1)}, bf16[4,48,1536]{2,1,0:T(8,128)(2,1)}, f32[4,1,48]{2,1,0:T(1,128)}) custom-call(bf16[2048,512]{1,0:T(8,128)(2,1)} %get-tuple-element.81.dqkv_in, bf16[1536,512]{1,0:T(8,128)(2,1)} %get-tuple-element.82.w_in, ...), custom_call_target="tpu_custom_call" | custom-call | flops 1000000 | bytes 100000 | tf_op jit(solution)/shard_map/last/pallas_call | solution.py:990
  306.2 5.5 %results.1 = (bf16[256,1536]{1,0:T(8,128)(2,1)}, f32[256,1536]{1,0:T(8,128)}, f32[1,48]{1,0:T(1,128)}, f32[48,1536]{1,0:T(8,128)}, f32[48,768]{1,0:T(8,128)}, /*...) custom-call(f32[256,1536]{1,0:T(8,128)} %get-tuple-element.88.dnorm,, ...), custom_call_target="tpu_custom_call" | custom-call | flops 1000000 | bytes 100000 | tf_op jit(solution)/shard_map/results/pallas_call | solution.py:2074
